TPU v7x, 256 devices: a whole 4x4x8 slice. The times are simulated.
256 devices in a mesh: seq: 8 (over x, core), exp: 32 (over z, y).
Axes of the slice: x: 4, y: 4, z: 8, core: 2. Of those that a mesh axis runs over, the one named last changes fastest.
Arguments:
- queries: bfloat16 [32, 1024, 2048], P('exp', 'seq'), may hold values from -14 to 14
- keys: bfloat16 [32, 1024, 2048], P('exp', 'seq'), may hold values from -6 to 6
- values: bfloat16 [32, 1024, 2048], P('exp', 'seq'), may hold values from -6 to 6
- out_grad: bfloat16 [32, 1024, 2048], P('exp', 'seq'), may hold values from -6 to 6
- norm_gain: float32 [2048], replicated, may hold values from 0.5 to 1.5
- gate_values: float32 [32, 1024, 2], P('exp', 'seq'), may hold values from 0.2 to 1
- expert_ids: int32 [32, 1024, 2], P('exp', 'seq'), may hold values from 0 to 63, all different within a row; in each aligned block of 128 rows (0 to 127, 128 to 255, ..., all dimensions but the last counted through in order) at most 5 rows name the same one
- tile_offsets: int32 [32, 16, 3], P('exp', 'seq'), may hold values from -2 to 2, as said below
- gate_weight: bfloat16 [32, 8, 2048, 512], P('exp', 'seq'), may hold values from -0.125 to 0.125
- up_weight: bfloat16 [32, 8, 2048, 512], P('exp', 'seq'), may hold values from -0.125 to 0.125
- down_weight: bfloat16 [32, 8, 512, 2048], P('exp', 'seq'), may hold values from -0.125 to 0.125
Outputs:
- key_grad: bfloat16 [32, 1024, 2048], P('exp', 'seq')
- value_grad: bfloat16 [32, 1024, 2048], P('exp', 'seq')
Inputs may be any that keep to these rules, and one draw needn't show every extreme that they name: `expert_ids`: a token's two ids differ; the tokens of one index pair (one device) name one expert at most 5 times. `tile_offsets`: each row holds 3 different offsets, the first of them 0.
All inputs are finite; a program needn't handle non-finite values.
Results may differ from a plain program's by a relative error of at most 0.013.
Values may be sent and summed in bfloat16 or wider, within the bound.
No kernel may reach another device: no remote copies, remote signals or barrier semaphores. Data moves between devices by JAX's collectives and lax.ppermute only.
A program may use at most 128 MiB of HBM per device.

v0:
```python
import jax
import jax.numpy as jnp
from jax import lax
from jax.sharding import PartitionSpec as P

HEAD_DIM = 128
TILE = 64


epsilon = 1e-06


def with_halo(cells, sides, width):
    for axis, dim in sides:
        count = lax.axis_size(axis)
        ends = count - 1
        head = lax.slice_in_dim(cells, 0, width, axis=dim)
        tail = lax.slice_in_dim(cells, cells.shape[dim] - width, cells.shape[dim], axis=dim)
        cells = jnp.concatenate(
            [
                lax.ppermute(tail, axis, [(i, (i + 1) % count) for i in range(ends)]),
                cells,
                lax.ppermute(head, axis, [((i + 1) % count, i) for i in range(ends)]),
            ],
            axis=dim,
        )
    return cells


def expert_part(rows_in, rows_grad, gate_w, up_w, down_w):
    part_width = gate_w.shape[1]
    both_w = jnp.concatenate([gate_w, up_w], axis=1)
    projected = jnp.dot(rows_in, both_w, preferred_element_type=jnp.float32)
    gate_proj = projected[:, :part_width]
    up_proj = projected[:, part_width:]
    hidden_grad = jnp.einsum("rd,fd->rf", rows_grad, down_w, preferred_element_type=jnp.float32)
    sig = jax.nn.sigmoid(gate_proj)
    grad_up = (hidden_grad * gate_proj * sig).astype(jnp.bfloat16)
    grad_gate = (hidden_grad * up_proj * sig * (1.0 + gate_proj * (1.0 - sig))).astype(jnp.bfloat16)
    both_grad = jnp.concatenate([grad_gate, grad_up], axis=1)
    total = jnp.einsum("rf,df->rd", both_grad, both_w, preferred_element_type=jnp.float32)
    return total.astype(jnp.bfloat16)


def on_device(
    queries,
    keys,
    values,
    out_grad,
    norm_gain,
    gate_values,
    expert_ids,
    tile_offsets,
    gate_weight,
    up_weight,
    down_weight,
):
    query_rows = queries[0]
    local_len, width = query_rows.shape
    heads = width // HEAD_DIM
    local_tiles = local_len // TILE
    halo_tiles = 2
    halo_len = halo_tiles * TILE
    ext_tiles = local_tiles + 2 * halo_tiles
    seq_count = lax.axis_size("seq")
    col_count = lax.axis_size("exp")
    group = seq_count // 2
    expert_count = 2 * col_count
    capacity = max(2, (5 * local_len + 2 * expert_count - 1) // (2 * expert_count))
    scale = HEAD_DIM ** (-0.5)
    key_value = jnp.stack([keys[0], values[0]])
    extended = with_halo(key_value, (("seq", 1),), halo_len)
    offsets = tile_offsets[0]
    neighbour_count = offsets.shape[1]
    tile_base = jnp.arange(local_tiles, dtype=jnp.int32)[:, None]
    ext_index = tile_base + halo_tiles + offsets
    global_tile = lax.axis_index("seq") * local_tiles + tile_base + offsets
    valid = (global_tile >= 0) & (global_tile < local_tiles * seq_count)
    key_mask = jnp.repeat(valid, TILE, axis=1)
    tile_shape = (ext_tiles, TILE, heads, HEAD_DIM)
    window_shape = (local_tiles, neighbour_count * TILE, heads, HEAD_DIM)
    key_tiles = extended[0].reshape(tile_shape)[ext_index].reshape(window_shape)
    value_tiles = extended[1].reshape(tile_shape)[ext_index].reshape(window_shape)
    query_tiles = query_rows.reshape(local_tiles, TILE, heads, HEAD_DIM)
    scores = (
        jnp.einsum("tqhd,tkhd->thqk", query_tiles, key_tiles, preferred_element_type=jnp.float32)
        * scale
    )
    scores = jnp.where(key_mask[:, None, None, :], scores, -jnp.inf)
    row_max = jnp.max(scores, axis=-1, keepdims=True)
    raised = jnp.exp(scores - row_max)
    attn_weights = raised / jnp.sum(raised, axis=-1, keepdims=True)
    weights_b = attn_weights.astype(jnp.bfloat16)
    attn_out = jnp.einsum(
        "thqk,tkhd->tqhd", weights_b, value_tiles, preferred_element_type=jnp.float32
    )
    attn_out = attn_out.reshape(local_len, width)
    inv_rms = lax.rsqrt(jnp.mean(attn_out * attn_out, axis=-1, keepdims=True) + epsilon)
    unit = attn_out * inv_rms
    normed = (unit * norm_gain).astype(jnp.bfloat16)
    grad_rows = out_grad[0]
    route_experts = expert_ids[0].reshape(-1)
    one_hot = (route_experts[:, None] == jnp.arange(expert_count, dtype=jnp.int32)[None, :]).astype(
        jnp.int32
    )
    rank_index = jnp.sum(jnp.cumsum(one_hot, axis=0) * one_hot, axis=1) - 1
    route_token = jnp.arange(2 * local_len, dtype=jnp.int32) // 2
    token_pair = jnp.stack([normed, grad_rows])
    route_pair = token_pair[:, route_token]
    part_gate = gate_weight[0, 0]
    part_up = up_weight[0, 0]
    part_down = down_weight[0, 0]
    half_index = route_experts % 2
    column = route_experts // 2
    slot_index = half_index * (col_count * capacity) + column * capacity + rank_index
    empty = jnp.zeros((2, 2 * col_count * capacity, width), jnp.bfloat16)
    send_pair = empty.at[:, slot_index].set(route_pair).reshape(2, 2, col_count, capacity, width)
    spread_pair = jnp.repeat(send_pair, group, axis=1)
    half_pair = lax.all_to_all(spread_pair, "seq", split_axis=1, concat_axis=1, tiled=True)
    expert_pair = lax.all_to_all(half_pair, "exp", split_axis=2, concat_axis=2, tiled=True)
    partial_value = expert_part(
        expert_pair[0].reshape(-1, width),
        expert_pair[1].reshape(-1, width),
        part_gate,
        part_up,
        part_down,
    )
    partial_value = partial_value.reshape(seq_count, col_count, capacity, width)
    backed = lax.all_to_all(partial_value, "exp", split_axis=1, concat_axis=1, tiled=True)
    homed = lax.all_to_all(backed, "seq", split_axis=0, concat_axis=0, tiled=True)
    summed = jnp.sum(homed.reshape(2, group, col_count, capacity, width), axis=1, dtype=jnp.float32)
    route_grad = summed.astype(jnp.bfloat16).reshape(2 * col_count * capacity, width)[slot_index]
    route_grad = route_grad.reshape(local_len, 2, width).astype(jnp.float32)
    normed_grad = jnp.sum(gate_values[0][:, :, None] * route_grad, axis=1)
    scaled = normed_grad * norm_gain
    attn_grad = grad_rows.astype(jnp.float32) + inv_rms * (
        scaled - unit * jnp.mean(scaled * unit, axis=-1, keepdims=True)
    )
    attn_grad_b = attn_grad.astype(jnp.bfloat16).reshape(local_tiles, TILE, heads, HEAD_DIM)
    prob_grad = jnp.einsum(
        "tqhd,tkhd->thqk", attn_grad_b, value_tiles, preferred_element_type=jnp.float32
    )
    inner_sum = jnp.sum(attn_weights * prob_grad, axis=-1, keepdims=True)
    score_grad = (attn_weights * (prob_grad - inner_sum)).astype(jnp.bfloat16)
    key_part = (
        jnp.einsum("thqk,tqhd->tkhd", score_grad, query_tiles, preferred_element_type=jnp.float32)
        * scale
    )
    value_part = jnp.einsum(
        "thqk,tqhd->tkhd", weights_b, attn_grad_b, preferred_element_type=jnp.float32
    )
    flat_index = ext_index.reshape(-1)
    part_shape = (local_tiles * neighbour_count, TILE, heads, HEAD_DIM)
    ext_grad = jnp.zeros((2, ext_tiles, TILE, heads, HEAD_DIM), jnp.float32)
    ext_grad = ext_grad.at[0, flat_index].add(key_part.reshape(part_shape))
    ext_grad = ext_grad.at[1, flat_index].add(value_part.reshape(part_shape))
    ext_grad = ext_grad.reshape(2, ext_tiles * TILE, width)
    rims = jnp.concatenate([ext_grad[:, :halo_len], ext_grad[:, -halo_len:]], axis=1)
    rims_in = with_halo(rims, (("seq", 1),), halo_len)
    inner_grad = ext_grad[:, halo_len : halo_len + local_len]
    inner_grad = inner_grad.at[:, :halo_len].add(rims_in[:, :halo_len])
    inner_grad = inner_grad.at[:, local_len - halo_len :].add(rims_in[:, -halo_len:])
    key_out = inner_grad[0].astype(jnp.bfloat16)[None]
    value_out = inner_grad[1].astype(jnp.bfloat16)[None]
    return (key_out, value_out)


def solution(mesh):
    return jax.shard_map(
        on_device,
        mesh=mesh,
        in_specs=(
            P("exp", "seq", None),
            P("exp", "seq", None),
            P("exp", "seq", None),
            P("exp", "seq", None),
            P(),
            P("exp", "seq", None),
            P("exp", "seq", None),
            P("exp", "seq", None),
            P("exp", "seq", None, None),
            P("exp", "seq", None, None),
            P("exp", "seq", None, None),
        ),
        out_specs=(P("exp", "seq", None), P("exp", "seq", None)),
        check_vma=False,
    )
```

profile of v0, /device:TPU:1, one launch (start us, length us, event | category | flops | bytes accessed | tf_op | source)
XLA Modules:
  0.0 863.1 jit_solution(793168862484973325)
XLA Ops:
  3.0 4.5 collective-permute-start
  14.4 4.8 collective-permute-done
  19.2 4.5 collective-permute-done.1
  49.5 11.7 %gather_fusion.2 = bf16[256,2,2048]{2,1,0:T(2,128)(2,1)} fusion(bf16[2,128,2048]{2,0,1:T(2,128)(2,1)} %copy.92, s32[1024]{0:T(1024)S(1)} %get-tuple-element.61), kind=kCustom, calls=%fused_computation.2 | custom fusion | bytes 4195328 | tf_op jit(solution)/shard_map/gather | solution.py:109
  64.0 32.5 %scatter_fusion = bf16[2,320,2048]{2,0,1:T(2,128)(2,1)} fusion(bf16[2,320,2048]{2,0,1:T(2,128)(2,1)} %broadcast_in_dim.27, s32[256]{0:T(256)S(1)} %bitcast.115, bf16[256,2,2048]{2,1,0:T(2,128)(2,1)} %gather_fusion.2), kind=kCustom, calls=%fused_computation.4 | custom fusion | bytes 6292480 | tf_op jit(solution)/shard_map/scatter | solution.py:117
  96.6 4.4 copy.93
  101.0 7.1 broadcast_in_dim.28
  108.1 122.8 %all_to_all.20 = bf16[2,8,32,5,2048]{4,2,3,0,1:T(8,128)(2,1)} all-to-all(bf16[2,8,32,5,2048]{4,2,3,0,1:T(8,128)(2,1)} %bitcast.96), channel_id=1, replica_groups=mesh['seq'=8,'exp'=32] {'seq'}, dimensions={1} | all-to-all | bytes 20971520 | tf_op jit(solution)/shard_map/all_to_all | solution.py:119
  230.9 13.8 %copy.94 = bf16[2,8,32,5,2048]{4,1,3,0,2:T(8,128)(2,1)} copy(bf16[2,8,32,5,2048]{4,2,3,0,1:T(8,128)(2,1)} %all_to_all.20) | data formatting | bytes 20971520 | tf_op jit(solution)/shard_map/all_to_all | solution.py:119
  244.7 241.0 %all_to_all.21 = bf16[2,8,32,5,2048]{4,1,3,0,2:T(8,128)(2,1)} all-to-all(bf16[2,8,32,5,2048]{4,1,3,0,2:T(8,128)(2,1)} %copy.94), channel_id=1, replica_groups=mesh['seq'=8,'exp'=32] {'exp'}, dimensions={2} | all-to-all | bytes 20971520 | tf_op jit(solution)/shard_map/all_to_all | solution.py:120
  485.7 10.2 %fusion.44 = (bf16[1,8,32,5,2048]{4,1,3,0,2:T(8,128)(2,1)}, bf16[1,8,32,5,2048]{4,1,3,0,2:T(8,128)(2,1)}) fusion(bf16[2,8,32,5,2048]{4,1,3,0,2:T(8,128)(2,1)} %all_to_all.21), kind=kLoop, calls=%fused_computation.108 | loop fusion | bytes 20971520 | tf_op jit(solution)/shard_map/slice | solution.py:122
  495.9 8.9 %copy.96 = bf16[1,8,32,5,2048]{4,3,2,1,0:T(8,128)(2,1)} copy(bf16[1,8,32,5,2048]{4,1,3,0,2:T(8,128)(2,1)} %get-tuple-element.44) | data formatting | bytes 10485760 | tf_op jit(solution)/shard_map/slice | solution.py:122
  504.8 10.0 %reshape_squeeze.23 = bf16[1280,2048]{1,0:T(8,128)(2,1)} reshape(bf16[1,8,32,5,2048]{4,3,2,1,0:T(8,128)(2,1)} %copy.96) | data formatting | bytes 10485760 | tf_op jit(solution)/shard_map/reshape;squeeze | solution.py:122
  514.8 8.9 %copy.95 = bf16[1,8,32,5,2048]{4,3,2,1,0:T(8,128)(2,1)} copy(bf16[1,8,32,5,2048]{4,1,3,0,2:T(8,128)(2,1)} %get-tuple-element.45) | data formatting | bytes 10485760 | tf_op jit(solution)/shard_map/slice | solution.py:123
  523.7 10.0 %reshape_squeeze.22 = bf16[1280,2048]{1,0:T(8,128)(2,1)} reshape(bf16[1,8,32,5,2048]{4,3,2,1,0:T(8,128)(2,1)} %copy.95) | data formatting | bytes 10485760 | tf_op jit(solution)/shard_map/reshape;squeeze | solution.py:123
  533.7 9.9 %fusion.1 = f32[1280,1024]{0,1:T(8,128)S(1)} fusion(bf16[1280,2048]{1,0:T(8,128)(2,1)} %reshape_squeeze.23, bf16[2048,512]{1,0:T(8,128)(2,1)} %bitcast.119, bf16[2048,512]{1,0:T(8,128)(2,1)} %bitcast.121), kind=kOutput, calls=%fused_computation.13 | convolution fusion | flops 5377097728 | bytes 14680064 | tf_op jit(solution)/shard_map/dot_general | solution.py:33
  543.7 3.7 fusion.4
  547.3 7.5 convolution_convert_fusion
  554.9 9.7 %reshape.494 = bf16[8,32,5,2048]{3,2,1,0:T(8,128)(2,1)} reshape(bf16[1280,2048]{1,0:T(8,128)(2,1)} %convolution_convert_fusion) | data formatting | bytes 10485760 | tf_op jit(solution)/shard_map/reshape | solution.py:128
  564.6 8.8 %copy.97 = bf16[8,32,5,2048]{3,0,2,1:T(8,128)(2,1)S(1)} copy(bf16[8,32,5,2048]{3,2,1,0:T(8,128)(2,1)} %reshape.494) | data formatting | bytes 10485760 | tf_op jit(solution)/shard_map/reshape | solution.py:128
  573.4 121.4 %all_to_all.22 = bf16[8,32,5,2048]{3,0,2,1:T(8,128)(2,1)S(1)} all-to-all(bf16[8,32,5,2048]{3,0,2,1:T(8,128)(2,1)S(1)} %copy.97), channel_id=1, replica_groups=mesh['seq'=8,'exp'=32] {'exp'}, dimensions={1} | all-to-all | bytes 10485760 | tf_op jit(solution)/shard_map/all_to_all | solution.py:129
  694.8 5.2 copy.98
  700.0 8.2 all-to-all-start.3
  709.9 58.5 %all-to-all-done.3 = bf16[8,32,5,2048]{3,1,2,0:T(8,128)(2,1)} async-done(((bf16[8,32,5,2048]{3,1,2,0:T(8,128)(2,1)}), bf16[8,32,5,2048]{3,1,2,0:T(8,128)(2,1)}, u32[]{:S(2)}, u32[]{:S(2)}) %all-to-all-start.3) | async-done | bytes 5242912 | tf_op jit(solution)/shard_map/all_to_all | solution.py:130
  768.3 3.5 bitcast_reduce_fusion
  789.9 3.5 copy.105
  795.7 3.5 copy.104
  802.4 8.7 %scatter_fusion.1 = f32[2,6,64,16,128]{4,3,2,1,0:T(8,128)} fusion(f32[2,6,64,16,128]{4,3,2,1,0:T(8,128)} %broadcast_in_dim.22, s32[6]{0:T(128)S(1)} %select_bitcast_fusion.1, f32[6,64,16,128]{3,2,1,0:T(8,128)} %bitcast.99), kind=kCustom, calls=%fused_computation.5 | custom fusion | flops 786432 | bytes 9437232 | tf_op jit(solution)/shard_map/scatter-add | solution.py:155
  811.1 8.7 %scatter_fusion.2 = f32[2,6,64,16,128]{4,3,2,1,0:T(8,128)} fusion(f32[2,6,64,16,128]{4,3,2,1,0:T(8,128)} %scatter_fusion.1, s32[6]{0:T(128)S(1)} %get-tuple-element.42, f32[6,64,16,128]{3,2,1,0:T(8,128)} %bitcast.98), kind=kCustom, calls=%fused_computation.6 | custom fusion | flops 786432 | bytes 9437232 | tf_op jit(solution)/shard_map/scatter-add | solution.py:156
  819.8 7.1 reshape.499
  834.0 21.0 %collective-permute-done.2 = f32[2,128,2048]{2,1,0:T(8,128)S(1)} collective-permute-done((f32[2,128,2048]{2,1,0:T(8,128)S(1)}, f32[2,128,2048]{2,1,0:T(8,128)S(1)}, u32[]{:S(2)}, u32[]{:S(2)}) %collective-permute-start.2) | collective-permute-done | bytes 2097184 | tf_op jit(solution)/shard_map/ppermute | solution.py:21
  855.0 4.4 collective-permute-done.3
  (103 shorter events, 73.2 us)
Async XLA Ops:
  0.6 543.0 %copy-start = (bf16[1,1,512,2048]{3,2,1,0:T(8,128)(2,1)S(1)}, bf16[1,1,512,2048]{3,2,1,0:T(8,128)(2,1)}, u32[]{:S(2)}) copy-start(bf16[1,1,512,2048]{3,2,1,0:T(8,128)(2,1)} %param.29) | copy-start | bytes 6291460
  0.6 9.8 %copy-start.11 = (s32[1,128,2]{1,2,0:T(2,128)S(1)}, s32[1,128,2]{1,2,0:T(2,128)}, u32[]{:S(2)}) copy-start(s32[1,128,2]{1,2,0:T(2,128)} %param.25) | copy-start | bytes 3076
  0.7 10.1 %copy-start.10 = (s32[1,2,3]{2,1,0:T(2,128)S(1)}, s32[1,2,3]{2,1,0:T(2,128)}, u32[]{:S(2)}) copy-start(s32[1,2,3]{2,1,0:T(2,128)} %param.26) | copy-start | bytes 76
  3.0 16.2 %collective-permute-start = (bf16[2,128,2048]{2,1,0:T(8,128)(2,1)S(1)}, bf16[2,128,2048]{2,1,0:T(8,128)(2,1)}, u32[]{:S(2)}, u32[]{:S(2)}) collective-permute-start(bf16[2,128,2048]{2,1,0:T(8,128)(2,1)S(1)} %constant_dynamic-update-slice_fusion), channel_id=1, source_target_pairs={{0,32},{32,64},{64,96},{96,128},{128,160},{160,192},{192,224},{1,3... | collective-permute-start | bytes 3145736 | tf_op jit(solution)/shard_map/ppermute | solution.py:21
  7.5 16.2 %collective-permute-start.1 = (bf16[2,128,2048]{2,1,0:T(8,128)(2,1)S(1)}, bf16[2,128,2048]{2,1,0:T(8,128)(2,1)}, u32[]{:S(2)}, u32[]{:S(2)}) collective-permute-start(bf16[2,128,2048]{2,1,0:T(8,128)(2,1)S(1)} %constant_dynamic-update-slice_fusion), channel_id=1, source_target_pairs={{32,0},{64,32},{96,64},{128,96},{160,128},{192,160},{224,192},{33,... | collective-permute-start | bytes 3145736 | tf_op jit(solution)/shard_map/ppermute | solution.py:23
  32.3 3.4 copy-start.5
  38.3 1.4 copy-start.7
  39.2 1.6 copy-start.15
  40.8 4.1 copy-start.9
  533.7 9.9 %copy-start.2 = (bf16[1280,2048]{1,0:T(8,128)(2,1)S(1)}, bf16[1280,2048]{1,0:T(8,128)(2,1)}, u32[]{:S(2)}) copy-start(bf16[1280,2048]{1,0:T(8,128)(2,1)} %reshape_squeeze.22) | copy-start | bytes 15728644
  543.6 3.7 copy-start.13
  543.6 3.7 copy-start.14
  700.0 8.3 copy-start.12
  700.0 8.4 copy-start.4
  700.0 68.3 %all-to-all-start.3 = ((bf16[8,32,5,2048]{3,1,2,0:T(8,128)(2,1)}), bf16[8,32,5,2048]{3,1,2,0:T(8,128)(2,1)}, u32[]{:S(2)}, u32[]{:S(2)}) async-start(bf16[8,32,5,2048]{3,1,2,0:T(8,128)(2,1)} %copy.98), calls=%async_computation.3 | async-start | bytes 10485760 | tf_op jit(solution)/shard_map/all_to_all | solution.py:130
  784.4 1.2 copy-start.3
  785.1 1.7 copy-start.16
  786.7 1.4 copy-start.8
  789.8 3.5 copy-start.6
  829.5 25.5 %collective-permute-start.2 = (f32[2,128,2048]{2,1,0:T(8,128)S(1)}, f32[2,128,2048]{2,1,0:T(8,128)S(1)}, u32[]{:S(2)}, u32[]{:S(2)}) collective-permute-start(f32[2,128,2048]{2,1,0:T(8,128)S(1)} %get-tuple-element.48), channel_id=1, source_target_pairs={{0,32},{32,64},{64,96},{96,128},{128,160},{160,192},{192,224},{1,3... | collective-permute-start | bytes 6291464 | tf_op jit(solution)/shard_map/ppermute | solution.py:21
  832.1 27.4 %collective-permute-start.3 = (f32[2,128,2048]{2,1,0:T(8,128)S(1)}, f32[2,128,2048]{2,1,0:T(8,128)S(1)}, u32[]{:S(2)}, u32[]{:S(2)}) collective-permute-start(f32[2,128,2048]{2,1,0:T(8,128)S(1)} %get-tuple-element.49), channel_id=1, source_target_pairs={{32,0},{64,32},{96,64},{128,96},{160,128},{192,160},{224,192},{33,... | collective-permute-start | bytes 6291464 | tf_op jit(solution)/shard_map/ppermute | solution.py:23
  859.4 3.2 copy-start.1
where the time goes:
time: 874 us; the launch traced here: 863 us
  blocking collectives  485 us (55%)
  local copies, waits for them, and re-layouts  199 us (23%)
  waiting for transfers between devices  93.2 us (11%)
  other arithmetic  33.6 us (4%)
  matrix products  30 us (3%)
  starting transfers between devices  20.1 us (2%)
    all_to_all x1, blocking collectives, on_device(): lax.all_to_all(half_pair, 'exp', split_axis=2, concat_axis=2, tiled=True)  241 us
    all_to_all x1, blocking collectives, on_device(): lax.all_to_all(spread_pair, 'seq', split_axis=1, concat_axis=1, tiled=True)  123 us
    all_to_all x1, blocking collectives, on_device(): lax.all_to_all(partial_value, 'exp', split_axis=1, concat_axis=1, tiled=T...  121 us
    all_to_all x1, waiting for transfers between devices, on_device(): lax.all_to_all(backed, 'seq', split_axis=0, concat_axis=0, tiled=True)  58.5 us
    scatter x1, local copies, waits for them, and re-layouts, on_device(): empty.at[:, slot_index].set(route_pair)  32.5 us
    ppermute x2, waiting for transfers between devices, with_halo(): lax.ppermute(tail, axis, [(i, (i + 1) % count) for i in range(ends)])  25.9 us
    slice x2, local copies, waits for them, and re-layouts, on_device(): expert_pair[0].reshape(-1, width)  19.1 us
    reshape x2, local copies, waits for them, and re-layouts, on_device(): partial_value = partial_value.reshape(seq_count, col_count, capacity, width)  18.6 us
  transfers between devices with their start and end apart: 5, of which 5 were waited for; matrix products, arithmetic and copies ran while one was open for 1% of the time, Pallas kernels for 0%

commit v1 on v0

v1 whole, which is shorter than its diff:
```python
import jax
import jax.numpy as jnp
import numpy as np
from jax import lax
from jax.experimental import pallas as pl
from jax.experimental.pallas import tpu as pltpu
from jax.sharding import PartitionSpec as P

HEAD_DIM = 128
TILE = 64
NBR = 3
CAP = 5
PIECES = 8
GROUP = 8
EPSILON = 1e-06
MICRO = 1 << 30
F32 = jnp.float32
BF16 = jnp.bfloat16

CELL = PIECES * CAP
CHUNK = GROUP * CELL
ROWS = GROUP * CAP


def shuffle_matrix():
    out = np.zeros((CHUNK, CHUNK), np.float32)
    for d in range(GROUP):
        for q in range(PIECES):
            for r in range(CAP):
                out[d * CELL + q * CAP + r, q * ROWS + d * CAP + r] = 1.0
    return out


def dot(a, b):
    return jnp.dot(a, b, preferred_element_type=F32)


def dot_nt(a, b):
    return lax.dot_general(a, b, (((1,), (1,)), ((), ())), preferred_element_type=F32)


def dot_tn(a, b):
    return lax.dot_general(a, b, (((0,), (0,)), ((), ())), preferred_element_type=F32)


def to_wire(rows_ref, base, perm, chunk, piece):
    start = base + chunk * ROWS
    stacked = jnp.concatenate(
        [rows_ref[start : start + ROWS, q * piece : (q + 1) * piece] for q in range(PIECES)], axis=0
    )
    return dot(perm, stacked.astype(BF16)).astype(BF16)


def from_wire(block_ref, rows_ref, base, perm_t, chunks, piece):
    if not isinstance(block_ref, list):
        block_ref = [block_ref[c * CHUNK : (c + 1) * CHUNK, :] for c in range(chunks)]
    for pair in range(chunks // 2):
        low = dot(perm_t, block_ref[2 * pair])
        high = dot(perm_t, block_ref[2 * pair + 1])
        start = base + 2 * pair * ROWS
        for q in range(PIECES):
            both = jnp.concatenate(
                [low[q * ROWS : (q + 1) * ROWS], high[q * ROWS : (q + 1) * ROWS]], axis=0
            )
            rows_ref[start : start + 2 * ROWS, q * piece : (q + 1) * piece] = both.astype(BF16)


def slot_rows(ids_ref, half, experts):
    tokens = ids_ref.shape[1]
    first = ids_ref[0:1, :]
    second = ids_ref[1:2, :]
    names = lax.broadcasted_iota(jnp.int32, (experts, tokens), 0)
    hot0 = (names == first).astype(F32)
    hot1 = (names == second).astype(F32)
    before = (
        lax.broadcasted_iota(jnp.int32, (tokens, tokens), 0)
        < lax.broadcasted_iota(jnp.int32, (tokens, tokens), 1)
    ).astype(F32).astype(BF16)
    seen0 = dot(hot0.astype(BF16), before)
    seen1 = dot(hot1.astype(BF16), before) + jnp.sum(hot0, axis=1, keepdims=True)
    rank0 = jnp.sum(hot0 * seen0, axis=0, keepdims=True).astype(jnp.int32)
    rank1 = jnp.sum(hot1 * seen1, axis=0, keepdims=True).astype(jnp.int32)
    slots = (experts // 2) * CAP
    slot0 = ((first & 1) ^ half) * slots + (first >> 1) * CAP + rank0
    slot1 = ((second & 1) ^ half) * slots + (second >> 1) * CAP + rank1
    return slot0, slot1


def slot_cols(ids_ref, half, experts):
    tokens = ids_ref.shape[0]
    first = ids_ref[:, 0:1]
    second = ids_ref[:, 1:2]
    names = lax.broadcasted_iota(jnp.int32, (tokens, experts), 1)
    hot0 = (names == first).astype(F32)
    hot1 = (names == second).astype(F32)
    before = (
        lax.broadcasted_iota(jnp.int32, (tokens, tokens), 1)
        < lax.broadcasted_iota(jnp.int32, (tokens, tokens), 0)
    ).astype(F32).astype(BF16)
    seen0 = dot(before, hot0.astype(BF16))
    seen1 = dot(before, hot1.astype(BF16)) + jnp.sum(hot0, axis=0, keepdims=True)
    rank0 = jnp.sum(hot0 * seen0, axis=1, keepdims=True).astype(jnp.int32)
    rank1 = jnp.sum(hot1 * seen1, axis=1, keepdims=True).astype(jnp.int32)
    slots = (experts // 2) * CAP
    slot0 = ((first & 1) ^ half) * slots + (first >> 1) * CAP + rank0
    slot1 = ((second & 1) ^ half) * slots + (second >> 1) * CAP + rank1
    return slot0, slot1


def place_rows(ids_ref, half, experts, x, rows_ref):
    slot0, slot1 = slot_rows(ids_ref, half, experts)
    places = lax.broadcasted_iota(jnp.int32, (rows_ref.shape[0], x.shape[0]), 0)
    hot = ((places == slot0) | (places == slot1)).astype(F32).astype(BF16)
    rows_ref[...] = dot(hot, x)


def send_rows(seq_ref, ids_ref, x, perm_ref, out_ref, rows_ref):
    columns = out_ref.shape[0]
    piece = out_ref.shape[3]
    place_rows(ids_ref, seq_ref[0] // 4, 2 * columns, x, rows_ref)
    perm = perm_ref[...]
    for rel in range(2):
        for chunk in range(columns // GROUP):
            block = to_wire(rows_ref, rel * columns * CAP, perm, chunk, piece)
            out_ref[chunk * GROUP : (chunk + 1) * GROUP, rel] = block.reshape(GROUP, CELL, piece)


def grad_kernel(seq_ref, ids_ref, x_ref, perm_ref, out_ref, rows_ref):
    send_rows(seq_ref, ids_ref, x_ref[...], perm_ref, out_ref, rows_ref)


def tile_places(seq_ref, offs_ref, tile, tiles, total):
    places = []
    valid = []
    for m in range(NBR):
        off = offs_ref[tile, m]
        places.append(pl.multiple_of((tile + 2 + off) * TILE, TILE))
        where = seq_ref[0] * tiles + tile + off
        valid.append((where >= 0) & (where < total))
    return places, valid


def fill_halo(dst_ref, left_ref, own_ref, right_ref):
    count = own_ref.shape[0]
    dst_ref[0:count, :] = left_ref[...]
    dst_ref[count : 2 * count, :] = own_ref[...]
    dst_ref[2 * count : 3 * count, :] = right_ref[...]


def forward_kernel(
    seq_ref, offs_ref, ids_ref, q_ref, kl_ref, k_ref, kr_ref, vl_ref, v_ref, vr_ref, gain_ref,
    perm_ref, wts_ref, unit_ref, inv_ref, sent_ref, kx_ref, vx_ref, out_ref, rows_ref, total_tiles,
):
    fill_halo(kx_ref, kl_ref, k_ref, kr_ref)
    fill_halo(vx_ref, vl_ref, v_ref, vr_ref)
    count, width = q_ref.shape
    heads = width // HEAD_DIM
    tiles = count // TILE
    scale = HEAD_DIM ** (-0.5)
    lane = lax.broadcasted_iota(jnp.int32, (TILE, NBR * TILE), 1) // TILE
    spots = []
    biases = []
    for t in range(tiles):
        places, valid = tile_places(seq_ref, offs_ref, t, tiles, total_tiles)
        bias = jnp.zeros((TILE, NBR * TILE), F32)
        for m in range(NBR):
            lost = jnp.where(valid[m], 0.0, -jnp.inf).astype(F32)
            bias = jnp.where(lane == m, lost, bias)
        spots.append(places)
        biases.append(bias)

    def one_head(h):
        lanes = pl.ds(pl.multiple_of(h * HEAD_DIM, HEAD_DIM), HEAD_DIM)
        for t in range(tiles):
            rows = slice(t * TILE, (t + 1) * TILE)
            k3 = jnp.concatenate([kx_ref[pl.ds(p, TILE), lanes] for p in spots[t]], axis=0)
            v3 = jnp.concatenate([vx_ref[pl.ds(p, TILE), lanes] for p in spots[t]], axis=0)
            scores = dot_nt(q_ref[rows, lanes], k3) * scale + biases[t]
            raised = jnp.exp(scores - jnp.max(scores, axis=-1, keepdims=True))
            weights = raised / jnp.sum(raised, axis=-1, keepdims=True)
            wts_ref[t * heads + h] = weights
            out_ref[rows, lanes] = dot(weights.astype(BF16), v3)

    def body(step, carry):
        for u in range(4):
            one_head(step * 4 + u)
        return carry

    lax.fori_loop(0, heads // 4, body, 0)
    out = out_ref[...]
    inv = lax.rsqrt(jnp.mean(out * out, axis=-1, keepdims=True) + EPSILON)
    unit = out * inv
    unit_ref[...] = unit
    inv_ref[...] = jnp.broadcast_to(inv, inv_ref.shape)
    normed = (unit * gain_ref[...]).astype(BF16)
    send_rows(seq_ref, ids_ref, normed, perm_ref, sent_ref, rows_ref)


def hidden_kernel(
    g0_ref, g1_ref, g2_ref, g3_ref, perm_t_ref, down0_ref, down1_ref, o0_ref, o1_ref, o2_ref,
    rows_ref, w_ref, sems,
):
    copies = [
        pltpu.make_async_copy(src, w_ref.at[i], sems.at[i])
        for i, src in enumerate((down0_ref, down1_ref))
    ]
    for copy in copies:
        copy.start()
    piece = g0_ref.shape[1]
    chunks = g0_ref.shape[0] // CHUNK
    slots = chunks * ROWS
    perm_t = perm_t_ref[...]
    for b, block in enumerate((g0_ref, g1_ref, g2_ref, g3_ref)):
        from_wire(block, rows_ref, b * slots, perm_t, chunks, piece)
    part = down0_ref.shape[0]
    for i, copy in enumerate(copies):
        copy.wait()
        cols = slice(i * part, (i + 1) * part)
        both = dot_nt(rows_ref[...], w_ref[i])
        o0_ref[:, cols] = both[:slots]
        o1_ref[:, cols] = both[slots : 3 * slots]
        o2_ref[:, cols] = both[3 * slots :]


def expert_kernel(*refs, blocks):
    ins = refs[:blocks]
    hg_ref, perm_ref, perm_t_ref = refs[blocks : blocks + 3]
    weights = refs[blocks + 3 : blocks + 7]
    outs = refs[blocks + 7 : 2 * blocks + 7]
    rows_ref, w_ref, act_ref, total_ref, sems = refs[2 * blocks + 7 :]
    copies = [pltpu.make_async_copy(src, w_ref.at[i], sems.at[i]) for i, src in enumerate(weights)]
    for copy in copies:
        copy.start()
    piece = ins[0].shape[1]
    chunks = ins[0].shape[0] // CHUNK
    perm_t = perm_t_ref[...]
    for b, block in enumerate(ins):
        from_wire(block, rows_ref, b * chunks * ROWS, perm_t, chunks, piece)
    part = w_ref.shape[2]
    for i in range(2):
        copies[2 * i].wait()
        gate_proj = dot(rows_ref[...], w_ref[2 * i])
        copies[2 * i + 1].wait()
        up_proj = dot(rows_ref[...], w_ref[2 * i + 1])
        hidden = hg_ref[:, i * part : (i + 1) * part]
        sig = jax.nn.sigmoid(gate_proj)
        act_ref[2 * i + 1] = (hidden * gate_proj * sig).astype(BF16)
        act_ref[2 * i] = (hidden * up_proj * sig * (1.0 + gate_proj * (1.0 - sig))).astype(BF16)
    width = total_ref.shape[1]
    for n in range(width // 512):
        cols = slice(n * 512, (n + 1) * 512)
        total = dot_nt(act_ref[0], w_ref[0, cols, :])
        for i in range(1, 4):
            total = total + dot_nt(act_ref[i], w_ref[i, cols, :])
        total_ref[:, cols] = total
    perm = perm_ref[...]
    for b, dst in enumerate(outs):
        for chunk in range(chunks):
            block = to_wire(total_ref, b * chunks * ROWS, perm, chunk, piece)
            dst[chunk * CHUNK : (chunk + 1) * CHUNK, :] = block


def backward_kernel(
    seq_ref, offs_ref, ids_ref, gates_ref, home_ref, grad_ref, unit_ref, inv_ref, q_ref,
    vl_ref, v_ref, vr_ref, wts_ref, gain_ref, perm_t_ref, k_out_ref, v_out_ref, left_ref,
    right_ref, vx_ref, rows_ref, ag_ref, ka_ref, va_ref, total_tiles,
):
    count, width = q_ref.shape
    heads = width // HEAD_DIM
    tiles = count // TILE
    scale = HEAD_DIM ** (-0.5)
    fill_halo(vx_ref, vl_ref, v_ref, vr_ref)
    ka_ref[...] = jnp.zeros_like(ka_ref)
    va_ref[...] = jnp.zeros_like(va_ref)
    columns, _, _, piece = home_ref.shape
    chunks = columns // GROUP
    perm_t = perm_t_ref[...]
    for rel in range(2):
        blocks = [
            home_ref[c * GROUP : (c + 1) * GROUP, rel].reshape(CHUNK, piece) for c in range(chunks)
        ]
        from_wire(blocks, rows_ref, rel * chunks * ROWS, perm_t, chunks, piece)
    slot0, slot1 = slot_cols(ids_ref, seq_ref[0] // 4, 2 * columns)
    places = lax.broadcasted_iota(jnp.int32, (count, rows_ref.shape[0]), 1)
    mix = jnp.where(places == slot0, gates_ref[:, 0:1], 0.0)
    mix = jnp.where(places == slot1, gates_ref[:, 1:2], mix)
    high = mix.astype(BF16)
    low = (mix - high.astype(F32)).astype(BF16)
    normed_grad = dot(high, rows_ref[...]) + dot(low, rows_ref[...])
    scaled = normed_grad * gain_ref[...]
    unit = unit_ref[...]
    inner = jnp.mean(scaled * unit, axis=-1, keepdims=True)
    attn_grad = grad_ref[...].astype(F32) + inv_ref[:, 0:1] * (scaled - unit * inner)
    ag_ref[...] = attn_grad.astype(BF16)
    spots = [tile_places(seq_ref, offs_ref, t, tiles, total_tiles)[0] for t in range(tiles)]

    def one_head(h):
        lanes = pl.ds(pl.multiple_of(h * HEAD_DIM, HEAD_DIM), HEAD_DIM)
        for t in range(tiles):
            rows = slice(t * TILE, (t + 1) * TILE)
            v3 = jnp.concatenate([vx_ref[pl.ds(p, TILE), lanes] for p in spots[t]], axis=0)
            ag = ag_ref[rows, lanes]
            weights = wts_ref[t * heads + h]
            prob_grad = dot_nt(ag, v3)
            sums = jnp.sum(weights * prob_grad, axis=-1, keepdims=True)
            score_grad = (weights * (prob_grad - sums)).astype(BF16)
            key_part = dot_tn(score_grad, q_ref[rows, lanes]) * scale
            value_part = dot_tn(weights.astype(BF16), ag)
            for m in range(NBR):
                at = pl.ds(spots[t][m], TILE)
                ka_ref[at, lanes] += key_part[m * TILE : (m + 1) * TILE]
                va_ref[at, lanes] += value_part[m * TILE : (m + 1) * TILE]

    def body(step, carry):
        for u in range(4):
            one_head(step * 4 + u)
        return carry

    lax.fori_loop(0, heads // 4, body, 0)
    k_out_ref[...] = ka_ref[count : 2 * count, :]
    v_out_ref[...] = va_ref[count : 2 * count, :]
    left_ref[0] = ka_ref[0:count, :].astype(BF16)
    left_ref[1] = va_ref[0:count, :].astype(BF16)
    right_ref[0] = ka_ref[2 * count : 3 * count, :].astype(BF16)
    right_ref[1] = va_ref[2 * count : 3 * count, :].astype(BF16)


def call(body, outs, kinds, scratch, name, flops):
    spaces = {"s": pltpu.SMEM, "v": pltpu.VMEM, "a": pl.ANY}
    return pl.pallas_call(
        body,
        out_shape=outs,
        in_specs=[pl.BlockSpec(memory_space=spaces[kind]) for kind in kinds],
        out_specs=jax.tree.map(lambda _: pl.BlockSpec(memory_space=pltpu.VMEM), outs),
        scratch_shapes=scratch,
        compiler_params=pltpu.CompilerParams(vmem_limit_bytes=56 * 1024 * 1024),
        cost_estimate=pl.CostEstimate(flops=flops, transcendentals=0, bytes_accessed=1 << 20),
        name=name,
    )


def shape(dims, kind):
    return jax.ShapeDtypeStruct(dims, kind)


def on_device(
    queries, keys, values, out_grad, norm_gain, gate_values, expert_ids, tile_offsets, gate_weight,
    up_weight, down_weight,
):
    count, width = queries.shape[1:]
    heads = width // HEAD_DIM
    tiles = count // TILE
    seq_count = lax.axis_size("seq")
    columns = lax.axis_size("exp")
    total_tiles = tiles * seq_count
    piece = width // PIECES
    slots = columns * CAP
    seq = lax.axis_index("seq").astype(jnp.int32).reshape(1)
    ids = expert_ids[0]
    ids_t = ids.T
    gain = norm_gain.reshape(1, width)
    perm = jnp.asarray(shuffle_matrix(), BF16)
    perm_t = jnp.asarray(shuffle_matrix().T, BF16)
    q, k, v, grad = queries[0], keys[0], values[0], out_grad[0]
    gate, up, down = gate_weight[0, 0], up_weight[0, 0], down_weight[0, 0]
    wire = (columns, 2, CELL, piece)
    flat = (columns * CELL, piece)

    up_by = [(i, i + 1) for i in range(seq_count - 1)]
    down_by = [(i + 1, i) for i in range(seq_count - 1)]

    def swap(x, bits):
        return lax.ppermute(x, "seq", [(i, i ^ bits) for i in range(seq_count)])

    def exchange(x):
        return lax.all_to_all(x, "exp", split_axis=0, concat_axis=0, tiled=True)

    kl, kr = lax.ppermute(k, "seq", up_by), lax.ppermute(k, "seq", down_by)
    vl, vr = lax.ppermute(v, "seq", up_by), lax.ppermute(v, "seq", down_by)

    barrier = lax.optimization_barrier
    sent_grad = call(
        grad_kernel, shape(wire, BF16), "svvv", [pltpu.VMEM((2 * slots, width), F32)],
        "place_grad", 4 * MICRO,
    )(seq, ids_t, grad, perm)
    got_grad = exchange(sent_grad)
    gate_s, up_s, down_s = swap(gate, 1), swap(up, 1), swap(down, 1)

    q_after, _ = barrier((q, sent_grad))
    wts, unit, inv, sent = call(
        lambda *refs: forward_kernel(*refs, total_tiles=total_tiles),
        (
            shape((tiles * heads, TILE, NBR * TILE), F32),
            shape((count, width), F32),
            shape((count, HEAD_DIM), F32),
            shape(wire, BF16),
        ),
        "ssv" + "v" * 9,
        [
            pltpu.VMEM((3 * count, width), BF16),
            pltpu.VMEM((3 * count, width), BF16),
            pltpu.VMEM((count, width), F32),
            pltpu.VMEM((2 * slots, width), F32),
        ],
        "attention", 16 * MICRO,
    )(seq, tile_offsets[0], ids_t, q_after, kl, k, kr, vl, v, vr, gain, perm)

    sent, got_grad = barrier((sent, got_grad))
    got = exchange(sent)
    g0, grad_oth = got_grad[:, 0].reshape(flat), got_grad[:, 1].reshape(flat)
    g1, g2, g3 = swap(grad_oth, 6), swap(g0, 2), swap(grad_oth, 4)
    got, g1, g2, g3 = barrier((got, g1, g2, g3))
    n0, oth = got[:, 0].reshape(flat), got[:, 1].reshape(flat)
    n1, n2 = swap(oth, 6), swap(n0, 2)

    part = down.shape[0]
    hidden = call(
        hidden_kernel,
        tuple(shape((m * slots, 2 * part), F32) for m in (1, 2, 1)),
        "vvvvvaa",
        [
            pltpu.VMEM((4 * slots, width), BF16),
            pltpu.VMEM((2, part, width), BF16),
            pltpu.SemaphoreType.DMA((2,)),
        ],
        "hidden", 8 * MICRO,
    )(g0, g1, g2, g3, perm_t, down, down_s)

    def expert(ins, hg, micros):
        blocks = len(ins)
        return call(
            lambda *refs: expert_kernel(*refs, blocks=blocks),
            (shape(flat, BF16),) * blocks,
            "v" * (blocks + 3) + "aaaa",
            [
                pltpu.VMEM((blocks * slots, width), BF16),
                pltpu.VMEM((4, width, part), BF16),
                pltpu.VMEM((4, blocks * slots, part), BF16),
                pltpu.VMEM((blocks * slots, width), F32),
                pltpu.SemaphoreType.DMA((4,)),
            ],
            "expert", micros * MICRO,
        )(*ins, hg, perm, perm_t, gate, up, gate_s, up_s)

    (p0,) = expert((n0,), hidden[0], 7)
    p0, n1, n2, oth = barrier((p0, n1, n2, oth))
    n3 = swap(oth, 4)
    p1, p2 = expert((n1, n2), hidden[1], 11)
    (p3,) = expert((n3,), hidden[2], 7)
    h1, h2 = swap(p1, 6), swap(p2, 2)
    h3 = swap(p3, 4)
    own = (p0.astype(F32) + h2.astype(F32)).astype(BF16).reshape(columns, 1, CELL, piece)
    oth = (h1.astype(F32) + h3.astype(F32)).astype(BF16).reshape(columns, 1, CELL, piece)
    home = exchange(jnp.concatenate([own, oth], axis=1))

    k_own, v_own, left, right = call(
        lambda *refs: backward_kernel(*refs, total_tiles=total_tiles),
        (
            shape((count, width), F32),
            shape((count, width), F32),
            shape((2, count, width), BF16),
            shape((2, count, width), BF16),
        ),
        "ss" + "v" * 13,
        [
            pltpu.VMEM((3 * count, width), BF16),
            pltpu.VMEM((2 * slots, width), BF16),
            pltpu.VMEM((count, width), BF16),
            pltpu.VMEM((3 * count, width), F32),
            pltpu.VMEM((3 * count, width), F32),
        ],
        "attention_grad", 13 * MICRO,
    )(
        seq, tile_offsets[0], ids, gate_values[0], home, grad, unit, inv, q, vl, v, vr, wts, gain,
        perm_t,
    )
    from_right = lax.ppermute(left, "seq", down_by).astype(F32)
    from_left = lax.ppermute(right, "seq", up_by).astype(F32)
    key_out = (k_own + from_right[0] + from_left[0]).astype(BF16)
    value_out = (v_own + from_right[1] + from_left[1]).astype(BF16)
    return (key_out[None], value_out[None])


def solution(mesh):
    rows = P("exp", "seq", None)
    weights = P("exp", "seq", None, None)
    return jax.shard_map(
        on_device,
        mesh=mesh,
        in_specs=(rows, rows, rows, rows, P(), rows, rows, rows, weights, weights, weights),
        out_specs=(rows, rows),
        check_vma=False,
    )
```

time: 874 us -> 243 us (0.28); the launches traced: 863 us -> 242 us
  blocking collectives: 485 us -> 0 us
  local copies, waits for them, and re-layouts: 199 us -> 5.09 us
  Pallas kernels: 0 us -> 70.6 us
  starting transfers between devices: 20.1 us -> 62.7 us
  other arithmetic: 33.6 us -> 3.37 us
  matrix products: 30 us -> 0 us
    all_to_all x3 -> x0, blocking collectives: 485 us -> none  [the longest x1 241 us: on_device(): lax.all_to_all(half_pair, 'exp', split_axis=2, concat_axis=2, tiled=True)]
    pallas_call x0 -> x7, Pallas kernels: none -> 70.6 us  [the longest x3 30.3 us: expert(): call(lambda *refs: expert_kernel(*refs, blocks=blocks), (shape(flat, BF16...]
    ppermute x4 -> x18, waiting for transfers between devices: 34.8 us -> 69.9 us  [the longest x12 46.9 us: swap(): return lax.ppermute(x, 'seq', [(i, i ^ bits) for i in range(seq_count)])]
    reshape x6 -> x0, local copies, waits for them, and re-layouts: 35 us -> none  [the longest x2 18.6 us: on_device(): partial_value = partial_value.reshape(seq_count, col_count, capacity, width)]
    scatter x1 -> x0, local copies, waits for them, and re-layouts: 32.5 us -> none  [on_device(): empty.at[:, slot_index].set(route_pair)]
    slice x5 -> x2, local copies, waits for them, and re-layouts: 31.6 us -> 0.17 us  [the longest x1 0.09 us: on_device(): g0, grad_oth = (got_grad[:, 0].reshape(flat), got_grad[:, 1].reshape(flat))]
    dot_general x8 -> x0, matrix products: 30 us -> none  [the longest x1 9.88 us: expert_part(): projected = jnp.dot(rows_in, both_w, preferred_element_type=jnp.float32)]
    all_to_all x1 -> x3, waiting for transfers between devices: 58.5 us -> 29.3 us  [exchange(): return lax.all_to_all(x, 'exp', split_axis=0, concat_axis=0, tiled=True)]
  transfers between devices with their start and end apart: 5 -> 21, of which waited for: 5 -> 12; matrix products, arithmetic and copies ran while one was open for 1% -> 1% of each run, Pallas kernels for 0% -> 22%
where the time goes in v1:
time: 243 us; the launch traced here: 242 us
  waiting for transfers between devices  99.2 us (41%)
  Pallas kernels  70.6 us (29%)
  starting transfers between devices  62.7 us (26%)
  local copies, waits for them, and re-layouts  5.09 us (2%)
  other arithmetic  3.37 us (1%)
    ppermute x12, waiting for transfers between devices, swap(): return lax.ppermute(x, 'seq', [(i, i ^ bits) for i in range(seq_count)])  46.9 us
    all_to_all x3, starting transfers between devices, exchange(): return lax.all_to_all(x, 'exp', split_axis=0, concat_axis=0, tiled=True)  31.4 us
    pallas_call x3, Pallas kernels, expert(): call(lambda *refs: expert_kernel(*refs, blocks=blocks), (shape(flat, BF16...  30.3 us
    all_to_all x3, waiting for transfers between devices, exchange(): return lax.all_to_all(x, 'exp', split_axis=0, concat_axis=0, tiled=True)  29.3 us
    pallas_call x1, Pallas kernels, on_device(): call(lambda *refs: forward_kernel(*refs, total_tiles=total_tiles), (shape...  16.1 us
    pallas_call x1, Pallas kernels, on_device(): call(lambda *refs: backward_kernel(*refs, total_tiles=total_tiles), (shap...  12.7 us
    ppermute x12, starting transfers between devices, swap(): return lax.ppermute(x, 'seq', [(i, i ^ bits) for i in range(seq_count)])  12.2 us
    ppermute x1, waiting for transfers between devices, on_device(): from_left = lax.ppermute(right, 'seq', up_by).astype(F32)  10.1 us
  transfers between devices with their start and end apart: 21, of which 12 were waited for; matrix products, arithmetic and copies ran while one was open for 1% of the time, Pallas kernels for 22%

profile of v1, /device:TPU:1, one launch (start us, length us, event | category | flops | bytes accessed | tf_op | source)
XLA Modules:
  0.0 241.9 jit_solution(6305622760021018752)
XLA Ops:
  2.1 3.5 %place_grad.1 = bf16[32,2,40,256]{3,2,1,0:T(8,128)(2,1)} custom-call(s32[1]{0:T(128)} %bitcast.seq_ref.refs_0_, s32[2,128]{1,0:T(2,128)} %copy.18.ids_ref.refs_2_, bf16[128,2048]{1,0:T(8,128)(2,1)} %bitcast.80, bf16[320,320]{1,0:T(8,128)(2,1)} %constant.8.clone.perm_ref.refs_11_.perm_t_ref.refs_2_.refs_3_.refs_4_.refs_14_), custom_call_target="tpu_custom_call" | custom-call | flops 4294967296 | bytes 1048576 | tf_op jit(solution)/shard_map/place_grad/pallas_call | solution.py:382
  5.6 12.2 %all-to-all-start = ((bf16[32,2,40,256]{3,2,1,0:T(8,128)(2,1)}), bf16[32,2,40,256]{3,2,1,0:T(8,128)(2,1)S(1)}, u32[]{:S(2)}, u32[]{:S(2)}) async-start(bf16[32,2,40,256]{3,2,1,0:T(8,128)(2,1)} %place_grad.1), calls=%async_computation | async-start | bytes 2621440 | tf_op jit(solution)/shard_map/all_to_all | solution.py:376
  17.8 4.0 %collective-permute-start = (bf16[128,2048]{1,0:T(8,128)(2,1)S(1)}, bf16[128,2048]{1,0:T(8,128)(2,1)S(1)}, u32[]{:S(2)}, u32[]{:S(2)}) collective-permute-start(bf16[128,2048]{1,0:T(8,128)(2,1)S(1)} %bitcast.72), channel_id=1, source_target_pairs={{0,32},{32,64},{64,96},{96,128},{128,160},{160,192},{192,224},{1,3... | collective-permute-start | bytes 1572872 | tf_op jit(solution)/shard_map/ppermute | solution.py:378
  21.8 1.9 collective-permute-start.1
  23.7 3.6 %collective-permute-start.2 = (bf16[128,2048]{1,0:T(8,128)(2,1)S(1)}, bf16[128,2048]{1,0:T(8,128)(2,1)S(1)}, u32[]{:S(2)}, u32[]{:S(2)}) collective-permute-start(bf16[128,2048]{1,0:T(8,128)(2,1)S(1)} %bitcast.78), channel_id=1, source_target_pairs={{0,32},{32,64},{64,96},{96,128},{128,160},{160,192},{192,224},{1,3... | collective-permute-start | bytes 1572872 | tf_op jit(solution)/shard_map/ppermute | solution.py:379
  27.4 1.9 collective-permute-start.3
  29.3 3.3 %collective-permute-done.1.refs_6_ = bf16[128,2048]{1,0:T(8,128)(2,1)S(1)} collective-permute-done((bf16[128,2048]{1,0:T(8,128)(2,1)S(1)}, bf16[128,2048]{1,0:T(8,128)(2,1)S(1)}, u32[]{:S(2)}, u32[]{:S(2)}) %collective-permute-start.1) | collective-permute-done | bytes 524320 | tf_op jit(solution)/shard_map/ppermute | solution.py:378
  33.5 4.7 %collective-permute-done.3.refs_9_.refs_11_ = bf16[128,2048]{1,0:T(8,128)(2,1)S(1)} collective-permute-done((bf16[128,2048]{1,0:T(8,128)(2,1)S(1)}, bf16[128,2048]{1,0:T(8,128)(2,1)S(1)}, u32[]{:S(2)}, u32[]{:S(2)}) %collective-permute-start.3) | collective-permute-done | bytes 524320 | tf_op jit(solution)/shard_map/ppermute | solution.py:379
  39.0 16.1 %attention.1 = (f32[32,64,192]{2,1,0:T(8,128)}, f32[128,2048]{1,0:T(8,128)}, f32[128,128]{1,0:T(8,128)}, bf16[32,2,40,256]{3,2,1,0:T(8,128)(2,1)}) custom-call(s32[1]{0:T(128)} %bitcast.seq_ref.refs_0_, s32[2,3]{1,0:T(2,128)} %bitcast.84, s32[2,128]{1,0:T(2,128)} %copy.18.ids_ref.refs_2_, bf16[128,2048]{1,0:T(8,128)(2,1)} %bitcast.74, ...), custom_call_target="tpu_custom_call" | custom-call | flops 17179869184 | bytes 1048576 | tf_op jit(solution)/shard_map/attention/pallas_call | solution.py:390
  55.1 9.5 %all-to-all-start.1 = ((bf16[32,2,40,256]{3,2,1,0:T(8,128)(2,1)}), bf16[32,2,40,256]{3,2,1,0:T(8,128)(2,1)S(1)}, u32[]{:S(2)}, u32[]{:S(2)}) async-start(bf16[32,2,40,256]{3,2,1,0:T(8,128)(2,1)} %get-tuple-element.28), calls=%async_computation.1 | async-start | bytes 2621440 | tf_op jit(solution)/shard_map/all_to_all | solution.py:376
  64.8 1.3 collective-permute-start.4
  66.6 1.2 collective-permute-start.5
  67.8 14.1 %collective-permute-done.4.g1_ref = bf16[1280,256]{1,0:T(8,128)(2,1)S(1)} collective-permute-done((bf16[1280,256]{1,0:T(8,128)(2,1)S(1)}, bf16[1280,256]{1,0:T(8,128)(2,1)S(1)}, u32[]{:S(2)}, u32[]{:S(2)}) %collective-permute-start.4) | collective-permute-done | bytes 655392 | tf_op jit(solution)/shard_map/ppermute | solution.py:373
  81.9 1.2 collective-permute-start.6
  83.2 15.3 %collective-permute-done.6.g3_ref = bf16[1280,256]{1,0:T(8,128)(2,1)} collective-permute-done((bf16[1280,256]{1,0:T(8,128)(2,1)S(1)}, bf16[1280,256]{1,0:T(8,128)(2,1)}, u32[]{:S(2)}, u32[]{:S(2)}) %collective-permute-start.6) | collective-permute-done | bytes 655392 | tf_op jit(solution)/shard_map/ppermute | solution.py:373
  98.6 2.4 collective-permute-start.10
  100.9 7.8 %hidden.1 = (f32[160,1024]{1,0:T(8,128)}, f32[320,1024]{1,0:T(8,128)}, f32[160,1024]{1,0:T(8,128)}) custom-call(bf16[1280,256]{1,0:T(8,128)(2,1)} %bitcast.59, bf16[1280,256]{1,0:T(8,128)(2,1)} %copy-done.8, bf16[1280,256]{1,0:T(8,128)(2,1)} %copy-done.9, bf16[1280,256]{1,0:T(8,128)(2,1)} %collective-permute-done.6.g3_ref, ...), custom_call_target="tpu_custom_call" | custom-call | flops 8589934592 | bytes 1048576 | tf_op jit(solution)/shard_map/hidden/pallas_call | solution.py:417
  108.8 9.5 %expert.3 = bf16[1280,256]{1,0:T(8,128)(2,1)} custom-call(bf16[1280,256]{1,0:T(8,128)(2,1)} %bitcast.63, f32[160,1024]{1,0:T(8,128)} %get-tuple-element.34.refs_1_, bf16[320,320]{1,0:T(8,128)(2,1)} %constant.8.clone.perm_ref.refs_11_.perm_t_ref.refs_2_.refs_3_.refs_4_.refs_14_, ...), custom_call_target="tpu_custom_call" | custom-call | flops 7516192768 | bytes 1048576 | tf_op jit(solution)/shard_map/expert/pallas_call | solution.py:431
  118.3 1.9 collective-permute-start.14
  120.2 11.3 %expert.4 = (bf16[1280,256]{1,0:T(8,128)(2,1)}, bf16[1280,256]{1,0:T(8,128)(2,1)}) custom-call(bf16[1280,256]{1,0:T(8,128)(2,1)} %copy-done.10, bf16[1280,256]{1,0:T(8,128)(2,1)} %copy-done.11, f32[320,1024]{1,0:T(8,128)} %get-tuple-element.38.refs_2_, bf16[320,320]{1,0:T(8,128)(2,1)} %constant.8.clone.perm_ref.refs_11_.perm_t_ref.refs_2_.refs_3_.refs_4_.refs_14_, ...), custom_call_target="tpu_custom_call" | custom-call | flops 11811160064 | bytes 1048576 | tf_op jit(solution)/shard_map/expert/pallas_call | solution.py:431
  131.5 2.4 collective-permute-start.13
  135.2 9.6 %expert.5 = bf16[1280,256]{1,0:T(8,128)(2,1)} custom-call(bf16[1280,256]{1,0:T(8,128)(2,1)} %copy-done.12, f32[160,1024]{1,0:T(8,128)} %get-tuple-element.42.refs_1_, bf16[320,320]{1,0:T(8,128)(2,1)} %constant.8.clone.perm_ref.refs_11_.perm_t_ref.refs_2_.refs_3_.refs_4_.refs_14_, ...), custom_call_target="tpu_custom_call" | custom-call | flops 7516192768 | bytes 1048576 | tf_op jit(solution)/shard_map/expert/pallas_call | solution.py:431
  146.0 1.5 collective-permute-done.12
  148.4 14.8 %collective-permute-done.15 = bf16[1280,256]{1,0:T(8,128)(2,1)S(1)} collective-permute-done((bf16[1280,256]{1,0:T(8,128)(2,1)}, bf16[1280,256]{1,0:T(8,128)(2,1)S(1)}, u32[]{:S(2)}, u32[]{:S(2)}) %collective-permute-start.15) | collective-permute-done | bytes 655392 | tf_op jit(solution)/shard_map/ppermute | solution.py:373
  164.6 9.7 %all-to-all-start.2 = ((bf16[32,2,40,256]{3,2,1,0:T(8,128)(2,1)}), bf16[32,2,40,256]{3,2,1,0:T(8,128)(2,1)S(1)}, u32[]{:S(2)}, u32[]{:S(2)}) async-start(bf16[32,2,40,256]{3,2,1,0:T(8,128)(2,1)} %pad_maximum_fusion), calls=%async_computation.2 | async-start | bytes 2621440 | tf_op jit(solution)/shard_map/all_to_all | solution.py:376
  175.1 29.2 %all-to-all-done.2.refs_4_ = bf16[32,2,40,256]{3,2,1,0:T(8,128)(2,1)S(1)} async-done(((bf16[32,2,40,256]{3,2,1,0:T(8,128)(2,1)}), bf16[32,2,40,256]{3,2,1,0:T(8,128)(2,1)S(1)}, u32[]{:S(2)}, u32[]{:S(2)}) %all-to-all-start.2) | async-done | bytes 1310752 | tf_op jit(solution)/shard_map/all_to_all | solution.py:376
  205.4 12.7 %attention_grad.1 = (f32[128,2048]{1,0:T(8,128)}, f32[128,2048]{1,0:T(8,128)}, bf16[2,128,2048]{2,1,0:T(8,128)(2,1)}, bf16[2,128,2048]{2,1,0:T(8,128)(2,1)}) custom-call(s32[1]{0:T(128)} %bitcast.seq_ref.refs_0_, s32[2,3]{1,0:T(2,128)} %bitcast.85, s32[128,2]{1,0:T(8,128)} %bitcast.67, f32[128,2]{1,0:T(8,128)} %bitcast.68, bf16[32,2,40,256]{3,2,1,0:T(8,128)(2,1)} %copy-done, ...), custom_call_target="tpu_custom_call" | custom-call | flops 13958643712 | bytes 1048576 | tf_op jit(solution)/shard_map/attention_grad/pallas_call | solution.py:456
  218.1 5.8 %collective-permute-start.17 = (bf16[2,128,2048]{2,1,0:T(8,128)(2,1)}, bf16[2,128,2048]{2,1,0:T(8,128)(2,1)S(1)}, u32[]{:S(2)}, u32[]{:S(2)}) collective-permute-start(bf16[2,128,2048]{2,1,0:T(8,128)(2,1)} %get-tuple-element.48), channel_id=1, source_target_pairs={{0,32},{32,64},{64,96},{96,128},{128,160},{160,192},{192,224},{1,3... | collective-permute-start | bytes 3145736 | tf_op jit(solution)/shard_map/ppermute | solution.py:478
  223.9 1.9 collective-permute-start.16
  225.8 10.1 %collective-permute-done.17 = bf16[2,128,2048]{2,1,0:T(8,128)(2,1)S(1)} collective-permute-done((bf16[2,128,2048]{2,1,0:T(8,128)(2,1)}, bf16[2,128,2048]{2,1,0:T(8,128)(2,1)S(1)}, u32[]{:S(2)}, u32[]{:S(2)}) %collective-permute-start.17) | collective-permute-done | bytes 1048608 | tf_op jit(solution)/shard_map/ppermute | solution.py:478
  236.2 4.0 %collective-permute-done.16 = bf16[2,128,2048]{2,1,0:T(8,128)(2,1)S(1)} collective-permute-done((bf16[2,128,2048]{2,1,0:T(8,128)(2,1)}, bf16[2,128,2048]{2,1,0:T(8,128)(2,1)S(1)}, u32[]{:S(2)}, u32[]{:S(2)}) %collective-permute-start.16) | collective-permute-done | bytes 1048608 | tf_op jit(solution)/shard_map/ppermute | solution.py:477
  240.5 1.4 fusion.7
  (66 shorter events, 11.0 us)
Async XLA Ops:
  5.6 12.2 %copy-start.13 = (bf16[1,128,2048]{2,1,0:T(8,128)(2,1)S(1)}, bf16[1,128,2048]{2,1,0:T(8,128)(2,1)}, u32[]{:S(2)}) copy-start(bf16[1,128,2048]{2,1,0:T(8,128)(2,1)} %param.14) | copy-start | bytes 1572868
  5.6 18.1 %copy-start.14 = (bf16[1,128,2048]{2,1,0:T(8,128)(2,1)S(1)}, bf16[1,128,2048]{2,1,0:T(8,128)(2,1)}, u32[]{:S(2)}) copy-start(bf16[1,128,2048]{2,1,0:T(8,128)(2,1)} %param.15) | copy-start | bytes 1572868
  5.6 49.5 %all-to-all-start = ((bf16[32,2,40,256]{3,2,1,0:T(8,128)(2,1)}), bf16[32,2,40,256]{3,2,1,0:T(8,128)(2,1)S(1)}, u32[]{:S(2)}, u32[]{:S(2)}) async-start(bf16[32,2,40,256]{3,2,1,0:T(8,128)(2,1)} %place_grad.1), calls=%async_computation | async-start | bytes 2621440 | tf_op jit(solution)/shard_map/all_to_all | solution.py:376
  17.8 11.5 %collective-permute-start = (bf16[128,2048]{1,0:T(8,128)(2,1)S(1)}, bf16[128,2048]{1,0:T(8,128)(2,1)S(1)}, u32[]{:S(2)}, u32[]{:S(2)}) collective-permute-start(bf16[128,2048]{1,0:T(8,128)(2,1)S(1)} %bitcast.72), channel_id=1, source_target_pairs={{0,32},{32,64},{64,96},{96,128},{128,160},{160,192},{192,224},{1,3... | collective-permute-start | bytes 1572872 | tf_op jit(solution)/shard_map/ppermute | solution.py:378
  21.8 10.8 %collective-permute-start.1 = (bf16[128,2048]{1,0:T(8,128)(2,1)S(1)}, bf16[128,2048]{1,0:T(8,128)(2,1)S(1)}, u32[]{:S(2)}, u32[]{:S(2)}) collective-permute-start(bf16[128,2048]{1,0:T(8,128)(2,1)S(1)} %bitcast.73), channel_id=1, source_target_pairs={{32,0},{64,32},{96,64},{128,96},{160,128},{192,160},{224,192},{33,... | collective-permute-start | bytes 1572872 | tf_op jit(solution)/shard_map/ppermute | solution.py:378
  23.7 9.8 %collective-permute-start.2 = (bf16[128,2048]{1,0:T(8,128)(2,1)S(1)}, bf16[128,2048]{1,0:T(8,128)(2,1)S(1)}, u32[]{:S(2)}, u32[]{:S(2)}) collective-permute-start(bf16[128,2048]{1,0:T(8,128)(2,1)S(1)} %bitcast.78), channel_id=1, source_target_pairs={{0,32},{32,64},{64,96},{96,128},{128,160},{160,192},{192,224},{1,3... | collective-permute-start | bytes 1572872 | tf_op jit(solution)/shard_map/ppermute | solution.py:379
  27.4 10.8 %collective-permute-start.3 = (bf16[128,2048]{1,0:T(8,128)(2,1)S(1)}, bf16[128,2048]{1,0:T(8,128)(2,1)S(1)}, u32[]{:S(2)}, u32[]{:S(2)}) collective-permute-start(bf16[128,2048]{1,0:T(8,128)(2,1)S(1)} %bitcast.79), channel_id=1, source_target_pairs={{32,0},{64,32},{96,64},{128,96},{160,128},{192,160},{224,192},{33,... | collective-permute-start | bytes 1572872 | tf_op jit(solution)/shard_map/ppermute | solution.py:379
  29.3 8.9 %copy-start.17 = (bf16[128,2048]{1,0:T(8,128)(2,1)}, bf16[128,2048]{1,0:T(8,128)(2,1)S(1)}, u32[]{:S(2)}) copy-start(bf16[128,2048]{1,0:T(8,128)(2,1)S(1)} %collective-permute-done.refs_4_) | copy-start | bytes 1572868
  32.6 5.6 %copy-start.18 = (bf16[128,2048]{1,0:T(8,128)(2,1)}, bf16[128,2048]{1,0:T(8,128)(2,1)S(1)}, u32[]{:S(2)}) copy-start(bf16[128,2048]{1,0:T(8,128)(2,1)S(1)} %collective-permute-done.1.refs_6_) | copy-start | bytes 1572868
  33.5 4.7 %copy-start.15 = (bf16[128,2048]{1,0:T(8,128)(2,1)}, bf16[128,2048]{1,0:T(8,128)(2,1)S(1)}, u32[]{:S(2)}) copy-start(bf16[128,2048]{1,0:T(8,128)(2,1)S(1)} %collective-permute-done.2.refs_7_.refs_9_) | copy-start | bytes 1572868
  55.1 43.3 %all-to-all-start.1 = ((bf16[32,2,40,256]{3,2,1,0:T(8,128)(2,1)}), bf16[32,2,40,256]{3,2,1,0:T(8,128)(2,1)S(1)}, u32[]{:S(2)}, u32[]{:S(2)}) async-start(bf16[32,2,40,256]{3,2,1,0:T(8,128)(2,1)} %get-tuple-element.28), calls=%async_computation.1 | async-start | bytes 2621440 | tf_op jit(solution)/shard_map/all_to_all | solution.py:376
  64.6 36.3 %collective-permute-start.7 = (bf16[512,2048]{1,0:T(8,128)(2,1)}, bf16[512,2048]{1,0:T(8,128)(2,1)}, u32[]{:S(2)}, u32[]{:S(2)}) collective-permute-start(bf16[512,2048]{1,0:T(8,128)(2,1)} %bitcast.69), channel_id=1, source_target_pairs={{0,32},{32,0},{64,96},{96,64},{128,160},{160,128},{192,224},{224,1... | collective-permute-start | bytes 6291464 | tf_op jit(solution)/shard_map/ppermute | solution.py:373
  64.8 33.7 %copy-start.3 = (bf16[32,1,40,256]{3,2,1,0:T(8,128)(2,1)}, bf16[32,1,40,256]{3,2,1,0:T(8,128)(2,1)S(1)}, u32[]{:S(2)}) copy-start(bf16[32,1,40,256]{3,2,1,0:T(8,128)(2,1)S(1)} %get-tuple-element.54) | copy-start | bytes 1966084
  64.8 17.1 %collective-permute-start.4 = (bf16[1280,256]{1,0:T(8,128)(2,1)S(1)}, bf16[1280,256]{1,0:T(8,128)(2,1)S(1)}, u32[]{:S(2)}, u32[]{:S(2)}) collective-permute-start(bf16[1280,256]{1,0:T(8,128)(2,1)S(1)} %bitcast.64), channel_id=1, source_target_pairs={{0,192},{32,224},{64,128},{96,160},{128,64},{160,96},{192,0},{224,... | collective-permute-start | bytes 1966088 | tf_op jit(solution)/shard_map/ppermute | solution.py:373
  66.1 42.7 %collective-permute-start.8 = (bf16[2048,512]{1,0:T(8,128)(2,1)}, bf16[2048,512]{1,0:T(8,128)(2,1)}, u32[]{:S(2)}, u32[]{:S(2)}) collective-permute-start(bf16[2048,512]{1,0:T(8,128)(2,1)} %bitcast.14.refs_4_.refs_5_), channel_id=1, source_target_pairs={{0,32},{32,0},{64,96},{96,64},{128,160},{160,128},{192,224},{224,1... | collective-permute-start | bytes 6291464 | tf_op jit(solution)/shard_map/ppermute | solution.py:373
  66.4 42.4 %collective-permute-start.9 = (bf16[2048,512]{1,0:T(8,128)(2,1)}, bf16[2048,512]{1,0:T(8,128)(2,1)}, u32[]{:S(2)}, u32[]{:S(2)}) collective-permute-start(bf16[2048,512]{1,0:T(8,128)(2,1)} %bitcast.15.refs_5_.refs_6_), channel_id=1, source_target_pairs={{0,32},{32,0},{64,96},{96,64},{128,160},{160,128},{192,224},{224,1... | collective-permute-start | bytes 6291464 | tf_op jit(solution)/shard_map/ppermute | solution.py:373
  66.6 16.6 %collective-permute-start.5 = (bf16[1280,256]{1,0:T(8,128)(2,1)S(1)}, bf16[1280,256]{1,0:T(8,128)(2,1)S(1)}, u32[]{:S(2)}, u32[]{:S(2)}) collective-permute-start(bf16[1280,256]{1,0:T(8,128)(2,1)S(1)} %bitcast.58), channel_id=1, source_target_pairs={{0,64},{32,96},{64,0},{96,32},{128,192},{160,224},{192,128},{224,1... | collective-permute-start | bytes 1966088 | tf_op jit(solution)/shard_map/ppermute | solution.py:373
  81.9 16.6 %copy-start.8 = (bf16[1280,256]{1,0:T(8,128)(2,1)}, bf16[1280,256]{1,0:T(8,128)(2,1)S(1)}, u32[]{:S(2)}) copy-start(bf16[1280,256]{1,0:T(8,128)(2,1)S(1)} %collective-permute-done.4.g1_ref) | copy-start | bytes 1966084
  81.9 16.5 %collective-permute-start.6 = (bf16[1280,256]{1,0:T(8,128)(2,1)S(1)}, bf16[1280,256]{1,0:T(8,128)(2,1)}, u32[]{:S(2)}, u32[]{:S(2)}) collective-permute-start(bf16[1280,256]{1,0:T(8,128)(2,1)S(1)} %bitcast.65), channel_id=1, source_target_pairs={{0,128},{32,160},{64,192},{96,224},{128,0},{160,32},{192,64},{224,... | collective-permute-start | bytes 1966088 | tf_op jit(solution)/shard_map/ppermute | solution.py:373
  83.2 15.4 %copy-start.9 = (bf16[1280,256]{1,0:T(8,128)(2,1)}, bf16[1280,256]{1,0:T(8,128)(2,1)S(1)}, u32[]{:S(2)}) copy-start(bf16[1280,256]{1,0:T(8,128)(2,1)S(1)} %collective-permute-done.5.g2_ref) | copy-start | bytes 1966084
  98.5 10.2 %copy-start.4 = (bf16[32,1,40,256]{3,2,1,0:T(8,128)(2,1)}, bf16[32,1,40,256]{3,2,1,0:T(8,128)(2,1)S(1)}, u32[]{:S(2)}) copy-start(bf16[32,1,40,256]{3,2,1,0:T(8,128)(2,1)S(1)} %get-tuple-element.53) | copy-start | bytes 1966084
  98.6 19.7 %collective-permute-start.10 = (bf16[1280,256]{1,0:T(8,128)(2,1)S(1)}, bf16[1280,256]{1,0:T(8,128)(2,1)S(1)}, u32[]{:S(2)}, u32[]{:S(2)}) collective-permute-start(bf16[1280,256]{1,0:T(8,128)(2,1)S(1)} %bitcast.60), channel_id=1, source_target_pairs={{0,192},{32,224},{64,128},{96,160},{128,64},{160,96},{192,0},{224,... | collective-permute-start | bytes 1966088 | tf_op jit(solution)/shard_map/ppermute | solution.py:373
  100.9 17.4 %collective-permute-start.11 = (bf16[1280,256]{1,0:T(8,128)(2,1)S(1)}, bf16[1280,256]{1,0:T(8,128)(2,1)S(1)}, u32[]{:S(2)}, u32[]{:S(2)}) collective-permute-start(bf16[1280,256]{1,0:T(8,128)(2,1)S(1)} %bitcast.62), channel_id=1, source_target_pairs={{0,64},{32,96},{64,0},{96,32},{128,192},{160,224},{192,128},{224,1... | collective-permute-start | bytes 1966088 | tf_op jit(solution)/shard_map/ppermute | solution.py:373
  118.3 16.1 %collective-permute-start.14 = (bf16[1280,256]{1,0:T(8,128)(2,1)S(1)}, bf16[1280,256]{1,0:T(8,128)(2,1)S(1)}, u32[]{:S(2)}, u32[]{:S(2)}) collective-permute-start(bf16[1280,256]{1,0:T(8,128)(2,1)S(1)} %bitcast.61), channel_id=1, source_target_pairs={{0,128},{32,160},{64,192},{96,224},{128,0},{160,32},{192,64},{224,... | collective-permute-start | bytes 1966088 | tf_op jit(solution)/shard_map/ppermute | solution.py:373
  131.5 16.9 %collective-permute-start.13 = (bf16[1280,256]{1,0:T(8,128)(2,1)}, bf16[1280,256]{1,0:T(8,128)(2,1)S(1)}, u32[]{:S(2)}, u32[]{:S(2)}) collective-permute-start(bf16[1280,256]{1,0:T(8,128)(2,1)} %get-tuple-element.40), channel_id=1, source_target_pairs={{0,192},{32,224},{64,128},{96,160},{128,64},{160,96},{192,0},{224,... | collective-permute-start | bytes 1966088 | tf_op jit(solution)/shard_map/ppermute | solution.py:373
  133.9 13.6 %collective-permute-start.12 = (bf16[1280,256]{1,0:T(8,128)(2,1)}, bf16[1280,256]{1,0:T(8,128)(2,1)S(1)}, u32[]{:S(2)}, u32[]{:S(2)}) collective-permute-start(bf16[1280,256]{1,0:T(8,128)(2,1)} %get-tuple-element.39), channel_id=1, source_target_pairs={{0,64},{32,96},{64,0},{96,32},{128,192},{160,224},{192,128},{224,1... | collective-permute-start | bytes 1966088 | tf_op jit(solution)/shard_map/ppermute | solution.py:373
  135.2 12.3 %copy-start.5 = (bf16[1280,256]{1,0:T(8,128)(2,1)S(1)}, bf16[1280,256]{1,0:T(8,128)(2,1)}, u32[]{:S(2)}) copy-start(bf16[1280,256]{1,0:T(8,128)(2,1)} %expert.3) | copy-start | bytes 1966084
  144.8 18.4 %collective-permute-start.15 = (bf16[1280,256]{1,0:T(8,128)(2,1)}, bf16[1280,256]{1,0:T(8,128)(2,1)S(1)}, u32[]{:S(2)}, u32[]{:S(2)}) collective-permute-start(bf16[1280,256]{1,0:T(8,128)(2,1)} %expert.5), channel_id=1, source_target_pairs={{0,128},{32,160},{64,192},{96,224},{128,0},{160,32},{192,64},{224,... | collective-permute-start | bytes 1966088 | tf_op jit(solution)/shard_map/ppermute | solution.py:373
  164.6 9.8 %copy-start.7 = (f32[1,128,2]{1,2,0:T(2,128)S(1)}, f32[1,128,2]{1,2,0:T(2,128)}, u32[]{:S(2)}) copy-start(f32[1,128,2]{1,2,0:T(2,128)} %param.18) | copy-start | bytes 3076
  164.6 39.8 %all-to-all-start.2 = ((bf16[32,2,40,256]{3,2,1,0:T(8,128)(2,1)}), bf16[32,2,40,256]{3,2,1,0:T(8,128)(2,1)S(1)}, u32[]{:S(2)}, u32[]{:S(2)}) async-start(bf16[32,2,40,256]{3,2,1,0:T(8,128)(2,1)} %pad_maximum_fusion), calls=%async_computation.2 | async-start | bytes 2621440 | tf_op jit(solution)/shard_map/all_to_all | solution.py:376
  218.1 17.8 %collective-permute-start.17 = (bf16[2,128,2048]{2,1,0:T(8,128)(2,1)}, bf16[2,128,2048]{2,1,0:T(8,128)(2,1)S(1)}, u32[]{:S(2)}, u32[]{:S(2)}) collective-permute-start(bf16[2,128,2048]{2,1,0:T(8,128)(2,1)} %get-tuple-element.48), channel_id=1, source_target_pairs={{0,32},{32,64},{64,96},{96,128},{128,160},{160,192},{192,224},{1,3... | collective-permute-start | bytes 3145736 | tf_op jit(solution)/shard_map/ppermute | solution.py:478
  223.9 16.3 %collective-permute-start.16 = (bf16[2,128,2048]{2,1,0:T(8,128)(2,1)}, bf16[2,128,2048]{2,1,0:T(8,128)(2,1)S(1)}, u32[]{:S(2)}, u32[]{:S(2)}) collective-permute-start(bf16[2,128,2048]{2,1,0:T(8,128)(2,1)} %get-tuple-element.47), channel_id=1, source_target_pairs={{32,0},{64,32},{96,64},{128,96},{160,128},{192,160},{224,192},{33,... | collective-permute-start | bytes 3145736 | tf_op jit(solution)/shard_map/ppermute | solution.py:477
  (8 other events, 19.3 us)

commit v2 on v1

--- a/solution.py
+++ b/solution.py
@@ -13,6 +13,7 @@
 PIECES = 8
 GROUP = 8
 EPSILON = 1e-06
+ATTN = 24
 MICRO = 1 << 30
 F32 = jnp.float32
 BF16 = jnp.bfloat16
@@ -86,27 +87,6 @@
     return slot0, slot1
 
 
-def slot_cols(ids_ref, half, experts):
-    tokens = ids_ref.shape[0]
-    first = ids_ref[:, 0:1]
-    second = ids_ref[:, 1:2]
-    names = lax.broadcasted_iota(jnp.int32, (tokens, experts), 1)
-    hot0 = (names == first).astype(F32)
-    hot1 = (names == second).astype(F32)
-    before = (
-        lax.broadcasted_iota(jnp.int32, (tokens, tokens), 1)
-        < lax.broadcasted_iota(jnp.int32, (tokens, tokens), 0)
-    ).astype(F32).astype(BF16)
-    seen0 = dot(before, hot0.astype(BF16))
-    seen1 = dot(before, hot1.astype(BF16)) + jnp.sum(hot0, axis=0, keepdims=True)
-    rank0 = jnp.sum(hot0 * seen0, axis=1, keepdims=True).astype(jnp.int32)
-    rank1 = jnp.sum(hot1 * seen1, axis=1, keepdims=True).astype(jnp.int32)
-    slots = (experts // 2) * CAP
-    slot0 = ((first & 1) ^ half) * slots + (first >> 1) * CAP + rank0
-    slot1 = ((second & 1) ^ half) * slots + (second >> 1) * CAP + rank1
-    return slot0, slot1
-
-
 def place_rows(ids_ref, half, experts, x, rows_ref):
     slot0, slot1 = slot_rows(ids_ref, half, experts)
     places = lax.broadcasted_iota(jnp.int32, (rows_ref.shape[0], x.shape[0]), 0)
@@ -125,8 +105,18 @@
             out_ref[chunk * GROUP : (chunk + 1) * GROUP, rel] = block.reshape(GROUP, CELL, piece)
 
 
-def grad_kernel(seq_ref, ids_ref, x_ref, perm_ref, out_ref, rows_ref):
+def grad_kernel(
+    seq_ref, ids_ref, x_ref, perm_ref, k_ref, v_ref, out_ref, pair_ref, rows_ref, sems
+):
+    copies = [
+        pltpu.make_async_copy(src, pair_ref.at[i], sems.at[i])
+        for i, src in enumerate((k_ref, v_ref))
+    ]
+    for copy in copies:
+        copy.start()
     send_rows(seq_ref, ids_ref, x_ref[...], perm_ref, out_ref, rows_ref)
+    for copy in copies:
+        copy.wait()
 
 
 def tile_places(seq_ref, offs_ref, tile, tiles, total):
@@ -140,19 +130,22 @@
     return places, valid
 
 
-def fill_halo(dst_ref, left_ref, own_ref, right_ref):
+def halo_copies(dst_ref, left_ref, own_ref, right_ref, which, sems, first):
     count = own_ref.shape[0]
-    dst_ref[0:count, :] = left_ref[...]
-    dst_ref[count : 2 * count, :] = own_ref[...]
-    dst_ref[2 * count : 3 * count, :] = right_ref[...]
+    return [
+        pltpu.make_async_copy(src, dst_ref.at[i * count : (i + 1) * count], sems.at[first + i])
+        for i, src in enumerate((left_ref.at[which], own_ref, right_ref.at[which]))
+    ]
 
 
 def forward_kernel(
-    seq_ref, offs_ref, ids_ref, q_ref, kl_ref, k_ref, kr_ref, vl_ref, v_ref, vr_ref, gain_ref,
-    perm_ref, wts_ref, unit_ref, inv_ref, sent_ref, kx_ref, vx_ref, out_ref, rows_ref, total_tiles,
+    seq_ref, offs_ref, ids_ref, q_ref, left_ref, k_ref, v_ref, right_ref, gain_ref, perm_ref,
+    wts_ref, unit_ref, inv_ref, sent_ref, kx_ref, vx_ref, out_ref, rows_ref, sems, total_tiles,
 ):
-    fill_halo(kx_ref, kl_ref, k_ref, kr_ref)
-    fill_halo(vx_ref, vl_ref, v_ref, vr_ref)
+    copies = halo_copies(kx_ref, left_ref, k_ref, right_ref, 0, sems, 0)
+    copies += halo_copies(vx_ref, left_ref, v_ref, right_ref, 1, sems, NBR)
+    for copy in copies:
+        copy.start()
     count, width = q_ref.shape
     heads = width // HEAD_DIM
     tiles = count // TILE
@@ -168,6 +161,9 @@
             bias = jnp.where(lane == m, lost, bias)
         spots.append(places)
         biases.append(bias)
+
+    for copy in copies:
+        copy.wait()
 
     def one_head(h):
         lanes = pl.ds(pl.multiple_of(h * HEAD_DIM, HEAD_DIM), HEAD_DIM)
@@ -260,18 +256,17 @@
             dst[chunk * CHUNK : (chunk + 1) * CHUNK, :] = block
 
 
-def backward_kernel(
-    seq_ref, offs_ref, ids_ref, gates_ref, home_ref, grad_ref, unit_ref, inv_ref, q_ref,
-    vl_ref, v_ref, vr_ref, wts_ref, gain_ref, perm_t_ref, k_out_ref, v_out_ref, left_ref,
-    right_ref, vx_ref, rows_ref, ag_ref, ka_ref, va_ref, total_tiles,
+def value_kernel(
+    seq_ref, offs_ref, ids_ref, gates_ref, home_ref, grad_ref, unit_ref, inv_ref, wts_hbm,
+    gain_ref, perm_t_ref, own_ref, left_ref, right_ref, ag_ref, wts_ref, rows_ref, acc_ref, sems,
+    total_tiles,
 ):
-    count, width = q_ref.shape
+    wts_copy = pltpu.make_async_copy(wts_hbm, wts_ref, sems.at[0])
+    wts_copy.start()
+    count, width = grad_ref.shape
     heads = width // HEAD_DIM
     tiles = count // TILE
-    scale = HEAD_DIM ** (-0.5)
-    fill_halo(vx_ref, vl_ref, v_ref, vr_ref)
-    ka_ref[...] = jnp.zeros_like(ka_ref)
-    va_ref[...] = jnp.zeros_like(va_ref)
+    acc_ref[...] = jnp.zeros_like(acc_ref)
     columns, _, _, piece = home_ref.shape
     chunks = columns // GROUP
     perm_t = perm_t_ref[...]
@@ -280,36 +275,68 @@
             home_ref[c * GROUP : (c + 1) * GROUP, rel].reshape(CHUNK, piece) for c in range(chunks)
         ]
         from_wire(blocks, rows_ref, rel * chunks * ROWS, perm_t, chunks, piece)
-    slot0, slot1 = slot_cols(ids_ref, seq_ref[0] // 4, 2 * columns)
-    places = lax.broadcasted_iota(jnp.int32, (count, rows_ref.shape[0]), 1)
-    mix = jnp.where(places == slot0, gates_ref[:, 0:1], 0.0)
-    mix = jnp.where(places == slot1, gates_ref[:, 1:2], mix)
+    slot0, slot1 = slot_rows(ids_ref, seq_ref[0] // 4, 2 * columns)
+    places = lax.broadcasted_iota(jnp.int32, (rows_ref.shape[0], count), 0)
+    mix = jnp.where(places == slot0, gates_ref[0:1, :], 0.0)
+    mix = jnp.where(places == slot1, gates_ref[1:2, :], mix)
     high = mix.astype(BF16)
     low = (mix - high.astype(F32)).astype(BF16)
-    normed_grad = dot(high, rows_ref[...]) + dot(low, rows_ref[...])
+    normed_grad = dot_tn(high, rows_ref[...]) + dot_tn(low, rows_ref[...])
     scaled = normed_grad * gain_ref[...]
     unit = unit_ref[...]
     inner = jnp.mean(scaled * unit, axis=-1, keepdims=True)
     attn_grad = grad_ref[...].astype(F32) + inv_ref[:, 0:1] * (scaled - unit * inner)
     ag_ref[...] = attn_grad.astype(BF16)
     spots = [tile_places(seq_ref, offs_ref, t, tiles, total_tiles)[0] for t in range(tiles)]
+    wts_copy.wait()
+
+    def one_head(h):
+        lanes = pl.ds(pl.multiple_of(h * HEAD_DIM, HEAD_DIM), HEAD_DIM)
+        for t in range(tiles):
+            rows = slice(t * TILE, (t + 1) * TILE)
+            part = dot_tn(wts_ref[t * heads + h].astype(BF16), ag_ref[rows, lanes])
+            for m in range(NBR):
+                acc_ref[pl.ds(spots[t][m], TILE), lanes] += part[m * TILE : (m + 1) * TILE]
+
+    def body(step, carry):
+        for u in range(4):
+            one_head(step * 4 + u)
+        return carry
+
+    lax.fori_loop(0, heads // 4, body, 0)
+    own_ref[...] = acc_ref[count : 2 * count, :]
+    left_ref[...] = acc_ref[0:count, :].astype(BF16)
+    right_ref[...] = acc_ref[2 * count : 3 * count, :].astype(BF16)
+
+
+def key_kernel(
+    seq_ref, offs_ref, ag_ref, q_ref, vl_ref, v_ref, vr_ref, wts_ref, own_ref, left_ref, right_ref,
+    vx_ref, acc_ref, sems, total_tiles,
+):
+    copies = halo_copies(vx_ref, vl_ref, v_ref, vr_ref, 1, sems, 0)
+    for copy in copies:
+        copy.start()
+    count, width = q_ref.shape
+    heads = width // HEAD_DIM
+    tiles = count // TILE
+    scale = HEAD_DIM ** (-0.5)
+    acc_ref[...] = jnp.zeros_like(acc_ref)
+    spots = [tile_places(seq_ref, offs_ref, t, tiles, total_tiles)[0] for t in range(tiles)]
+    for copy in copies:
+        copy.wait()
 
     def one_head(h):
         lanes = pl.ds(pl.multiple_of(h * HEAD_DIM, HEAD_DIM), HEAD_DIM)
         for t in range(tiles):
             rows = slice(t * TILE, (t + 1) * TILE)
             v3 = jnp.concatenate([vx_ref[pl.ds(p, TILE), lanes] for p in spots[t]], axis=0)
-            ag = ag_ref[rows, lanes]
             weights = wts_ref[t * heads + h]
-            prob_grad = dot_nt(ag, v3)
+            prob_grad = dot_nt(ag_ref[rows, lanes], v3)
             sums = jnp.sum(weights * prob_grad, axis=-1, keepdims=True)
             score_grad = (weights * (prob_grad - sums)).astype(BF16)
-            key_part = dot_tn(score_grad, q_ref[rows, lanes]) * scale
-            value_part = dot_tn(weights.astype(BF16), ag)
+            part = dot_tn(score_grad, q_ref[rows, lanes]) * scale
             for m in range(NBR):
-                at = pl.ds(spots[t][m], TILE)
-                ka_ref[at, lanes] += key_part[m * TILE : (m + 1) * TILE]
-                va_ref[at, lanes] += value_part[m * TILE : (m + 1) * TILE]
+                acc_ref[pl.ds(spots[t][m], TILE), lanes] += part[m * TILE : (m + 1) * TILE]
 
     def body(step, carry):
         for u in range(4):
@@ -317,21 +344,18 @@
         return carry
 
     lax.fori_loop(0, heads // 4, body, 0)
-    k_out_ref[...] = ka_ref[count : 2 * count, :]
-    v_out_ref[...] = va_ref[count : 2 * count, :]
-    left_ref[0] = ka_ref[0:count, :].astype(BF16)
-    left_ref[1] = va_ref[0:count, :].astype(BF16)
-    right_ref[0] = ka_ref[2 * count : 3 * count, :].astype(BF16)
-    right_ref[1] = va_ref[2 * count : 3 * count, :].astype(BF16)
-
-
-def call(body, outs, kinds, scratch, name, flops):
+    own_ref[...] = acc_ref[count : 2 * count, :]
+    left_ref[...] = acc_ref[0:count, :].astype(BF16)
+    right_ref[...] = acc_ref[2 * count : 3 * count, :].astype(BF16)
+
+
+def call(body, outs, kinds, scratch, name, flops, out_kinds=None):
     spaces = {"s": pltpu.SMEM, "v": pltpu.VMEM, "a": pl.ANY}
     return pl.pallas_call(
         body,
         out_shape=outs,
         in_specs=[pl.BlockSpec(memory_space=spaces[kind]) for kind in kinds],
-        out_specs=jax.tree.map(lambda _: pl.BlockSpec(memory_space=pltpu.VMEM), outs),
+        out_specs=[pl.BlockSpec(memory_space=spaces[kind]) for kind in out_kinds or "v" * len(outs)],
         scratch_shapes=scratch,
         compiler_params=pltpu.CompilerParams(vmem_limit_bytes=56 * 1024 * 1024),
         cost_estimate=pl.CostEstimate(flops=flops, transcendentals=0, bytes_accessed=1 << 20),
@@ -356,8 +380,9 @@
     piece = width // PIECES
     slots = columns * CAP
     seq = lax.axis_index("seq").astype(jnp.int32).reshape(1)
-    ids = expert_ids[0]
-    ids_t = ids.T
+    ids_t = expert_ids[0].T
+    gates_t = gate_values[0].T
+    offsets = tile_offsets[0]
     gain = norm_gain.reshape(1, width)
     perm = jnp.asarray(shuffle_matrix(), BF16)
     perm_t = jnp.asarray(shuffle_matrix().T, BF16)
@@ -375,18 +400,19 @@
     def exchange(x):
         return lax.all_to_all(x, "exp", split_axis=0, concat_axis=0, tiled=True)
 
-    kl, kr = lax.ppermute(k, "seq", up_by), lax.ppermute(k, "seq", down_by)
-    vl, vr = lax.ppermute(v, "seq", up_by), lax.ppermute(v, "seq", down_by)
-
     barrier = lax.optimization_barrier
-    sent_grad = call(
-        grad_kernel, shape(wire, BF16), "svvv", [pltpu.VMEM((2 * slots, width), F32)],
-        "place_grad", 4 * MICRO,
-    )(seq, ids_t, grad, perm)
+    pair = (2, count, width)
+    sent_grad, kv = call(
+        grad_kernel,
+        (shape(wire, BF16), shape(pair, BF16)),
+        "svvvaa",
+        [pltpu.VMEM((2 * slots, width), F32), pltpu.SemaphoreType.DMA((2,))],
+        "place_grad", 4 * MICRO, "va",
+    )(seq, ids_t, grad, perm, k, v)
+    left, right = lax.ppermute(kv, "seq", up_by), lax.ppermute(kv, "seq", down_by)
     got_grad = exchange(sent_grad)
     gate_s, up_s, down_s = swap(gate, 1), swap(up, 1), swap(down, 1)
 
-    q_after, _ = barrier((q, sent_grad))
     wts, unit, inv, sent = call(
         lambda *refs: forward_kernel(*refs, total_tiles=total_tiles),
         (
@@ -395,24 +421,25 @@
             shape((count, HEAD_DIM), F32),
             shape(wire, BF16),
         ),
-        "ssv" + "v" * 9,
+        "ssvvaaaavv",
         [
             pltpu.VMEM((3 * count, width), BF16),
             pltpu.VMEM((3 * count, width), BF16),
             pltpu.VMEM((count, width), F32),
             pltpu.VMEM((2 * slots, width), F32),
+            pltpu.SemaphoreType.DMA((2 * NBR,)),
         ],
-        "attention", 16 * MICRO,
-    )(seq, tile_offsets[0], ids_t, q_after, kl, k, kr, vl, v, vr, gain, perm)
-
-    sent, got_grad = barrier((sent, got_grad))
+        "attention", ATTN * MICRO,
+    )(seq, offsets, ids_t, q, left, k, v, right, gain, perm)
+
+    sent, got_grad, gate_s, up_s, down_s = barrier((sent, got_grad, gate_s, up_s, down_s))
     got = exchange(sent)
     g0, grad_oth = got_grad[:, 0].reshape(flat), got_grad[:, 1].reshape(flat)
     g1, g2, g3 = swap(grad_oth, 6), swap(g0, 2), swap(grad_oth, 4)
-    got, g1, g2, g3 = barrier((got, g1, g2, g3))
     n0, oth = got[:, 0].reshape(flat), got[:, 1].reshape(flat)
     n1, n2 = swap(oth, 6), swap(n0, 2)
 
+    n0, g0, g1, g2, g3 = barrier((n0, g0, g1, g2, g3))
     part = down.shape[0]
     hidden = call(
         hidden_kernel,
@@ -442,9 +469,10 @@
             "expert", micros * MICRO,
         )(*ins, hg, perm, perm_t, gate, up, gate_s, up_s)
 
+    n1, n2, oth = barrier((n1, n2, oth))
+    n3 = swap(oth, 4)
     (p0,) = expert((n0,), hidden[0], 7)
-    p0, n1, n2, oth = barrier((p0, n1, n2, oth))
-    n3 = swap(oth, 4)
+    p0, n1, n2 = barrier((p0, n1, n2))
     p1, p2 = expert((n1, n2), hidden[1], 11)
     (p3,) = expert((n3,), hidden[2], 7)
     h1, h2 = swap(p1, 6), swap(p2, 2)
@@ -453,32 +481,43 @@
     oth = (h1.astype(F32) + h3.astype(F32)).astype(BF16).reshape(columns, 1, CELL, piece)
     home = exchange(jnp.concatenate([own, oth], axis=1))
 
-    k_own, v_own, left, right = call(
-        lambda *refs: backward_kernel(*refs, total_tiles=total_tiles),
-        (
-            shape((count, width), F32),
-            shape((count, width), F32),
-            shape((2, count, width), BF16),
-            shape((2, count, width), BF16),
-        ),
-        "ss" + "v" * 13,
+    rows = shape((count, width), F32)
+    half = shape((count, width), BF16)
+    v_own, v_left, v_right, attn_grad = call(
+        lambda *refs: value_kernel(*refs, total_tiles=total_tiles),
+        (rows, half, half, half),
+        "ssvvvvvvavv",
+        [
+            pltpu.VMEM(wts.shape, F32),
+            pltpu.VMEM((2 * slots, width), BF16),
+            pltpu.VMEM((3 * count, width), F32),
+            pltpu.SemaphoreType.DMA((1,)),
+        ],
+        "value_grad", 7 * MICRO,
+    )(seq, offsets, ids_t, gates_t, home, grad, unit, inv, wts, gain, perm_t)
+
+    def gather(left_part, right_part):
+        from_right = lax.ppermute(left_part, "seq", down_by)
+        from_left = lax.ppermute(right_part, "seq", up_by)
+        return from_right, from_left
+
+    def finish(own_part, parts):
+        return (own_part + parts[0].astype(F32) + parts[1].astype(F32)).astype(BF16)[None]
+
+    v_parts = gather(v_left, v_right)
+    k_own, k_left, k_right = call(
+        lambda *refs: key_kernel(*refs, total_tiles=total_tiles),
+        (rows, half, half),
+        "ssvvaaav",
         [
             pltpu.VMEM((3 * count, width), BF16),
-            pltpu.VMEM((2 * slots, width), BF16),
-            pltpu.VMEM((count, width), BF16),
             pltpu.VMEM((3 * count, width), F32),
-            pltpu.VMEM((3 * count, width), F32),
+            pltpu.SemaphoreType.DMA((NBR,)),
         ],
-        "attention_grad", 13 * MICRO,
-    )(
-        seq, tile_offsets[0], ids, gate_values[0], home, grad, unit, inv, q, vl, v, vr, wts, gain,
-        perm_t,
-    )
-    from_right = lax.ppermute(left, "seq", down_by).astype(F32)
-    from_left = lax.ppermute(right, "seq", up_by).astype(F32)
-    key_out = (k_own + from_right[0] + from_left[0]).astype(BF16)
-    value_out = (v_own + from_right[1] + from_left[1]).astype(BF16)
-    return (key_out[None], value_out[None])
+        "key_grad", 9 * MICRO,
+    )(seq, offsets, attn_grad, q, left, v, right, wts)
+    k_parts = gather(k_left, k_right)
+    return (finish(k_own, k_parts), finish(v_own, v_parts))
 
 
 def solution(mesh):

time: 243 us -> 270 us (1.11)
  Pallas kernels: 70.6 us -> 111 us
  waiting for transfers between devices: 99.2 us -> 60.8 us
  blocking collectives: 0 us -> 37.3 us
  starting transfers between devices: 62.7 us -> 51 us
    pallas_call x2 -> x3, Pallas kernels: 16.3 us -> 56.4 us  [the longest x1 35.1 us: on_device(): call(grad_kernel, (shape(wire, BF16), shape(pair, BF16)), 'svvvaa', [pltp...]
    all_to_all x0 -> x1, blocking collectives: none -> 37.3 us  [exchange(): return lax.all_to_all(x, 'exp', split_axis=0, concat_axis=0, tiled=True)]
    ppermute x12, waiting for transfers between devices: 46.9 us -> 14.8 us  [swap(): return lax.ppermute(x, 'seq', [(i, i ^ bits) for i in range(seq_count)])]
    all_to_all x3 -> x2, starting transfers between devices: 31.4 us -> 15.8 us  [exchange(): return lax.all_to_all(x, 'exp', split_axis=0, concat_axis=0, tiled=True)]
    ppermute x6, waiting for transfers between devices: 23 us -> 8.02 us  [the longest x2 4.11 us: gather(): from_right = lax.ppermute(left_part, 'seq', down_by)]
    all_to_all x3 -> x2, waiting for transfers between devices: 29.3 us -> 37.9 us  [exchange(): return lax.all_to_all(x, 'exp', split_axis=0, concat_axis=0, tiled=True)]
    ppermute x6, starting transfers between devices: 19.1 us -> 23.7 us  [the longest x2 11 us: gather(): from_right = lax.ppermute(left_part, 'seq', down_by)]
  transfers between devices with their start and end apart: 21 -> 20, of which waited for: 12 -> 8; matrix products, arithmetic and copies ran while one was open for 1% -> 1% of each run, Pallas kernels for 22% -> 26%
where the time goes in v2:
time: 270 us; the launch traced here: 269 us
  Pallas kernels  111 us (41%)
  waiting for transfers between devices  60.8 us (23%)
  starting transfers between devices  51 us (19%)
  blocking collectives  37.3 us (14%)
  local copies, waits for them, and re-layouts  5.21 us (2%)
    all_to_all x2, waiting for transfers between devices, exchange(): return lax.all_to_all(x, 'exp', split_axis=0, concat_axis=0, tiled=True)  37.9 us
    all_to_all x1, blocking collectives, exchange(): return lax.all_to_all(x, 'exp', split_axis=0, concat_axis=0, tiled=True)  37.3 us
    pallas_call x1, Pallas kernels, on_device(): call(grad_kernel, (shape(wire, BF16), shape(pair, BF16)), 'svvvaa', [pltp...  35.1 us
    pallas_call x3, Pallas kernels, expert(): call(lambda *refs: expert_kernel(*refs, blocks=blocks), (shape(flat, BF16...  30.3 us
    pallas_call x1, Pallas kernels, on_device(): call(lambda *refs: forward_kernel(*refs, total_tiles=total_tiles), (shape...  16.9 us
    all_to_all x2, starting transfers between devices, exchange(): return lax.all_to_all(x, 'exp', split_axis=0, concat_axis=0, tiled=True)  15.8 us
    ppermute x12, waiting for transfers between devices, swap(): return lax.ppermute(x, 'seq', [(i, i ^ bits) for i in range(seq_count)])  14.8 us
    pallas_call x1, Pallas kernels, on_device(): call(lambda *refs: key_kernel(*refs, total_tiles=total_tiles), (rows, hal...  14.3 us
  transfers between devices with their start and end apart: 20, of which 8 were waited for; matrix products, arithmetic and copies ran while one was open for 1% of the time, Pallas kernels for 26%

profile of v2, /device:TPU:1, one launch (start us, length us, event | category | flops | bytes accessed | tf_op | source)
XLA Modules:
  0.0 269.1 jit_solution(3686314225040294565)
XLA Ops:
  0.6 35.1 %place_grad.1 = (bf16[32,2,40,256]{3,2,1,0:T(8,128)(2,1)}, bf16[2,128,2048]{2,1,0:T(8,128)(2,1)}) custom-call(s32[1]{0:T(128)} %bitcast.seq_ref.refs_0_, s32[2,128]{1,0:T(2,128)} %bitcast.55, bf16[128,2048]{1,0:T(8,128)(2,1)} %bitcast.46, bf16[320,320]{1,0:T(8,128)(2,1)} %constant.8.clone.perm_ref.refs_9_.perm_t_ref.refs_2_.refs_3_.refs_4_.refs_10_, ...), custom_call_target="tpu_custom_call" | custom-call | flops 4294967296 | bytes 1048576 | tf_op jit(solution)/shard_map/place_grad/pallas_call | solution.py:405
  35.7 4.5 %collective-permute-start = (bf16[2,128,2048]{2,1,0:T(8,128)(2,1)}, bf16[2,128,2048]{2,1,0:T(8,128)(2,1)}, u32[]{:S(2)}, u32[]{:S(2)}) collective-permute-start(bf16[2,128,2048]{2,1,0:T(8,128)(2,1)} %get-tuple-element.36), channel_id=1, source_target_pairs={{0,32},{32,64},{64,96},{96,128},{128,160},{160,192},{192,224},{1,3... | collective-permute-start | bytes 3145736 | tf_op jit(solution)/shard_map/ppermute | solution.py:412
  40.2 2.9 %collective-permute-start.1 = (bf16[2,128,2048]{2,1,0:T(8,128)(2,1)}, bf16[2,128,2048]{2,1,0:T(8,128)(2,1)}, u32[]{:S(2)}, u32[]{:S(2)}) collective-permute-start(bf16[2,128,2048]{2,1,0:T(8,128)(2,1)} %get-tuple-element.36), channel_id=1, source_target_pairs={{32,0},{64,32},{96,64},{128,96},{160,128},{192,160},{224,192},{33,... | collective-permute-start | bytes 3145736 | tf_op jit(solution)/shard_map/ppermute | solution.py:412
  43.2 10.3 %all-to-all-start = ((bf16[32,2,40,256]{3,2,1,0:T(8,128)(2,1)}), bf16[32,2,40,256]{3,2,1,0:T(8,128)(2,1)S(1)}, u32[]{:S(2)}, u32[]{:S(2)}) async-start(bf16[32,2,40,256]{3,2,1,0:T(8,128)(2,1)} %get-tuple-element.38), calls=%async_computation | async-start | bytes 2621440 | tf_op jit(solution)/shard_map/all_to_all | solution.py:401
  54.2 2.6 collective-permute-done.1.refs_7_.refs_6_
  56.9 16.9 %attention.1 = (f32[32,64,192]{2,1,0:T(8,128)}, f32[128,2048]{1,0:T(8,128)}, f32[128,128]{1,0:T(8,128)}, bf16[32,2,40,256]{3,2,1,0:T(8,128)(2,1)}) custom-call(s32[1]{0:T(128)} %bitcast.seq_ref.refs_0_, s32[2,3]{1,0:T(2,128)} %bitcast.59, s32[2,128]{1,0:T(2,128)} %bitcast.56, bf16[128,2048]{1,0:T(8,128)(2,1)} %bitcast.48, ...), custom_call_target="tpu_custom_call" | custom-call | flops 25769803776 | bytes 1048576 | tf_op jit(solution)/shard_map/attention/pallas_call | solution.py:416
  73.8 1.3 copy-done.6
  75.1 1.4 copy-done.7
  76.5 10.5 %all-to-all-done = bf16[32,2,40,256]{3,2,1,0:T(8,128)(2,1)S(1)} async-done(((bf16[32,2,40,256]{3,2,1,0:T(8,128)(2,1)}), bf16[32,2,40,256]{3,2,1,0:T(8,128)(2,1)S(1)}, u32[]{:S(2)}, u32[]{:S(2)}) %all-to-all-start) | async-done | bytes 1310752 | tf_op jit(solution)/shard_map/all_to_all | solution.py:401
  86.9 5.5 %all-to-all-start.1 = ((bf16[32,2,40,256]{3,2,1,0:T(8,128)(2,1)}), bf16[32,2,40,256]{3,2,1,0:T(8,128)(2,1)S(1)}, u32[]{:S(2)}, u32[]{:S(2)}) async-start(bf16[32,2,40,256]{3,2,1,0:T(8,128)(2,1)} %get-tuple-element.39), calls=%async_computation.1 | async-start | bytes 2621440 | tf_op jit(solution)/shard_map/all_to_all | solution.py:401
  93.4 1.6 collective-permute-start.5
  95.0 2.3 collective-permute-start.7
  97.2 27.4 %all-to-all-done.1 = bf16[32,2,40,256]{3,2,1,0:T(8,128)(2,1)S(1)} async-done(((bf16[32,2,40,256]{3,2,1,0:T(8,128)(2,1)}), bf16[32,2,40,256]{3,2,1,0:T(8,128)(2,1)S(1)}, u32[]{:S(2)}, u32[]{:S(2)}) %all-to-all-start.1) | async-done | bytes 1310752 | tf_op jit(solution)/shard_map/all_to_all | solution.py:401
  125.8 7.8 %hidden.1 = (f32[160,1024]{1,0:T(8,128)}, f32[320,1024]{1,0:T(8,128)}, f32[160,1024]{1,0:T(8,128)}) custom-call(bf16[1280,256]{1,0:T(8,128)(2,1)} %bitcast.31, bf16[1280,256]{1,0:T(8,128)(2,1)} %copy-done.8, bf16[1280,256]{1,0:T(8,128)(2,1)} %collective-permute-done.6.g2_ref, bf16[1280,256]{1,0:T(8,128)(2,1)} %collective-permute-done.7.g3_ref, ...), custom_call_target="tpu_custom_call" | custom-call | flops 8589934592 | bytes 1048576 | tf_op jit(solution)/shard_map/hidden/pallas_call | solution.py:444
  133.7 9.5 %expert.3 = bf16[1280,256]{1,0:T(8,128)(2,1)} custom-call(bf16[1280,256]{1,0:T(8,128)(2,1)} %bitcast.33, f32[160,1024]{1,0:T(8,128)} %get-tuple-element.47.refs_1_, bf16[320,320]{1,0:T(8,128)(2,1)} %constant.8.clone.perm_ref.refs_9_.perm_t_ref.refs_2_.refs_3_.refs_4_.refs_10_, ...), custom_call_target="tpu_custom_call" | custom-call | flops 7516192768 | bytes 1048576 | tf_op jit(solution)/shard_map/expert/pallas_call | solution.py:458
  143.2 2.9 %collective-permute-start.12 = (bf16[1280,256]{1,0:T(8,128)(2,1)S(1)}, bf16[1280,256]{1,0:T(8,128)(2,1)S(1)}, u32[]{:S(2)}, u32[]{:S(2)}) collective-permute-start(bf16[1280,256]{1,0:T(8,128)(2,1)S(1)} %bitcast.29), channel_id=1, source_target_pairs={{0,128},{32,160},{64,192},{96,224},{128,0},{160,32},{192,64},{224,... | collective-permute-start | bytes 1966088 | tf_op jit(solution)/shard_map/ppermute | solution.py:398
  146.1 11.3 %expert.4 = (bf16[1280,256]{1,0:T(8,128)(2,1)}, bf16[1280,256]{1,0:T(8,128)(2,1)}) custom-call(bf16[1280,256]{1,0:T(8,128)(2,1)} %copy-done.10, bf16[1280,256]{1,0:T(8,128)(2,1)} %copy-done.9, f32[320,1024]{1,0:T(8,128)} %get-tuple-element.55.refs_2_, bf16[320,320]{1,0:T(8,128)(2,1)} %constant.8.clone.perm_ref.refs_9_.perm_t_ref.refs_2_.refs_3_.refs_4_.refs_10_, ...), custom_call_target="tpu_custom_call" | custom-call | flops 11811160064 | bytes 1048576 | tf_op jit(solution)/shard_map/expert/pallas_call | solution.py:458
  157.5 1.2 collective-permute-start.11
  159.7 9.6 %expert.5 = bf16[1280,256]{1,0:T(8,128)(2,1)} custom-call(bf16[1280,256]{1,0:T(8,128)(2,1)} %copy-done.11, f32[160,1024]{1,0:T(8,128)} %get-tuple-element.59.refs_1_, bf16[320,320]{1,0:T(8,128)(2,1)} %constant.8.clone.perm_ref.refs_9_.perm_t_ref.refs_2_.refs_3_.refs_4_.refs_10_, ...), custom_call_target="tpu_custom_call" | custom-call | flops 7516192768 | bytes 1048576 | tf_op jit(solution)/shard_map/expert/pallas_call | solution.py:458
  169.3 2.3 collective-permute-start.13
  171.6 1.3 collective-permute-done.10
  173.0 13.4 %collective-permute-done.13 = bf16[1280,256]{1,0:T(8,128)(2,1)S(1)} collective-permute-done((bf16[1280,256]{1,0:T(8,128)(2,1)}, bf16[1280,256]{1,0:T(8,128)(2,1)S(1)}, u32[]{:S(2)}, u32[]{:S(2)}) %collective-permute-start.13) | collective-permute-done | bytes 655392 | tf_op jit(solution)/shard_map/ppermute | solution.py:398
  186.7 37.3 %all_to_all.15.refs_4_ = bf16[32,2,40,256]{3,2,1,0:T(8,128)(2,1)} all-to-all(bf16[32,2,40,256]{3,2,1,0:T(8,128)(2,1)S(1)} %pad_maximum_fusion), channel_id=1, replica_groups=mesh['seq'=8,'exp'=32] {'exp'}, dimensions={0} | all-to-all | bytes 2621440 | tf_op jit(solution)/shard_map/all_to_all | solution.py:401
  224.0 7.1 %value_grad.1 = (f32[128,2048]{1,0:T(8,128)}, bf16[128,2048]{1,0:T(8,128)(2,1)}, bf16[128,2048]{1,0:T(8,128)(2,1)}, bf16[128,2048]{1,0:T(8,128)(2,1)}) custom-call(s32[1]{0:T(128)} %bitcast.seq_ref.refs_0_, s32[2,3]{1,0:T(2,128)} %bitcast.60, s32[2,128]{1,0:T(2,128)} %bitcast.57, f32[2,128]{1,0:T(2,128)} %bitcast.58, ...), custom_call_target="tpu_custom_call" | custom-call | flops 7516192768 | bytes 1048576 | tf_op jit(solution)/shard_map/value_grad/pallas_call | solution.py:486
  231.1 8.7 %collective-permute-start.16 = (bf16[128,2048]{1,0:T(8,128)(2,1)}, bf16[128,2048]{1,0:T(8,128)(2,1)S(1)}, u32[]{:S(2)}, u32[]{:S(2)}) collective-permute-start(bf16[128,2048]{1,0:T(8,128)(2,1)} %get-tuple-element.68), channel_id=1, source_target_pairs={{32,0},{64,32},{96,64},{128,96},{160,128},{192,160},{224,192},{33,... | collective-permute-start | bytes 1572872 | tf_op jit(solution)/shard_map/ppermute | solution.py:500
  239.8 2.0 collective-permute-start.17
  241.8 14.3 %key_grad.1 = (f32[128,2048]{1,0:T(8,128)}, bf16[128,2048]{1,0:T(8,128)(2,1)}, bf16[128,2048]{1,0:T(8,128)(2,1)}) custom-call(s32[1]{0:T(128)} %bitcast.seq_ref.refs_0_, s32[2,3]{1,0:T(2,128)} %bitcast.61, bf16[128,2048]{1,0:T(8,128)(2,1)} %get-tuple-element.63.refs_2_, bf16[128,2048]{1,0:T(8,128)(2,1)} %bitcast.49, ...), custom_call_target="tpu_custom_call" | custom-call | flops 9663676416 | bytes 1048576 | tf_op jit(solution)/shard_map/key_grad/pallas_call | solution.py:508
  256.1 2.3 collective-permute-start.14
  258.4 3.2 %collective-permute-start.15 = (bf16[128,2048]{1,0:T(8,128)(2,1)}, bf16[128,2048]{1,0:T(8,128)(2,1)S(1)}, u32[]{:S(2)}, u32[]{:S(2)}) collective-permute-start(bf16[128,2048]{1,0:T(8,128)(2,1)} %get-tuple-element.66), channel_id=1, source_target_pairs={{0,32},{32,64},{64,96},{96,128},{128,160},{160,192},{192,224},{1,3... | collective-permute-start | bytes 1572872 | tf_op jit(solution)/shard_map/ppermute | solution.py:501
  261.7 1.0 fusion.1
  262.7 4.1 %collective-permute-done.14 = bf16[128,2048]{1,0:T(8,128)(2,1)S(1)} collective-permute-done((bf16[128,2048]{1,0:T(8,128)(2,1)}, bf16[128,2048]{1,0:T(8,128)(2,1)S(1)}, u32[]{:S(2)}, u32[]{:S(2)}) %collective-permute-start.14) | collective-permute-done | bytes 524320 | tf_op jit(solution)/shard_map/ppermute | solution.py:500
  266.8 1.3 collective-permute-done.15
  (48 shorter events, 5.3 us)
Async XLA Ops:
  35.7 18.5 %collective-permute-start = (bf16[2,128,2048]{2,1,0:T(8,128)(2,1)}, bf16[2,128,2048]{2,1,0:T(8,128)(2,1)}, u32[]{:S(2)}, u32[]{:S(2)}) collective-permute-start(bf16[2,128,2048]{2,1,0:T(8,128)(2,1)} %get-tuple-element.36), channel_id=1, source_target_pairs={{0,32},{32,64},{64,96},{96,128},{128,160},{160,192},{192,224},{1,3... | collective-permute-start | bytes 3145736 | tf_op jit(solution)/shard_map/ppermute | solution.py:412
  40.2 16.6 %collective-permute-start.1 = (bf16[2,128,2048]{2,1,0:T(8,128)(2,1)}, bf16[2,128,2048]{2,1,0:T(8,128)(2,1)}, u32[]{:S(2)}, u32[]{:S(2)}) collective-permute-start(bf16[2,128,2048]{2,1,0:T(8,128)(2,1)} %get-tuple-element.36), channel_id=1, source_target_pairs={{32,0},{64,32},{96,64},{128,96},{160,128},{192,160},{224,192},{33,... | collective-permute-start | bytes 3145736 | tf_op jit(solution)/shard_map/ppermute | solution.py:412
  43.2 11.0 %copy-start.5 = (bf16[1,1,512,2048]{3,2,1,0:T(8,128)(2,1)S(1)}, bf16[1,1,512,2048]{3,2,1,0:T(8,128)(2,1)}, u32[]{:S(2)}) copy-start(bf16[1,1,512,2048]{3,2,1,0:T(8,128)(2,1)} %param.23) | copy-start | bytes 6291460
  43.2 43.8 %all-to-all-start = ((bf16[32,2,40,256]{3,2,1,0:T(8,128)(2,1)}), bf16[32,2,40,256]{3,2,1,0:T(8,128)(2,1)S(1)}, u32[]{:S(2)}, u32[]{:S(2)}) async-start(bf16[32,2,40,256]{3,2,1,0:T(8,128)(2,1)} %get-tuple-element.38), calls=%async_computation | async-start | bytes 2621440 | tf_op jit(solution)/shard_map/all_to_all | solution.py:401
  53.5 20.2 %collective-permute-start.2 = (bf16[2048,512]{1,0:T(8,128)(2,1)}, bf16[2048,512]{1,0:T(8,128)(2,1)S(1)}, u32[]{:S(2)}, u32[]{:S(2)}) collective-permute-start(bf16[2048,512]{1,0:T(8,128)(2,1)} %bitcast.36), channel_id=1, source_target_pairs={{0,32},{32,0},{64,96},{96,64},{128,160},{160,128},{192,224},{224,1... | collective-permute-start | bytes 6291464 | tf_op jit(solution)/shard_map/ppermute | solution.py:398
  53.6 20.1 %collective-permute-start.3 = (bf16[2048,512]{1,0:T(8,128)(2,1)}, bf16[2048,512]{1,0:T(8,128)(2,1)S(1)}, u32[]{:S(2)}, u32[]{:S(2)}) collective-permute-start(bf16[2048,512]{1,0:T(8,128)(2,1)} %bitcast.40), channel_id=1, source_target_pairs={{0,32},{32,0},{64,96},{96,64},{128,160},{160,128},{192,224},{224,1... | collective-permute-start | bytes 6291464 | tf_op jit(solution)/shard_map/ppermute | solution.py:398
  54.1 22.3 %collective-permute-start.4 = (bf16[512,2048]{1,0:T(8,128)(2,1)S(1)}, bf16[512,2048]{1,0:T(8,128)(2,1)}, u32[]{:S(2)}, u32[]{:S(2)}) collective-permute-start(bf16[512,2048]{1,0:T(8,128)(2,1)S(1)} %bitcast.35), channel_id=1, source_target_pairs={{0,32},{32,0},{64,96},{96,64},{128,160},{160,128},{192,224},{224,1... | collective-permute-start | bytes 6291464 | tf_op jit(solution)/shard_map/ppermute | solution.py:398
  73.7 1.3 copy-start.6
  75.1 1.4 copy-start.7
  86.9 37.7 %all-to-all-start.1 = ((bf16[32,2,40,256]{3,2,1,0:T(8,128)(2,1)}), bf16[32,2,40,256]{3,2,1,0:T(8,128)(2,1)S(1)}, u32[]{:S(2)}, u32[]{:S(2)}) async-start(bf16[32,2,40,256]{3,2,1,0:T(8,128)(2,1)} %get-tuple-element.39), calls=%async_computation.1 | async-start | bytes 2621440 | tf_op jit(solution)/shard_map/all_to_all | solution.py:401
  93.4 31.4 %copy-start.2 = (bf16[32,1,40,256]{3,2,1,0:T(8,128)(2,1)}, bf16[32,1,40,256]{3,2,1,0:T(8,128)(2,1)S(1)}, u32[]{:S(2)}) copy-start(bf16[32,1,40,256]{3,2,1,0:T(8,128)(2,1)S(1)} %get-tuple-element.71) | copy-start | bytes 1966084
  93.4 31.5 %collective-permute-start.5 = (bf16[1280,256]{1,0:T(8,128)(2,1)}, bf16[1280,256]{1,0:T(8,128)(2,1)S(1)}, u32[]{:S(2)}, u32[]{:S(2)}) collective-permute-start(bf16[1280,256]{1,0:T(8,128)(2,1)} %bitcast.17), channel_id=1, source_target_pairs={{0,192},{32,224},{64,128},{96,160},{128,64},{160,96},{192,0},{224,... | collective-permute-start | bytes 1966088 | tf_op jit(solution)/shard_map/ppermute | solution.py:398
  95.0 30.0 %collective-permute-start.6 = (bf16[1280,256]{1,0:T(8,128)(2,1)S(1)}, bf16[1280,256]{1,0:T(8,128)(2,1)}, u32[]{:S(2)}, u32[]{:S(2)}) collective-permute-start(bf16[1280,256]{1,0:T(8,128)(2,1)S(1)} %bitcast.30), channel_id=1, source_target_pairs={{0,64},{32,96},{64,0},{96,32},{128,192},{160,224},{192,128},{224,1... | collective-permute-start | bytes 1966088 | tf_op jit(solution)/shard_map/ppermute | solution.py:398
  95.0 30.1 %collective-permute-start.7 = (bf16[1280,256]{1,0:T(8,128)(2,1)}, bf16[1280,256]{1,0:T(8,128)(2,1)}, u32[]{:S(2)}, u32[]{:S(2)}) collective-permute-start(bf16[1280,256]{1,0:T(8,128)(2,1)} %bitcast.17), channel_id=1, source_target_pairs={{0,128},{32,160},{64,192},{96,224},{128,0},{160,32},{192,64},{224,... | collective-permute-start | bytes 1966088 | tf_op jit(solution)/shard_map/ppermute | solution.py:398
  124.8 8.9 %copy-start.3 = (bf16[32,1,40,256]{3,2,1,0:T(8,128)(2,1)}, bf16[32,1,40,256]{3,2,1,0:T(8,128)(2,1)S(1)}, u32[]{:S(2)}) copy-start(bf16[32,1,40,256]{3,2,1,0:T(8,128)(2,1)S(1)} %get-tuple-element.72) | copy-start | bytes 1966084
  124.8 18.4 %collective-permute-start.9 = (bf16[1280,256]{1,0:T(8,128)(2,1)S(1)}, bf16[1280,256]{1,0:T(8,128)(2,1)S(1)}, u32[]{:S(2)}, u32[]{:S(2)}) collective-permute-start(bf16[1280,256]{1,0:T(8,128)(2,1)S(1)} %bitcast.32), channel_id=1, source_target_pairs={{0,64},{32,96},{64,0},{96,32},{128,192},{160,224},{192,128},{224,1... | collective-permute-start | bytes 1966088 | tf_op jit(solution)/shard_map/ppermute | solution.py:398
  124.9 0.9 copy-start.8
  125.1 18.1 %collective-permute-start.8 = (bf16[1280,256]{1,0:T(8,128)(2,1)S(1)}, bf16[1280,256]{1,0:T(8,128)(2,1)S(1)}, u32[]{:S(2)}, u32[]{:S(2)}) collective-permute-start(bf16[1280,256]{1,0:T(8,128)(2,1)S(1)} %bitcast.28), channel_id=1, source_target_pairs={{0,192},{32,224},{64,128},{96,160},{128,64},{160,96},{192,0},{224,... | collective-permute-start | bytes 1966088 | tf_op jit(solution)/shard_map/ppermute | solution.py:398
  143.2 2.9 %copy-start.10 = (bf16[1280,256]{1,0:T(8,128)(2,1)}, bf16[1280,256]{1,0:T(8,128)(2,1)S(1)}, u32[]{:S(2)}) copy-start(bf16[1280,256]{1,0:T(8,128)(2,1)S(1)} %collective-permute-done.8.refs_0_) | copy-start | bytes 1966084
  143.2 2.9 %copy-start.9 = (bf16[1280,256]{1,0:T(8,128)(2,1)}, bf16[1280,256]{1,0:T(8,128)(2,1)S(1)}, u32[]{:S(2)}) copy-start(bf16[1280,256]{1,0:T(8,128)(2,1)S(1)} %collective-permute-done.9.refs_1_) | copy-start | bytes 1966084
  143.2 15.5 %collective-permute-start.12 = (bf16[1280,256]{1,0:T(8,128)(2,1)S(1)}, bf16[1280,256]{1,0:T(8,128)(2,1)S(1)}, u32[]{:S(2)}, u32[]{:S(2)}) collective-permute-start(bf16[1280,256]{1,0:T(8,128)(2,1)S(1)} %bitcast.29), channel_id=1, source_target_pairs={{0,128},{32,160},{64,192},{96,224},{128,0},{160,32},{192,64},{224,... | collective-permute-start | bytes 1966088 | tf_op jit(solution)/shard_map/ppermute | solution.py:398
  157.4 15.5 %collective-permute-start.10 = (bf16[1280,256]{1,0:T(8,128)(2,1)}, bf16[1280,256]{1,0:T(8,128)(2,1)S(1)}, u32[]{:S(2)}, u32[]{:S(2)}) collective-permute-start(bf16[1280,256]{1,0:T(8,128)(2,1)} %get-tuple-element.56), channel_id=1, source_target_pairs={{0,64},{32,96},{64,0},{96,32},{128,192},{160,224},{192,128},{224,1... | collective-permute-start | bytes 1966088 | tf_op jit(solution)/shard_map/ppermute | solution.py:398
  157.5 15.5 %collective-permute-start.11 = (bf16[1280,256]{1,0:T(8,128)(2,1)}, bf16[1280,256]{1,0:T(8,128)(2,1)S(1)}, u32[]{:S(2)}, u32[]{:S(2)}) collective-permute-start(bf16[1280,256]{1,0:T(8,128)(2,1)} %get-tuple-element.57), channel_id=1, source_target_pairs={{0,192},{32,224},{64,128},{96,160},{128,64},{160,96},{192,0},{224,... | collective-permute-start | bytes 1966088 | tf_op jit(solution)/shard_map/ppermute | solution.py:398
  158.8 0.9 copy-start.11
  159.7 13.2 %copy-start.4 = (bf16[1280,256]{1,0:T(8,128)(2,1)S(1)}, bf16[1280,256]{1,0:T(8,128)(2,1)}, u32[]{:S(2)}) copy-start(bf16[1280,256]{1,0:T(8,128)(2,1)} %expert.3) | copy-start | bytes 1966084
  169.3 17.1 %collective-permute-start.13 = (bf16[1280,256]{1,0:T(8,128)(2,1)}, bf16[1280,256]{1,0:T(8,128)(2,1)S(1)}, u32[]{:S(2)}, u32[]{:S(2)}) collective-permute-start(bf16[1280,256]{1,0:T(8,128)(2,1)} %expert.5), channel_id=1, source_target_pairs={{0,128},{32,160},{64,192},{96,224},{128,0},{160,32},{192,64},{224,... | collective-permute-start | bytes 1966088 | tf_op jit(solution)/shard_map/ppermute | solution.py:398
  231.1 30.6 %collective-permute-start.16 = (bf16[128,2048]{1,0:T(8,128)(2,1)}, bf16[128,2048]{1,0:T(8,128)(2,1)S(1)}, u32[]{:S(2)}, u32[]{:S(2)}) collective-permute-start(bf16[128,2048]{1,0:T(8,128)(2,1)} %get-tuple-element.68), channel_id=1, source_target_pairs={{32,0},{64,32},{96,64},{128,96},{160,128},{192,160},{224,192},{33,... | collective-permute-start | bytes 1572872 | tf_op jit(solution)/shard_map/ppermute | solution.py:500
  239.8 21.9 %collective-permute-start.17 = (bf16[128,2048]{1,0:T(8,128)(2,1)}, bf16[128,2048]{1,0:T(8,128)(2,1)S(1)}, u32[]{:S(2)}, u32[]{:S(2)}) collective-permute-start(bf16[128,2048]{1,0:T(8,128)(2,1)} %get-tuple-element.69), channel_id=1, source_target_pairs={{0,32},{32,64},{64,96},{96,128},{128,160},{160,192},{192,224},{1,3... | collective-permute-start | bytes 1572872 | tf_op jit(solution)/shard_map/ppermute | solution.py:501
  241.8 19.9 %copy-start = (f32[128,2048]{1,0:T(8,128)S(1)}, f32[128,2048]{1,0:T(8,128)}, u32[]{:S(2)}) copy-start(f32[128,2048]{1,0:T(8,128)} %get-tuple-element.67) | copy-start | bytes 3145732
  256.1 10.7 %collective-permute-start.14 = (bf16[128,2048]{1,0:T(8,128)(2,1)}, bf16[128,2048]{1,0:T(8,128)(2,1)S(1)}, u32[]{:S(2)}, u32[]{:S(2)}) collective-permute-start(bf16[128,2048]{1,0:T(8,128)(2,1)} %get-tuple-element.65), channel_id=1, source_target_pairs={{32,0},{64,32},{96,64},{128,96},{160,128},{192,160},{224,192},{33,... | collective-permute-start | bytes 1572872 | tf_op jit(solution)/shard_map/ppermute | solution.py:500
  258.4 9.7 %collective-permute-start.15 = (bf16[128,2048]{1,0:T(8,128)(2,1)}, bf16[128,2048]{1,0:T(8,128)(2,1)S(1)}, u32[]{:S(2)}, u32[]{:S(2)}) collective-permute-start(bf16[128,2048]{1,0:T(8,128)(2,1)} %get-tuple-element.66), channel_id=1, source_target_pairs={{0,32},{32,64},{64,96},{96,128},{128,160},{160,192},{192,224},{1,3... | collective-permute-start | bytes 1572872 | tf_op jit(solution)/shard_map/ppermute | solution.py:501
  261.7 6.4 %copy-start.1 = (f32[128,2048]{1,0:T(8,128)S(1)}, f32[128,2048]{1,0:T(8,128)}, u32[]{:S(2)}) copy-start(f32[128,2048]{1,0:T(8,128)} %get-tuple-element.64) | copy-start | bytes 3145732

commit v3 on v2

--- a/solution.py
+++ b/solution.py
@@ -13,7 +13,8 @@
 PIECES = 8
 GROUP = 8
 EPSILON = 1e-06
-ATTN = 24
+ATTN = 16
+UNROLL = 4
 MICRO = 1 << 30
 F32 = jnp.float32
 BF16 = jnp.bfloat16
@@ -105,18 +106,10 @@
             out_ref[chunk * GROUP : (chunk + 1) * GROUP, rel] = block.reshape(GROUP, CELL, piece)
 
 
-def grad_kernel(
-    seq_ref, ids_ref, x_ref, perm_ref, k_ref, v_ref, out_ref, pair_ref, rows_ref, sems
-):
-    copies = [
-        pltpu.make_async_copy(src, pair_ref.at[i], sems.at[i])
-        for i, src in enumerate((k_ref, v_ref))
-    ]
-    for copy in copies:
-        copy.start()
+def grad_kernel(seq_ref, ids_ref, x_ref, perm_ref, k_ref, v_ref, out_ref, pair_ref, rows_ref):
+    pair_ref[0] = k_ref[...]
+    pair_ref[1] = v_ref[...]
     send_rows(seq_ref, ids_ref, x_ref[...], perm_ref, out_ref, rows_ref)
-    for copy in copies:
-        copy.wait()
 
 
 def tile_places(seq_ref, offs_ref, tile, tiles, total):
@@ -128,6 +121,19 @@
         where = seq_ref[0] * tiles + tile + off
         valid.append((where >= 0) & (where < total))
     return places, valid
+
+
+def head_spans(step, heads, tiles):
+    spans = []
+    for u in range(UNROLL):
+        h = step * UNROLL + u
+        lanes = pl.ds(pl.multiple_of(h * HEAD_DIM, HEAD_DIM), HEAD_DIM)
+        spans += [(t, h, slice(t * TILE, (t + 1) * TILE), lanes) for t in range(tiles)]
+    return spans
+
+
+def window(ref, places, lanes):
+    return jnp.concatenate([ref[pl.ds(p, TILE), lanes] for p in places], axis=0)
 
 
 def halo_copies(dst_ref, left_ref, own_ref, right_ref, which, sems, first):
@@ -165,24 +171,22 @@
     for copy in copies:
         copy.wait()
 
-    def one_head(h):
-        lanes = pl.ds(pl.multiple_of(h * HEAD_DIM, HEAD_DIM), HEAD_DIM)
-        for t in range(tiles):
-            rows = slice(t * TILE, (t + 1) * TILE)
-            k3 = jnp.concatenate([kx_ref[pl.ds(p, TILE), lanes] for p in spots[t]], axis=0)
-            v3 = jnp.concatenate([vx_ref[pl.ds(p, TILE), lanes] for p in spots[t]], axis=0)
-            scores = dot_nt(q_ref[rows, lanes], k3) * scale + biases[t]
-            raised = jnp.exp(scores - jnp.max(scores, axis=-1, keepdims=True))
-            weights = raised / jnp.sum(raised, axis=-1, keepdims=True)
-            wts_ref[t * heads + h] = weights
-            out_ref[rows, lanes] = dot(weights.astype(BF16), v3)
-
     def body(step, carry):
-        for u in range(4):
-            one_head(step * 4 + u)
+        spans = head_spans(step, heads, tiles)
+        scores = [
+            dot_nt(q_ref[rows, lanes], window(kx_ref, spots[t], lanes)) * scale + biases[t]
+            for t, h, rows, lanes in spans
+        ]
+        tops = [jnp.max(x, axis=-1, keepdims=True) for x in scores]
+        raised = [jnp.exp(x - top) for x, top in zip(scores, tops)]
+        sums = [jnp.sum(x, axis=-1, keepdims=True) for x in raised]
+        weights = [x / total for x, total in zip(raised, sums)]
+        for x, (t, h, rows, lanes) in zip(weights, spans):
+            wts_ref[t * heads + h] = x
+            out_ref[rows, lanes] = dot(x.astype(BF16), window(vx_ref, spots[t], lanes))
         return carry
 
-    lax.fori_loop(0, heads // 4, body, 0)
+    lax.fori_loop(0, heads // UNROLL, body, 0)
     out = out_ref[...]
     inv = lax.rsqrt(jnp.mean(out * out, axis=-1, keepdims=True) + EPSILON)
     unit = out * inv
@@ -192,30 +196,24 @@
     send_rows(seq_ref, ids_ref, normed, perm_ref, sent_ref, rows_ref)
 
 
-def hidden_kernel(
-    g0_ref, g1_ref, g2_ref, g3_ref, perm_t_ref, down0_ref, down1_ref, o0_ref, o1_ref, o2_ref,
-    rows_ref, w_ref, sems,
-):
+def hidden_kernel(*refs, blocks):
+    ins = refs[:blocks]
+    perm_t_ref, down0_ref, down1_ref, out_ref, rows_ref, w_ref, sems = refs[blocks:]
     copies = [
         pltpu.make_async_copy(src, w_ref.at[i], sems.at[i])
         for i, src in enumerate((down0_ref, down1_ref))
     ]
     for copy in copies:
         copy.start()
-    piece = g0_ref.shape[1]
-    chunks = g0_ref.shape[0] // CHUNK
-    slots = chunks * ROWS
+    piece = ins[0].shape[1]
+    chunks = ins[0].shape[0] // CHUNK
     perm_t = perm_t_ref[...]
-    for b, block in enumerate((g0_ref, g1_ref, g2_ref, g3_ref)):
-        from_wire(block, rows_ref, b * slots, perm_t, chunks, piece)
+    for b, block in enumerate(ins):
+        from_wire(block, rows_ref, b * chunks * ROWS, perm_t, chunks, piece)
     part = down0_ref.shape[0]
     for i, copy in enumerate(copies):
         copy.wait()
-        cols = slice(i * part, (i + 1) * part)
-        both = dot_nt(rows_ref[...], w_ref[i])
-        o0_ref[:, cols] = both[:slots]
-        o1_ref[:, cols] = both[slots : 3 * slots]
-        o2_ref[:, cols] = both[3 * slots :]
+        out_ref[:, i * part : (i + 1) * part] = dot_nt(rows_ref[...], w_ref[i])
 
 
 def expert_kernel(*refs, blocks):
@@ -256,17 +254,22 @@
             dst[chunk * CHUNK : (chunk + 1) * CHUNK, :] = block
 
 
-def value_kernel(
-    seq_ref, offs_ref, ids_ref, gates_ref, home_ref, grad_ref, unit_ref, inv_ref, wts_hbm,
-    gain_ref, perm_t_ref, own_ref, left_ref, right_ref, ag_ref, wts_ref, rows_ref, acc_ref, sems,
-    total_tiles,
+def backward_kernel(
+    seq_ref, offs_ref, ids_ref, gates_ref, home_ref, grad_ref, unit_ref, inv_ref, gain_ref,
+    perm_t_ref, q_hbm, left_ref, v_ref, right_ref, wts_hbm, k_out_ref, v_out_ref, to_left_ref,
+    to_right_ref, vx_ref, q_ref, wts_ref, rows_ref, ag_ref, ka_ref, va_ref, sems, total_tiles,
 ):
-    wts_copy = pltpu.make_async_copy(wts_hbm, wts_ref, sems.at[0])
-    wts_copy.start()
-    count, width = grad_ref.shape
+    copies = halo_copies(vx_ref, left_ref, v_ref, right_ref, 1, sems, 0)
+    copies.append(pltpu.make_async_copy(q_hbm, q_ref, sems.at[NBR]))
+    copies.append(pltpu.make_async_copy(wts_hbm, wts_ref, sems.at[NBR + 1]))
+    for copy in copies:
+        copy.start()
+    count, width = q_ref.shape
     heads = width // HEAD_DIM
     tiles = count // TILE
-    acc_ref[...] = jnp.zeros_like(acc_ref)
+    scale = HEAD_DIM ** (-0.5)
+    ka_ref[...] = jnp.zeros_like(ka_ref)
+    va_ref[...] = jnp.zeros_like(va_ref)
     columns, _, _, piece = home_ref.shape
     chunks = columns // GROUP
     perm_t = perm_t_ref[...]
@@ -288,65 +291,44 @@
     attn_grad = grad_ref[...].astype(F32) + inv_ref[:, 0:1] * (scaled - unit * inner)
     ag_ref[...] = attn_grad.astype(BF16)
     spots = [tile_places(seq_ref, offs_ref, t, tiles, total_tiles)[0] for t in range(tiles)]
-    wts_copy.wait()
-
-    def one_head(h):
-        lanes = pl.ds(pl.multiple_of(h * HEAD_DIM, HEAD_DIM), HEAD_DIM)
-        for t in range(tiles):
-            rows = slice(t * TILE, (t + 1) * TILE)
-            part = dot_tn(wts_ref[t * heads + h].astype(BF16), ag_ref[rows, lanes])
-            for m in range(NBR):
-                acc_ref[pl.ds(spots[t][m], TILE), lanes] += part[m * TILE : (m + 1) * TILE]
-
-    def body(step, carry):
-        for u in range(4):
-            one_head(step * 4 + u)
-        return carry
-
-    lax.fori_loop(0, heads // 4, body, 0)
-    own_ref[...] = acc_ref[count : 2 * count, :]
-    left_ref[...] = acc_ref[0:count, :].astype(BF16)
-    right_ref[...] = acc_ref[2 * count : 3 * count, :].astype(BF16)
-
-
-def key_kernel(
-    seq_ref, offs_ref, ag_ref, q_ref, vl_ref, v_ref, vr_ref, wts_ref, own_ref, left_ref, right_ref,
-    vx_ref, acc_ref, sems, total_tiles,
-):
-    copies = halo_copies(vx_ref, vl_ref, v_ref, vr_ref, 1, sems, 0)
-    for copy in copies:
-        copy.start()
-    count, width = q_ref.shape
-    heads = width // HEAD_DIM
-    tiles = count // TILE
-    scale = HEAD_DIM ** (-0.5)
-    acc_ref[...] = jnp.zeros_like(acc_ref)
-    spots = [tile_places(seq_ref, offs_ref, t, tiles, total_tiles)[0] for t in range(tiles)]
     for copy in copies:
         copy.wait()
 
-    def one_head(h):
-        lanes = pl.ds(pl.multiple_of(h * HEAD_DIM, HEAD_DIM), HEAD_DIM)
-        for t in range(tiles):
-            rows = slice(t * TILE, (t + 1) * TILE)
-            v3 = jnp.concatenate([vx_ref[pl.ds(p, TILE), lanes] for p in spots[t]], axis=0)
-            weights = wts_ref[t * heads + h]
-            prob_grad = dot_nt(ag_ref[rows, lanes], v3)
-            sums = jnp.sum(weights * prob_grad, axis=-1, keepdims=True)
-            score_grad = (weights * (prob_grad - sums)).astype(BF16)
-            part = dot_tn(score_grad, q_ref[rows, lanes]) * scale
-            for m in range(NBR):
-                acc_ref[pl.ds(spots[t][m], TILE), lanes] += part[m * TILE : (m + 1) * TILE]
-
     def body(step, carry):
-        for u in range(4):
-            one_head(step * 4 + u)
+        spans = head_spans(step, heads, tiles)
+        prob_grads = [
+            dot_nt(ag_ref[rows, lanes], window(vx_ref, spots[t], lanes))
+            for t, h, rows, lanes in spans
+        ]
+        values = [
+            dot_tn(wts_ref[t * heads + h].astype(BF16), ag_ref[rows, lanes])
+            for t, h, rows, lanes in spans
+        ]
+        sums = [
+            jnp.sum(wts_ref[t * heads + h] * x, axis=-1, keepdims=True)
+            for x, (t, h, rows, lanes) in zip(prob_grads, spans)
+        ]
+        score_grads = [
+            (wts_ref[t * heads + h] * (x - total)).astype(BF16)
+            for x, total, (t, h, rows, lanes) in zip(prob_grads, sums, spans)
+        ]
+        keys = [
+            dot_tn(x, q_ref[rows, lanes]) * scale
+            for x, (t, h, rows, lanes) in zip(score_grads, spans)
+        ]
+        for acc_ref, parts in ((va_ref, values), (ka_ref, keys)):
+            for x, (t, h, rows, lanes) in zip(parts, spans):
+                for m in range(NBR):
+                    acc_ref[pl.ds(spots[t][m], TILE), lanes] += x[m * TILE : (m + 1) * TILE]
         return carry
 
-    lax.fori_loop(0, heads // 4, body, 0)
-    own_ref[...] = acc_ref[count : 2 * count, :]
-    left_ref[...] = acc_ref[0:count, :].astype(BF16)
-    right_ref[...] = acc_ref[2 * count : 3 * count, :].astype(BF16)
+    lax.fori_loop(0, heads // UNROLL, body, 0)
+    k_out_ref[...] = ka_ref[count : 2 * count, :]
+    v_out_ref[...] = va_ref[count : 2 * count, :]
+    to_left_ref[0] = ka_ref[0:count, :].astype(BF16)
+    to_left_ref[1] = va_ref[0:count, :].astype(BF16)
+    to_right_ref[0] = ka_ref[2 * count : 3 * count, :].astype(BF16)
+    to_right_ref[1] = va_ref[2 * count : 3 * count, :].astype(BF16)
 
 
 def call(body, outs, kinds, scratch, name, flops, out_kinds=None):
@@ -405,9 +387,9 @@
     sent_grad, kv = call(
         grad_kernel,
         (shape(wire, BF16), shape(pair, BF16)),
-        "svvvaa",
-        [pltpu.VMEM((2 * slots, width), F32), pltpu.SemaphoreType.DMA((2,))],
-        "place_grad", 4 * MICRO, "va",
+        "svvvvv",
+        [pltpu.VMEM((2 * slots, width), F32)],
+        "place_grad", 4 * MICRO,
     )(seq, ids_t, grad, perm, k, v)
     left, right = lax.ppermute(kv, "seq", up_by), lax.ppermute(kv, "seq", down_by)
     got_grad = exchange(sent_grad)
@@ -435,23 +417,30 @@
     sent, got_grad, gate_s, up_s, down_s = barrier((sent, got_grad, gate_s, up_s, down_s))
     got = exchange(sent)
     g0, grad_oth = got_grad[:, 0].reshape(flat), got_grad[:, 1].reshape(flat)
-    g1, g2, g3 = swap(grad_oth, 6), swap(g0, 2), swap(grad_oth, 4)
+    g1, g2 = swap(grad_oth, 6), swap(g0, 2)
+    g1, g2, grad_oth = barrier((g1, g2, grad_oth))
+    g3 = swap(grad_oth, 4)
     n0, oth = got[:, 0].reshape(flat), got[:, 1].reshape(flat)
     n1, n2 = swap(oth, 6), swap(n0, 2)
-
-    n0, g0, g1, g2, g3 = barrier((n0, g0, g1, g2, g3))
+    n1, n2, oth = barrier((n1, n2, oth))
+    n3 = swap(oth, 4)
+
     part = down.shape[0]
-    hidden = call(
-        hidden_kernel,
-        tuple(shape((m * slots, 2 * part), F32) for m in (1, 2, 1)),
-        "vvvvvaa",
-        [
-            pltpu.VMEM((4 * slots, width), BF16),
-            pltpu.VMEM((2, part, width), BF16),
-            pltpu.SemaphoreType.DMA((2,)),
-        ],
-        "hidden", 8 * MICRO,
-    )(g0, g1, g2, g3, perm_t, down, down_s)
+
+    def hidden(ins, micros):
+        blocks = len(ins)
+        (out,) = call(
+            lambda *refs: hidden_kernel(*refs, blocks=blocks),
+            (shape((blocks * slots, 2 * part), F32),),
+            "v" * (blocks + 1) + "aa",
+            [
+                pltpu.VMEM((blocks * slots, width), BF16),
+                pltpu.VMEM((2, part, width), BF16),
+                pltpu.SemaphoreType.DMA((2,)),
+            ],
+            "hidden", micros * MICRO,
+        )(*ins, perm_t, down, down_s)
+        return out
 
     def expert(ins, hg, micros):
         blocks = len(ins)
@@ -469,55 +458,43 @@
             "expert", micros * MICRO,
         )(*ins, hg, perm, perm_t, gate, up, gate_s, up_s)
 
-    n1, n2, oth = barrier((n1, n2, oth))
-    n3 = swap(oth, 4)
-    (p0,) = expert((n0,), hidden[0], 7)
-    p0, n1, n2 = barrier((p0, n1, n2))
-    p1, p2 = expert((n1, n2), hidden[1], 11)
-    (p3,) = expert((n3,), hidden[2], 7)
+    hidden_own = hidden((g0,), 4)
+    hidden_near = hidden((g1, g2), 5)
+    (p0,) = expert((n0,), hidden_own, 9)
+    p0, g3 = barrier((p0, g3))
+    hidden_far = hidden((g3,), 4)
+    hidden_far, n1, n2 = barrier((hidden_far, n1, n2))
+    p1, p2 = expert((n1, n2), hidden_near, 11)
+    (p3,) = expert((n3,), hidden_far, 9)
     h1, h2 = swap(p1, 6), swap(p2, 2)
     h3 = swap(p3, 4)
     own = (p0.astype(F32) + h2.astype(F32)).astype(BF16).reshape(columns, 1, CELL, piece)
     oth = (h1.astype(F32) + h3.astype(F32)).astype(BF16).reshape(columns, 1, CELL, piece)
     home = exchange(jnp.concatenate([own, oth], axis=1))
 
-    rows = shape((count, width), F32)
-    half = shape((count, width), BF16)
-    v_own, v_left, v_right, attn_grad = call(
-        lambda *refs: value_kernel(*refs, total_tiles=total_tiles),
-        (rows, half, half, half),
-        "ssvvvvvvavv",
+    k_own, v_own, to_left, to_right = call(
+        lambda *refs: backward_kernel(*refs, total_tiles=total_tiles),
+        (shape((count, width), F32), shape((count, width), F32), shape(pair, BF16), shape(pair, BF16)),
+        "ssvvvvvvvvaaaaa",
         [
+            pltpu.VMEM((3 * count, width), BF16),
+            pltpu.VMEM((count, width), BF16),
             pltpu.VMEM(wts.shape, F32),
             pltpu.VMEM((2 * slots, width), BF16),
+            pltpu.VMEM((count, width), BF16),
             pltpu.VMEM((3 * count, width), F32),
-            pltpu.SemaphoreType.DMA((1,)),
+            pltpu.VMEM((3 * count, width), F32),
+            pltpu.SemaphoreType.DMA((NBR + 2,)),
         ],
-        "value_grad", 7 * MICRO,
-    )(seq, offsets, ids_t, gates_t, home, grad, unit, inv, wts, gain, perm_t)
-
-    def gather(left_part, right_part):
-        from_right = lax.ppermute(left_part, "seq", down_by)
-        from_left = lax.ppermute(right_part, "seq", up_by)
-        return from_right, from_left
-
-    def finish(own_part, parts):
-        return (own_part + parts[0].astype(F32) + parts[1].astype(F32)).astype(BF16)[None]
-
-    v_parts = gather(v_left, v_right)
-    k_own, k_left, k_right = call(
-        lambda *refs: key_kernel(*refs, total_tiles=total_tiles),
-        (rows, half, half),
-        "ssvvaaav",
-        [
-            pltpu.VMEM((3 * count, width), BF16),
-            pltpu.VMEM((3 * count, width), F32),
-            pltpu.SemaphoreType.DMA((NBR,)),
-        ],
-        "key_grad", 9 * MICRO,
-    )(seq, offsets, attn_grad, q, left, v, right, wts)
-    k_parts = gather(k_left, k_right)
-    return (finish(k_own, k_parts), finish(v_own, v_parts))
+        "attention_grad", 12 * MICRO,
+    )(seq, offsets, ids_t, gates_t, home, grad, unit, inv, gain, perm_t, q, left, v, right, wts)
+    from_right = lax.ppermute(to_left, "seq", down_by)
+    from_left = lax.ppermute(to_right, "seq", up_by)
+
+    def finish(own_part, i):
+        return (own_part + from_right[i].astype(F32) + from_left[i].astype(F32)).astype(BF16)[None]
+
+    return (finish(k_own, 0), finish(v_own, 1))
 
 
 def solution(mesh):

time: 270 us -> 228 us (0.84)
  Pallas kernels: 111 us -> 69.1 us
  starting transfers between devices: 51 us -> 42 us
  waiting for transfers between devices: 60.8 us -> 65.9 us
  blocking collectives: 37.3 us -> 40 us
    pallas_call x4 -> x5, Pallas kernels: 64.3 us -> 30.5 us  [the longest x3 16.4 us: hidden(): call(lambda *refs: hidden_kernel(*refs, blocks=blocks), (shape((blocks *...]
    all_to_all x2, waiting for transfers between devices: 37.9 us -> 27.5 us  [exchange(): return lax.all_to_all(x, 'exp', split_axis=0, concat_axis=0, tiled=True)]
    ppermute x12, waiting for transfers between devices: 14.8 us -> 23.7 us  [swap(): return lax.ppermute(x, 'seq', [(i, i ^ bits) for i in range(seq_count)])]
    pallas_call x1, Pallas kernels: 16.9 us -> 8.31 us  [on_device(): call(lambda *refs: forward_kernel(*refs, total_tiles=total_tiles), (shape...]
    ppermute x4 -> x2, starting transfers between devices: 16.3 us -> 9.13 us  [the longest x1 7.21 us: on_device(): from_right = lax.ppermute(to_left, 'seq', down_by)]
    ppermute x4 -> x2, waiting for transfers between devices: 5.4 us -> 12 us  [the longest x1 10.6 us: on_device(): from_right = lax.ppermute(to_left, 'seq', down_by)]
  transfers between devices with their start and end apart: 20 -> 18, of which waited for: 8 -> 9; matrix products, arithmetic and copies ran while one was open for 1% -> 0% of each run, Pallas kernels for 26% -> 24%
where the time goes in v3:
time: 228 us; the launch traced here: 227 us
  Pallas kernels  69.1 us (30%)
  waiting for transfers between devices  65.9 us (29%)
  starting transfers between devices  42 us (18%)
  blocking collectives  40 us (18%)
  local copies, waits for them, and re-layouts  6.1 us (3%)
  other arithmetic  3.48 us (2%)
    all_to_all x1, blocking collectives, exchange(): return lax.all_to_all(x, 'exp', split_axis=0, concat_axis=0, tiled=True)  40 us
    pallas_call x3, Pallas kernels, expert(): call(lambda *refs: expert_kernel(*refs, blocks=blocks), (shape(flat, BF16...  30.3 us
    all_to_all x2, waiting for transfers between devices, exchange(): return lax.all_to_all(x, 'exp', split_axis=0, concat_axis=0, tiled=True)  27.5 us
    ppermute x12, waiting for transfers between devices, swap(): return lax.ppermute(x, 'seq', [(i, i ^ bits) for i in range(seq_count)])  23.7 us
    pallas_call x3, Pallas kernels, hidden(): call(lambda *refs: hidden_kernel(*refs, blocks=blocks), (shape((blocks *...  16.4 us
    all_to_all x2, starting transfers between devices, exchange(): return lax.all_to_all(x, 'exp', split_axis=0, concat_axis=0, tiled=True)  15.8 us
    ppermute x1, waiting for transfers between devices, on_device(): from_right = lax.ppermute(to_left, 'seq', down_by)  10.6 us
    pallas_call x1, Pallas kernels, on_device(): call(lambda *refs: backward_kernel(*refs, total_tiles=total_tiles), (shap...  9.87 us
  transfers between devices with their start and end apart: 18, of which 9 were waited for; matrix products, arithmetic and copies ran while one was open for 0% of the time, Pallas kernels for 24%

profile of v3, /device:TPU:1, one launch (start us, length us, event | category | flops | bytes accessed | tf_op | source)
XLA Modules:
  0.0 227.5 jit_solution(71572305362659910)
XLA Ops:
  0.6 4.3 %place_grad.1 = (bf16[32,2,40,256]{3,2,1,0:T(8,128)(2,1)}, bf16[2,128,2048]{2,1,0:T(8,128)(2,1)}) custom-call(s32[1]{0:T(128)} %bitcast.seq_ref.refs_0_, s32[2,128]{1,0:T(2,128)} %bitcast.81, bf16[128,2048]{1,0:T(8,128)(2,1)} %bitcast.72, bf16[320,320]{1,0:T(8,128)(2,1)} %constant.8.clone.perm_ref.refs_9_.refs_1_.refs_2_.refs_3_.refs_4_, ...), custom_call_target="tpu_custom_call" | custom-call | flops 4294967296 | bytes 1048576 | tf_op jit(solution)/shard_map/place_grad/pallas_call | solution.py:387
  4.9 4.5 %collective-permute-start = (bf16[2,128,2048]{2,1,0:T(8,128)(2,1)}, bf16[2,128,2048]{2,1,0:T(8,128)(2,1)}, u32[]{:S(2)}, u32[]{:S(2)}) collective-permute-start(bf16[2,128,2048]{2,1,0:T(8,128)(2,1)} %get-tuple-element.30), channel_id=1, source_target_pairs={{0,32},{32,64},{64,96},{96,128},{128,160},{160,192},{192,224},{1,3... | collective-permute-start | bytes 3145736 | tf_op jit(solution)/shard_map/ppermute | solution.py:394
  9.4 2.9 %collective-permute-start.1 = (bf16[2,128,2048]{2,1,0:T(8,128)(2,1)}, bf16[2,128,2048]{2,1,0:T(8,128)(2,1)}, u32[]{:S(2)}, u32[]{:S(2)}) collective-permute-start(bf16[2,128,2048]{2,1,0:T(8,128)(2,1)} %get-tuple-element.30), channel_id=1, source_target_pairs={{32,0},{64,32},{96,64},{128,96},{160,128},{192,160},{224,192},{33,... | collective-permute-start | bytes 3145736 | tf_op jit(solution)/shard_map/ppermute | solution.py:394
  12.4 10.3 %all-to-all-start = ((bf16[32,2,40,256]{3,2,1,0:T(8,128)(2,1)}), bf16[32,2,40,256]{3,2,1,0:T(8,128)(2,1)S(1)}, u32[]{:S(2)}, u32[]{:S(2)}) async-start(bf16[32,2,40,256]{3,2,1,0:T(8,128)(2,1)} %get-tuple-element.32), calls=%async_computation | async-start | bytes 2621440 | tf_op jit(solution)/shard_map/all_to_all | solution.py:383
  23.4 2.6 %collective-permute-done.1.refs_7_.refs_13_ = bf16[2,128,2048]{2,1,0:T(8,128)(2,1)} collective-permute-done((bf16[2,128,2048]{2,1,0:T(8,128)(2,1)}, bf16[2,128,2048]{2,1,0:T(8,128)(2,1)}, u32[]{:S(2)}, u32[]{:S(2)}) %collective-permute-start.1) | collective-permute-done | bytes 1048608 | tf_op jit(solution)/shard_map/ppermute | solution.py:394
  26.1 8.3 %attention.1 = (f32[32,64,192]{2,1,0:T(8,128)}, f32[128,2048]{1,0:T(8,128)}, f32[128,128]{1,0:T(8,128)}, bf16[32,2,40,256]{3,2,1,0:T(8,128)(2,1)}) custom-call(s32[1]{0:T(128)} %bitcast.seq_ref.refs_0_, s32[2,3]{1,0:T(2,128)} %bitcast.79, s32[2,128]{1,0:T(2,128)} %bitcast.82, bf16[128,2048]{1,0:T(8,128)(2,1)} %bitcast.70, ...), custom_call_target="tpu_custom_call" | custom-call | flops 17179869184 | bytes 1048576 | tf_op jit(solution)/shard_map/attention/pallas_call | solution.py:398
  34.4 1.3 copy-done.4
  35.7 1.4 copy-done.5
  37.1 19.0 %all-to-all-done = bf16[32,2,40,256]{3,2,1,0:T(8,128)(2,1)S(1)} async-done(((bf16[32,2,40,256]{3,2,1,0:T(8,128)(2,1)}), bf16[32,2,40,256]{3,2,1,0:T(8,128)(2,1)S(1)}, u32[]{:S(2)}, u32[]{:S(2)}) %all-to-all-start) | async-done | bytes 1310752 | tf_op jit(solution)/shard_map/all_to_all | solution.py:383
  56.1 5.4 %all-to-all-start.1 = ((bf16[32,2,40,256]{3,2,1,0:T(8,128)(2,1)}), bf16[32,2,40,256]{3,2,1,0:T(8,128)(2,1)S(1)}, u32[]{:S(2)}, u32[]{:S(2)}) async-start(bf16[32,2,40,256]{3,2,1,0:T(8,128)(2,1)} %get-tuple-element.33), calls=%async_computation.1 | async-start | bytes 2621440 | tf_op jit(solution)/shard_map/all_to_all | solution.py:383
  61.7 1.7 collective-permute-start.5
  63.4 5.3 %hidden.3.refs_1_ = f32[160,1024]{1,0:T(8,128)} custom-call(bf16[1280,256]{1,0:T(8,128)(2,1)} %bitcast.55, bf16[320,320]{1,0:T(8,128)(2,1)} %constant.8.clone.perm_ref.refs_9_.refs_1_.refs_2_.refs_3_.refs_4_, bf16[512,2048]{1,0:T(8,128)(2,1)} %bitcast.56, bf16[512,2048]{1,0:T(8,128)(2,1)} %collective-permute-done.4.refs_3_.refs_4_), custom_call_target="tpu_custom_call" | custom-call | flops 4294967296 | bytes 1048576 | tf_op jit(solution)/shard_map/hidden/pallas_call | solution.py:432
  68.7 9.7 %collective-permute-done.5.refs_0_ = bf16[1280,256]{1,0:T(8,128)(2,1)S(1)} collective-permute-done((bf16[1280,256]{1,0:T(8,128)(2,1)S(1)}, bf16[1280,256]{1,0:T(8,128)(2,1)S(1)}, u32[]{:S(2)}, u32[]{:S(2)}) %collective-permute-start.5) | collective-permute-done | bytes 655392 | tf_op jit(solution)/shard_map/ppermute | solution.py:380
  79.5 5.8 %hidden.5.refs_2_ = f32[320,1024]{1,0:T(8,128)} custom-call(bf16[1280,256]{1,0:T(8,128)(2,1)} %copy-done.10, bf16[1280,256]{1,0:T(8,128)(2,1)} %copy-done.11, bf16[320,320]{1,0:T(8,128)(2,1)} %constant.8.clone.perm_ref.refs_9_.refs_1_.refs_2_.refs_3_.refs_4_, bf16[512,2048]{1,0:T(8,128)(2,1)} %bitcast.57, ...), custom_call_target="tpu_custom_call" | custom-call | flops 5368709120 | bytes 1048576 | tf_op jit(solution)/shard_map/hidden/pallas_call | solution.py:432
  85.3 8.5 %all-to-all-done.1 = bf16[32,2,40,256]{3,2,1,0:T(8,128)(2,1)S(1)} async-done(((bf16[32,2,40,256]{3,2,1,0:T(8,128)(2,1)}), bf16[32,2,40,256]{3,2,1,0:T(8,128)(2,1)S(1)}, u32[]{:S(2)}, u32[]{:S(2)}) %all-to-all-start.1) | async-done | bytes 1310752 | tf_op jit(solution)/shard_map/all_to_all | solution.py:383
  94.7 9.5 %expert.3 = bf16[1280,256]{1,0:T(8,128)(2,1)} custom-call(bf16[1280,256]{1,0:T(8,128)(2,1)} %bitcast.53, f32[160,1024]{1,0:T(8,128)} %hidden.3.refs_1_, bf16[320,320]{1,0:T(8,128)(2,1)} %constant.8.clone.perm_ref.refs_9_.refs_1_.refs_2_.refs_3_.refs_4_, bf16[320,320]{1,0:T(8,128)(2,1)} %constant.8.clone.perm_ref.refs_9_.refs_1_.refs_2_.refs_3_.refs_4_, ...), custom_call_target="tpu_custom_call" | custom-call | flops 9663676416 | bytes 1048576 | tf_op jit(solution)/shard_map/expert/pallas_call | solution.py:447
  105.1 5.3 %hidden.4.refs_1_ = f32[160,1024]{1,0:T(8,128)} custom-call(bf16[1280,256]{1,0:T(8,128)(2,1)} %copy-done.6, bf16[320,320]{1,0:T(8,128)(2,1)} %constant.8.clone.perm_ref.refs_9_.refs_1_.refs_2_.refs_3_.refs_4_, bf16[512,2048]{1,0:T(8,128)(2,1)} %bitcast.58, bf16[512,2048]{1,0:T(8,128)(2,1)} %collective-permute-done.4.refs_3_.refs_4_), custom_call_target="tpu_custom_call" | custom-call | flops 4294967296 | bytes 1048576 | tf_op jit(solution)/shard_map/hidden/pallas_call | solution.py:432
  110.4 3.2 %collective-permute-start.12 = (bf16[1280,256]{1,0:T(8,128)(2,1)S(1)}, bf16[1280,256]{1,0:T(8,128)(2,1)S(1)}, u32[]{:S(2)}, u32[]{:S(2)}) collective-permute-start(bf16[1280,256]{1,0:T(8,128)(2,1)S(1)} %bitcast.51), channel_id=1, source_target_pairs={{0,128},{32,160},{64,192},{96,224},{128,0},{160,32},{192,64},{224,... | collective-permute-start | bytes 1966088 | tf_op jit(solution)/shard_map/ppermute | solution.py:380
  113.6 11.3 %expert.4 = (bf16[1280,256]{1,0:T(8,128)(2,1)}, bf16[1280,256]{1,0:T(8,128)(2,1)}) custom-call(bf16[1280,256]{1,0:T(8,128)(2,1)} %copy-done.7, bf16[1280,256]{1,0:T(8,128)(2,1)} %copy-done.8, f32[320,1024]{1,0:T(8,128)} %hidden.5.refs_2_, bf16[320,320]{1,0:T(8,128)(2,1)} %constant.8.clone.perm_ref.refs_9_.refs_1_.refs_2_.refs_3_.refs_4_, ...), custom_call_target="tpu_custom_call" | custom-call | flops 11811160064 | bytes 1048576 | tf_op jit(solution)/shard_map/expert/pallas_call | solution.py:447
  125.0 1.3 collective-permute-start.11
  126.3 0.9 copy-done.9
  127.2 9.5 %expert.5 = bf16[1280,256]{1,0:T(8,128)(2,1)} custom-call(bf16[1280,256]{1,0:T(8,128)(2,1)} %copy-done.9, f32[160,1024]{1,0:T(8,128)} %hidden.4.refs_1_, bf16[320,320]{1,0:T(8,128)(2,1)} %constant.8.clone.perm_ref.refs_9_.refs_1_.refs_2_.refs_3_.refs_4_, bf16[320,320]{1,0:T(8,128)(2,1)} %constant.8.clone.perm_ref.refs_9_.refs_1_.refs_2_.refs_3_.refs_4_, ...), custom_call_target="tpu_custom_call" | custom-call | flops 9663676416 | bytes 1048576 | tf_op jit(solution)/shard_map/expert/pallas_call | solution.py:447
  136.7 2.3 collective-permute-start.13
  139.0 0.9 collective-permute-done.10
  140.2 13.0 %collective-permute-done.13 = bf16[1280,256]{1,0:T(8,128)(2,1)S(1)} collective-permute-done((bf16[1280,256]{1,0:T(8,128)(2,1)}, bf16[1280,256]{1,0:T(8,128)(2,1)S(1)}, u32[]{:S(2)}, u32[]{:S(2)}) %collective-permute-start.13) | collective-permute-done | bytes 655392 | tf_op jit(solution)/shard_map/ppermute | solution.py:380
  153.4 40.0 %all_to_all.15.refs_4_ = bf16[32,2,40,256]{3,2,1,0:T(8,128)(2,1)} all-to-all(bf16[32,2,40,256]{3,2,1,0:T(8,128)(2,1)S(1)} %pad_maximum_fusion), channel_id=1, replica_groups=mesh['seq'=8,'exp'=32] {'exp'}, dimensions={0} | all-to-all | bytes 2621440 | tf_op jit(solution)/shard_map/all_to_all | solution.py:383
  193.4 9.9 %attention_grad.1 = (f32[128,2048]{1,0:T(8,128)}, f32[128,2048]{1,0:T(8,128)}, bf16[2,128,2048]{2,1,0:T(8,128)(2,1)}, bf16[2,128,2048]{2,1,0:T(8,128)(2,1)}) custom-call(s32[1]{0:T(128)} %bitcast.seq_ref.refs_0_, s32[2,3]{1,0:T(2,128)} %bitcast.80, s32[2,128]{1,0:T(2,128)} %bitcast.83, f32[2,128]{1,0:T(2,128)} %bitcast.84, ...), custom_call_target="tpu_custom_call" | custom-call | flops 12884901888 | bytes 1048576 | tf_op jit(solution)/shard_map/attention_grad/pallas_call | solution.py:475
  203.3 7.2 %collective-permute-start.14 = (bf16[2,128,2048]{2,1,0:T(8,128)(2,1)}, bf16[2,128,2048]{2,1,0:T(8,128)(2,1)S(1)}, u32[]{:S(2)}, u32[]{:S(2)}) collective-permute-start(bf16[2,128,2048]{2,1,0:T(8,128)(2,1)} %get-tuple-element.55), channel_id=1, source_target_pairs={{32,0},{64,32},{96,64},{128,96},{160,128},{192,160},{224,192},{33,... | collective-permute-start | bytes 3145736 | tf_op jit(solution)/shard_map/ppermute | solution.py:491
  210.5 1.9 collective-permute-start.15
  212.4 10.6 %collective-permute-done.14 = bf16[2,128,2048]{2,1,0:T(8,128)(2,1)S(1)} collective-permute-done((bf16[2,128,2048]{2,1,0:T(8,128)(2,1)}, bf16[2,128,2048]{2,1,0:T(8,128)(2,1)S(1)}, u32[]{:S(2)}, u32[]{:S(2)}) %collective-permute-start.14) | collective-permute-done | bytes 1048608 | tf_op jit(solution)/shard_map/ppermute | solution.py:491
  223.0 1.4 collective-permute-done.15
  224.5 3.0 %fusion.3 = (bf16[1,128,2048]{2,1,0:T(8,128)(2,1)}, bf16[1,128,2048]{2,1,0:T(8,128)(2,1)}) fusion(f32[128,2048]{1,0:T(8,128)} %get-tuple-element.57, bf16[2,128,2048]{2,1,0:T(8,128)(2,1)S(1)} %collective-permute-done.15, bf16[2,128,2048]{2,1,0:T(8,128)(2,1)S(1)} %collective-permute-done.14, f32[128,2048]{1,0:T(8,128)} %get-tuple-element.54), kind=kLoop, calls=%fused_computation.10 | loop fusion | flops 2621440 | bytes 5242880 | tf_op jit(solution)/shard_map/broadcast_in_dim | solution.py:495
  (44 shorter events, 4.3 us)
Async XLA Ops:
  4.9 18.5 %collective-permute-start = (bf16[2,128,2048]{2,1,0:T(8,128)(2,1)}, bf16[2,128,2048]{2,1,0:T(8,128)(2,1)}, u32[]{:S(2)}, u32[]{:S(2)}) collective-permute-start(bf16[2,128,2048]{2,1,0:T(8,128)(2,1)} %get-tuple-element.30), channel_id=1, source_target_pairs={{0,32},{32,64},{64,96},{96,128},{128,160},{160,192},{192,224},{1,3... | collective-permute-start | bytes 3145736 | tf_op jit(solution)/shard_map/ppermute | solution.py:394
  9.4 16.6 %collective-permute-start.1 = (bf16[2,128,2048]{2,1,0:T(8,128)(2,1)}, bf16[2,128,2048]{2,1,0:T(8,128)(2,1)}, u32[]{:S(2)}, u32[]{:S(2)}) collective-permute-start(bf16[2,128,2048]{2,1,0:T(8,128)(2,1)} %get-tuple-element.30), channel_id=1, source_target_pairs={{32,0},{64,32},{96,64},{128,96},{160,128},{192,160},{224,192},{33,... | collective-permute-start | bytes 3145736 | tf_op jit(solution)/shard_map/ppermute | solution.py:394
  12.4 11.0 %copy-start.3 = (bf16[1,1,512,2048]{3,2,1,0:T(8,128)(2,1)S(1)}, bf16[1,1,512,2048]{3,2,1,0:T(8,128)(2,1)}, u32[]{:S(2)}) copy-start(bf16[1,1,512,2048]{3,2,1,0:T(8,128)(2,1)} %param.23) | copy-start | bytes 6291460
  12.4 43.8 %all-to-all-start = ((bf16[32,2,40,256]{3,2,1,0:T(8,128)(2,1)}), bf16[32,2,40,256]{3,2,1,0:T(8,128)(2,1)S(1)}, u32[]{:S(2)}, u32[]{:S(2)}) async-start(bf16[32,2,40,256]{3,2,1,0:T(8,128)(2,1)} %get-tuple-element.32), calls=%async_computation | async-start | bytes 2621440 | tf_op jit(solution)/shard_map/all_to_all | solution.py:383
  22.7 11.6 %collective-permute-start.2 = (bf16[2048,512]{1,0:T(8,128)(2,1)}, bf16[2048,512]{1,0:T(8,128)(2,1)S(1)}, u32[]{:S(2)}, u32[]{:S(2)}) collective-permute-start(bf16[2048,512]{1,0:T(8,128)(2,1)} %bitcast.60), channel_id=1, source_target_pairs={{0,32},{32,0},{64,96},{96,64},{128,160},{160,128},{192,224},{224,1... | collective-permute-start | bytes 6291464 | tf_op jit(solution)/shard_map/ppermute | solution.py:380
  22.8 11.6 %collective-permute-start.3 = (bf16[2048,512]{1,0:T(8,128)(2,1)}, bf16[2048,512]{1,0:T(8,128)(2,1)S(1)}, u32[]{:S(2)}, u32[]{:S(2)}) collective-permute-start(bf16[2048,512]{1,0:T(8,128)(2,1)} %bitcast.64), channel_id=1, source_target_pairs={{0,32},{32,0},{64,96},{96,64},{128,160},{160,128},{192,224},{224,1... | collective-permute-start | bytes 6291464 | tf_op jit(solution)/shard_map/ppermute | solution.py:380
  23.3 13.8 %collective-permute-start.4 = (bf16[512,2048]{1,0:T(8,128)(2,1)S(1)}, bf16[512,2048]{1,0:T(8,128)(2,1)}, u32[]{:S(2)}, u32[]{:S(2)}) collective-permute-start(bf16[512,2048]{1,0:T(8,128)(2,1)S(1)} %bitcast.59), channel_id=1, source_target_pairs={{0,32},{32,0},{64,96},{96,64},{128,160},{160,128},{192,224},{224,1... | collective-permute-start | bytes 6291464 | tf_op jit(solution)/shard_map/ppermute | solution.py:380
  34.4 1.3 copy-start.4
  35.7 1.4 copy-start.5
  56.1 37.6 %all-to-all-start.1 = ((bf16[32,2,40,256]{3,2,1,0:T(8,128)(2,1)}), bf16[32,2,40,256]{3,2,1,0:T(8,128)(2,1)S(1)}, u32[]{:S(2)}, u32[]{:S(2)}) async-start(bf16[32,2,40,256]{3,2,1,0:T(8,128)(2,1)} %get-tuple-element.33), calls=%async_computation.1 | async-start | bytes 2621440 | tf_op jit(solution)/shard_map/all_to_all | solution.py:383
  61.7 1.7 copy-start.1
  61.7 16.7 %collective-permute-start.5 = (bf16[1280,256]{1,0:T(8,128)(2,1)S(1)}, bf16[1280,256]{1,0:T(8,128)(2,1)S(1)}, u32[]{:S(2)}, u32[]{:S(2)}) collective-permute-start(bf16[1280,256]{1,0:T(8,128)(2,1)S(1)} %bitcast.48), channel_id=1, source_target_pairs={{0,192},{32,224},{64,128},{96,160},{128,64},{160,96},{192,0},{224,... | collective-permute-start | bytes 1966088 | tf_op jit(solution)/shard_map/ppermute | solution.py:380
  63.4 15.0 %collective-permute-start.6 = (bf16[1280,256]{1,0:T(8,128)(2,1)S(1)}, bf16[1280,256]{1,0:T(8,128)(2,1)S(1)}, u32[]{:S(2)}, u32[]{:S(2)}) collective-permute-start(bf16[1280,256]{1,0:T(8,128)(2,1)S(1)} %bitcast.54), channel_id=1, source_target_pairs={{0,64},{32,96},{64,0},{96,32},{128,192},{160,224},{192,128},{224,1... | collective-permute-start | bytes 1966088 | tf_op jit(solution)/shard_map/ppermute | solution.py:380
  78.4 0.9 copy-start.10
  78.4 1.1 copy-start.11
  78.4 25.8 %collective-permute-start.7 = (bf16[1280,256]{1,0:T(8,128)(2,1)S(1)}, bf16[1280,256]{1,0:T(8,128)(2,1)S(1)}, u32[]{:S(2)}, u32[]{:S(2)}) collective-permute-start(bf16[1280,256]{1,0:T(8,128)(2,1)S(1)} %bitcast.49), channel_id=1, source_target_pairs={{0,128},{32,160},{64,192},{96,224},{128,0},{160,32},{192,64},{224,... | collective-permute-start | bytes 1966088 | tf_op jit(solution)/shard_map/ppermute | solution.py:380
  93.9 0.9 copy-start
  93.9 16.5 %collective-permute-start.8 = (bf16[1280,256]{1,0:T(8,128)(2,1)S(1)}, bf16[1280,256]{1,0:T(8,128)(2,1)S(1)}, u32[]{:S(2)}, u32[]{:S(2)}) collective-permute-start(bf16[1280,256]{1,0:T(8,128)(2,1)S(1)} %bitcast.50), channel_id=1, source_target_pairs={{0,192},{32,224},{64,128},{96,160},{128,64},{160,96},{192,0},{224,... | collective-permute-start | bytes 1966088 | tf_op jit(solution)/shard_map/ppermute | solution.py:380
  94.0 16.4 %collective-permute-start.9 = (bf16[1280,256]{1,0:T(8,128)(2,1)S(1)}, bf16[1280,256]{1,0:T(8,128)(2,1)S(1)}, u32[]{:S(2)}, u32[]{:S(2)}) collective-permute-start(bf16[1280,256]{1,0:T(8,128)(2,1)S(1)} %bitcast.52), channel_id=1, source_target_pairs={{0,64},{32,96},{64,0},{96,32},{128,192},{160,224},{192,128},{224,1... | collective-permute-start | bytes 1966088 | tf_op jit(solution)/shard_map/ppermute | solution.py:380
  104.2 0.8 copy-start.6
  110.4 3.2 %copy-start.7 = (bf16[1280,256]{1,0:T(8,128)(2,1)}, bf16[1280,256]{1,0:T(8,128)(2,1)S(1)}, u32[]{:S(2)}) copy-start(bf16[1280,256]{1,0:T(8,128)(2,1)S(1)} %collective-permute-done.8.refs_0_) | copy-start | bytes 1966084
  110.4 3.2 %copy-start.8 = (bf16[1280,256]{1,0:T(8,128)(2,1)}, bf16[1280,256]{1,0:T(8,128)(2,1)S(1)}, u32[]{:S(2)}) copy-start(bf16[1280,256]{1,0:T(8,128)(2,1)S(1)} %collective-permute-done.9.refs_1_) | copy-start | bytes 1966084
  110.4 15.9 %collective-permute-start.12 = (bf16[1280,256]{1,0:T(8,128)(2,1)S(1)}, bf16[1280,256]{1,0:T(8,128)(2,1)S(1)}, u32[]{:S(2)}, u32[]{:S(2)}) collective-permute-start(bf16[1280,256]{1,0:T(8,128)(2,1)S(1)} %bitcast.51), channel_id=1, source_target_pairs={{0,128},{32,160},{64,192},{96,224},{128,0},{160,32},{192,64},{224,... | collective-permute-start | bytes 1966088 | tf_op jit(solution)/shard_map/ppermute | solution.py:380
  124.9 15.0 %collective-permute-start.10 = (bf16[1280,256]{1,0:T(8,128)(2,1)}, bf16[1280,256]{1,0:T(8,128)(2,1)S(1)}, u32[]{:S(2)}, u32[]{:S(2)}) collective-permute-start(bf16[1280,256]{1,0:T(8,128)(2,1)} %get-tuple-element.47), channel_id=1, source_target_pairs={{0,64},{32,96},{64,0},{96,32},{128,192},{160,224},{192,128},{224,1... | collective-permute-start | bytes 1966088 | tf_op jit(solution)/shard_map/ppermute | solution.py:380
  125.0 14.9 %copy-start.2 = (bf16[1280,256]{1,0:T(8,128)(2,1)S(1)}, bf16[1280,256]{1,0:T(8,128)(2,1)}, u32[]{:S(2)}) copy-start(bf16[1280,256]{1,0:T(8,128)(2,1)} %expert.3) | copy-start | bytes 1966084
  125.0 15.2 %collective-permute-start.11 = (bf16[1280,256]{1,0:T(8,128)(2,1)}, bf16[1280,256]{1,0:T(8,128)(2,1)S(1)}, u32[]{:S(2)}, u32[]{:S(2)}) collective-permute-start(bf16[1280,256]{1,0:T(8,128)(2,1)} %get-tuple-element.48), channel_id=1, source_target_pairs={{0,192},{32,224},{64,128},{96,160},{128,64},{160,96},{192,0},{224,... | collective-permute-start | bytes 1966088 | tf_op jit(solution)/shard_map/ppermute | solution.py:380
  126.3 0.9 copy-start.9
  136.7 16.4 %collective-permute-start.13 = (bf16[1280,256]{1,0:T(8,128)(2,1)}, bf16[1280,256]{1,0:T(8,128)(2,1)S(1)}, u32[]{:S(2)}, u32[]{:S(2)}) collective-permute-start(bf16[1280,256]{1,0:T(8,128)(2,1)} %expert.5), channel_id=1, source_target_pairs={{0,128},{32,160},{64,192},{96,224},{128,0},{160,32},{192,64},{224,... | collective-permute-start | bytes 1966088 | tf_op jit(solution)/shard_map/ppermute | solution.py:380
  203.3 19.8 %collective-permute-start.14 = (bf16[2,128,2048]{2,1,0:T(8,128)(2,1)}, bf16[2,128,2048]{2,1,0:T(8,128)(2,1)S(1)}, u32[]{:S(2)}, u32[]{:S(2)}) collective-permute-start(bf16[2,128,2048]{2,1,0:T(8,128)(2,1)} %get-tuple-element.55), channel_id=1, source_target_pairs={{32,0},{64,32},{96,64},{128,96},{160,128},{192,160},{224,192},{33,... | collective-permute-start | bytes 3145736 | tf_op jit(solution)/shard_map/ppermute | solution.py:491
  210.5 14.0 %collective-permute-start.15 = (bf16[2,128,2048]{2,1,0:T(8,128)(2,1)}, bf16[2,128,2048]{2,1,0:T(8,128)(2,1)S(1)}, u32[]{:S(2)}, u32[]{:S(2)}) collective-permute-start(bf16[2,128,2048]{2,1,0:T(8,128)(2,1)} %get-tuple-element.56), channel_id=1, source_target_pairs={{0,32},{32,64},{64,96},{96,128},{128,160},{160,192},{192,224},{1,3... | collective-permute-start | bytes 3145736 | tf_op jit(solution)/shard_map/ppermute | solution.py:492

commit v4 on v3

--- a/solution.py
+++ b/solution.py
@@ -13,7 +13,7 @@
 PIECES = 8
 GROUP = 8
 EPSILON = 1e-06
-ATTN = 16
+ATTN = 8
 UNROLL = 4
 MICRO = 1 << 30
 F32 = jnp.float32
@@ -106,9 +106,7 @@
             out_ref[chunk * GROUP : (chunk + 1) * GROUP, rel] = block.reshape(GROUP, CELL, piece)
 
 
-def grad_kernel(seq_ref, ids_ref, x_ref, perm_ref, k_ref, v_ref, out_ref, pair_ref, rows_ref):
-    pair_ref[0] = k_ref[...]
-    pair_ref[1] = v_ref[...]
+def grad_kernel(seq_ref, ids_ref, x_ref, perm_ref, out_ref, rows_ref):
     send_rows(seq_ref, ids_ref, x_ref[...], perm_ref, out_ref, rows_ref)
 
 
@@ -136,22 +134,18 @@
     return jnp.concatenate([ref[pl.ds(p, TILE), lanes] for p in places], axis=0)
 
 
-def halo_copies(dst_ref, left_ref, own_ref, right_ref, which, sems, first):
+def fill_halo(dst_ref, left_ref, own_ref, right_ref):
     count = own_ref.shape[0]
-    return [
-        pltpu.make_async_copy(src, dst_ref.at[i * count : (i + 1) * count], sems.at[first + i])
-        for i, src in enumerate((left_ref.at[which], own_ref, right_ref.at[which]))
-    ]
+    for i, src in enumerate((left_ref, own_ref, right_ref)):
+        dst_ref[i * count : (i + 1) * count, :] = src[...]
 
 
 def forward_kernel(
-    seq_ref, offs_ref, ids_ref, q_ref, left_ref, k_ref, v_ref, right_ref, gain_ref, perm_ref,
-    wts_ref, unit_ref, inv_ref, sent_ref, kx_ref, vx_ref, out_ref, rows_ref, sems, total_tiles,
+    seq_ref, offs_ref, ids_ref, q_ref, kl_ref, k_ref, kr_ref, vl_ref, v_ref, vr_ref, gain_ref,
+    perm_ref, wts_ref, unit_ref, inv_ref, sent_ref, kx_ref, vx_ref, out_ref, rows_ref, total_tiles,
 ):
-    copies = halo_copies(kx_ref, left_ref, k_ref, right_ref, 0, sems, 0)
-    copies += halo_copies(vx_ref, left_ref, v_ref, right_ref, 1, sems, NBR)
-    for copy in copies:
-        copy.start()
+    fill_halo(kx_ref, kl_ref, k_ref, kr_ref)
+    fill_halo(vx_ref, vl_ref, v_ref, vr_ref)
     count, width = q_ref.shape
     heads = width // HEAD_DIM
     tiles = count // TILE
@@ -168,9 +162,6 @@
         spots.append(places)
         biases.append(bias)
 
-    for copy in copies:
-        copy.wait()
-
     def body(step, carry):
         spans = head_spans(step, heads, tiles)
         scores = [
@@ -198,22 +189,15 @@
 
 def hidden_kernel(*refs, blocks):
     ins = refs[:blocks]
-    perm_t_ref, down0_ref, down1_ref, out_ref, rows_ref, w_ref, sems = refs[blocks:]
-    copies = [
-        pltpu.make_async_copy(src, w_ref.at[i], sems.at[i])
-        for i, src in enumerate((down0_ref, down1_ref))
-    ]
-    for copy in copies:
-        copy.start()
+    perm_t_ref, down0_ref, down1_ref, out_ref, rows_ref = refs[blocks:]
     piece = ins[0].shape[1]
     chunks = ins[0].shape[0] // CHUNK
     perm_t = perm_t_ref[...]
     for b, block in enumerate(ins):
         from_wire(block, rows_ref, b * chunks * ROWS, perm_t, chunks, piece)
     part = down0_ref.shape[0]
-    for i, copy in enumerate(copies):
-        copy.wait()
-        out_ref[:, i * part : (i + 1) * part] = dot_nt(rows_ref[...], w_ref[i])
+    for i, w_ref in enumerate((down0_ref, down1_ref)):
+        out_ref[:, i * part : (i + 1) * part] = dot_nt(rows_ref[...], w_ref[...])
 
 
 def expert_kernel(*refs, blocks):
@@ -221,31 +205,25 @@
     hg_ref, perm_ref, perm_t_ref = refs[blocks : blocks + 3]
     weights = refs[blocks + 3 : blocks + 7]
     outs = refs[blocks + 7 : 2 * blocks + 7]
-    rows_ref, w_ref, act_ref, total_ref, sems = refs[2 * blocks + 7 :]
-    copies = [pltpu.make_async_copy(src, w_ref.at[i], sems.at[i]) for i, src in enumerate(weights)]
-    for copy in copies:
-        copy.start()
+    rows_ref, act_ref, total_ref = refs[2 * blocks + 7 :]
     piece = ins[0].shape[1]
     chunks = ins[0].shape[0] // CHUNK
     perm_t = perm_t_ref[...]
     for b, block in enumerate(ins):
         from_wire(block, rows_ref, b * chunks * ROWS, perm_t, chunks, piece)
-    part = w_ref.shape[2]
+    width, part = weights[0].shape
     for i in range(2):
-        copies[2 * i].wait()
-        gate_proj = dot(rows_ref[...], w_ref[2 * i])
-        copies[2 * i + 1].wait()
-        up_proj = dot(rows_ref[...], w_ref[2 * i + 1])
+        gate_proj = dot(rows_ref[...], weights[2 * i][...])
+        up_proj = dot(rows_ref[...], weights[2 * i + 1][...])
         hidden = hg_ref[:, i * part : (i + 1) * part]
         sig = jax.nn.sigmoid(gate_proj)
         act_ref[2 * i + 1] = (hidden * gate_proj * sig).astype(BF16)
         act_ref[2 * i] = (hidden * up_proj * sig * (1.0 + gate_proj * (1.0 - sig))).astype(BF16)
-    width = total_ref.shape[1]
     for n in range(width // 512):
         cols = slice(n * 512, (n + 1) * 512)
-        total = dot_nt(act_ref[0], w_ref[0, cols, :])
+        total = dot_nt(act_ref[0], weights[0][cols, :])
         for i in range(1, 4):
-            total = total + dot_nt(act_ref[i], w_ref[i, cols, :])
+            total = total + dot_nt(act_ref[i], weights[i][cols, :])
         total_ref[:, cols] = total
     perm = perm_ref[...]
     for b, dst in enumerate(outs):
@@ -256,14 +234,10 @@
 
 def backward_kernel(
     seq_ref, offs_ref, ids_ref, gates_ref, home_ref, grad_ref, unit_ref, inv_ref, gain_ref,
-    perm_t_ref, q_hbm, left_ref, v_ref, right_ref, wts_hbm, k_out_ref, v_out_ref, to_left_ref,
-    to_right_ref, vx_ref, q_ref, wts_ref, rows_ref, ag_ref, ka_ref, va_ref, sems, total_tiles,
+    perm_t_ref, q_ref, vl_ref, v_ref, vr_ref, wts_ref, k_out_ref, v_out_ref, to_left_ref,
+    to_right_ref, vx_ref, rows_ref, ag_ref, ka_ref, va_ref, total_tiles,
 ):
-    copies = halo_copies(vx_ref, left_ref, v_ref, right_ref, 1, sems, 0)
-    copies.append(pltpu.make_async_copy(q_hbm, q_ref, sems.at[NBR]))
-    copies.append(pltpu.make_async_copy(wts_hbm, wts_ref, sems.at[NBR + 1]))
-    for copy in copies:
-        copy.start()
+    fill_halo(vx_ref, vl_ref, v_ref, vr_ref)
     count, width = q_ref.shape
     heads = width // HEAD_DIM
     tiles = count // TILE
@@ -291,9 +265,6 @@
     attn_grad = grad_ref[...].astype(F32) + inv_ref[:, 0:1] * (scaled - unit * inner)
     ag_ref[...] = attn_grad.astype(BF16)
     spots = [tile_places(seq_ref, offs_ref, t, tiles, total_tiles)[0] for t in range(tiles)]
-    for copy in copies:
-        copy.wait()
-
     def body(step, carry):
         spans = head_spans(step, heads, tiles)
         prob_grads = [
@@ -331,15 +302,15 @@
     to_right_ref[1] = va_ref[2 * count : 3 * count, :].astype(BF16)
 
 
-def call(body, outs, kinds, scratch, name, flops, out_kinds=None):
-    spaces = {"s": pltpu.SMEM, "v": pltpu.VMEM, "a": pl.ANY}
+def call(body, outs, kinds, scratch, name, flops, megabytes):
+    spaces = {"s": pltpu.SMEM, "v": pltpu.VMEM}
     return pl.pallas_call(
         body,
         out_shape=outs,
         in_specs=[pl.BlockSpec(memory_space=spaces[kind]) for kind in kinds],
-        out_specs=[pl.BlockSpec(memory_space=spaces[kind]) for kind in out_kinds or "v" * len(outs)],
+        out_specs=[pl.BlockSpec(memory_space=pltpu.VMEM) for _ in outs],
         scratch_shapes=scratch,
-        compiler_params=pltpu.CompilerParams(vmem_limit_bytes=56 * 1024 * 1024),
+        compiler_params=pltpu.CompilerParams(vmem_limit_bytes=megabytes << 20),
         cost_estimate=pl.CostEstimate(flops=flops, transcendentals=0, bytes_accessed=1 << 20),
         name=name,
     )
@@ -384,14 +355,12 @@
 
     barrier = lax.optimization_barrier
     pair = (2, count, width)
-    sent_grad, kv = call(
-        grad_kernel,
-        (shape(wire, BF16), shape(pair, BF16)),
-        "svvvvv",
-        [pltpu.VMEM((2 * slots, width), F32)],
-        "place_grad", 4 * MICRO,
-    )(seq, ids_t, grad, perm, k, v)
-    left, right = lax.ppermute(kv, "seq", up_by), lax.ppermute(kv, "seq", down_by)
+    kl, kr = lax.ppermute(k, "seq", up_by), lax.ppermute(k, "seq", down_by)
+    vl, vr = lax.ppermute(v, "seq", up_by), lax.ppermute(v, "seq", down_by)
+    (sent_grad,) = call(
+        grad_kernel, (shape(wire, BF16),), "svvv", [pltpu.VMEM((2 * slots, width), F32)],
+        "place_grad", 4 * MICRO, 12,
+    )(seq, ids_t, grad, perm)
     got_grad = exchange(sent_grad)
     gate_s, up_s, down_s = swap(gate, 1), swap(up, 1), swap(down, 1)
 
@@ -403,16 +372,15 @@
             shape((count, HEAD_DIM), F32),
             shape(wire, BF16),
         ),
-        "ssvvaaaavv",
+        "ssv" + "v" * 9,
         [
             pltpu.VMEM((3 * count, width), BF16),
             pltpu.VMEM((3 * count, width), BF16),
             pltpu.VMEM((count, width), F32),
             pltpu.VMEM((2 * slots, width), F32),
-            pltpu.SemaphoreType.DMA((2 * NBR,)),
         ],
-        "attention", ATTN * MICRO,
-    )(seq, offsets, ids_t, q, left, k, v, right, gain, perm)
+        "attention", ATTN * MICRO, 20,
+    )(seq, offsets, ids_t, q, kl, k, kr, vl, v, vr, gain, perm)
 
     sent, got_grad, gate_s, up_s, down_s = barrier((sent, got_grad, gate_s, up_s, down_s))
     got = exchange(sent)
@@ -432,13 +400,9 @@
         (out,) = call(
             lambda *refs: hidden_kernel(*refs, blocks=blocks),
             (shape((blocks * slots, 2 * part), F32),),
-            "v" * (blocks + 1) + "aa",
-            [
-                pltpu.VMEM((blocks * slots, width), BF16),
-                pltpu.VMEM((2, part, width), BF16),
-                pltpu.SemaphoreType.DMA((2,)),
-            ],
-            "hidden", micros * MICRO,
+            "v" * (blocks + 3),
+            [pltpu.VMEM((blocks * slots, width), BF16)],
+            "hidden", micros * MICRO, 14,
         )(*ins, perm_t, down, down_s)
         return out
 
@@ -447,15 +411,13 @@
         return call(
             lambda *refs: expert_kernel(*refs, blocks=blocks),
             (shape(flat, BF16),) * blocks,
-            "v" * (blocks + 3) + "aaaa",
+            "v" * (blocks + 7),
             [
                 pltpu.VMEM((blocks * slots, width), BF16),
-                pltpu.VMEM((4, width, part), BF16),
                 pltpu.VMEM((4, blocks * slots, part), BF16),
                 pltpu.VMEM((blocks * slots, width), F32),
-                pltpu.SemaphoreType.DMA((4,)),
             ],
-            "expert", micros * MICRO,
+            "expert", micros * MICRO, 24,
         )(*ins, hg, perm, perm_t, gate, up, gate_s, up_s)
 
     hidden_own = hidden((g0,), 4)
@@ -475,24 +437,21 @@
     k_own, v_own, to_left, to_right = call(
         lambda *refs: backward_kernel(*refs, total_tiles=total_tiles),
         (shape((count, width), F32), shape((count, width), F32), shape(pair, BF16), shape(pair, BF16)),
-        "ssvvvvvvvvaaaaa",
+        "ss" + "v" * 13,
         [
             pltpu.VMEM((3 * count, width), BF16),
-            pltpu.VMEM((count, width), BF16),
-            pltpu.VMEM(wts.shape, F32),
             pltpu.VMEM((2 * slots, width), BF16),
             pltpu.VMEM((count, width), BF16),
             pltpu.VMEM((3 * count, width), F32),
             pltpu.VMEM((3 * count, width), F32),
-            pltpu.SemaphoreType.DMA((NBR + 2,)),
         ],
-        "attention_grad", 12 * MICRO,
-    )(seq, offsets, ids_t, gates_t, home, grad, unit, inv, gain, perm_t, q, left, v, right, wts)
-    from_right = lax.ppermute(to_left, "seq", down_by)
-    from_left = lax.ppermute(to_right, "seq", up_by)
+        "attention_grad", 10 * MICRO, 24,
+    )(seq, offsets, ids_t, gates_t, home, grad, unit, inv, gain, perm_t, q, vl, v, vr, wts)
+    from_right = lax.ppermute(to_left, "seq", down_by).astype(F32)
+    from_left = lax.ppermute(to_right, "seq", up_by).astype(F32)
 
     def finish(own_part, i):
-        return (own_part + from_right[i].astype(F32) + from_left[i].astype(F32)).astype(BF16)[None]
+        return (own_part + from_right[i] + from_left[i]).astype(BF16)[None]
 
     return (finish(k_own, 0), finish(v_own, 1))
 

time: 228 us -> 238 us (1.044)
  Pallas kernels: 69.1 us -> 38.9 us
  starting transfers between devices: 42 us -> 61.9 us
  local copies, waits for them, and re-layouts: 6.1 us -> 22.5 us
  blocking collectives: 40 us -> 43.4 us
    all_to_all x2, waiting for transfers between devices: 27.5 us -> 2.64 us  [exchange(): return lax.all_to_all(x, 'exp', split_axis=0, concat_axis=0, tiled=True)]
    ppermute x12, waiting for transfers between devices: 23.7 us -> 38.7 us  [swap(): return lax.ppermute(x, 'seq', [(i, i ^ bits) for i in range(seq_count)])]
    pallas_call x3, Pallas kernels: 30.3 us -> 17.6 us  [expert(): call(lambda *refs: expert_kernel(*refs, blocks=blocks), (shape(flat, BF16...]
    unnamed x24 -> x80, local copies, waits for them, and re-layouts: 5.93 us -> 18.6 us
    ppermute x4 -> x6, waiting for transfers between devices: 14.7 us -> 25.9 us  [the longest x1 10.5 us: on_device(): from_right = lax.ppermute(to_left, 'seq', down_by).astype(F32)]
    ppermute x12, starting transfers between devices: 9.69 us -> 20.9 us  [swap(): return lax.ppermute(x, 'seq', [(i, i ^ bits) for i in range(seq_count)])]
    pallas_call x3, Pallas kernels: 16.4 us -> 5.86 us  [hidden(): call(lambda *refs: hidden_kernel(*refs, blocks=blocks), (shape((blocks *...]
    all_to_all x2, starting transfers between devices: 15.8 us -> 22 us  [exchange(): return lax.all_to_all(x, 'exp', split_axis=0, concat_axis=0, tiled=True)]
  transfers between devices with their start and end apart: 18 -> 20, of which waited for: 9 -> 13; matrix products, arithmetic and copies ran while one was open for 0% -> 2% of each run, Pallas kernels for 24% -> 12%
where the time goes in v4:
time: 238 us; the launch traced here: 237 us
  waiting for transfers between devices  67.3 us (28%)
  starting transfers between devices  61.9 us (26%)
  blocking collectives  43.4 us (18%)
  Pallas kernels  38.9 us (16%)
  local copies, waits for them, and re-layouts  22.5 us (9%)
    all_to_all x1, blocking collectives, exchange(): return lax.all_to_all(x, 'exp', split_axis=0, concat_axis=0, tiled=True)  43.4 us
    ppermute x12, waiting for transfers between devices, swap(): return lax.ppermute(x, 'seq', [(i, i ^ bits) for i in range(seq_count)])  38.7 us
    all_to_all x2, starting transfers between devices, exchange(): return lax.all_to_all(x, 'exp', split_axis=0, concat_axis=0, tiled=True)  22 us
    ppermute x12, starting transfers between devices, swap(): return lax.ppermute(x, 'seq', [(i, i ^ bits) for i in range(seq_count)])  20.9 us
    unnamed x80, local copies, waits for them, and re-layouts  18.6 us
    pallas_call x3, Pallas kernels, expert(): call(lambda *refs: expert_kernel(*refs, blocks=blocks), (shape(flat, BF16...  17.6 us
    ppermute x1, waiting for transfers between devices, on_device(): from_right = lax.ppermute(to_left, 'seq', down_by).astype(F32)  10.5 us
    ppermute x2, waiting for transfers between devices, on_device(): kl, kr = (lax.ppermute(k, 'seq', up_by), lax.ppermute(k, 'seq', down_by))  8.97 us
  transfers between devices with their start and end apart: 20, of which 13 were waited for; matrix products, arithmetic and copies ran while one was open for 2% of the time, Pallas kernels for 12%

profile of v4, /device:TPU:1, one launch (start us, length us, event | category | flops | bytes accessed | tf_op | source)
XLA Modules:
  0.0 237.4 jit_solution(771599218383162526)
XLA Ops:
  3.3 2.5 %place_grad.1 = bf16[32,2,40,256]{3,2,1,0:T(8,128)(2,1)} custom-call(s32[1]{0:T(128)} %bitcast.refs_0_.seq_ref, s32[2,128]{1,0:T(2,128)S(1)} %bitcast.89, bf16[128,2048]{1,0:T(8,128)(2,1)S(1)} %bitcast.83, bf16[320,320]{1,0:T(8,128)(2,1)S(1)} %copy-done.28), custom_call_target="tpu_custom_call" | custom-call | flops 4294967296 | bytes 1048576 | tf_op jit(solution)/shard_map/place_grad/pallas_call | solution.py:360
  5.8 12.4 %all-to-all-start = ((bf16[32,2,40,256]{3,2,1,0:T(8,128)(2,1)}), bf16[32,2,40,256]{3,2,1,0:T(8,128)(2,1)}, u32[]{:S(2)}, u32[]{:S(2)}) async-start(bf16[32,2,40,256]{3,2,1,0:T(8,128)(2,1)} %place_grad.1), calls=%async_computation | async-start | bytes 2621440 | tf_op jit(solution)/shard_map/all_to_all | solution.py:354
  19.8 3.1 %collective-permute-start.2 = (bf16[128,2048]{1,0:T(8,128)(2,1)}, bf16[128,2048]{1,0:T(8,128)(2,1)S(1)}, u32[]{:S(2)}, u32[]{:S(2)}) collective-permute-start(bf16[128,2048]{1,0:T(8,128)(2,1)} %bitcast.79), channel_id=1, source_target_pairs={{0,32},{32,64},{64,96},{96,128},{128,160},{160,192},{192,224},{1,3... | collective-permute-start | bytes 1572872 | tf_op jit(solution)/shard_map/ppermute | solution.py:359
  22.9 1.9 collective-permute-start.3
  24.8 5.1 %collective-permute-done.2.refs_7_.refs_11_ = bf16[128,2048]{1,0:T(8,128)(2,1)S(1)} collective-permute-done((bf16[128,2048]{1,0:T(8,128)(2,1)}, bf16[128,2048]{1,0:T(8,128)(2,1)S(1)}, u32[]{:S(2)}, u32[]{:S(2)}) %collective-permute-start.2) | collective-permute-done | bytes 524320 | tf_op jit(solution)/shard_map/ppermute | solution.py:359
  29.9 3.7 %collective-permute-start = (bf16[128,2048]{1,0:T(8,128)(2,1)S(1)}, bf16[128,2048]{1,0:T(8,128)(2,1)S(1)}, u32[]{:S(2)}, u32[]{:S(2)}) collective-permute-start(bf16[128,2048]{1,0:T(8,128)(2,1)S(1)} %bitcast.74), channel_id=1, source_target_pairs={{0,32},{32,64},{64,96},{96,128},{128,160},{160,192},{192,224},{1,3... | collective-permute-start | bytes 1572872 | tf_op jit(solution)/shard_map/ppermute | solution.py:358
  34.0 1.9 collective-permute-start.1
  35.9 3.8 %collective-permute-done.refs_4_ = bf16[128,2048]{1,0:T(8,128)(2,1)S(1)} collective-permute-done((bf16[128,2048]{1,0:T(8,128)(2,1)S(1)}, bf16[128,2048]{1,0:T(8,128)(2,1)S(1)}, u32[]{:S(2)}, u32[]{:S(2)}) %collective-permute-start) | collective-permute-done | bytes 524320 | tf_op jit(solution)/shard_map/ppermute | solution.py:358
  39.7 5.2 %collective-permute-done.1.refs_6_ = bf16[128,2048]{1,0:T(8,128)(2,1)S(1)} collective-permute-done((bf16[128,2048]{1,0:T(8,128)(2,1)S(1)}, bf16[128,2048]{1,0:T(8,128)(2,1)S(1)}, u32[]{:S(2)}, u32[]{:S(2)}) %collective-permute-start.1) | collective-permute-done | bytes 524320 | tf_op jit(solution)/shard_map/ppermute | solution.py:358
  46.0 6.0 %attention.1 = (f32[32,64,192]{2,1,0:T(8,128)S(1)}, f32[128,2048]{1,0:T(8,128)S(1)}, f32[128,128]{1,0:T(8,128)S(1)}, bf16[32,2,40,256]{3,2,1,0:T(8,128)(2,1)}) custom-call(s32[1]{0:T(128)} %bitcast.refs_0_.seq_ref, s32[2,3]{1,0:T(2,128)S(1)} %bitcast.87, s32[2,128]{1,0:T(2,128)S(1)} %bitcast.90, bf16[128,2048]{1,0:T(8,128)(2,1)S(1)} %bitcast.77, ...), custom_call_target="tpu_custom_call" | custom-call | flops 8589934592 | bytes 1048576 | tf_op jit(solution)/shard_map/attention/pallas_call | solution.py:367
  59.1 9.5 %all-to-all-start.1 = ((bf16[32,2,40,256]{3,2,1,0:T(8,128)(2,1)}), bf16[32,2,40,256]{3,2,1,0:T(8,128)(2,1)}, u32[]{:S(2)}, u32[]{:S(2)}) async-start(bf16[32,2,40,256]{3,2,1,0:T(8,128)(2,1)} %get-tuple-element.29), calls=%async_computation.1 | async-start | bytes 2621440 | tf_op jit(solution)/shard_map/all_to_all | solution.py:354
  68.6 2.4 fusion.8
  75.6 12.0 %collective-permute-done.7.refs_0_ = bf16[1280,256]{1,0:T(8,128)(2,1)S(1)} collective-permute-done((bf16[1280,256]{1,0:T(8,128)(2,1)}, bf16[1280,256]{1,0:T(8,128)(2,1)S(1)}, u32[]{:S(2)}, u32[]{:S(2)}) %collective-permute-start.7) | collective-permute-done | bytes 655392 | tf_op jit(solution)/shard_map/ppermute | solution.py:351
  87.6 2.6 %collective-permute-start.9 = (bf16[1280,256]{1,0:T(8,128)(2,1)}, bf16[1280,256]{1,0:T(8,128)(2,1)S(1)}, u32[]{:S(2)}, u32[]{:S(2)}) collective-permute-start(bf16[1280,256]{1,0:T(8,128)(2,1)} %bitcast.17), channel_id=1, source_target_pairs={{0,128},{32,160},{64,192},{96,224},{128,0},{160,32},{192,64},{224,... | collective-permute-start | bytes 1966088 | tf_op jit(solution)/shard_map/ppermute | solution.py:351
  90.2 2.2 hidden.5.refs_2_
  93.5 2.6 %all-to-all-done.1 = bf16[32,2,40,256]{3,2,1,0:T(8,128)(2,1)} async-done(((bf16[32,2,40,256]{3,2,1,0:T(8,128)(2,1)}), bf16[32,2,40,256]{3,2,1,0:T(8,128)(2,1)}, u32[]{:S(2)}, u32[]{:S(2)}) %all-to-all-start.1) | async-done | bytes 1310752 | tf_op jit(solution)/shard_map/all_to_all | solution.py:354
  97.7 7.7 %collective-permute-start.11 = (bf16[1280,256]{1,0:T(8,128)(2,1)S(1)}, bf16[1280,256]{1,0:T(8,128)(2,1)S(1)}, u32[]{:S(2)}, u32[]{:S(2)}) collective-permute-start(bf16[1280,256]{1,0:T(8,128)(2,1)S(1)} %bitcast.58), channel_id=1, source_target_pairs={{0,64},{32,96},{64,0},{96,32},{128,192},{160,224},{192,128},{224,1... | collective-permute-start | bytes 1966088 | tf_op jit(solution)/shard_map/ppermute | solution.py:351
  111.3 5.1 %expert.3 = bf16[1280,256]{1,0:T(8,128)(2,1)S(1)} custom-call(bf16[1280,256]{1,0:T(8,128)(2,1)S(1)} %bitcast.59, f32[160,1024]{1,0:T(8,128)S(1)} %copy-done.33, bf16[320,320]{1,0:T(8,128)(2,1)S(1)} %copy-done.29, bf16[320,320]{1,0:T(8,128)(2,1)S(1)} %copy-done.29, bf16[2048,512]{1,0:T(8,128)(2,1)S(1)} %bitcast.67, bf16[2048,512]{1,0:T(8,128)(2,1)S(1)} %bitcast.71, ...), custom_call_target="tpu_custom_call" | custom-call | flops 9663676416 | bytes 1048576 | tf_op jit(solution)/shard_map/expert/pallas_call | solution.py:411
  120.0 2.1 collective-permute-start.14
  122.2 7.3 %expert.4 = (bf16[1280,256]{1,0:T(8,128)(2,1)S(1)}, bf16[1280,256]{1,0:T(8,128)(2,1)S(1)}) custom-call(bf16[1280,256]{1,0:T(8,128)(2,1)S(1)} %collective-permute-done.10.refs_0_, bf16[1280,256]{1,0:T(8,128)(2,1)S(1)} %collective-permute-done.11.refs_1_, f32[320,1024]{1,0:T(8,128)S(1)} %copy-done.31, bf16[320,320]{1,0:T(8,128)(2,1)S(1)} %copy-done.29, ...), custom_call_target="tpu_custom_call" | custom-call | flops 11811160064 | bytes 1048576 | tf_op jit(solution)/shard_map/expert/pallas_call | solution.py:411
  129.5 2.6 %collective-permute-start.13 = (bf16[1280,256]{1,0:T(8,128)(2,1)S(1)}, bf16[1280,256]{1,0:T(8,128)(2,1)S(1)}, u32[]{:S(2)}, u32[]{:S(2)}) collective-permute-start(bf16[1280,256]{1,0:T(8,128)(2,1)S(1)} %get-tuple-element.44), channel_id=1, source_target_pairs={{0,192},{32,224},{64,128},{96,160},{128,64},{160,96},{192,0},{224,... | collective-permute-start | bytes 1966088 | tf_op jit(solution)/shard_map/ppermute | solution.py:351
  132.2 4.5 %collective-permute-done.14.refs_0_ = bf16[1280,256]{1,0:T(8,128)(2,1)S(1)} collective-permute-done((bf16[1280,256]{1,0:T(8,128)(2,1)S(1)}, bf16[1280,256]{1,0:T(8,128)(2,1)S(1)}, u32[]{:S(2)}, u32[]{:S(2)}) %collective-permute-start.14) | collective-permute-done | bytes 655392 | tf_op jit(solution)/shard_map/ppermute | solution.py:351
  136.7 5.2 %expert.5 = bf16[1280,256]{1,0:T(8,128)(2,1)S(1)} custom-call(bf16[1280,256]{1,0:T(8,128)(2,1)S(1)} %collective-permute-done.14.refs_0_, f32[160,1024]{1,0:T(8,128)S(1)} %hidden.4.refs_1_, bf16[320,320]{1,0:T(8,128)(2,1)S(1)} %copy-done.29, bf16[320,320]{1,0:T(8,128)(2,1)S(1)} %copy-done.29, bf16[2048,512]{1,0:T(8,128)(2,1)S(1)} %bitcast.69, ...), custom_call_target="tpu_custom_call" | custom-call | flops 9663676416 | bytes 1048576 | tf_op jit(solution)/shard_map/expert/pallas_call | solution.py:411
  141.9 2.3 collective-permute-start.15
  144.2 6.4 %collective-permute-done.12 = bf16[1280,256]{1,0:T(8,128)(2,1)S(1)} collective-permute-done((bf16[1280,256]{1,0:T(8,128)(2,1)S(1)}, bf16[1280,256]{1,0:T(8,128)(2,1)S(1)}, u32[]{:S(2)}, u32[]{:S(2)}) %collective-permute-start.12) | collective-permute-done | bytes 655392 | tf_op jit(solution)/shard_map/ppermute | solution.py:351
  150.7 2.9 %collective-permute-done.13 = bf16[1280,256]{1,0:T(8,128)(2,1)S(1)} collective-permute-done((bf16[1280,256]{1,0:T(8,128)(2,1)S(1)}, bf16[1280,256]{1,0:T(8,128)(2,1)S(1)}, u32[]{:S(2)}, u32[]{:S(2)}) %collective-permute-start.13) | collective-permute-done | bytes 655392 | tf_op jit(solution)/shard_map/ppermute | solution.py:351
  153.7 11.1 %collective-permute-done.15 = bf16[1280,256]{1,0:T(8,128)(2,1)S(1)} collective-permute-done((bf16[1280,256]{1,0:T(8,128)(2,1)S(1)}, bf16[1280,256]{1,0:T(8,128)(2,1)S(1)}, u32[]{:S(2)}, u32[]{:S(2)}) %collective-permute-start.15) | collective-permute-done | bytes 655392 | tf_op jit(solution)/shard_map/ppermute | solution.py:351
  165.2 43.4 %all_to_all.15.refs_4_ = bf16[32,2,40,256]{3,2,1,0:T(8,128)(2,1)S(1)} all-to-all(bf16[32,2,40,256]{3,2,1,0:T(8,128)(2,1)S(1)} %pad_maximum_fusion), channel_id=1, replica_groups=mesh['seq'=8,'exp'=32] {'exp'}, dimensions={0} | all-to-all | bytes 2621440 | tf_op jit(solution)/shard_map/all_to_all | solution.py:354
  208.7 6.9 %attention_grad.1 = (f32[128,2048]{1,0:T(8,128)S(1)}, f32[128,2048]{1,0:T(8,128)S(1)}, bf16[2,128,2048]{2,1,0:T(8,128)(2,1)S(1)}, bf16[2,128,2048]{2,1,0:T(8,128)(2,1)S(1)}) custom-call(s32[1]{0:T(128)} %bitcast.refs_0_.seq_ref, s32[2,3]{1,0:T(2,128)S(1)} %bitcast.88, s32[2,128]{1,0:T(2,128)S(1)} %bitcast.91, f32[2,128]{1,0:T(2,128)S(1)} %bitcast.92, ...), custom_call_target="tpu_custom_call" | custom-call | flops 10737418240 | bytes 1048576 | tf_op jit(solution)/shard_map/attention_grad/pallas_call | solution.py:437
  215.6 4.6 %collective-permute-start.16 = (bf16[2,128,2048]{2,1,0:T(8,128)(2,1)S(1)}, bf16[2,128,2048]{2,1,0:T(8,128)(2,1)S(1)}, u32[]{:S(2)}, u32[]{:S(2)}) collective-permute-start(bf16[2,128,2048]{2,1,0:T(8,128)(2,1)S(1)} %get-tuple-element.51), channel_id=1, source_target_pairs={{32,0},{64,32},{96,64},{128,96},{160,128},{192,160},{224,192},{33,... | collective-permute-start | bytes 3145736 | tf_op jit(solution)/shard_map/ppermute | solution.py:450
  220.2 3.7 %collective-permute-start.17 = (bf16[2,128,2048]{2,1,0:T(8,128)(2,1)S(1)}, bf16[2,128,2048]{2,1,0:T(8,128)(2,1)S(1)}, u32[]{:S(2)}, u32[]{:S(2)}) collective-permute-start(bf16[2,128,2048]{2,1,0:T(8,128)(2,1)S(1)} %get-tuple-element.52), channel_id=1, source_target_pairs={{0,32},{32,64},{64,96},{96,128},{128,160},{160,192},{192,224},{1,3... | collective-permute-start | bytes 3145736 | tf_op jit(solution)/shard_map/ppermute | solution.py:451
  224.0 10.5 %collective-permute-done.16 = bf16[2,128,2048]{2,1,0:T(8,128)(2,1)S(1)} collective-permute-done((bf16[2,128,2048]{2,1,0:T(8,128)(2,1)S(1)}, bf16[2,128,2048]{2,1,0:T(8,128)(2,1)S(1)}, u32[]{:S(2)}, u32[]{:S(2)}) %collective-permute-start.16) | collective-permute-done | bytes 1048608 | tf_op jit(solution)/shard_map/ppermute | solution.py:450
  (106 shorter events, 32.7 us)
Async XLA Ops:
  3.3 41.6 %copy-start.14 = (bf16[1,128,2048]{2,1,0:T(8,128)(2,1)S(1)}, bf16[1,128,2048]{2,1,0:T(8,128)(2,1)}, u32[]{:S(2)}) copy-start(bf16[1,128,2048]{2,1,0:T(8,128)(2,1)} %param.13) | copy-start | bytes 1572868
  3.3 41.6 %copy-start.29 = (bf16[320,320]{1,0:T(8,128)(2,1)S(1)}, bf16[320,320]{1,0:T(8,128)(2,1)}, u32[]{:S(2)}) copy-start(bf16[320,320]{1,0:T(8,128)(2,1)} %constant.8.clone.refs_11_.perm_ref.refs_1_.refs_2_.refs_3_.refs_4_.refs_9_) | copy-start | bytes 614404
  5.8 39.1 %copy-start.24 = (s32[1,2,3]{2,1,0:T(2,128)S(1)}, s32[1,2,3]{2,1,0:T(2,128)}, u32[]{:S(2)}) copy-start(s32[1,2,3]{2,1,0:T(2,128)} %param.20) | copy-start | bytes 76
  5.8 39.1 %copy-start.26 = (s32[1,128,2]{1,2,0:T(2,128)S(1)}, s32[1,128,2]{1,2,0:T(2,128)}, u32[]{:S(2)}) copy-start(s32[1,128,2]{1,2,0:T(2,128)} %param.19) | copy-start | bytes 3076
  5.8 53.3 %all-to-all-start = ((bf16[32,2,40,256]{3,2,1,0:T(8,128)(2,1)}), bf16[32,2,40,256]{3,2,1,0:T(8,128)(2,1)}, u32[]{:S(2)}, u32[]{:S(2)}) async-start(bf16[32,2,40,256]{3,2,1,0:T(8,128)(2,1)} %place_grad.1), calls=%async_computation | async-start | bytes 2621440 | tf_op jit(solution)/shard_map/all_to_all | solution.py:354
  18.3 36.7 %collective-permute-start.4 = (bf16[2048,512]{1,0:T(8,128)(2,1)}, bf16[2048,512]{1,0:T(8,128)(2,1)S(1)}, u32[]{:S(2)}, u32[]{:S(2)}) collective-permute-start(bf16[2048,512]{1,0:T(8,128)(2,1)} %bitcast.66), channel_id=1, source_target_pairs={{0,32},{32,0},{64,96},{96,64},{128,160},{160,128},{192,224},{224,1... | collective-permute-start | bytes 6291464 | tf_op jit(solution)/shard_map/ppermute | solution.py:351
  19.3 37.0 %collective-permute-start.5 = (bf16[2048,512]{1,0:T(8,128)(2,1)}, bf16[2048,512]{1,0:T(8,128)(2,1)S(1)}, u32[]{:S(2)}, u32[]{:S(2)}) collective-permute-start(bf16[2048,512]{1,0:T(8,128)(2,1)} %bitcast.70), channel_id=1, source_target_pairs={{0,32},{32,0},{64,96},{96,64},{128,160},{160,128},{192,224},{224,1... | collective-permute-start | bytes 6291464 | tf_op jit(solution)/shard_map/ppermute | solution.py:351
  19.4 38.3 %collective-permute-start.6 = (bf16[512,2048]{1,0:T(8,128)(2,1)S(1)}, bf16[512,2048]{1,0:T(8,128)(2,1)S(1)}, u32[]{:S(2)}, u32[]{:S(2)}) collective-permute-start(bf16[512,2048]{1,0:T(8,128)(2,1)S(1)} %bitcast.62), channel_id=1, source_target_pairs={{0,32},{32,0},{64,96},{96,64},{128,160},{160,128},{192,224},{224,1... | collective-permute-start | bytes 6291464 | tf_op jit(solution)/shard_map/ppermute | solution.py:351
  19.8 10.1 %collective-permute-start.2 = (bf16[128,2048]{1,0:T(8,128)(2,1)}, bf16[128,2048]{1,0:T(8,128)(2,1)S(1)}, u32[]{:S(2)}, u32[]{:S(2)}) collective-permute-start(bf16[128,2048]{1,0:T(8,128)(2,1)} %bitcast.79), channel_id=1, source_target_pairs={{0,32},{32,64},{64,96},{96,128},{128,160},{160,192},{192,224},{1,3... | collective-permute-start | bytes 1572872 | tf_op jit(solution)/shard_map/ppermute | solution.py:359
  22.9 11.1 %collective-permute-start.3 = (bf16[128,2048]{1,0:T(8,128)(2,1)}, bf16[128,2048]{1,0:T(8,128)(2,1)S(1)}, u32[]{:S(2)}, u32[]{:S(2)}) collective-permute-start(bf16[128,2048]{1,0:T(8,128)(2,1)} %bitcast.80), channel_id=1, source_target_pairs={{32,0},{64,32},{96,64},{128,96},{160,128},{192,160},{224,192},{33,... | collective-permute-start | bytes 1572872 | tf_op jit(solution)/shard_map/ppermute | solution.py:359
  29.9 9.8 %collective-permute-start = (bf16[128,2048]{1,0:T(8,128)(2,1)S(1)}, bf16[128,2048]{1,0:T(8,128)(2,1)S(1)}, u32[]{:S(2)}, u32[]{:S(2)}) collective-permute-start(bf16[128,2048]{1,0:T(8,128)(2,1)S(1)} %bitcast.74), channel_id=1, source_target_pairs={{0,32},{32,64},{64,96},{96,128},{128,160},{160,192},{192,224},{1,3... | collective-permute-start | bytes 1572872 | tf_op jit(solution)/shard_map/ppermute | solution.py:358
  34.0 10.9 %collective-permute-start.1 = (bf16[128,2048]{1,0:T(8,128)(2,1)S(1)}, bf16[128,2048]{1,0:T(8,128)(2,1)S(1)}, u32[]{:S(2)}, u32[]{:S(2)}) collective-permute-start(bf16[128,2048]{1,0:T(8,128)(2,1)S(1)} %bitcast.75), channel_id=1, source_target_pairs={{32,0},{64,32},{96,64},{128,96},{160,128},{192,160},{224,192},{33,... | collective-permute-start | bytes 1572872 | tf_op jit(solution)/shard_map/ppermute | solution.py:358
  59.1 37.0 %all-to-all-start.1 = ((bf16[32,2,40,256]{3,2,1,0:T(8,128)(2,1)}), bf16[32,2,40,256]{3,2,1,0:T(8,128)(2,1)}, u32[]{:S(2)}, u32[]{:S(2)}) async-start(bf16[32,2,40,256]{3,2,1,0:T(8,128)(2,1)} %get-tuple-element.29), calls=%async_computation.1 | async-start | bytes 2621440 | tf_op jit(solution)/shard_map/all_to_all | solution.py:354
  71.0 16.6 %collective-permute-start.7 = (bf16[1280,256]{1,0:T(8,128)(2,1)}, bf16[1280,256]{1,0:T(8,128)(2,1)S(1)}, u32[]{:S(2)}, u32[]{:S(2)}) collective-permute-start(bf16[1280,256]{1,0:T(8,128)(2,1)} %bitcast.17), channel_id=1, source_target_pairs={{0,192},{32,224},{64,128},{96,160},{128,64},{160,96},{192,0},{224,... | collective-permute-start | bytes 1966088 | tf_op jit(solution)/shard_map/ppermute | solution.py:351
  71.0 16.6 %collective-permute-start.8 = (bf16[1280,256]{1,0:T(8,128)(2,1)S(1)}, bf16[1280,256]{1,0:T(8,128)(2,1)S(1)}, u32[]{:S(2)}, u32[]{:S(2)}) collective-permute-start(bf16[1280,256]{1,0:T(8,128)(2,1)S(1)} %bitcast.60), channel_id=1, source_target_pairs={{0,64},{32,96},{64,0},{96,32},{128,192},{160,224},{192,128},{224,1... | collective-permute-start | bytes 1966088 | tf_op jit(solution)/shard_map/ppermute | solution.py:351
  87.6 28.9 %collective-permute-start.9 = (bf16[1280,256]{1,0:T(8,128)(2,1)}, bf16[1280,256]{1,0:T(8,128)(2,1)S(1)}, u32[]{:S(2)}, u32[]{:S(2)}) collective-permute-start(bf16[1280,256]{1,0:T(8,128)(2,1)} %bitcast.17), channel_id=1, source_target_pairs={{0,128},{32,160},{64,192},{96,224},{128,0},{160,32},{192,64},{224,... | collective-permute-start | bytes 1966088 | tf_op jit(solution)/shard_map/ppermute | solution.py:351
  97.6 22.4 %collective-permute-start.10 = (bf16[1280,256]{1,0:T(8,128)(2,1)S(1)}, bf16[1280,256]{1,0:T(8,128)(2,1)S(1)}, u32[]{:S(2)}, u32[]{:S(2)}) collective-permute-start(bf16[1280,256]{1,0:T(8,128)(2,1)S(1)} %bitcast.95), channel_id=1, source_target_pairs={{0,192},{32,224},{64,128},{96,160},{128,64},{160,96},{192,0},{224,... | collective-permute-start | bytes 1966088 | tf_op jit(solution)/shard_map/ppermute | solution.py:351
  97.7 22.3 %collective-permute-start.11 = (bf16[1280,256]{1,0:T(8,128)(2,1)S(1)}, bf16[1280,256]{1,0:T(8,128)(2,1)S(1)}, u32[]{:S(2)}, u32[]{:S(2)}) collective-permute-start(bf16[1280,256]{1,0:T(8,128)(2,1)S(1)} %bitcast.58), channel_id=1, source_target_pairs={{0,64},{32,96},{64,0},{96,32},{128,192},{160,224},{192,128},{224,1... | collective-permute-start | bytes 1966088 | tf_op jit(solution)/shard_map/ppermute | solution.py:351
  120.0 16.7 %collective-permute-start.14 = (bf16[1280,256]{1,0:T(8,128)(2,1)S(1)}, bf16[1280,256]{1,0:T(8,128)(2,1)S(1)}, u32[]{:S(2)}, u32[]{:S(2)}) collective-permute-start(bf16[1280,256]{1,0:T(8,128)(2,1)S(1)} %bitcast.96), channel_id=1, source_target_pairs={{0,128},{32,160},{64,192},{96,224},{128,0},{160,32},{192,64},{224,... | collective-permute-start | bytes 1966088 | tf_op jit(solution)/shard_map/ppermute | solution.py:351
  129.4 21.1 %collective-permute-start.12 = (bf16[1280,256]{1,0:T(8,128)(2,1)S(1)}, bf16[1280,256]{1,0:T(8,128)(2,1)S(1)}, u32[]{:S(2)}, u32[]{:S(2)}) collective-permute-start(bf16[1280,256]{1,0:T(8,128)(2,1)S(1)} %get-tuple-element.43), channel_id=1, source_target_pairs={{0,64},{32,96},{64,0},{96,32},{128,192},{160,224},{192,128},{224,1... | collective-permute-start | bytes 1966088 | tf_op jit(solution)/shard_map/ppermute | solution.py:351
  129.5 24.1 %collective-permute-start.13 = (bf16[1280,256]{1,0:T(8,128)(2,1)S(1)}, bf16[1280,256]{1,0:T(8,128)(2,1)S(1)}, u32[]{:S(2)}, u32[]{:S(2)}) collective-permute-start(bf16[1280,256]{1,0:T(8,128)(2,1)S(1)} %get-tuple-element.44), channel_id=1, source_target_pairs={{0,192},{32,224},{64,128},{96,160},{128,64},{160,96},{192,0},{224,... | collective-permute-start | bytes 1966088 | tf_op jit(solution)/shard_map/ppermute | solution.py:351
  141.9 22.9 %collective-permute-start.15 = (bf16[1280,256]{1,0:T(8,128)(2,1)S(1)}, bf16[1280,256]{1,0:T(8,128)(2,1)S(1)}, u32[]{:S(2)}, u32[]{:S(2)}) collective-permute-start(bf16[1280,256]{1,0:T(8,128)(2,1)S(1)} %expert.5), channel_id=1, source_target_pairs={{0,128},{32,160},{64,192},{96,224},{128,0},{160,32},{192,64},{224,... | collective-permute-start | bytes 1966088 | tf_op jit(solution)/shard_map/ppermute | solution.py:351
  164.8 43.8 %copy-start.39 = (f32[128,128]{1,0:T(8,128)S(1)}, f32[128,128]{1,0:T(8,128)}, u32[]{:S(2)}) copy-start(f32[128,128]{1,0:T(8,128)} %copy-done.38) | copy-start | bytes 196612
  165.0 43.7 %copy-start.35 = (f32[32,64,192]{2,1,0:T(8,128)S(1)}, f32[32,64,192]{2,1,0:T(8,128)}, u32[]{:S(2)}) copy-start(f32[32,64,192]{2,1,0:T(8,128)} %copy-done.34) | copy-start | bytes 4718596
  165.0 43.6 %copy-start.37 = (f32[128,2048]{1,0:T(8,128)S(1)}, f32[128,2048]{1,0:T(8,128)}, u32[]{:S(2)}) copy-start(f32[128,2048]{1,0:T(8,128)} %copy-done.36) | copy-start | bytes 3145732
  165.1 43.5 %copy-start.16 = (bf16[1,128,2048]{2,1,0:T(8,128)(2,1)S(1)}, bf16[1,128,2048]{2,1,0:T(8,128)(2,1)}, u32[]{:S(2)}) copy-start(bf16[1,128,2048]{2,1,0:T(8,128)(2,1)} %param.15) | copy-start | bytes 1572868
  165.2 43.5 %copy-start.18 = (bf16[1,128,2048]{2,1,0:T(8,128)(2,1)S(1)}, bf16[1,128,2048]{2,1,0:T(8,128)(2,1)}, u32[]{:S(2)}) copy-start(bf16[1,128,2048]{2,1,0:T(8,128)(2,1)} %param.16) | copy-start | bytes 1572868
  165.2 43.5 %copy-start.20 = (bf16[128,2048]{1,0:T(8,128)(2,1)S(1)}, bf16[128,2048]{1,0:T(8,128)(2,1)}, u32[]{:S(2)}) copy-start(bf16[128,2048]{1,0:T(8,128)(2,1)} %copy-done.19) | copy-start | bytes 1572868
  165.2 43.5 %copy-start.22 = (bf16[128,2048]{1,0:T(8,128)(2,1)S(1)}, bf16[128,2048]{1,0:T(8,128)(2,1)}, u32[]{:S(2)}) copy-start(bf16[128,2048]{1,0:T(8,128)(2,1)} %copy-done.21) | copy-start | bytes 1572868
  165.2 43.5 %copy-start.27 = (f32[1,128,2]{1,2,0:T(2,128)S(1)}, f32[1,128,2]{1,2,0:T(2,128)}, u32[]{:S(2)}) copy-start(f32[1,128,2]{1,2,0:T(2,128)} %param.18) | copy-start | bytes 3076
  215.6 18.9 %collective-permute-start.16 = (bf16[2,128,2048]{2,1,0:T(8,128)(2,1)S(1)}, bf16[2,128,2048]{2,1,0:T(8,128)(2,1)S(1)}, u32[]{:S(2)}, u32[]{:S(2)}) collective-permute-start(bf16[2,128,2048]{2,1,0:T(8,128)(2,1)S(1)} %get-tuple-element.51), channel_id=1, source_target_pairs={{32,0},{64,32},{96,64},{128,96},{160,128},{192,160},{224,192},{33,... | collective-permute-start | bytes 3145736 | tf_op jit(solution)/shard_map/ppermute | solution.py:450
  220.2 15.5 %collective-permute-start.17 = (bf16[2,128,2048]{2,1,0:T(8,128)(2,1)S(1)}, bf16[2,128,2048]{2,1,0:T(8,128)(2,1)S(1)}, u32[]{:S(2)}, u32[]{:S(2)}) collective-permute-start(bf16[2,128,2048]{2,1,0:T(8,128)(2,1)S(1)} %get-tuple-element.52), channel_id=1, source_target_pairs={{0,32},{32,64},{64,96},{96,128},{128,160},{160,192},{192,224},{1,3... | collective-permute-start | bytes 3145736 | tf_op jit(solution)/shard_map/ppermute | solution.py:451
  (28 other events, 177.1 us)

commit v5 on v4

--- a/solution.py
+++ b/solution.py
@@ -355,14 +355,15 @@
 
     barrier = lax.optimization_barrier
     pair = (2, count, width)
-    kl, kr = lax.ppermute(k, "seq", up_by), lax.ppermute(k, "seq", down_by)
-    vl, vr = lax.ppermute(v, "seq", up_by), lax.ppermute(v, "seq", down_by)
     (sent_grad,) = call(
         grad_kernel, (shape(wire, BF16),), "svvv", [pltpu.VMEM((2 * slots, width), F32)],
         "place_grad", 4 * MICRO, 12,
     )(seq, ids_t, grad, perm)
+    k, v, sent_grad = barrier((k, v, sent_grad))
+    kl, kr = lax.ppermute(k, "seq", up_by), lax.ppermute(k, "seq", down_by)
+    vl, vr = lax.ppermute(v, "seq", up_by), lax.ppermute(v, "seq", down_by)
     got_grad = exchange(sent_grad)
-    gate_s, up_s, down_s = swap(gate, 1), swap(up, 1), swap(down, 1)
+
 
     wts, unit, inv, sent = call(
         lambda *refs: forward_kernel(*refs, total_tiles=total_tiles),
@@ -382,16 +383,16 @@
         "attention", ATTN * MICRO, 20,
     )(seq, offsets, ids_t, q, kl, k, kr, vl, v, vr, gain, perm)
 
-    sent, got_grad, gate_s, up_s, down_s = barrier((sent, got_grad, gate_s, up_s, down_s))
+    sent, *weights = barrier((sent, gate, up, down))
+    sent, got_grad = barrier((sent, got_grad))
+    gate_s, up_s, down_s = [swap(x, 1) for x in weights]
     got = exchange(sent)
     g0, grad_oth = got_grad[:, 0].reshape(flat), got_grad[:, 1].reshape(flat)
     g1, g2 = swap(grad_oth, 6), swap(g0, 2)
-    g1, g2, grad_oth = barrier((g1, g2, grad_oth))
     g3 = swap(grad_oth, 4)
     n0, oth = got[:, 0].reshape(flat), got[:, 1].reshape(flat)
     n1, n2 = swap(oth, 6), swap(n0, 2)
-    n1, n2, oth = barrier((n1, n2, oth))
-    n3 = swap(oth, 4)
+    n3 = swap(n1, 2)
 
     part = down.shape[0]
 

time: 238 us -> 225 us (0.945)
  starting transfers between devices: 61.9 us -> 50.2 us
  Pallas kernels: 38.9 us -> 50.4 us
  local copies, waits for them, and re-layouts: 22.5 us -> 14.4 us
  waiting for transfers between devices: 67.3 us -> 59.8 us
  blocking collectives: 43.4 us -> 46.3 us
    ppermute x12, starting transfers between devices: 20.9 us -> 11.4 us  [swap(): return lax.ppermute(x, 'seq', [(i, i ^ bits) for i in range(seq_count)])]
    ppermute x12, waiting for transfers between devices: 38.7 us -> 30.6 us  [swap(): return lax.ppermute(x, 'seq', [(i, i ^ bits) for i in range(seq_count)])]
    unnamed x80 -> x64, local copies, waits for them, and re-layouts: 18.6 us -> 10.7 us
    pallas_call x3, Pallas kernels: 17.6 us -> 24.2 us  [expert(): call(lambda *refs: expert_kernel(*refs, blocks=blocks), (shape(flat, BF16...]
    all_to_all x2, waiting for transfers between devices: 2.64 us -> 8.7 us  [exchange(): return lax.all_to_all(x, 'exp', split_axis=0, concat_axis=0, tiled=True)]
    pallas_call x3, Pallas kernels: 5.86 us -> 10.8 us  [hidden(): call(lambda *refs: hidden_kernel(*refs, blocks=blocks), (shape((blocks *...]
    ppermute x2, waiting for transfers between devices: 8.97 us -> 5.61 us  [on_device(): kl, kr = (lax.ppermute(k, 'seq', up_by), lax.ppermute(k, 'seq', down_by))]
    all_to_all x1, blocking collectives: 43.4 us -> 46.3 us  [exchange(): return lax.all_to_all(x, 'exp', split_axis=0, concat_axis=0, tiled=True)]
  transfers between devices with their start and end apart: 20 -> 20, of which waited for: 13 -> 12; matrix products, arithmetic and copies ran while one was open for 2% -> 2% of each run, Pallas kernels for 12% -> 18%
where the time goes in v5:
time: 225 us; the launch traced here: 224 us
  waiting for transfers between devices  59.8 us (27%)
  Pallas kernels  50.4 us (22%)
  starting transfers between devices  50.2 us (22%)
  blocking collectives  46.3 us (21%)
  local copies, waits for them, and re-layouts  14.4 us (6%)
  other arithmetic  2.32 us (1%)
    all_to_all x1, blocking collectives, exchange(): return lax.all_to_all(x, 'exp', split_axis=0, concat_axis=0, tiled=True)  46.3 us
    ppermute x12, waiting for transfers between devices, swap(): return lax.ppermute(x, 'seq', [(i, i ^ bits) for i in range(seq_count)])  30.6 us
    pallas_call x3, Pallas kernels, expert(): call(lambda *refs: expert_kernel(*refs, blocks=blocks), (shape(flat, BF16...  24.2 us
    all_to_all x2, starting transfers between devices, exchange(): return lax.all_to_all(x, 'exp', split_axis=0, concat_axis=0, tiled=True)  20.5 us
    ppermute x12, starting transfers between devices, swap(): return lax.ppermute(x, 'seq', [(i, i ^ bits) for i in range(seq_count)])  11.4 us
    pallas_call x3, Pallas kernels, hidden(): call(lambda *refs: hidden_kernel(*refs, blocks=blocks), (shape((blocks *...  10.8 us
    unnamed x64, local copies, waits for them, and re-layouts  10.7 us
    ppermute x1, waiting for transfers between devices, on_device(): from_right = lax.ppermute(to_left, 'seq', down_by).astype(F32)  10.1 us
  transfers between devices with their start and end apart: 20, of which 12 were waited for; matrix products, arithmetic and copies ran while one was open for 2% of the time, Pallas kernels for 18%

profile of v5, /device:TPU:1, one launch (start us, length us, event | category | flops | bytes accessed | tf_op | source)
XLA Modules:
  0.0 224.5 jit_solution(4933798493748451367)
XLA Ops:
  3.3 2.5 %place_grad.1 = bf16[32,2,40,256]{3,2,1,0:T(8,128)(2,1)} custom-call(s32[1]{0:T(128)} %bitcast.seq_ref.refs_0_, s32[2,128]{1,0:T(2,128)S(1)} %bitcast.89, bf16[128,2048]{1,0:T(8,128)(2,1)S(1)} %bitcast.83, bf16[320,320]{1,0:T(8,128)(2,1)S(1)} %copy-done.20), custom_call_target="tpu_custom_call" | custom-call | flops 4294967296 | bytes 1048576 | tf_op jit(solution)/shard_map/place_grad/pallas_call | solution.py:358
  5.8 12.3 %all-to-all-start = ((bf16[32,2,40,256]{3,2,1,0:T(8,128)(2,1)}), bf16[32,2,40,256]{3,2,1,0:T(8,128)(2,1)}, u32[]{:S(2)}, u32[]{:S(2)}) async-start(bf16[32,2,40,256]{3,2,1,0:T(8,128)(2,1)} %place_grad.1), calls=%async_computation | async-start | bytes 2621440 | tf_op jit(solution)/shard_map/all_to_all | solution.py:354
  18.1 4.0 %collective-permute-start.2 = (bf16[128,2048]{1,0:T(8,128)(2,1)S(1)}, bf16[128,2048]{1,0:T(8,128)(2,1)S(1)}, u32[]{:S(2)}, u32[]{:S(2)}) collective-permute-start(bf16[128,2048]{1,0:T(8,128)(2,1)S(1)} %bitcast.79), channel_id=1, source_target_pairs={{0,32},{32,64},{64,96},{96,128},{128,160},{160,192},{192,224},{1,3... | collective-permute-start | bytes 1572872 | tf_op jit(solution)/shard_map/ppermute | solution.py:364
  22.1 1.9 collective-permute-start.3
  24.0 3.6 %collective-permute-start = (bf16[128,2048]{1,0:T(8,128)(2,1)S(1)}, bf16[128,2048]{1,0:T(8,128)(2,1)S(1)}, u32[]{:S(2)}, u32[]{:S(2)}) collective-permute-start(bf16[128,2048]{1,0:T(8,128)(2,1)S(1)} %bitcast.74), channel_id=1, source_target_pairs={{0,32},{32,64},{64,96},{96,128},{128,160},{160,192},{192,224},{1,3... | collective-permute-start | bytes 1572872 | tf_op jit(solution)/shard_map/ppermute | solution.py:363
  27.7 1.9 collective-permute-start.1
  29.6 3.4 %collective-permute-done.3.refs_9_.refs_13_ = bf16[128,2048]{1,0:T(8,128)(2,1)S(1)} collective-permute-done((bf16[128,2048]{1,0:T(8,128)(2,1)S(1)}, bf16[128,2048]{1,0:T(8,128)(2,1)S(1)}, u32[]{:S(2)}, u32[]{:S(2)}) %collective-permute-start.3) | collective-permute-done | bytes 524320 | tf_op jit(solution)/shard_map/ppermute | solution.py:364
  33.8 4.8 %collective-permute-done.1.refs_6_ = bf16[128,2048]{1,0:T(8,128)(2,1)S(1)} collective-permute-done((bf16[128,2048]{1,0:T(8,128)(2,1)S(1)}, bf16[128,2048]{1,0:T(8,128)(2,1)S(1)}, u32[]{:S(2)}, u32[]{:S(2)}) %collective-permute-start.1) | collective-permute-done | bytes 524320 | tf_op jit(solution)/shard_map/ppermute | solution.py:363
  39.7 6.0 %attention.1 = (f32[32,64,192]{2,1,0:T(8,128)S(1)}, f32[128,2048]{1,0:T(8,128)S(1)}, f32[128,128]{1,0:T(8,128)S(1)}, bf16[32,2,40,256]{3,2,1,0:T(8,128)(2,1)}) custom-call(s32[1]{0:T(128)} %bitcast.seq_ref.refs_0_, s32[2,3]{1,0:T(2,128)S(1)} %bitcast.87, s32[2,128]{1,0:T(2,128)S(1)} %bitcast.90, bf16[128,2048]{1,0:T(8,128)(2,1)S(1)} %bitcast.77, ...), custom_call_target="tpu_custom_call" | custom-call | flops 8589934592 | bytes 1048576 | tf_op jit(solution)/shard_map/attention/pallas_call | solution.py:368
  48.0 1.9 all-to-all-done
  49.9 8.3 %all-to-all-start.1 = ((bf16[32,2,40,256]{3,2,1,0:T(8,128)(2,1)}), bf16[32,2,40,256]{3,2,1,0:T(8,128)(2,1)}, u32[]{:S(2)}, u32[]{:S(2)}) async-start(bf16[32,2,40,256]{3,2,1,0:T(8,128)(2,1)} %get-tuple-element.31), calls=%async_computation.1 | async-start | bytes 2621440 | tf_op jit(solution)/shard_map/all_to_all | solution.py:354
  58.8 2.2 fusion.8
  61.0 2.3 %collective-permute-start.10 = (bf16[1280,256]{1,0:T(8,128)(2,1)}, bf16[1280,256]{1,0:T(8,128)(2,1)S(1)}, u32[]{:S(2)}, u32[]{:S(2)}) collective-permute-start(bf16[1280,256]{1,0:T(8,128)(2,1)} %bitcast.17), channel_id=1, source_target_pairs={{0,192},{32,224},{64,128},{96,160},{128,64},{160,96},{192,0},{224,... | collective-permute-start | bytes 1966088 | tf_op jit(solution)/shard_map/ppermute | solution.py:351
  63.3 1.6 collective-permute-start.7
  64.9 3.4 %hidden.3.refs_1_ = f32[160,1024]{1,0:T(8,128)S(1)} custom-call(bf16[1280,256]{1,0:T(8,128)(2,1)S(1)} %bitcast.61, bf16[320,320]{1,0:T(8,128)(2,1)S(1)} %copy-done.21, bf16[512,2048]{1,0:T(8,128)(2,1)S(1)} %bitcast.63, bf16[512,2048]{1,0:T(8,128)(2,1)} %collective-permute-done.4.refs_3_.refs_4_), custom_call_target="tpu_custom_call" | custom-call | flops 4294967296 | bytes 1048576 | tf_op jit(solution)/shard_map/hidden/pallas_call | solution.py:401
  69.2 9.5 %collective-permute-done.10.refs_0_ = bf16[1280,256]{1,0:T(8,128)(2,1)S(1)} collective-permute-done((bf16[1280,256]{1,0:T(8,128)(2,1)}, bf16[1280,256]{1,0:T(8,128)(2,1)S(1)}, u32[]{:S(2)}, u32[]{:S(2)}) %collective-permute-start.10) | collective-permute-done | bytes 655392 | tf_op jit(solution)/shard_map/ppermute | solution.py:351
  79.0 3.8 %hidden.5.refs_2_ = f32[320,1024]{1,0:T(8,128)S(1)} custom-call(bf16[1280,256]{1,0:T(8,128)(2,1)S(1)} %collective-permute-done.10.refs_0_, bf16[1280,256]{1,0:T(8,128)(2,1)S(1)} %collective-permute-done.11.refs_1_, bf16[320,320]{1,0:T(8,128)(2,1)S(1)} %copy-done.21, bf16[512,2048]{1,0:T(8,128)(2,1)S(1)} %bitcast.64, ...), custom_call_target="tpu_custom_call" | custom-call | flops 5368709120 | bytes 1048576 | tf_op jit(solution)/shard_map/hidden/pallas_call | solution.py:401
  83.9 6.8 %all-to-all-done.1 = bf16[32,2,40,256]{3,2,1,0:T(8,128)(2,1)} async-done(((bf16[32,2,40,256]{3,2,1,0:T(8,128)(2,1)}), bf16[32,2,40,256]{3,2,1,0:T(8,128)(2,1)}, u32[]{:S(2)}, u32[]{:S(2)}) %all-to-all-start.1) | async-done | bytes 1310752 | tf_op jit(solution)/shard_map/all_to_all | solution.py:354
  92.3 2.0 collective-permute-start.9
  94.4 1.6 copy-done.2
  97.0 7.4 %expert.3 = bf16[1280,256]{1,0:T(8,128)(2,1)S(1)} custom-call(bf16[1280,256]{1,0:T(8,128)(2,1)S(1)} %bitcast.59, f32[160,1024]{1,0:T(8,128)S(1)} %copy-done.25, bf16[320,320]{1,0:T(8,128)(2,1)S(1)} %copy-done.21, bf16[320,320]{1,0:T(8,128)(2,1)S(1)} %copy-done.21, bf16[2048,512]{1,0:T(8,128)(2,1)S(1)} %bitcast.67, bf16[2048,512]{1,0:T(8,128)(2,1)S(1)} %bitcast.71, ...), custom_call_target="tpu_custom_call" | custom-call | flops 9663676416 | bytes 1048576 | tf_op jit(solution)/shard_map/expert/pallas_call | solution.py:412
  104.4 3.6 %hidden.4.refs_1_ = f32[160,1024]{1,0:T(8,128)S(1)} custom-call(bf16[1280,256]{1,0:T(8,128)(2,1)S(1)} %collective-permute-done.7.refs_0_, bf16[320,320]{1,0:T(8,128)(2,1)S(1)} %copy-done.21, bf16[512,2048]{1,0:T(8,128)(2,1)S(1)} %bitcast.65, bf16[512,2048]{1,0:T(8,128)(2,1)} %collective-permute-done.4.refs_3_.refs_4_), custom_call_target="tpu_custom_call" | custom-call | flops 4294967296 | bytes 1048576 | tf_op jit(solution)/shard_map/hidden/pallas_call | solution.py:401
  108.2 9.5 %expert.4 = (bf16[1280,256]{1,0:T(8,128)(2,1)S(1)}, bf16[1280,256]{1,0:T(8,128)(2,1)S(1)}) custom-call(bf16[1280,256]{1,0:T(8,128)(2,1)S(1)} %collective-permute-done.8.refs_0_, bf16[1280,256]{1,0:T(8,128)(2,1)S(1)} %collective-permute-done.9.refs_1_, f32[320,1024]{1,0:T(8,128)S(1)} %copy-done.23, bf16[320,320]{1,0:T(8,128)(2,1)S(1)} %copy-done.21, ...), custom_call_target="tpu_custom_call" | custom-call | flops 11811160064 | bytes 1048576 | tf_op jit(solution)/shard_map/expert/pallas_call | solution.py:412
  121.7 7.4 %expert.5 = bf16[1280,256]{1,0:T(8,128)(2,1)S(1)} custom-call(bf16[1280,256]{1,0:T(8,128)(2,1)S(1)} %collective-permute-done.14.refs_0_, f32[160,1024]{1,0:T(8,128)S(1)} %hidden.4.refs_1_, bf16[320,320]{1,0:T(8,128)(2,1)S(1)} %copy-done.21, bf16[320,320]{1,0:T(8,128)(2,1)S(1)} %copy-done.21, bf16[2048,512]{1,0:T(8,128)(2,1)S(1)} %bitcast.69, ...), custom_call_target="tpu_custom_call" | custom-call | flops 9663676416 | bytes 1048576 | tf_op jit(solution)/shard_map/expert/pallas_call | solution.py:412
  129.1 1.9 collective-permute-start.15
  131.0 4.7 %collective-permute-done.12 = bf16[1280,256]{1,0:T(8,128)(2,1)S(1)} collective-permute-done((bf16[1280,256]{1,0:T(8,128)(2,1)S(1)}, bf16[1280,256]{1,0:T(8,128)(2,1)S(1)}, u32[]{:S(2)}, u32[]{:S(2)}) %collective-permute-start.12) | collective-permute-done | bytes 655392 | tf_op jit(solution)/shard_map/ppermute | solution.py:351
  135.9 14.7 %collective-permute-done.15 = bf16[1280,256]{1,0:T(8,128)(2,1)S(1)} collective-permute-done((bf16[1280,256]{1,0:T(8,128)(2,1)S(1)}, bf16[1280,256]{1,0:T(8,128)(2,1)S(1)}, u32[]{:S(2)}, u32[]{:S(2)}) %collective-permute-start.15) | collective-permute-done | bytes 655392 | tf_op jit(solution)/shard_map/ppermute | solution.py:351
  151.0 46.3 %all_to_all.15.refs_4_ = bf16[32,2,40,256]{3,2,1,0:T(8,128)(2,1)S(1)} all-to-all(bf16[32,2,40,256]{3,2,1,0:T(8,128)(2,1)S(1)} %pad_maximum_fusion), channel_id=1, replica_groups=mesh['seq'=8,'exp'=32] {'exp'}, dimensions={0} | all-to-all | bytes 2621440 | tf_op jit(solution)/shard_map/all_to_all | solution.py:354
  197.3 6.9 %attention_grad.1 = (f32[128,2048]{1,0:T(8,128)S(1)}, f32[128,2048]{1,0:T(8,128)S(1)}, bf16[2,128,2048]{2,1,0:T(8,128)(2,1)S(1)}, bf16[2,128,2048]{2,1,0:T(8,128)(2,1)S(1)}) custom-call(s32[1]{0:T(128)} %bitcast.seq_ref.refs_0_, s32[2,3]{1,0:T(2,128)S(1)} %bitcast.88, s32[2,128]{1,0:T(2,128)S(1)} %bitcast.91, f32[2,128]{1,0:T(2,128)S(1)} %bitcast.92, ...), custom_call_target="tpu_custom_call" | custom-call | flops 10737418240 | bytes 1048576 | tf_op jit(solution)/shard_map/attention_grad/pallas_call | solution.py:438
  204.3 4.9 %collective-permute-start.16 = (bf16[2,128,2048]{2,1,0:T(8,128)(2,1)S(1)}, bf16[2,128,2048]{2,1,0:T(8,128)(2,1)S(1)}, u32[]{:S(2)}, u32[]{:S(2)}) collective-permute-start(bf16[2,128,2048]{2,1,0:T(8,128)(2,1)S(1)} %get-tuple-element.47), channel_id=1, source_target_pairs={{32,0},{64,32},{96,64},{128,96},{160,128},{192,160},{224,192},{33,... | collective-permute-start | bytes 3145736 | tf_op jit(solution)/shard_map/ppermute | solution.py:451
  209.2 1.9 collective-permute-start.17
  211.1 10.1 %collective-permute-done.16 = bf16[2,128,2048]{2,1,0:T(8,128)(2,1)S(1)} collective-permute-done((bf16[2,128,2048]{2,1,0:T(8,128)(2,1)S(1)}, bf16[2,128,2048]{2,1,0:T(8,128)(2,1)S(1)}, u32[]{:S(2)}, u32[]{:S(2)}) %collective-permute-start.16) | collective-permute-done | bytes 1048608 | tf_op jit(solution)/shard_map/ppermute | solution.py:451
  (90 shorter events, 20.4 us)
Async XLA Ops:
  5.8 32.8 %copy-start.5 = (bf16[1,128,2048]{2,1,0:T(8,128)(2,1)S(1)}, bf16[1,128,2048]{2,1,0:T(8,128)(2,1)}, u32[]{:S(2)}) copy-start(bf16[1,128,2048]{2,1,0:T(8,128)(2,1)} %param.13) | copy-start | bytes 1572868
  5.8 32.8 %copy-start.15 = (f32[2048]{0:T(1024)S(1)}, f32[2048]{0:T(1024)}, u32[]{:S(2)}) copy-start(f32[2048]{0:T(1024)} %param.17) | copy-start | bytes 24580
  5.8 32.8 %copy-start.16 = (s32[1,2,3]{2,1,0:T(2,128)S(1)}, s32[1,2,3]{2,1,0:T(2,128)}, u32[]{:S(2)}) copy-start(s32[1,2,3]{2,1,0:T(2,128)} %param.20) | copy-start | bytes 76
  5.8 32.8 %copy-start.18 = (s32[1,128,2]{1,2,0:T(2,128)S(1)}, s32[1,128,2]{1,2,0:T(2,128)}, u32[]{:S(2)}) copy-start(s32[1,128,2]{1,2,0:T(2,128)} %param.19) | copy-start | bytes 3076
  5.8 44.1 %all-to-all-start = ((bf16[32,2,40,256]{3,2,1,0:T(8,128)(2,1)}), bf16[32,2,40,256]{3,2,1,0:T(8,128)(2,1)}, u32[]{:S(2)}, u32[]{:S(2)}) async-start(bf16[32,2,40,256]{3,2,1,0:T(8,128)(2,1)} %place_grad.1), calls=%async_computation | async-start | bytes 2621440 | tf_op jit(solution)/shard_map/all_to_all | solution.py:354
  18.1 11.5 %collective-permute-start.2 = (bf16[128,2048]{1,0:T(8,128)(2,1)S(1)}, bf16[128,2048]{1,0:T(8,128)(2,1)S(1)}, u32[]{:S(2)}, u32[]{:S(2)}) collective-permute-start(bf16[128,2048]{1,0:T(8,128)(2,1)S(1)} %bitcast.79), channel_id=1, source_target_pairs={{0,32},{32,64},{64,96},{96,128},{128,160},{160,192},{192,224},{1,3... | collective-permute-start | bytes 1572872 | tf_op jit(solution)/shard_map/ppermute | solution.py:364
  22.1 10.9 %collective-permute-start.3 = (bf16[128,2048]{1,0:T(8,128)(2,1)S(1)}, bf16[128,2048]{1,0:T(8,128)(2,1)S(1)}, u32[]{:S(2)}, u32[]{:S(2)}) collective-permute-start(bf16[128,2048]{1,0:T(8,128)(2,1)S(1)} %bitcast.80), channel_id=1, source_target_pairs={{32,0},{64,32},{96,64},{128,96},{160,128},{192,160},{224,192},{33,... | collective-permute-start | bytes 1572872 | tf_op jit(solution)/shard_map/ppermute | solution.py:364
  24.0 9.8 %collective-permute-start = (bf16[128,2048]{1,0:T(8,128)(2,1)S(1)}, bf16[128,2048]{1,0:T(8,128)(2,1)S(1)}, u32[]{:S(2)}, u32[]{:S(2)}) collective-permute-start(bf16[128,2048]{1,0:T(8,128)(2,1)S(1)} %bitcast.74), channel_id=1, source_target_pairs={{0,32},{32,64},{64,96},{96,128},{128,160},{160,192},{192,224},{1,3... | collective-permute-start | bytes 1572872 | tf_op jit(solution)/shard_map/ppermute | solution.py:363
  27.7 10.9 %collective-permute-start.1 = (bf16[128,2048]{1,0:T(8,128)(2,1)S(1)}, bf16[128,2048]{1,0:T(8,128)(2,1)S(1)}, u32[]{:S(2)}, u32[]{:S(2)}) collective-permute-start(bf16[128,2048]{1,0:T(8,128)(2,1)S(1)} %bitcast.75), channel_id=1, source_target_pairs={{32,0},{64,32},{96,64},{128,96},{160,128},{192,160},{224,192},{33,... | collective-permute-start | bytes 1572872 | tf_op jit(solution)/shard_map/ppermute | solution.py:363
  48.0 15.3 %collective-permute-start.4 = (bf16[512,2048]{1,0:T(8,128)(2,1)S(1)}, bf16[512,2048]{1,0:T(8,128)(2,1)}, u32[]{:S(2)}, u32[]{:S(2)}) collective-permute-start(bf16[512,2048]{1,0:T(8,128)(2,1)S(1)} %bitcast.62), channel_id=1, source_target_pairs={{0,32},{32,0},{64,96},{96,64},{128,160},{160,128},{192,224},{224,1... | collective-permute-start | bytes 6291464 | tf_op jit(solution)/shard_map/ppermute | solution.py:351
  49.9 40.7 %all-to-all-start.1 = ((bf16[32,2,40,256]{3,2,1,0:T(8,128)(2,1)}), bf16[32,2,40,256]{3,2,1,0:T(8,128)(2,1)}, u32[]{:S(2)}, u32[]{:S(2)}) async-start(bf16[32,2,40,256]{3,2,1,0:T(8,128)(2,1)} %get-tuple-element.31), calls=%async_computation.1 | async-start | bytes 2621440 | tf_op jit(solution)/shard_map/all_to_all | solution.py:354
  58.2 36.1 %collective-permute-start.5 = (bf16[2048,512]{1,0:T(8,128)(2,1)}, bf16[2048,512]{1,0:T(8,128)(2,1)}, u32[]{:S(2)}, u32[]{:S(2)}) collective-permute-start(bf16[2048,512]{1,0:T(8,128)(2,1)} %bitcast.66), channel_id=1, source_target_pairs={{0,32},{32,0},{64,96},{96,64},{128,160},{160,128},{192,224},{224,1... | collective-permute-start | bytes 6291464 | tf_op jit(solution)/shard_map/ppermute | solution.py:351
  58.5 35.8 %collective-permute-start.6 = (bf16[2048,512]{1,0:T(8,128)(2,1)}, bf16[2048,512]{1,0:T(8,128)(2,1)}, u32[]{:S(2)}, u32[]{:S(2)}) collective-permute-start(bf16[2048,512]{1,0:T(8,128)(2,1)} %bitcast.70), channel_id=1, source_target_pairs={{0,32},{32,0},{64,96},{96,64},{128,160},{160,128},{192,224},{224,1... | collective-permute-start | bytes 6291464 | tf_op jit(solution)/shard_map/ppermute | solution.py:351
  61.0 17.6 %collective-permute-start.10 = (bf16[1280,256]{1,0:T(8,128)(2,1)}, bf16[1280,256]{1,0:T(8,128)(2,1)S(1)}, u32[]{:S(2)}, u32[]{:S(2)}) collective-permute-start(bf16[1280,256]{1,0:T(8,128)(2,1)} %bitcast.17), channel_id=1, source_target_pairs={{0,192},{32,224},{64,128},{96,160},{128,64},{160,96},{192,0},{224,... | collective-permute-start | bytes 1966088 | tf_op jit(solution)/shard_map/ppermute | solution.py:351
  63.3 15.7 %collective-permute-start.11 = (bf16[1280,256]{1,0:T(8,128)(2,1)S(1)}, bf16[1280,256]{1,0:T(8,128)(2,1)S(1)}, u32[]{:S(2)}, u32[]{:S(2)}) collective-permute-start(bf16[1280,256]{1,0:T(8,128)(2,1)S(1)} %bitcast.60), channel_id=1, source_target_pairs={{0,64},{32,96},{64,0},{96,32},{128,192},{160,224},{192,128},{224,1... | collective-permute-start | bytes 1966088 | tf_op jit(solution)/shard_map/ppermute | solution.py:351
  63.3 41.1 %collective-permute-start.7 = (bf16[1280,256]{1,0:T(8,128)(2,1)}, bf16[1280,256]{1,0:T(8,128)(2,1)S(1)}, u32[]{:S(2)}, u32[]{:S(2)}) collective-permute-start(bf16[1280,256]{1,0:T(8,128)(2,1)} %bitcast.17), channel_id=1, source_target_pairs={{0,128},{32,160},{64,192},{96,224},{128,0},{160,32},{192,64},{224,... | collective-permute-start | bytes 1966088 | tf_op jit(solution)/shard_map/ppermute | solution.py:351
  92.2 15.8 %collective-permute-start.8 = (bf16[1280,256]{1,0:T(8,128)(2,1)S(1)}, bf16[1280,256]{1,0:T(8,128)(2,1)S(1)}, u32[]{:S(2)}, u32[]{:S(2)}) collective-permute-start(bf16[1280,256]{1,0:T(8,128)(2,1)S(1)} %bitcast.95), channel_id=1, source_target_pairs={{0,192},{32,224},{64,128},{96,160},{128,64},{160,96},{192,0},{224,... | collective-permute-start | bytes 1966088 | tf_op jit(solution)/shard_map/ppermute | solution.py:351
  92.3 15.7 %collective-permute-start.9 = (bf16[1280,256]{1,0:T(8,128)(2,1)S(1)}, bf16[1280,256]{1,0:T(8,128)(2,1)S(1)}, u32[]{:S(2)}, u32[]{:S(2)}) collective-permute-start(bf16[1280,256]{1,0:T(8,128)(2,1)S(1)} %bitcast.58), channel_id=1, source_target_pairs={{0,64},{32,96},{64,0},{96,32},{128,192},{160,224},{192,128},{224,1... | collective-permute-start | bytes 1966088 | tf_op jit(solution)/shard_map/ppermute | solution.py:351
  108.0 13.6 %collective-permute-start.14 = (bf16[1280,256]{1,0:T(8,128)(2,1)S(1)}, bf16[1280,256]{1,0:T(8,128)(2,1)S(1)}, u32[]{:S(2)}, u32[]{:S(2)}) collective-permute-start(bf16[1280,256]{1,0:T(8,128)(2,1)S(1)} %collective-permute-done.8.refs_0_), channel_id=1, source_target_pairs={{0,64},{32,96},{64,0},{96,32},{128,192},{160,224},{192,128},{224,1... | collective-permute-start | bytes 1966088 | tf_op jit(solution)/shard_map/ppermute | solution.py:351
  117.7 18.1 %collective-permute-start.12 = (bf16[1280,256]{1,0:T(8,128)(2,1)S(1)}, bf16[1280,256]{1,0:T(8,128)(2,1)S(1)}, u32[]{:S(2)}, u32[]{:S(2)}) collective-permute-start(bf16[1280,256]{1,0:T(8,128)(2,1)S(1)} %get-tuple-element.40), channel_id=1, source_target_pairs={{0,64},{32,96},{64,0},{96,32},{128,192},{160,224},{192,128},{224,1... | collective-permute-start | bytes 1966088 | tf_op jit(solution)/shard_map/ppermute | solution.py:351
  119.2 16.7 %collective-permute-start.13 = (bf16[1280,256]{1,0:T(8,128)(2,1)S(1)}, bf16[1280,256]{1,0:T(8,128)(2,1)S(1)}, u32[]{:S(2)}, u32[]{:S(2)}) collective-permute-start(bf16[1280,256]{1,0:T(8,128)(2,1)S(1)} %get-tuple-element.41), channel_id=1, source_target_pairs={{0,192},{32,224},{64,128},{96,160},{128,64},{160,96},{192,0},{224,... | collective-permute-start | bytes 1966088 | tf_op jit(solution)/shard_map/ppermute | solution.py:351
  129.1 21.6 %collective-permute-start.15 = (bf16[1280,256]{1,0:T(8,128)(2,1)S(1)}, bf16[1280,256]{1,0:T(8,128)(2,1)S(1)}, u32[]{:S(2)}, u32[]{:S(2)}) collective-permute-start(bf16[1280,256]{1,0:T(8,128)(2,1)S(1)} %expert.5), channel_id=1, source_target_pairs={{0,128},{32,160},{64,192},{96,224},{128,0},{160,32},{192,64},{224,... | collective-permute-start | bytes 1966088 | tf_op jit(solution)/shard_map/ppermute | solution.py:351
  150.6 46.6 %copy-start.31 = (f32[128,128]{1,0:T(8,128)S(1)}, f32[128,128]{1,0:T(8,128)}, u32[]{:S(2)}) copy-start(f32[128,128]{1,0:T(8,128)} %copy-done.30) | copy-start | bytes 196612
  150.8 46.5 %copy-start.27 = (f32[32,64,192]{2,1,0:T(8,128)S(1)}, f32[32,64,192]{2,1,0:T(8,128)}, u32[]{:S(2)}) copy-start(f32[32,64,192]{2,1,0:T(8,128)} %copy-done.26) | copy-start | bytes 4718596
  150.8 46.5 %copy-start.29 = (f32[128,2048]{1,0:T(8,128)S(1)}, f32[128,2048]{1,0:T(8,128)}, u32[]{:S(2)}) copy-start(f32[128,2048]{1,0:T(8,128)} %copy-done.28) | copy-start | bytes 3145732
  151.0 46.3 %copy-start.8 = (bf16[1,128,2048]{2,1,0:T(8,128)(2,1)S(1)}, bf16[1,128,2048]{2,1,0:T(8,128)(2,1)}, u32[]{:S(2)}) copy-start(bf16[1,128,2048]{2,1,0:T(8,128)(2,1)} %param.15) | copy-start | bytes 1572868
  151.0 46.3 %copy-start.10 = (bf16[1,128,2048]{2,1,0:T(8,128)(2,1)S(1)}, bf16[1,128,2048]{2,1,0:T(8,128)(2,1)}, u32[]{:S(2)}) copy-start(bf16[1,128,2048]{2,1,0:T(8,128)(2,1)} %param.16) | copy-start | bytes 1572868
  151.0 46.3 %copy-start.12 = (bf16[128,2048]{1,0:T(8,128)(2,1)S(1)}, bf16[128,2048]{1,0:T(8,128)(2,1)}, u32[]{:S(2)}) copy-start(bf16[128,2048]{1,0:T(8,128)(2,1)} %copy-done.11) | copy-start | bytes 1572868
  151.0 46.3 %copy-start.14 = (bf16[128,2048]{1,0:T(8,128)(2,1)S(1)}, bf16[128,2048]{1,0:T(8,128)(2,1)}, u32[]{:S(2)}) copy-start(bf16[128,2048]{1,0:T(8,128)(2,1)} %copy-done.13) | copy-start | bytes 1572868
  151.0 46.3 %copy-start.19 = (f32[1,128,2]{1,2,0:T(2,128)S(1)}, f32[1,128,2]{1,2,0:T(2,128)}, u32[]{:S(2)}) copy-start(f32[1,128,2]{1,2,0:T(2,128)} %param.18) | copy-start | bytes 3076
  204.3 16.9 %collective-permute-start.16 = (bf16[2,128,2048]{2,1,0:T(8,128)(2,1)S(1)}, bf16[2,128,2048]{2,1,0:T(8,128)(2,1)S(1)}, u32[]{:S(2)}, u32[]{:S(2)}) collective-permute-start(bf16[2,128,2048]{2,1,0:T(8,128)(2,1)S(1)} %get-tuple-element.47), channel_id=1, source_target_pairs={{32,0},{64,32},{96,64},{128,96},{160,128},{192,160},{224,192},{33,... | collective-permute-start | bytes 3145736 | tf_op jit(solution)/shard_map/ppermute | solution.py:451
  209.2 13.7 %collective-permute-start.17 = (bf16[2,128,2048]{2,1,0:T(8,128)(2,1)S(1)}, bf16[2,128,2048]{2,1,0:T(8,128)(2,1)S(1)}, u32[]{:S(2)}, u32[]{:S(2)}) collective-permute-start(bf16[2,128,2048]{2,1,0:T(8,128)(2,1)S(1)} %get-tuple-element.48), channel_id=1, source_target_pairs={{0,32},{32,64},{64,96},{96,128},{128,160},{160,192},{192,224},{1,3... | collective-permute-start | bytes 3145736 | tf_op jit(solution)/shard_map/ppermute | solution.py:452
  (20 other events, 124.3 us)

commit v6 on v5

--- a/solution.py
+++ b/solution.py
@@ -54,11 +54,9 @@
 
 
 def from_wire(block_ref, rows_ref, base, perm_t, chunks, piece):
-    if not isinstance(block_ref, list):
-        block_ref = [block_ref[c * CHUNK : (c + 1) * CHUNK, :] for c in range(chunks)]
     for pair in range(chunks // 2):
-        low = dot(perm_t, block_ref[2 * pair])
-        high = dot(perm_t, block_ref[2 * pair + 1])
+        low = dot(perm_t, block_ref[2 * pair * CHUNK : (2 * pair + 1) * CHUNK, :])
+        high = dot(perm_t, block_ref[(2 * pair + 1) * CHUNK : (2 * pair + 2) * CHUNK, :])
         start = base + 2 * pair * ROWS
         for q in range(PIECES):
             both = jnp.concatenate(
@@ -203,9 +201,16 @@
 def expert_kernel(*refs, blocks):
     ins = refs[:blocks]
     hg_ref, perm_ref, perm_t_ref = refs[blocks : blocks + 3]
-    weights = refs[blocks + 3 : blocks + 7]
+    gate_ref, up_ref, gate_hbm, up_hbm = refs[blocks + 3 : blocks + 7]
     outs = refs[blocks + 7 : 2 * blocks + 7]
-    rows_ref, act_ref, total_ref = refs[2 * blocks + 7 :]
+    rows_ref, act_ref, total_ref, w_ref, sems = refs[2 * blocks + 7 :]
+    copies = [
+        pltpu.make_async_copy(src, w_ref.at[i], sems.at[i])
+        for i, src in enumerate((gate_hbm, up_hbm))
+    ]
+    for copy in copies:
+        copy.start()
+    weights = (gate_ref, up_ref, w_ref.at[0], w_ref.at[1])
     piece = ins[0].shape[1]
     chunks = ins[0].shape[0] // CHUNK
     perm_t = perm_t_ref[...]
@@ -213,6 +218,9 @@
         from_wire(block, rows_ref, b * chunks * ROWS, perm_t, chunks, piece)
     width, part = weights[0].shape
     for i in range(2):
+        if i == 1:
+            for copy in copies:
+                copy.wait()
         gate_proj = dot(rows_ref[...], weights[2 * i][...])
         up_proj = dot(rows_ref[...], weights[2 * i + 1][...])
         hidden = hg_ref[:, i * part : (i + 1) * part]
@@ -233,7 +241,7 @@
 
 
 def backward_kernel(
-    seq_ref, offs_ref, ids_ref, gates_ref, home_ref, grad_ref, unit_ref, inv_ref, gain_ref,
+    seq_ref, offs_ref, ids_ref, gates_ref, own_ref, oth_ref, grad_ref, unit_ref, inv_ref, gain_ref,
     perm_t_ref, q_ref, vl_ref, v_ref, vr_ref, wts_ref, k_out_ref, v_out_ref, to_left_ref,
     to_right_ref, vx_ref, rows_ref, ag_ref, ka_ref, va_ref, total_tiles,
 ):
@@ -244,14 +252,12 @@
     scale = HEAD_DIM ** (-0.5)
     ka_ref[...] = jnp.zeros_like(ka_ref)
     va_ref[...] = jnp.zeros_like(va_ref)
-    columns, _, _, piece = home_ref.shape
-    chunks = columns // GROUP
+    piece = own_ref.shape[1]
+    chunks = own_ref.shape[0] // CHUNK
+    columns = chunks * GROUP
     perm_t = perm_t_ref[...]
-    for rel in range(2):
-        blocks = [
-            home_ref[c * GROUP : (c + 1) * GROUP, rel].reshape(CHUNK, piece) for c in range(chunks)
-        ]
-        from_wire(blocks, rows_ref, rel * chunks * ROWS, perm_t, chunks, piece)
+    from_wire(own_ref, rows_ref, 0, perm_t, chunks, piece)
+    from_wire(oth_ref, rows_ref, chunks * ROWS, perm_t, chunks, piece)
     slot0, slot1 = slot_rows(ids_ref, seq_ref[0] // 4, 2 * columns)
     places = lax.broadcasted_iota(jnp.int32, (rows_ref.shape[0], count), 0)
     mix = jnp.where(places == slot0, gates_ref[0:1, :], 0.0)
@@ -303,7 +309,7 @@
 
 
 def call(body, outs, kinds, scratch, name, flops, megabytes):
-    spaces = {"s": pltpu.SMEM, "v": pltpu.VMEM}
+    spaces = {"s": pltpu.SMEM, "v": pltpu.VMEM, "a": pl.ANY}
     return pl.pallas_call(
         body,
         out_shape=outs,
@@ -357,7 +363,7 @@
     pair = (2, count, width)
     (sent_grad,) = call(
         grad_kernel, (shape(wire, BF16),), "svvv", [pltpu.VMEM((2 * slots, width), F32)],
-        "place_grad", 4 * MICRO, 12,
+        "place_grad", 4 * MICRO, 56,
     )(seq, ids_t, grad, perm)
     k, v, sent_grad = barrier((k, v, sent_grad))
     kl, kr = lax.ppermute(k, "seq", up_by), lax.ppermute(k, "seq", down_by)
@@ -380,7 +386,7 @@
             pltpu.VMEM((count, width), F32),
             pltpu.VMEM((2 * slots, width), F32),
         ],
-        "attention", ATTN * MICRO, 20,
+        "attention", ATTN * MICRO, 16,
     )(seq, offsets, ids_t, q, kl, k, kr, vl, v, vr, gain, perm)
 
     sent, *weights = barrier((sent, gate, up, down))
@@ -403,7 +409,7 @@
             (shape((blocks * slots, 2 * part), F32),),
             "v" * (blocks + 3),
             [pltpu.VMEM((blocks * slots, width), BF16)],
-            "hidden", micros * MICRO, 14,
+            "hidden", micros * MICRO, 8,
         )(*ins, perm_t, down, down_s)
         return out
 
@@ -412,13 +418,15 @@
         return call(
             lambda *refs: expert_kernel(*refs, blocks=blocks),
             (shape(flat, BF16),) * blocks,
-            "v" * (blocks + 7),
+            "v" * (blocks + 5) + "aa",
             [
                 pltpu.VMEM((blocks * slots, width), BF16),
                 pltpu.VMEM((4, blocks * slots, part), BF16),
                 pltpu.VMEM((blocks * slots, width), F32),
+                pltpu.VMEM((2, width, part), BF16),
+                pltpu.SemaphoreType.DMA((2,)),
             ],
-            "expert", micros * MICRO, 24,
+            "expert", micros * MICRO, 20,
         )(*ins, hg, perm, perm_t, gate, up, gate_s, up_s)
 
     hidden_own = hidden((g0,), 4)
@@ -430,15 +438,19 @@
     p1, p2 = expert((n1, n2), hidden_near, 11)
     (p3,) = expert((n3,), hidden_far, 9)
     h1, h2 = swap(p1, 6), swap(p2, 2)
+    half_wire = (columns, CELL, piece)
+    h1, h2, p3 = barrier((h1, h2, p3))
     h3 = swap(p3, 4)
-    own = (p0.astype(F32) + h2.astype(F32)).astype(BF16).reshape(columns, 1, CELL, piece)
-    oth = (h1.astype(F32) + h3.astype(F32)).astype(BF16).reshape(columns, 1, CELL, piece)
-    home = exchange(jnp.concatenate([own, oth], axis=1))
+    own = (p0.astype(F32) + h2.astype(F32)).astype(BF16)
+    oth = (h1.astype(F32) + h3.astype(F32)).astype(BF16)
+    home_own = exchange(own.reshape(half_wire)).reshape(flat)
+    home_own, oth = barrier((home_own, oth))
+    home_oth = exchange(oth.reshape(half_wire)).reshape(flat)
 
     k_own, v_own, to_left, to_right = call(
         lambda *refs: backward_kernel(*refs, total_tiles=total_tiles),
         (shape((count, width), F32), shape((count, width), F32), shape(pair, BF16), shape(pair, BF16)),
-        "ss" + "v" * 13,
+        "ss" + "v" * 14,
         [
             pltpu.VMEM((3 * count, width), BF16),
             pltpu.VMEM((2 * slots, width), BF16),
@@ -446,8 +458,8 @@
             pltpu.VMEM((3 * count, width), F32),
             pltpu.VMEM((3 * count, width), F32),
         ],
-        "attention_grad", 10 * MICRO, 24,
-    )(seq, offsets, ids_t, gates_t, home, grad, unit, inv, gain, perm_t, q, vl, v, vr, wts)
+        "attention_grad", 10 * MICRO, 18,
+    )(seq, offsets, ids_t, gates_t, home_own, home_oth, grad, unit, inv, gain, perm_t, q, vl, v, vr, wts)
     from_right = lax.ppermute(to_left, "seq", down_by).astype(F32)
     from_left = lax.ppermute(to_right, "seq", up_by).astype(F32)
 

time: 225 us -> 226 us (level)
  blocking collectives: 46.3 us -> 24.5 us
  starting transfers between devices: 50.2 us -> 65.9 us
  waiting for transfers between devices: 59.8 us -> 63.6 us
  Pallas kernels: 50.4 us -> 47.9 us
  local copies, waits for them, and re-layouts: 14.4 us -> 16.7 us
    all_to_all x1, blocking collectives: 46.3 us -> 24.5 us  [exchange(): return lax.all_to_all(x, 'exp', split_axis=0, concat_axis=0, tiled=True)]
    all_to_all x2 -> x3, starting transfers between devices: 20.5 us -> 32.4 us  [exchange(): return lax.all_to_all(x, 'exp', split_axis=0, concat_axis=0, tiled=True)]
    ppermute x12, waiting for transfers between devices: 30.6 us -> 34.3 us  [swap(): return lax.ppermute(x, 'seq', [(i, i ^ bits) for i in range(seq_count)])]
    pallas_call x3, Pallas kernels: 24.2 us -> 20.7 us  [expert(): call(lambda *refs: expert_kernel(*refs, blocks=blocks), (shape(flat, BF16...]
    ppermute x1, starting transfers between devices: 4.89 us -> 7.47 us  [on_device(): from_right = lax.ppermute(to_left, 'seq', down_by).astype(F32)]
    unnamed x64 -> x60, local copies, waits for them, and re-layouts: 10.7 us -> 12.9 us
    all_to_all x2 -> x3, waiting for transfers between devices: 8.7 us -> 8.81 us  [exchange(): return lax.all_to_all(x, 'exp', split_axis=0, concat_axis=0, tiled=True)]
  transfers between devices with their start and end apart: 20 -> 21, of which waited for: 12 -> 15; matrix products, arithmetic and copies ran while one was open for 2% -> 2% of each run, Pallas kernels for 18% -> 17%
where the time goes in v6:
time: 226 us; the launch traced here: 224 us
  starting transfers between devices  65.9 us (29%)
  waiting for transfers between devices  63.6 us (28%)
  Pallas kernels  47.9 us (21%)
  blocking collectives  24.5 us (11%)
  local copies, waits for them, and re-layouts  16.7 us (7%)
  other arithmetic  4.12 us (2%)
    ppermute x12, waiting for transfers between devices, swap(): return lax.ppermute(x, 'seq', [(i, i ^ bits) for i in range(seq_count)])  34.3 us
    all_to_all x3, starting transfers between devices, exchange(): return lax.all_to_all(x, 'exp', split_axis=0, concat_axis=0, tiled=True)  32.4 us
    all_to_all x1, blocking collectives, exchange(): return lax.all_to_all(x, 'exp', split_axis=0, concat_axis=0, tiled=True)  24.5 us
    pallas_call x3, Pallas kernels, expert(): call(lambda *refs: expert_kernel(*refs, blocks=blocks), (shape(flat, BF16...  20.7 us
    unnamed x60, local copies, waits for them, and re-layouts  12.9 us
    ppermute x12, starting transfers between devices, swap(): return lax.ppermute(x, 'seq', [(i, i ^ bits) for i in range(seq_count)])  11.8 us
    pallas_call x3, Pallas kernels, hidden(): call(lambda *refs: hidden_kernel(*refs, blocks=blocks), (shape((blocks *...  10.8 us
    ppermute x1, waiting for transfers between devices, on_device(): from_right = lax.ppermute(to_left, 'seq', down_by).astype(F32)  10.5 us
  transfers between devices with their start and end apart: 21, of which 15 were waited for; matrix products, arithmetic and copies ran while one was open for 2% of the time, Pallas kernels for 17%

profile of v6, /device:TPU:1, one launch (start us, length us, event | category | flops | bytes accessed | tf_op | source)
XLA Modules:
  0.0 223.7 jit_solution(9949798719681009913)
XLA Ops:
  0.6 3.6 %place_grad.1 = bf16[32,2,40,256]{3,2,1,0:T(8,128)(2,1)} custom-call(s32[1]{0:T(128)} %bitcast.seq_ref.refs_0_, s32[2,128]{1,0:T(2,128)} %bitcast.93, bf16[128,2048]{1,0:T(8,128)(2,1)} %bitcast.87, bf16[320,320]{1,0:T(8,128)(2,1)} %constant.8.clone.perm_ref.refs_11_.refs_1_.refs_2_.refs_3_.refs_4_.refs_10_), custom_call_target="tpu_custom_call" | custom-call | flops 4294967296 | bytes 1048576 | tf_op jit(solution)/shard_map/place_grad/pallas_call | solution.py:364
  4.3 12.3 %all-to-all-start = ((bf16[32,2,40,256]{3,2,1,0:T(8,128)(2,1)}), bf16[32,2,40,256]{3,2,1,0:T(8,128)(2,1)}, u32[]{:S(2)}, u32[]{:S(2)}) async-start(bf16[32,2,40,256]{3,2,1,0:T(8,128)(2,1)} %place_grad.1), calls=%async_computation | async-start | bytes 2621440 | tf_op jit(solution)/shard_map/all_to_all | solution.py:360
  16.6 4.0 %collective-permute-start.2 = (bf16[128,2048]{1,0:T(8,128)(2,1)S(1)}, bf16[128,2048]{1,0:T(8,128)(2,1)S(1)}, u32[]{:S(2)}, u32[]{:S(2)}) collective-permute-start(bf16[128,2048]{1,0:T(8,128)(2,1)S(1)} %bitcast.83), channel_id=1, source_target_pairs={{0,32},{32,64},{64,96},{96,128},{128,160},{160,192},{192,224},{1,3... | collective-permute-start | bytes 1572872 | tf_op jit(solution)/shard_map/ppermute | solution.py:370
  20.5 1.9 collective-permute-start.3
  22.5 3.6 %collective-permute-start = (bf16[128,2048]{1,0:T(8,128)(2,1)S(1)}, bf16[128,2048]{1,0:T(8,128)(2,1)S(1)}, u32[]{:S(2)}, u32[]{:S(2)}) collective-permute-start(bf16[128,2048]{1,0:T(8,128)(2,1)S(1)} %bitcast.78), channel_id=1, source_target_pairs={{0,32},{32,64},{64,96},{96,128},{128,160},{160,192},{192,224},{1,3... | collective-permute-start | bytes 1572872 | tf_op jit(solution)/shard_map/ppermute | solution.py:369
  26.1 1.9 collective-permute-start.1
  28.1 3.4 %collective-permute-done.3.refs_9_.refs_14_ = bf16[128,2048]{1,0:T(8,128)(2,1)S(1)} collective-permute-done((bf16[128,2048]{1,0:T(8,128)(2,1)S(1)}, bf16[128,2048]{1,0:T(8,128)(2,1)S(1)}, u32[]{:S(2)}, u32[]{:S(2)}) %collective-permute-start.3) | collective-permute-done | bytes 524320 | tf_op jit(solution)/shard_map/ppermute | solution.py:370
  32.3 4.8 %collective-permute-done.1.refs_6_ = bf16[128,2048]{1,0:T(8,128)(2,1)S(1)} collective-permute-done((bf16[128,2048]{1,0:T(8,128)(2,1)S(1)}, bf16[128,2048]{1,0:T(8,128)(2,1)S(1)}, u32[]{:S(2)}, u32[]{:S(2)}) %collective-permute-start.1) | collective-permute-done | bytes 524320 | tf_op jit(solution)/shard_map/ppermute | solution.py:369
  38.1 6.0 %attention.1 = (f32[32,64,192]{2,1,0:T(8,128)S(1)}, f32[128,2048]{1,0:T(8,128)S(1)}, f32[128,128]{1,0:T(8,128)S(1)}, bf16[32,2,40,256]{3,2,1,0:T(8,128)(2,1)}) custom-call(s32[1]{0:T(128)} %bitcast.seq_ref.refs_0_, s32[2,3]{1,0:T(2,128)S(1)} %bitcast.91, s32[2,128]{1,0:T(2,128)S(1)} %bitcast.94, bf16[128,2048]{1,0:T(8,128)(2,1)S(1)} %bitcast.81, ...), custom_call_target="tpu_custom_call" | custom-call | flops 8589934592 | bytes 1048576 | tf_op jit(solution)/shard_map/attention/pallas_call | solution.py:374
  48.3 8.3 %all-to-all-start.1 = ((bf16[32,2,40,256]{3,2,1,0:T(8,128)(2,1)}), bf16[32,2,40,256]{3,2,1,0:T(8,128)(2,1)}, u32[]{:S(2)}, u32[]{:S(2)}) async-start(bf16[32,2,40,256]{3,2,1,0:T(8,128)(2,1)} %get-tuple-element.36), calls=%async_computation.1 | async-start | bytes 2621440 | tf_op jit(solution)/shard_map/all_to_all | solution.py:360
  57.3 2.2 fusion.9
  59.5 2.3 %collective-permute-start.10 = (bf16[1280,256]{1,0:T(8,128)(2,1)}, bf16[1280,256]{1,0:T(8,128)(2,1)S(1)}, u32[]{:S(2)}, u32[]{:S(2)}) collective-permute-start(bf16[1280,256]{1,0:T(8,128)(2,1)} %bitcast.17), channel_id=1, source_target_pairs={{0,192},{32,224},{64,128},{96,160},{128,64},{160,96},{192,0},{224,... | collective-permute-start | bytes 1966088 | tf_op jit(solution)/shard_map/ppermute | solution.py:357
  63.3 3.4 %hidden.3.refs_1_ = f32[160,1024]{1,0:T(8,128)S(1)} custom-call(bf16[1280,256]{1,0:T(8,128)(2,1)S(1)} %bitcast.63, bf16[320,320]{1,0:T(8,128)(2,1)S(1)} %copy-done.18, bf16[512,2048]{1,0:T(8,128)(2,1)S(1)} %bitcast.67, bf16[512,2048]{1,0:T(8,128)(2,1)} %collective-permute-done.4.refs_3_.refs_4_), custom_call_target="tpu_custom_call" | custom-call | flops 4294967296 | bytes 1048576 | tf_op jit(solution)/shard_map/hidden/pallas_call | solution.py:407
  67.6 9.5 %collective-permute-done.10.refs_0_ = bf16[1280,256]{1,0:T(8,128)(2,1)S(1)} collective-permute-done((bf16[1280,256]{1,0:T(8,128)(2,1)}, bf16[1280,256]{1,0:T(8,128)(2,1)S(1)}, u32[]{:S(2)}, u32[]{:S(2)}) %collective-permute-start.10) | collective-permute-done | bytes 655392 | tf_op jit(solution)/shard_map/ppermute | solution.py:357
  77.5 3.8 %hidden.5.refs_2_ = f32[320,1024]{1,0:T(8,128)S(1)} custom-call(bf16[1280,256]{1,0:T(8,128)(2,1)S(1)} %collective-permute-done.10.refs_0_, bf16[1280,256]{1,0:T(8,128)(2,1)S(1)} %collective-permute-done.11.refs_1_, bf16[320,320]{1,0:T(8,128)(2,1)S(1)} %copy-done.18, bf16[512,2048]{1,0:T(8,128)(2,1)S(1)} %bitcast.68, ...), custom_call_target="tpu_custom_call" | custom-call | flops 5368709120 | bytes 1048576 | tf_op jit(solution)/shard_map/hidden/pallas_call | solution.py:407
  82.3 6.8 %all-to-all-done.1 = bf16[32,2,40,256]{3,2,1,0:T(8,128)(2,1)} async-done(((bf16[32,2,40,256]{3,2,1,0:T(8,128)(2,1)}), bf16[32,2,40,256]{3,2,1,0:T(8,128)(2,1)}, u32[]{:S(2)}, u32[]{:S(2)}) %all-to-all-start.1) | async-done | bytes 1310752 | tf_op jit(solution)/shard_map/all_to_all | solution.py:360
  90.8 2.0 collective-permute-start.9
  95.5 6.3 %expert.3 = bf16[1280,256]{1,0:T(8,128)(2,1)S(1)} custom-call(bf16[1280,256]{1,0:T(8,128)(2,1)S(1)} %bitcast.61, f32[160,1024]{1,0:T(8,128)S(1)} %copy-done.22, bf16[320,320]{1,0:T(8,128)(2,1)S(1)} %copy-done.18, bf16[320,320]{1,0:T(8,128)(2,1)S(1)} %copy-done.18, bf16[2048,512]{1,0:T(8,128)(2,1)S(1)} %bitcast.71, bf16[2048,512]{1,0:T(8,128)(2,1)S(1)} %bitcast.75, ...), custom_call_target="tpu_custom_call" | custom-call | flops 9663676416 | bytes 1048576 | tf_op jit(solution)/shard_map/expert/pallas_call | solution.py:418
  101.9 3.6 %hidden.4.refs_1_ = f32[160,1024]{1,0:T(8,128)S(1)} custom-call(bf16[1280,256]{1,0:T(8,128)(2,1)S(1)} %collective-permute-done.7.refs_0_, bf16[320,320]{1,0:T(8,128)(2,1)S(1)} %copy-done.18, bf16[512,2048]{1,0:T(8,128)(2,1)S(1)} %bitcast.69, bf16[512,2048]{1,0:T(8,128)(2,1)} %collective-permute-done.4.refs_3_.refs_4_), custom_call_target="tpu_custom_call" | custom-call | flops 4294967296 | bytes 1048576 | tf_op jit(solution)/shard_map/hidden/pallas_call | solution.py:407
  106.6 8.0 %expert.4 = (bf16[1280,256]{1,0:T(8,128)(2,1)S(1)}, bf16[1280,256]{1,0:T(8,128)(2,1)S(1)}) custom-call(bf16[1280,256]{1,0:T(8,128)(2,1)S(1)} %collective-permute-done.8.refs_0_, bf16[1280,256]{1,0:T(8,128)(2,1)S(1)} %collective-permute-done.9.refs_1_, f32[320,1024]{1,0:T(8,128)S(1)} %copy-done.20, bf16[320,320]{1,0:T(8,128)(2,1)S(1)} %copy-done.18, ...), custom_call_target="tpu_custom_call" | custom-call | flops 11811160064 | bytes 1048576 | tf_op jit(solution)/shard_map/expert/pallas_call | solution.py:418
  116.3 3.1 %collective-permute-done.14.refs_0_ = bf16[1280,256]{1,0:T(8,128)(2,1)S(1)} collective-permute-done((bf16[1280,256]{1,0:T(8,128)(2,1)S(1)}, bf16[1280,256]{1,0:T(8,128)(2,1)S(1)}, u32[]{:S(2)}, u32[]{:S(2)}) %collective-permute-start.14) | collective-permute-done | bytes 655392 | tf_op jit(solution)/shard_map/ppermute | solution.py:357
  119.4 6.3 %expert.5 = bf16[1280,256]{1,0:T(8,128)(2,1)S(1)} custom-call(bf16[1280,256]{1,0:T(8,128)(2,1)S(1)} %collective-permute-done.14.refs_0_, f32[160,1024]{1,0:T(8,128)S(1)} %hidden.4.refs_1_, bf16[320,320]{1,0:T(8,128)(2,1)S(1)} %copy-done.18, bf16[320,320]{1,0:T(8,128)(2,1)S(1)} %copy-done.18, bf16[2048,512]{1,0:T(8,128)(2,1)S(1)} %bitcast.73, ...), custom_call_target="tpu_custom_call" | custom-call | flops 9663676416 | bytes 1048576 | tf_op jit(solution)/shard_map/expert/pallas_call | solution.py:418
  125.7 2.8 %collective-permute-done.12 = bf16[1280,256]{1,0:T(8,128)(2,1)S(1)} collective-permute-done((bf16[1280,256]{1,0:T(8,128)(2,1)S(1)}, bf16[1280,256]{1,0:T(8,128)(2,1)S(1)}, u32[]{:S(2)}, u32[]{:S(2)}) %collective-permute-start.12) | collective-permute-done | bytes 655392 | tf_op jit(solution)/shard_map/ppermute | solution.py:357
  128.5 4.9 %collective-permute-done.13 = bf16[1280,256]{1,0:T(8,128)(2,1)S(1)} collective-permute-done((bf16[1280,256]{1,0:T(8,128)(2,1)S(1)}, bf16[1280,256]{1,0:T(8,128)(2,1)S(1)}, u32[]{:S(2)}, u32[]{:S(2)}) %collective-permute-start.13) | collective-permute-done | bytes 655392 | tf_op jit(solution)/shard_map/ppermute | solution.py:357
  134.4 11.9 %all-to-all-start.2 = ((bf16[32,40,256]{2,1,0:T(8,128)(2,1)}), bf16[32,40,256]{2,1,0:T(8,128)(2,1)S(1)}, u32[]{:S(2)}, u32[]{:S(2)}) async-start(bf16[32,40,256]{2,1,0:T(8,128)(2,1)} %bitcast.19), calls=%async_computation.2 | async-start | bytes 1310720 | tf_op jit(solution)/shard_map/all_to_all | solution.py:360
  146.3 3.0 %collective-permute-start.15 = (bf16[1280,256]{1,0:T(8,128)(2,1)S(1)}, bf16[1280,256]{1,0:T(8,128)(2,1)S(1)}, u32[]{:S(2)}, u32[]{:S(2)}) collective-permute-start(bf16[1280,256]{1,0:T(8,128)(2,1)S(1)} %expert.5), channel_id=1, source_target_pairs={{0,128},{32,160},{64,192},{96,224},{128,0},{160,32},{192,64},{224,... | collective-permute-start | bytes 1966088 | tf_op jit(solution)/shard_map/ppermute | solution.py:357
  149.4 13.0 %collective-permute-done.15 = bf16[1280,256]{1,0:T(8,128)(2,1)S(1)} collective-permute-done((bf16[1280,256]{1,0:T(8,128)(2,1)S(1)}, bf16[1280,256]{1,0:T(8,128)(2,1)S(1)}, u32[]{:S(2)}, u32[]{:S(2)}) %collective-permute-start.15) | collective-permute-done | bytes 655392 | tf_op jit(solution)/shard_map/ppermute | solution.py:357
  163.8 24.5 %all_to_all.20 = bf16[32,40,256]{2,1,0:T(8,128)(2,1)S(1)} all-to-all(bf16[32,40,256]{2,1,0:T(8,128)(2,1)S(1)} %bitcast.97), channel_id=1, replica_groups=mesh['seq'=8,'exp'=32] {'exp'}, dimensions={0} | all-to-all | bytes 1310720 | tf_op jit(solution)/shard_map/all_to_all | solution.py:360
  193.3 6.8 %attention_grad.1 = (f32[128,2048]{1,0:T(8,128)S(1)}, f32[128,2048]{1,0:T(8,128)S(1)}, bf16[2,128,2048]{2,1,0:T(8,128)(2,1)S(1)}, bf16[2,128,2048]{2,1,0:T(8,128)(2,1)S(1)}) custom-call(s32[1]{0:T(128)} %bitcast.seq_ref.refs_0_, s32[2,3]{1,0:T(2,128)S(1)} %bitcast.92, s32[2,128]{1,0:T(2,128)S(1)} %bitcast.95, f32[2,128]{1,0:T(2,128)S(1)} %bitcast.96, ...), custom_call_target="tpu_custom_call" | custom-call | flops 10737418240 | bytes 1048576 | tf_op jit(solution)/shard_map/attention_grad/pallas_call | solution.py:450
  200.1 7.5 %collective-permute-start.16 = (bf16[2,128,2048]{2,1,0:T(8,128)(2,1)S(1)}, bf16[2,128,2048]{2,1,0:T(8,128)(2,1)S(1)}, u32[]{:S(2)}, u32[]{:S(2)}) collective-permute-start(bf16[2,128,2048]{2,1,0:T(8,128)(2,1)S(1)} %get-tuple-element.57), channel_id=1, source_target_pairs={{32,0},{64,32},{96,64},{128,96},{160,128},{192,160},{224,192},{33,... | collective-permute-start | bytes 3145736 | tf_op jit(solution)/shard_map/ppermute | solution.py:463
  207.6 2.8 %collective-permute-start.17 = (bf16[2,128,2048]{2,1,0:T(8,128)(2,1)S(1)}, bf16[2,128,2048]{2,1,0:T(8,128)(2,1)S(1)}, u32[]{:S(2)}, u32[]{:S(2)}) collective-permute-start(bf16[2,128,2048]{2,1,0:T(8,128)(2,1)S(1)} %get-tuple-element.58), channel_id=1, source_target_pairs={{0,32},{32,64},{64,96},{96,128},{128,160},{160,192},{192,224},{1,3... | collective-permute-start | bytes 3145736 | tf_op jit(solution)/shard_map/ppermute | solution.py:464
  210.4 10.5 %collective-permute-done.16 = bf16[2,128,2048]{2,1,0:T(8,128)(2,1)S(1)} collective-permute-done((bf16[2,128,2048]{2,1,0:T(8,128)(2,1)S(1)}, bf16[2,128,2048]{2,1,0:T(8,128)(2,1)S(1)}, u32[]{:S(2)}, u32[]{:S(2)}) %collective-permute-start.16) | collective-permute-done | bytes 1048608 | tf_op jit(solution)/shard_map/ppermute | solution.py:463
  (87 shorter events, 27.8 us)
Async XLA Ops:
  4.2 18.3 %copy-start.4 = (bf16[1,128,2048]{2,1,0:T(8,128)(2,1)S(1)}, bf16[1,128,2048]{2,1,0:T(8,128)(2,1)}, u32[]{:S(2)}) copy-start(bf16[1,128,2048]{2,1,0:T(8,128)(2,1)} %param.14) | copy-start | bytes 1572868
  4.2 32.8 %copy-start.5 = (bf16[1,128,2048]{2,1,0:T(8,128)(2,1)S(1)}, bf16[1,128,2048]{2,1,0:T(8,128)(2,1)}, u32[]{:S(2)}) copy-start(bf16[1,128,2048]{2,1,0:T(8,128)(2,1)} %param.13) | copy-start | bytes 1572868
  4.2 32.8 %copy-start.14 = (f32[2048]{0:T(1024)S(1)}, f32[2048]{0:T(1024)}, u32[]{:S(2)}) copy-start(f32[2048]{0:T(1024)} %param.17) | copy-start | bytes 24580
  4.2 32.8 %copy-start.15 = (s32[1,2,3]{2,1,0:T(2,128)S(1)}, s32[1,2,3]{2,1,0:T(2,128)}, u32[]{:S(2)}) copy-start(s32[1,2,3]{2,1,0:T(2,128)} %param.20) | copy-start | bytes 76
  4.2 32.8 %copy-start.16 = (s32[1,128,2]{1,2,0:T(2,128)S(1)}, s32[1,128,2]{1,2,0:T(2,128)}, u32[]{:S(2)}) copy-start(s32[1,128,2]{1,2,0:T(2,128)} %param.19) | copy-start | bytes 3076
  4.3 32.8 %copy-start.18 = (bf16[320,320]{1,0:T(8,128)(2,1)S(1)}, bf16[320,320]{1,0:T(8,128)(2,1)}, u32[]{:S(2)}) copy-start(bf16[320,320]{1,0:T(8,128)(2,1)} %constant.8.clone.perm_ref.refs_11_.refs_1_.refs_2_.refs_3_.refs_4_.refs_10_) | copy-start | bytes 614404
  4.3 44.1 %all-to-all-start = ((bf16[32,2,40,256]{3,2,1,0:T(8,128)(2,1)}), bf16[32,2,40,256]{3,2,1,0:T(8,128)(2,1)}, u32[]{:S(2)}, u32[]{:S(2)}) async-start(bf16[32,2,40,256]{3,2,1,0:T(8,128)(2,1)} %place_grad.1), calls=%async_computation | async-start | bytes 2621440 | tf_op jit(solution)/shard_map/all_to_all | solution.py:360
  16.6 11.5 %collective-permute-start.2 = (bf16[128,2048]{1,0:T(8,128)(2,1)S(1)}, bf16[128,2048]{1,0:T(8,128)(2,1)S(1)}, u32[]{:S(2)}, u32[]{:S(2)}) collective-permute-start(bf16[128,2048]{1,0:T(8,128)(2,1)S(1)} %bitcast.83), channel_id=1, source_target_pairs={{0,32},{32,64},{64,96},{96,128},{128,160},{160,192},{192,224},{1,3... | collective-permute-start | bytes 1572872 | tf_op jit(solution)/shard_map/ppermute | solution.py:370
  20.5 10.9 %collective-permute-start.3 = (bf16[128,2048]{1,0:T(8,128)(2,1)S(1)}, bf16[128,2048]{1,0:T(8,128)(2,1)S(1)}, u32[]{:S(2)}, u32[]{:S(2)}) collective-permute-start(bf16[128,2048]{1,0:T(8,128)(2,1)S(1)} %bitcast.84), channel_id=1, source_target_pairs={{32,0},{64,32},{96,64},{128,96},{160,128},{192,160},{224,192},{33,... | collective-permute-start | bytes 1572872 | tf_op jit(solution)/shard_map/ppermute | solution.py:370
  22.5 9.8 %collective-permute-start = (bf16[128,2048]{1,0:T(8,128)(2,1)S(1)}, bf16[128,2048]{1,0:T(8,128)(2,1)S(1)}, u32[]{:S(2)}, u32[]{:S(2)}) collective-permute-start(bf16[128,2048]{1,0:T(8,128)(2,1)S(1)} %bitcast.78), channel_id=1, source_target_pairs={{0,32},{32,64},{64,96},{96,128},{128,160},{160,192},{192,224},{1,3... | collective-permute-start | bytes 1572872 | tf_op jit(solution)/shard_map/ppermute | solution.py:369
  26.1 10.9 %collective-permute-start.1 = (bf16[128,2048]{1,0:T(8,128)(2,1)S(1)}, bf16[128,2048]{1,0:T(8,128)(2,1)S(1)}, u32[]{:S(2)}, u32[]{:S(2)}) collective-permute-start(bf16[128,2048]{1,0:T(8,128)(2,1)S(1)} %bitcast.79), channel_id=1, source_target_pairs={{32,0},{64,32},{96,64},{128,96},{160,128},{192,160},{224,192},{33,... | collective-permute-start | bytes 1572872 | tf_op jit(solution)/shard_map/ppermute | solution.py:369
  28.1 16.1 %copy-start.10 = (bf16[128,2048]{1,0:T(8,128)(2,1)}, bf16[128,2048]{1,0:T(8,128)(2,1)S(1)}, u32[]{:S(2)}) copy-start(bf16[128,2048]{1,0:T(8,128)(2,1)S(1)} %collective-permute-done.2.refs_7_.refs_12_) | copy-start | bytes 1572868
  46.5 15.3 %collective-permute-start.4 = (bf16[512,2048]{1,0:T(8,128)(2,1)S(1)}, bf16[512,2048]{1,0:T(8,128)(2,1)}, u32[]{:S(2)}, u32[]{:S(2)}) collective-permute-start(bf16[512,2048]{1,0:T(8,128)(2,1)S(1)} %bitcast.66), channel_id=1, source_target_pairs={{0,32},{32,0},{64,96},{96,64},{128,160},{160,128},{192,224},{224,1... | collective-permute-start | bytes 6291464 | tf_op jit(solution)/shard_map/ppermute | solution.py:357
  48.3 40.8 %all-to-all-start.1 = ((bf16[32,2,40,256]{3,2,1,0:T(8,128)(2,1)}), bf16[32,2,40,256]{3,2,1,0:T(8,128)(2,1)}, u32[]{:S(2)}, u32[]{:S(2)}) async-start(bf16[32,2,40,256]{3,2,1,0:T(8,128)(2,1)} %get-tuple-element.36), calls=%async_computation.1 | async-start | bytes 2621440 | tf_op jit(solution)/shard_map/all_to_all | solution.py:360
  56.7 36.1 %collective-permute-start.5 = (bf16[2048,512]{1,0:T(8,128)(2,1)}, bf16[2048,512]{1,0:T(8,128)(2,1)}, u32[]{:S(2)}, u32[]{:S(2)}) collective-permute-start(bf16[2048,512]{1,0:T(8,128)(2,1)} %bitcast.70), channel_id=1, source_target_pairs={{0,32},{32,0},{64,96},{96,64},{128,160},{160,128},{192,224},{224,1... | collective-permute-start | bytes 6291464 | tf_op jit(solution)/shard_map/ppermute | solution.py:357
  57.0 35.8 %collective-permute-start.6 = (bf16[2048,512]{1,0:T(8,128)(2,1)}, bf16[2048,512]{1,0:T(8,128)(2,1)}, u32[]{:S(2)}, u32[]{:S(2)}) collective-permute-start(bf16[2048,512]{1,0:T(8,128)(2,1)} %bitcast.74), channel_id=1, source_target_pairs={{0,32},{32,0},{64,96},{96,64},{128,160},{160,128},{192,224},{224,1... | collective-permute-start | bytes 6291464 | tf_op jit(solution)/shard_map/ppermute | solution.py:357
  59.5 17.6 %collective-permute-start.10 = (bf16[1280,256]{1,0:T(8,128)(2,1)}, bf16[1280,256]{1,0:T(8,128)(2,1)S(1)}, u32[]{:S(2)}, u32[]{:S(2)}) collective-permute-start(bf16[1280,256]{1,0:T(8,128)(2,1)} %bitcast.17), channel_id=1, source_target_pairs={{0,192},{32,224},{64,128},{96,160},{128,64},{160,96},{192,0},{224,... | collective-permute-start | bytes 1966088 | tf_op jit(solution)/shard_map/ppermute | solution.py:357
  61.8 15.7 %collective-permute-start.11 = (bf16[1280,256]{1,0:T(8,128)(2,1)S(1)}, bf16[1280,256]{1,0:T(8,128)(2,1)S(1)}, u32[]{:S(2)}, u32[]{:S(2)}) collective-permute-start(bf16[1280,256]{1,0:T(8,128)(2,1)S(1)} %bitcast.62), channel_id=1, source_target_pairs={{0,64},{32,96},{64,0},{96,32},{128,192},{160,224},{192,128},{224,1... | collective-permute-start | bytes 1966088 | tf_op jit(solution)/shard_map/ppermute | solution.py:357
  61.8 40.1 %collective-permute-start.7 = (bf16[1280,256]{1,0:T(8,128)(2,1)}, bf16[1280,256]{1,0:T(8,128)(2,1)S(1)}, u32[]{:S(2)}, u32[]{:S(2)}) collective-permute-start(bf16[1280,256]{1,0:T(8,128)(2,1)} %bitcast.17), channel_id=1, source_target_pairs={{0,128},{32,160},{64,192},{96,224},{128,0},{160,32},{192,64},{224,... | collective-permute-start | bytes 1966088 | tf_op jit(solution)/shard_map/ppermute | solution.py:357
  90.7 15.5 %collective-permute-start.8 = (bf16[1280,256]{1,0:T(8,128)(2,1)S(1)}, bf16[1280,256]{1,0:T(8,128)(2,1)S(1)}, u32[]{:S(2)}, u32[]{:S(2)}) collective-permute-start(bf16[1280,256]{1,0:T(8,128)(2,1)S(1)} %bitcast.98), channel_id=1, source_target_pairs={{0,192},{32,224},{64,128},{96,160},{128,64},{160,96},{192,0},{224,... | collective-permute-start | bytes 1966088 | tf_op jit(solution)/shard_map/ppermute | solution.py:357
  90.8 15.4 %collective-permute-start.9 = (bf16[1280,256]{1,0:T(8,128)(2,1)S(1)}, bf16[1280,256]{1,0:T(8,128)(2,1)S(1)}, u32[]{:S(2)}, u32[]{:S(2)}) collective-permute-start(bf16[1280,256]{1,0:T(8,128)(2,1)S(1)} %bitcast.60), channel_id=1, source_target_pairs={{0,64},{32,96},{64,0},{96,32},{128,192},{160,224},{192,128},{224,1... | collective-permute-start | bytes 1966088 | tf_op jit(solution)/shard_map/ppermute | solution.py:357
  106.1 13.2 %collective-permute-start.14 = (bf16[1280,256]{1,0:T(8,128)(2,1)S(1)}, bf16[1280,256]{1,0:T(8,128)(2,1)S(1)}, u32[]{:S(2)}, u32[]{:S(2)}) collective-permute-start(bf16[1280,256]{1,0:T(8,128)(2,1)S(1)} %collective-permute-done.8.refs_0_), channel_id=1, source_target_pairs={{0,64},{32,96},{64,0},{96,32},{128,192},{160,224},{192,128},{224,1... | collective-permute-start | bytes 1966088 | tf_op jit(solution)/shard_map/ppermute | solution.py:357
  114.7 13.8 %collective-permute-start.12 = (bf16[1280,256]{1,0:T(8,128)(2,1)S(1)}, bf16[1280,256]{1,0:T(8,128)(2,1)S(1)}, u32[]{:S(2)}, u32[]{:S(2)}) collective-permute-start(bf16[1280,256]{1,0:T(8,128)(2,1)S(1)} %get-tuple-element.45), channel_id=1, source_target_pairs={{0,192},{32,224},{64,128},{96,160},{128,64},{160,96},{192,0},{224,... | collective-permute-start | bytes 1966088 | tf_op jit(solution)/shard_map/ppermute | solution.py:357
  116.1 17.3 %collective-permute-start.13 = (bf16[1280,256]{1,0:T(8,128)(2,1)S(1)}, bf16[1280,256]{1,0:T(8,128)(2,1)S(1)}, u32[]{:S(2)}, u32[]{:S(2)}) collective-permute-start(bf16[1280,256]{1,0:T(8,128)(2,1)S(1)} %get-tuple-element.46), channel_id=1, source_target_pairs={{0,64},{32,96},{64,0},{96,32},{128,192},{160,224},{192,128},{224,1... | collective-permute-start | bytes 1966088 | tf_op jit(solution)/shard_map/ppermute | solution.py:357
  134.4 29.4 %all-to-all-start.2 = ((bf16[32,40,256]{2,1,0:T(8,128)(2,1)}), bf16[32,40,256]{2,1,0:T(8,128)(2,1)S(1)}, u32[]{:S(2)}, u32[]{:S(2)}) async-start(bf16[32,40,256]{2,1,0:T(8,128)(2,1)} %bitcast.19), calls=%async_computation.2 | async-start | bytes 1310720 | tf_op jit(solution)/shard_map/all_to_all | solution.py:360
  146.3 42.0 %copy-start.8 = (bf16[1,128,2048]{2,1,0:T(8,128)(2,1)S(1)}, bf16[1,128,2048]{2,1,0:T(8,128)(2,1)}, u32[]{:S(2)}) copy-start(bf16[1,128,2048]{2,1,0:T(8,128)(2,1)} %param.15) | copy-start | bytes 1572868
  146.3 42.0 %copy-start.9 = (bf16[1,128,2048]{2,1,0:T(8,128)(2,1)S(1)}, bf16[1,128,2048]{2,1,0:T(8,128)(2,1)}, u32[]{:S(2)}) copy-start(bf16[1,128,2048]{2,1,0:T(8,128)(2,1)} %param.16) | copy-start | bytes 1572868
  146.3 42.0 %copy-start.17 = (f32[1,128,2]{1,2,0:T(2,128)S(1)}, f32[1,128,2]{1,2,0:T(2,128)}, u32[]{:S(2)}) copy-start(f32[1,128,2]{1,2,0:T(2,128)} %param.18) | copy-start | bytes 3076
  146.3 42.0 %copy-start.28 = (f32[128,128]{1,0:T(8,128)S(1)}, f32[128,128]{1,0:T(8,128)}, u32[]{:S(2)}) copy-start(f32[128,128]{1,0:T(8,128)} %copy-done.27) | copy-start | bytes 196612
  146.3 16.1 %collective-permute-start.15 = (bf16[1280,256]{1,0:T(8,128)(2,1)S(1)}, bf16[1280,256]{1,0:T(8,128)(2,1)S(1)}, u32[]{:S(2)}, u32[]{:S(2)}) collective-permute-start(bf16[1280,256]{1,0:T(8,128)(2,1)S(1)} %expert.5), channel_id=1, source_target_pairs={{0,128},{32,160},{64,192},{96,224},{128,0},{160,32},{192,64},{224,... | collective-permute-start | bytes 1966088 | tf_op jit(solution)/shard_map/ppermute | solution.py:357
  200.1 20.8 %collective-permute-start.16 = (bf16[2,128,2048]{2,1,0:T(8,128)(2,1)S(1)}, bf16[2,128,2048]{2,1,0:T(8,128)(2,1)S(1)}, u32[]{:S(2)}, u32[]{:S(2)}) collective-permute-start(bf16[2,128,2048]{2,1,0:T(8,128)(2,1)S(1)} %get-tuple-element.57), channel_id=1, source_target_pairs={{32,0},{64,32},{96,64},{128,96},{160,128},{192,160},{224,192},{33,... | collective-permute-start | bytes 3145736 | tf_op jit(solution)/shard_map/ppermute | solution.py:463
  207.6 14.5 %collective-permute-start.17 = (bf16[2,128,2048]{2,1,0:T(8,128)(2,1)S(1)}, bf16[2,128,2048]{2,1,0:T(8,128)(2,1)S(1)}, u32[]{:S(2)}, u32[]{:S(2)}) collective-permute-start(bf16[2,128,2048]{2,1,0:T(8,128)(2,1)S(1)} %get-tuple-element.58), channel_id=1, source_target_pairs={{0,32},{32,64},{64,96},{96,128},{128,160},{160,192},{192,224},{1,3... | collective-permute-start | bytes 3145736 | tf_op jit(solution)/shard_map/ppermute | solution.py:464
  (19 other events, 67.4 us)

commit v7 on v5

--- a/solution.py
+++ b/solution.py
@@ -203,9 +203,16 @@
 def expert_kernel(*refs, blocks):
     ins = refs[:blocks]
     hg_ref, perm_ref, perm_t_ref = refs[blocks : blocks + 3]
-    weights = refs[blocks + 3 : blocks + 7]
+    gate_ref, up_ref, gate_hbm, up_hbm = refs[blocks + 3 : blocks + 7]
     outs = refs[blocks + 7 : 2 * blocks + 7]
-    rows_ref, act_ref, total_ref = refs[2 * blocks + 7 :]
+    rows_ref, act_ref, total_ref, w_ref, sems = refs[2 * blocks + 7 :]
+    copies = [
+        pltpu.make_async_copy(src, w_ref.at[i], sems.at[i])
+        for i, src in enumerate((gate_hbm, up_hbm))
+    ]
+    for copy in copies:
+        copy.start()
+    weights = (gate_ref, up_ref, w_ref.at[0], w_ref.at[1])
     piece = ins[0].shape[1]
     chunks = ins[0].shape[0] // CHUNK
     perm_t = perm_t_ref[...]
@@ -213,6 +220,9 @@
         from_wire(block, rows_ref, b * chunks * ROWS, perm_t, chunks, piece)
     width, part = weights[0].shape
     for i in range(2):
+        if i == 1:
+            for copy in copies:
+                copy.wait()
         gate_proj = dot(rows_ref[...], weights[2 * i][...])
         up_proj = dot(rows_ref[...], weights[2 * i + 1][...])
         hidden = hg_ref[:, i * part : (i + 1) * part]
@@ -303,7 +313,7 @@
 
 
 def call(body, outs, kinds, scratch, name, flops, megabytes):
-    spaces = {"s": pltpu.SMEM, "v": pltpu.VMEM}
+    spaces = {"s": pltpu.SMEM, "v": pltpu.VMEM, "a": pl.ANY}
     return pl.pallas_call(
         body,
         out_shape=outs,
@@ -357,7 +367,7 @@
     pair = (2, count, width)
     (sent_grad,) = call(
         grad_kernel, (shape(wire, BF16),), "svvv", [pltpu.VMEM((2 * slots, width), F32)],
-        "place_grad", 4 * MICRO, 12,
+        "place_grad", 4 * MICRO, 56,
     )(seq, ids_t, grad, perm)
     k, v, sent_grad = barrier((k, v, sent_grad))
     kl, kr = lax.ppermute(k, "seq", up_by), lax.ppermute(k, "seq", down_by)
@@ -412,13 +422,15 @@
         return call(
             lambda *refs: expert_kernel(*refs, blocks=blocks),
             (shape(flat, BF16),) * blocks,
-            "v" * (blocks + 7),
+            "v" * (blocks + 5) + "aa",
             [
                 pltpu.VMEM((blocks * slots, width), BF16),
                 pltpu.VMEM((4, blocks * slots, part), BF16),
                 pltpu.VMEM((blocks * slots, width), F32),
+                pltpu.VMEM((2, width, part), BF16),
+                pltpu.SemaphoreType.DMA((2,)),
             ],
-            "expert", micros * MICRO, 24,
+            "expert", micros * MICRO, 20,
         )(*ins, hg, perm, perm_t, gate, up, gate_s, up_s)
 
     hidden_own = hidden((g0,), 4)

time: 225 us -> 224 us (level)
  waiting for transfers between devices: 59.8 us -> 63 us
  local copies, waits for them, and re-layouts: 14.4 us -> 11.8 us
  Pallas kernels: 50.4 us -> 48 us
    pallas_call x3, Pallas kernels: 24.2 us -> 20.7 us  [expert(): call(lambda *refs: expert_kernel(*refs, blocks=blocks), (shape(flat, BF16...]
    ppermute x12, waiting for transfers between devices: 30.6 us -> 33.9 us  [swap(): return lax.ppermute(x, 'seq', [(i, i ^ bits) for i in range(seq_count)])]
    unnamed x64 -> x58, local copies, waits for them, and re-layouts: 10.7 us -> 8.03 us
  transfers between devices with their start and end apart: 20 -> 20, of which waited for: 12 -> 13; matrix products, arithmetic and copies ran while one was open for 2% -> 2% of each run, Pallas kernels for 18% -> 17%
where the time goes in v7:
time: 224 us; the launch traced here: 223 us
  waiting for transfers between devices  63 us (28%)
  starting transfers between devices  49.7 us (22%)
  Pallas kernels  48 us (21%)
  blocking collectives  47 us (21%)
  local copies, waits for them, and re-layouts  11.8 us (5%)
  other arithmetic  2.32 us (1%)
    all_to_all x1, blocking collectives, exchange(): return lax.all_to_all(x, 'exp', split_axis=0, concat_axis=0, tiled=True)  47 us
    ppermute x12, waiting for transfers between devices, swap(): return lax.ppermute(x, 'seq', [(i, i ^ bits) for i in range(seq_count)])  33.9 us
    pallas_call x3, Pallas kernels, expert(): call(lambda *refs: expert_kernel(*refs, blocks=blocks), (shape(flat, BF16...  20.7 us
    all_to_all x2, starting transfers between devices, exchange(): return lax.all_to_all(x, 'exp', split_axis=0, concat_axis=0, tiled=True)  20.6 us
    ppermute x12, starting transfers between devices, swap(): return lax.ppermute(x, 'seq', [(i, i ^ bits) for i in range(seq_count)])  10.9 us
    pallas_call x3, Pallas kernels, hidden(): call(lambda *refs: hidden_kernel(*refs, blocks=blocks), (shape((blocks *...  10.8 us
    ppermute x1, waiting for transfers between devices, on_device(): from_right = lax.ppermute(to_left, 'seq', down_by).astype(F32)  10.1 us
    all_to_all x2, waiting for transfers between devices, exchange(): return lax.all_to_all(x, 'exp', split_axis=0, concat_axis=0, tiled=True)  8.67 us
  transfers between devices with their start and end apart: 20, of which 13 were waited for; matrix products, arithmetic and copies ran while one was open for 2% of the time, Pallas kernels for 17%

profile of v7, /device:TPU:1, one launch (start us, length us, event | category | flops | bytes accessed | tf_op | source)
XLA Modules:
  0.0 222.9 jit_solution(7540070735736862263)
XLA Ops:
  0.6 3.6 %place_grad.1 = bf16[32,2,40,256]{3,2,1,0:T(8,128)(2,1)} custom-call(s32[1]{0:T(128)} %bitcast.seq_ref.refs_0_, s32[2,128]{1,0:T(2,128)} %bitcast.89, bf16[128,2048]{1,0:T(8,128)(2,1)} %bitcast.83, bf16[320,320]{1,0:T(8,128)(2,1)} %constant.8.clone.perm_ref.refs_11_.refs_1_.refs_2_.refs_3_.refs_4_.refs_9_), custom_call_target="tpu_custom_call" | custom-call | flops 4294967296 | bytes 1048576 | tf_op jit(solution)/shard_map/place_grad/pallas_call | solution.py:368
  4.3 12.3 %all-to-all-start = ((bf16[32,2,40,256]{3,2,1,0:T(8,128)(2,1)}), bf16[32,2,40,256]{3,2,1,0:T(8,128)(2,1)}, u32[]{:S(2)}, u32[]{:S(2)}) async-start(bf16[32,2,40,256]{3,2,1,0:T(8,128)(2,1)} %place_grad.1), calls=%async_computation | async-start | bytes 2621440 | tf_op jit(solution)/shard_map/all_to_all | solution.py:364
  16.6 4.0 %collective-permute-start.2 = (bf16[128,2048]{1,0:T(8,128)(2,1)S(1)}, bf16[128,2048]{1,0:T(8,128)(2,1)S(1)}, u32[]{:S(2)}, u32[]{:S(2)}) collective-permute-start(bf16[128,2048]{1,0:T(8,128)(2,1)S(1)} %bitcast.79), channel_id=1, source_target_pairs={{0,32},{32,64},{64,96},{96,128},{128,160},{160,192},{192,224},{1,3... | collective-permute-start | bytes 1572872 | tf_op jit(solution)/shard_map/ppermute | solution.py:374
  20.5 1.9 collective-permute-start.3
  22.5 3.6 %collective-permute-start = (bf16[128,2048]{1,0:T(8,128)(2,1)S(1)}, bf16[128,2048]{1,0:T(8,128)(2,1)S(1)}, u32[]{:S(2)}, u32[]{:S(2)}) collective-permute-start(bf16[128,2048]{1,0:T(8,128)(2,1)S(1)} %bitcast.74), channel_id=1, source_target_pairs={{0,32},{32,64},{64,96},{96,128},{128,160},{160,192},{192,224},{1,3... | collective-permute-start | bytes 1572872 | tf_op jit(solution)/shard_map/ppermute | solution.py:373
  26.1 1.9 collective-permute-start.1
  28.1 3.4 %collective-permute-done.3.refs_9_.refs_13_ = bf16[128,2048]{1,0:T(8,128)(2,1)S(1)} collective-permute-done((bf16[128,2048]{1,0:T(8,128)(2,1)S(1)}, bf16[128,2048]{1,0:T(8,128)(2,1)S(1)}, u32[]{:S(2)}, u32[]{:S(2)}) %collective-permute-start.3) | collective-permute-done | bytes 524320 | tf_op jit(solution)/shard_map/ppermute | solution.py:374
  32.3 4.8 %collective-permute-done.1.refs_6_ = bf16[128,2048]{1,0:T(8,128)(2,1)S(1)} collective-permute-done((bf16[128,2048]{1,0:T(8,128)(2,1)S(1)}, bf16[128,2048]{1,0:T(8,128)(2,1)S(1)}, u32[]{:S(2)}, u32[]{:S(2)}) %collective-permute-start.1) | collective-permute-done | bytes 524320 | tf_op jit(solution)/shard_map/ppermute | solution.py:373
  38.1 6.0 %attention.1 = (f32[32,64,192]{2,1,0:T(8,128)S(1)}, f32[128,2048]{1,0:T(8,128)S(1)}, f32[128,128]{1,0:T(8,128)S(1)}, bf16[32,2,40,256]{3,2,1,0:T(8,128)(2,1)}) custom-call(s32[1]{0:T(128)} %bitcast.seq_ref.refs_0_, s32[2,3]{1,0:T(2,128)S(1)} %bitcast.87, s32[2,128]{1,0:T(2,128)S(1)} %bitcast.90, bf16[128,2048]{1,0:T(8,128)(2,1)S(1)} %bitcast.77, ...), custom_call_target="tpu_custom_call" | custom-call | flops 8589934592 | bytes 1048576 | tf_op jit(solution)/shard_map/attention/pallas_call | solution.py:378
  46.5 1.9 all-to-all-done
  48.3 8.3 %all-to-all-start.1 = ((bf16[32,2,40,256]{3,2,1,0:T(8,128)(2,1)}), bf16[32,2,40,256]{3,2,1,0:T(8,128)(2,1)}, u32[]{:S(2)}, u32[]{:S(2)}) async-start(bf16[32,2,40,256]{3,2,1,0:T(8,128)(2,1)} %get-tuple-element.31), calls=%async_computation.1 | async-start | bytes 2621440 | tf_op jit(solution)/shard_map/all_to_all | solution.py:364
  57.3 2.2 fusion.8
  59.5 2.3 %collective-permute-start.10 = (bf16[1280,256]{1,0:T(8,128)(2,1)}, bf16[1280,256]{1,0:T(8,128)(2,1)S(1)}, u32[]{:S(2)}, u32[]{:S(2)}) collective-permute-start(bf16[1280,256]{1,0:T(8,128)(2,1)} %bitcast.17), channel_id=1, source_target_pairs={{0,192},{32,224},{64,128},{96,160},{128,64},{160,96},{192,0},{224,... | collective-permute-start | bytes 1966088 | tf_op jit(solution)/shard_map/ppermute | solution.py:361
  61.8 1.6 collective-permute-start.7
  63.3 3.4 %hidden.3.refs_1_ = f32[160,1024]{1,0:T(8,128)S(1)} custom-call(bf16[1280,256]{1,0:T(8,128)(2,1)S(1)} %bitcast.61, bf16[320,320]{1,0:T(8,128)(2,1)S(1)} %copy-done.18, bf16[512,2048]{1,0:T(8,128)(2,1)S(1)} %bitcast.63, bf16[512,2048]{1,0:T(8,128)(2,1)} %collective-permute-done.4.refs_3_.refs_4_), custom_call_target="tpu_custom_call" | custom-call | flops 4294967296 | bytes 1048576 | tf_op jit(solution)/shard_map/hidden/pallas_call | solution.py:411
  67.6 9.5 %collective-permute-done.10.refs_0_ = bf16[1280,256]{1,0:T(8,128)(2,1)S(1)} collective-permute-done((bf16[1280,256]{1,0:T(8,128)(2,1)}, bf16[1280,256]{1,0:T(8,128)(2,1)S(1)}, u32[]{:S(2)}, u32[]{:S(2)}) %collective-permute-start.10) | collective-permute-done | bytes 655392 | tf_op jit(solution)/shard_map/ppermute | solution.py:361
  77.5 3.8 %hidden.5.refs_2_ = f32[320,1024]{1,0:T(8,128)S(1)} custom-call(bf16[1280,256]{1,0:T(8,128)(2,1)S(1)} %collective-permute-done.10.refs_0_, bf16[1280,256]{1,0:T(8,128)(2,1)S(1)} %collective-permute-done.11.refs_1_, bf16[320,320]{1,0:T(8,128)(2,1)S(1)} %copy-done.18, bf16[512,2048]{1,0:T(8,128)(2,1)S(1)} %bitcast.64, ...), custom_call_target="tpu_custom_call" | custom-call | flops 5368709120 | bytes 1048576 | tf_op jit(solution)/shard_map/hidden/pallas_call | solution.py:411
  82.3 6.8 %all-to-all-done.1 = bf16[32,2,40,256]{3,2,1,0:T(8,128)(2,1)} async-done(((bf16[32,2,40,256]{3,2,1,0:T(8,128)(2,1)}), bf16[32,2,40,256]{3,2,1,0:T(8,128)(2,1)}, u32[]{:S(2)}, u32[]{:S(2)}) %all-to-all-start.1) | async-done | bytes 1310752 | tf_op jit(solution)/shard_map/all_to_all | solution.py:364
  90.8 2.0 collective-permute-start.9
  92.8 1.6 copy-done.2
  95.5 6.3 %expert.3 = bf16[1280,256]{1,0:T(8,128)(2,1)S(1)} custom-call(bf16[1280,256]{1,0:T(8,128)(2,1)S(1)} %bitcast.59, f32[160,1024]{1,0:T(8,128)S(1)} %copy-done.22, bf16[320,320]{1,0:T(8,128)(2,1)S(1)} %copy-done.18, bf16[320,320]{1,0:T(8,128)(2,1)S(1)} %copy-done.18, bf16[2048,512]{1,0:T(8,128)(2,1)S(1)} %bitcast.67, bf16[2048,512]{1,0:T(8,128)(2,1)S(1)} %bitcast.71, ...), custom_call_target="tpu_custom_call" | custom-call | flops 9663676416 | bytes 1048576 | tf_op jit(solution)/shard_map/expert/pallas_call | solution.py:422
  101.9 3.6 %hidden.4.refs_1_ = f32[160,1024]{1,0:T(8,128)S(1)} custom-call(bf16[1280,256]{1,0:T(8,128)(2,1)S(1)} %collective-permute-done.7.refs_0_, bf16[320,320]{1,0:T(8,128)(2,1)S(1)} %copy-done.18, bf16[512,2048]{1,0:T(8,128)(2,1)S(1)} %bitcast.65, bf16[512,2048]{1,0:T(8,128)(2,1)} %collective-permute-done.4.refs_3_.refs_4_), custom_call_target="tpu_custom_call" | custom-call | flops 4294967296 | bytes 1048576 | tf_op jit(solution)/shard_map/hidden/pallas_call | solution.py:411
  106.6 8.0 %expert.4 = (bf16[1280,256]{1,0:T(8,128)(2,1)S(1)}, bf16[1280,256]{1,0:T(8,128)(2,1)S(1)}) custom-call(bf16[1280,256]{1,0:T(8,128)(2,1)S(1)} %collective-permute-done.8.refs_0_, bf16[1280,256]{1,0:T(8,128)(2,1)S(1)} %collective-permute-done.9.refs_1_, f32[320,1024]{1,0:T(8,128)S(1)} %copy-done.20, bf16[320,320]{1,0:T(8,128)(2,1)S(1)} %copy-done.18, ...), custom_call_target="tpu_custom_call" | custom-call | flops 11811160064 | bytes 1048576 | tf_op jit(solution)/shard_map/expert/pallas_call | solution.py:422
  116.9 2.5 %collective-permute-done.14.refs_0_ = bf16[1280,256]{1,0:T(8,128)(2,1)S(1)} collective-permute-done((bf16[1280,256]{1,0:T(8,128)(2,1)S(1)}, bf16[1280,256]{1,0:T(8,128)(2,1)S(1)}, u32[]{:S(2)}, u32[]{:S(2)}) %collective-permute-start.14) | collective-permute-done | bytes 655392 | tf_op jit(solution)/shard_map/ppermute | solution.py:361
  119.4 6.3 %expert.5 = bf16[1280,256]{1,0:T(8,128)(2,1)S(1)} custom-call(bf16[1280,256]{1,0:T(8,128)(2,1)S(1)} %collective-permute-done.14.refs_0_, f32[160,1024]{1,0:T(8,128)S(1)} %hidden.4.refs_1_, bf16[320,320]{1,0:T(8,128)(2,1)S(1)} %copy-done.18, bf16[320,320]{1,0:T(8,128)(2,1)S(1)} %copy-done.18, bf16[2048,512]{1,0:T(8,128)(2,1)S(1)} %bitcast.69, ...), custom_call_target="tpu_custom_call" | custom-call | flops 9663676416 | bytes 1048576 | tf_op jit(solution)/shard_map/expert/pallas_call | solution.py:422
  127.3 6.2 %collective-permute-done.12 = bf16[1280,256]{1,0:T(8,128)(2,1)S(1)} collective-permute-done((bf16[1280,256]{1,0:T(8,128)(2,1)S(1)}, bf16[1280,256]{1,0:T(8,128)(2,1)S(1)}, u32[]{:S(2)}, u32[]{:S(2)}) %collective-permute-start.12) | collective-permute-done | bytes 655392 | tf_op jit(solution)/shard_map/ppermute | solution.py:361
  133.6 14.7 %collective-permute-done.15 = bf16[1280,256]{1,0:T(8,128)(2,1)S(1)} collective-permute-done((bf16[1280,256]{1,0:T(8,128)(2,1)S(1)}, bf16[1280,256]{1,0:T(8,128)(2,1)S(1)}, u32[]{:S(2)}, u32[]{:S(2)}) %collective-permute-start.15) | collective-permute-done | bytes 655392 | tf_op jit(solution)/shard_map/ppermute | solution.py:361
  148.7 47.0 %all_to_all.15.refs_4_ = bf16[32,2,40,256]{3,2,1,0:T(8,128)(2,1)S(1)} all-to-all(bf16[32,2,40,256]{3,2,1,0:T(8,128)(2,1)S(1)} %pad_maximum_fusion), channel_id=1, replica_groups=mesh['seq'=8,'exp'=32] {'exp'}, dimensions={0} | all-to-all | bytes 2621440 | tf_op jit(solution)/shard_map/all_to_all | solution.py:364
  195.8 6.9 %attention_grad.1 = (f32[128,2048]{1,0:T(8,128)S(1)}, f32[128,2048]{1,0:T(8,128)S(1)}, bf16[2,128,2048]{2,1,0:T(8,128)(2,1)S(1)}, bf16[2,128,2048]{2,1,0:T(8,128)(2,1)S(1)}) custom-call(s32[1]{0:T(128)} %bitcast.seq_ref.refs_0_, s32[2,3]{1,0:T(2,128)S(1)} %bitcast.88, s32[2,128]{1,0:T(2,128)S(1)} %bitcast.91, f32[2,128]{1,0:T(2,128)S(1)} %bitcast.92, ...), custom_call_target="tpu_custom_call" | custom-call | flops 10737418240 | bytes 1048576 | tf_op jit(solution)/shard_map/attention_grad/pallas_call | solution.py:450
  202.7 4.9 %collective-permute-start.16 = (bf16[2,128,2048]{2,1,0:T(8,128)(2,1)S(1)}, bf16[2,128,2048]{2,1,0:T(8,128)(2,1)S(1)}, u32[]{:S(2)}, u32[]{:S(2)}) collective-permute-start(bf16[2,128,2048]{2,1,0:T(8,128)(2,1)S(1)} %get-tuple-element.47), channel_id=1, source_target_pairs={{32,0},{64,32},{96,64},{128,96},{160,128},{192,160},{224,192},{33,... | collective-permute-start | bytes 3145736 | tf_op jit(solution)/shard_map/ppermute | solution.py:463
  207.6 1.9 collective-permute-start.17
  209.5 10.1 %collective-permute-done.16 = bf16[2,128,2048]{2,1,0:T(8,128)(2,1)S(1)} collective-permute-done((bf16[2,128,2048]{2,1,0:T(8,128)(2,1)S(1)}, bf16[2,128,2048]{2,1,0:T(8,128)(2,1)S(1)}, u32[]{:S(2)}, u32[]{:S(2)}) %collective-permute-start.16) | collective-permute-done | bytes 1048608 | tf_op jit(solution)/shard_map/ppermute | solution.py:463
  (84 shorter events, 18.5 us)
Async XLA Ops:
  4.2 32.8 %copy-start.5 = (bf16[1,128,2048]{2,1,0:T(8,128)(2,1)S(1)}, bf16[1,128,2048]{2,1,0:T(8,128)(2,1)}, u32[]{:S(2)}) copy-start(bf16[1,128,2048]{2,1,0:T(8,128)(2,1)} %param.13) | copy-start | bytes 1572868
  4.2 32.8 %copy-start.14 = (f32[2048]{0:T(1024)S(1)}, f32[2048]{0:T(1024)}, u32[]{:S(2)}) copy-start(f32[2048]{0:T(1024)} %param.17) | copy-start | bytes 24580
  4.2 32.8 %copy-start.15 = (s32[1,2,3]{2,1,0:T(2,128)S(1)}, s32[1,2,3]{2,1,0:T(2,128)}, u32[]{:S(2)}) copy-start(s32[1,2,3]{2,1,0:T(2,128)} %param.20) | copy-start | bytes 76
  4.2 32.8 %copy-start.16 = (s32[1,128,2]{1,2,0:T(2,128)S(1)}, s32[1,128,2]{1,2,0:T(2,128)}, u32[]{:S(2)}) copy-start(s32[1,128,2]{1,2,0:T(2,128)} %param.19) | copy-start | bytes 3076
  4.3 44.1 %all-to-all-start = ((bf16[32,2,40,256]{3,2,1,0:T(8,128)(2,1)}), bf16[32,2,40,256]{3,2,1,0:T(8,128)(2,1)}, u32[]{:S(2)}, u32[]{:S(2)}) async-start(bf16[32,2,40,256]{3,2,1,0:T(8,128)(2,1)} %place_grad.1), calls=%async_computation | async-start | bytes 2621440 | tf_op jit(solution)/shard_map/all_to_all | solution.py:364
  16.6 11.5 %collective-permute-start.2 = (bf16[128,2048]{1,0:T(8,128)(2,1)S(1)}, bf16[128,2048]{1,0:T(8,128)(2,1)S(1)}, u32[]{:S(2)}, u32[]{:S(2)}) collective-permute-start(bf16[128,2048]{1,0:T(8,128)(2,1)S(1)} %bitcast.79), channel_id=1, source_target_pairs={{0,32},{32,64},{64,96},{96,128},{128,160},{160,192},{192,224},{1,3... | collective-permute-start | bytes 1572872 | tf_op jit(solution)/shard_map/ppermute | solution.py:374
  20.5 10.9 %collective-permute-start.3 = (bf16[128,2048]{1,0:T(8,128)(2,1)S(1)}, bf16[128,2048]{1,0:T(8,128)(2,1)S(1)}, u32[]{:S(2)}, u32[]{:S(2)}) collective-permute-start(bf16[128,2048]{1,0:T(8,128)(2,1)S(1)} %bitcast.80), channel_id=1, source_target_pairs={{32,0},{64,32},{96,64},{128,96},{160,128},{192,160},{224,192},{33,... | collective-permute-start | bytes 1572872 | tf_op jit(solution)/shard_map/ppermute | solution.py:374
  22.5 9.8 %collective-permute-start = (bf16[128,2048]{1,0:T(8,128)(2,1)S(1)}, bf16[128,2048]{1,0:T(8,128)(2,1)S(1)}, u32[]{:S(2)}, u32[]{:S(2)}) collective-permute-start(bf16[128,2048]{1,0:T(8,128)(2,1)S(1)} %bitcast.74), channel_id=1, source_target_pairs={{0,32},{32,64},{64,96},{96,128},{128,160},{160,192},{192,224},{1,3... | collective-permute-start | bytes 1572872 | tf_op jit(solution)/shard_map/ppermute | solution.py:373
  26.1 10.9 %collective-permute-start.1 = (bf16[128,2048]{1,0:T(8,128)(2,1)S(1)}, bf16[128,2048]{1,0:T(8,128)(2,1)S(1)}, u32[]{:S(2)}, u32[]{:S(2)}) collective-permute-start(bf16[128,2048]{1,0:T(8,128)(2,1)S(1)} %bitcast.75), channel_id=1, source_target_pairs={{32,0},{64,32},{96,64},{128,96},{160,128},{192,160},{224,192},{33,... | collective-permute-start | bytes 1572872 | tf_op jit(solution)/shard_map/ppermute | solution.py:373
  46.5 15.3 %collective-permute-start.4 = (bf16[512,2048]{1,0:T(8,128)(2,1)S(1)}, bf16[512,2048]{1,0:T(8,128)(2,1)}, u32[]{:S(2)}, u32[]{:S(2)}) collective-permute-start(bf16[512,2048]{1,0:T(8,128)(2,1)S(1)} %bitcast.62), channel_id=1, source_target_pairs={{0,32},{32,0},{64,96},{96,64},{128,160},{160,128},{192,224},{224,1... | collective-permute-start | bytes 6291464 | tf_op jit(solution)/shard_map/ppermute | solution.py:361
  48.3 40.8 %all-to-all-start.1 = ((bf16[32,2,40,256]{3,2,1,0:T(8,128)(2,1)}), bf16[32,2,40,256]{3,2,1,0:T(8,128)(2,1)}, u32[]{:S(2)}, u32[]{:S(2)}) async-start(bf16[32,2,40,256]{3,2,1,0:T(8,128)(2,1)} %get-tuple-element.31), calls=%async_computation.1 | async-start | bytes 2621440 | tf_op jit(solution)/shard_map/all_to_all | solution.py:364
  56.7 36.1 %collective-permute-start.5 = (bf16[2048,512]{1,0:T(8,128)(2,1)}, bf16[2048,512]{1,0:T(8,128)(2,1)}, u32[]{:S(2)}, u32[]{:S(2)}) collective-permute-start(bf16[2048,512]{1,0:T(8,128)(2,1)} %bitcast.66), channel_id=1, source_target_pairs={{0,32},{32,0},{64,96},{96,64},{128,160},{160,128},{192,224},{224,1... | collective-permute-start | bytes 6291464 | tf_op jit(solution)/shard_map/ppermute | solution.py:361
  57.0 35.8 %collective-permute-start.6 = (bf16[2048,512]{1,0:T(8,128)(2,1)}, bf16[2048,512]{1,0:T(8,128)(2,1)}, u32[]{:S(2)}, u32[]{:S(2)}) collective-permute-start(bf16[2048,512]{1,0:T(8,128)(2,1)} %bitcast.70), channel_id=1, source_target_pairs={{0,32},{32,0},{64,96},{96,64},{128,160},{160,128},{192,224},{224,1... | collective-permute-start | bytes 6291464 | tf_op jit(solution)/shard_map/ppermute | solution.py:361
  59.5 17.6 %collective-permute-start.10 = (bf16[1280,256]{1,0:T(8,128)(2,1)}, bf16[1280,256]{1,0:T(8,128)(2,1)S(1)}, u32[]{:S(2)}, u32[]{:S(2)}) collective-permute-start(bf16[1280,256]{1,0:T(8,128)(2,1)} %bitcast.17), channel_id=1, source_target_pairs={{0,192},{32,224},{64,128},{96,160},{128,64},{160,96},{192,0},{224,... | collective-permute-start | bytes 1966088 | tf_op jit(solution)/shard_map/ppermute | solution.py:361
  61.8 15.7 %collective-permute-start.11 = (bf16[1280,256]{1,0:T(8,128)(2,1)S(1)}, bf16[1280,256]{1,0:T(8,128)(2,1)S(1)}, u32[]{:S(2)}, u32[]{:S(2)}) collective-permute-start(bf16[1280,256]{1,0:T(8,128)(2,1)S(1)} %bitcast.60), channel_id=1, source_target_pairs={{0,64},{32,96},{64,0},{96,32},{128,192},{160,224},{192,128},{224,1... | collective-permute-start | bytes 1966088 | tf_op jit(solution)/shard_map/ppermute | solution.py:361
  61.8 40.1 %collective-permute-start.7 = (bf16[1280,256]{1,0:T(8,128)(2,1)}, bf16[1280,256]{1,0:T(8,128)(2,1)S(1)}, u32[]{:S(2)}, u32[]{:S(2)}) collective-permute-start(bf16[1280,256]{1,0:T(8,128)(2,1)} %bitcast.17), channel_id=1, source_target_pairs={{0,128},{32,160},{64,192},{96,224},{128,0},{160,32},{192,64},{224,... | collective-permute-start | bytes 1966088 | tf_op jit(solution)/shard_map/ppermute | solution.py:361
  90.7 15.5 %collective-permute-start.8 = (bf16[1280,256]{1,0:T(8,128)(2,1)S(1)}, bf16[1280,256]{1,0:T(8,128)(2,1)S(1)}, u32[]{:S(2)}, u32[]{:S(2)}) collective-permute-start(bf16[1280,256]{1,0:T(8,128)(2,1)S(1)} %bitcast.95), channel_id=1, source_target_pairs={{0,192},{32,224},{64,128},{96,160},{128,64},{160,96},{192,0},{224,... | collective-permute-start | bytes 1966088 | tf_op jit(solution)/shard_map/ppermute | solution.py:361
  90.8 15.4 %collective-permute-start.9 = (bf16[1280,256]{1,0:T(8,128)(2,1)S(1)}, bf16[1280,256]{1,0:T(8,128)(2,1)S(1)}, u32[]{:S(2)}, u32[]{:S(2)}) collective-permute-start(bf16[1280,256]{1,0:T(8,128)(2,1)S(1)} %bitcast.58), channel_id=1, source_target_pairs={{0,64},{32,96},{64,0},{96,32},{128,192},{160,224},{192,128},{224,1... | collective-permute-start | bytes 1966088 | tf_op jit(solution)/shard_map/ppermute | solution.py:361
  106.1 13.2 %collective-permute-start.14 = (bf16[1280,256]{1,0:T(8,128)(2,1)S(1)}, bf16[1280,256]{1,0:T(8,128)(2,1)S(1)}, u32[]{:S(2)}, u32[]{:S(2)}) collective-permute-start(bf16[1280,256]{1,0:T(8,128)(2,1)S(1)} %collective-permute-done.8.refs_0_), channel_id=1, source_target_pairs={{0,64},{32,96},{64,0},{96,32},{128,192},{160,224},{192,128},{224,1... | collective-permute-start | bytes 1966088 | tf_op jit(solution)/shard_map/ppermute | solution.py:361
  114.7 18.7 %collective-permute-start.12 = (bf16[1280,256]{1,0:T(8,128)(2,1)S(1)}, bf16[1280,256]{1,0:T(8,128)(2,1)S(1)}, u32[]{:S(2)}, u32[]{:S(2)}) collective-permute-start(bf16[1280,256]{1,0:T(8,128)(2,1)S(1)} %get-tuple-element.40), channel_id=1, source_target_pairs={{0,64},{32,96},{64,0},{96,32},{128,192},{160,224},{192,128},{224,1... | collective-permute-start | bytes 1966088 | tf_op jit(solution)/shard_map/ppermute | solution.py:361
  115.7 17.9 %collective-permute-start.13 = (bf16[1280,256]{1,0:T(8,128)(2,1)S(1)}, bf16[1280,256]{1,0:T(8,128)(2,1)S(1)}, u32[]{:S(2)}, u32[]{:S(2)}) collective-permute-start(bf16[1280,256]{1,0:T(8,128)(2,1)S(1)} %get-tuple-element.41), channel_id=1, source_target_pairs={{0,192},{32,224},{64,128},{96,160},{128,64},{160,96},{192,0},{224,... | collective-permute-start | bytes 1966088 | tf_op jit(solution)/shard_map/ppermute | solution.py:361
  125.7 22.6 %collective-permute-start.15 = (bf16[1280,256]{1,0:T(8,128)(2,1)S(1)}, bf16[1280,256]{1,0:T(8,128)(2,1)S(1)}, u32[]{:S(2)}, u32[]{:S(2)}) collective-permute-start(bf16[1280,256]{1,0:T(8,128)(2,1)S(1)} %expert.5), channel_id=1, source_target_pairs={{0,128},{32,160},{64,192},{96,224},{128,0},{160,32},{192,64},{224,... | collective-permute-start | bytes 1966088 | tf_op jit(solution)/shard_map/ppermute | solution.py:361
  148.3 47.4 %copy-start.28 = (f32[128,128]{1,0:T(8,128)S(1)}, f32[128,128]{1,0:T(8,128)}, u32[]{:S(2)}) copy-start(f32[128,128]{1,0:T(8,128)} %copy-done.27) | copy-start | bytes 196612
  148.5 47.3 %copy-start.24 = (f32[32,64,192]{2,1,0:T(8,128)S(1)}, f32[32,64,192]{2,1,0:T(8,128)}, u32[]{:S(2)}) copy-start(f32[32,64,192]{2,1,0:T(8,128)} %copy-done.23) | copy-start | bytes 4718596
  148.5 47.3 %copy-start.26 = (f32[128,2048]{1,0:T(8,128)S(1)}, f32[128,2048]{1,0:T(8,128)}, u32[]{:S(2)}) copy-start(f32[128,2048]{1,0:T(8,128)} %copy-done.25) | copy-start | bytes 3145732
  148.6 47.1 %copy-start.8 = (bf16[1,128,2048]{2,1,0:T(8,128)(2,1)S(1)}, bf16[1,128,2048]{2,1,0:T(8,128)(2,1)}, u32[]{:S(2)}) copy-start(bf16[1,128,2048]{2,1,0:T(8,128)(2,1)} %param.15) | copy-start | bytes 1572868
  148.6 47.1 %copy-start.9 = (bf16[1,128,2048]{2,1,0:T(8,128)(2,1)S(1)}, bf16[1,128,2048]{2,1,0:T(8,128)(2,1)}, u32[]{:S(2)}) copy-start(bf16[1,128,2048]{2,1,0:T(8,128)(2,1)} %param.16) | copy-start | bytes 1572868
  148.6 47.1 %copy-start.11 = (bf16[128,2048]{1,0:T(8,128)(2,1)S(1)}, bf16[128,2048]{1,0:T(8,128)(2,1)}, u32[]{:S(2)}) copy-start(bf16[128,2048]{1,0:T(8,128)(2,1)} %copy-done.10) | copy-start | bytes 1572868
  148.7 47.1 %copy-start.13 = (bf16[128,2048]{1,0:T(8,128)(2,1)S(1)}, bf16[128,2048]{1,0:T(8,128)(2,1)}, u32[]{:S(2)}) copy-start(bf16[128,2048]{1,0:T(8,128)(2,1)} %copy-done.12) | copy-start | bytes 1572868
  148.7 47.1 %copy-start.17 = (f32[1,128,2]{1,2,0:T(2,128)S(1)}, f32[1,128,2]{1,2,0:T(2,128)}, u32[]{:S(2)}) copy-start(f32[1,128,2]{1,2,0:T(2,128)} %param.18) | copy-start | bytes 3076
  202.7 16.9 %collective-permute-start.16 = (bf16[2,128,2048]{2,1,0:T(8,128)(2,1)S(1)}, bf16[2,128,2048]{2,1,0:T(8,128)(2,1)S(1)}, u32[]{:S(2)}, u32[]{:S(2)}) collective-permute-start(bf16[2,128,2048]{2,1,0:T(8,128)(2,1)S(1)} %get-tuple-element.47), channel_id=1, source_target_pairs={{32,0},{64,32},{96,64},{128,96},{160,128},{192,160},{224,192},{33,... | collective-permute-start | bytes 3145736 | tf_op jit(solution)/shard_map/ppermute | solution.py:463
  207.6 13.7 %collective-permute-start.17 = (bf16[2,128,2048]{2,1,0:T(8,128)(2,1)S(1)}, bf16[2,128,2048]{2,1,0:T(8,128)(2,1)S(1)}, u32[]{:S(2)}, u32[]{:S(2)}) collective-permute-start(bf16[2,128,2048]{2,1,0:T(8,128)(2,1)S(1)} %get-tuple-element.48), channel_id=1, source_target_pairs={{0,32},{32,64},{64,96},{96,128},{128,160},{160,192},{192,224},{1,3... | collective-permute-start | bytes 3145736 | tf_op jit(solution)/shard_map/ppermute | solution.py:464
  (17 other events, 123.7 us)

commit v8 on v7

--- a/solution.py
+++ b/solution.py
@@ -244,10 +244,15 @@
 
 def backward_kernel(
     seq_ref, offs_ref, ids_ref, gates_ref, home_ref, grad_ref, unit_ref, inv_ref, gain_ref,
-    perm_t_ref, q_ref, vl_ref, v_ref, vr_ref, wts_ref, k_out_ref, v_out_ref, to_left_ref,
-    to_right_ref, vx_ref, rows_ref, ag_ref, ka_ref, va_ref, total_tiles,
+    perm_t_ref, q_hbm, vl_ref, v_ref, vr_ref, wts_hbm, k_out_ref, v_out_ref, to_left_ref,
+    to_right_ref, vx_ref, rows_ref, ag_ref, ka_ref, va_ref, q_ref, wts_ref, sems, total_tiles,
 ):
-    fill_halo(vx_ref, vl_ref, v_ref, vr_ref)
+    span = v_ref.shape[0]
+    pairs = [(src, vx_ref.at[i * span : (i + 1) * span]) for i, src in enumerate((vl_ref, v_ref, vr_ref))]
+    pairs += [(q_hbm, q_ref), (wts_hbm, wts_ref)]
+    copies = [pltpu.make_async_copy(src, dst, sems.at[i]) for i, (src, dst) in enumerate(pairs)]
+    for copy in copies:
+        copy.start()
     count, width = q_ref.shape
     heads = width // HEAD_DIM
     tiles = count // TILE
@@ -275,6 +280,9 @@
     attn_grad = grad_ref[...].astype(F32) + inv_ref[:, 0:1] * (scaled - unit * inner)
     ag_ref[...] = attn_grad.astype(BF16)
     spots = [tile_places(seq_ref, offs_ref, t, tiles, total_tiles)[0] for t in range(tiles)]
+    for copy in copies:
+        copy.wait()
+
     def body(step, carry):
         spans = head_spans(step, heads, tiles)
         prob_grads = [
@@ -450,15 +458,18 @@
     k_own, v_own, to_left, to_right = call(
         lambda *refs: backward_kernel(*refs, total_tiles=total_tiles),
         (shape((count, width), F32), shape((count, width), F32), shape(pair, BF16), shape(pair, BF16)),
-        "ss" + "v" * 13,
+        "ss" + "v" * 8 + "aaaaa",
         [
             pltpu.VMEM((3 * count, width), BF16),
             pltpu.VMEM((2 * slots, width), BF16),
             pltpu.VMEM((count, width), BF16),
             pltpu.VMEM((3 * count, width), F32),
             pltpu.VMEM((3 * count, width), F32),
+            pltpu.VMEM((count, width), BF16),
+            pltpu.VMEM(wts.shape, F32),
+            pltpu.SemaphoreType.DMA((5,)),
         ],
-        "attention_grad", 10 * MICRO, 24,
+        "attention_grad", 10 * MICRO, 56,
     )(seq, offsets, ids_t, gates_t, home, grad, unit, inv, gain, perm_t, q, vl, v, vr, wts)
     from_right = lax.ppermute(to_left, "seq", down_by).astype(F32)
     from_left = lax.ppermute(to_right, "seq", up_by).astype(F32)

time: 224 us -> 227 us (1.013)
  Pallas kernels: 48 us -> 50.9 us
    pallas_call x1, Pallas kernels: 6.91 us -> 9.88 us  [on_device(): call(lambda *refs: backward_kernel(*refs, total_tiles=total_tiles), (shap...]
    unnamed x58 -> x46, local copies, waits for them, and re-layouts: 8.03 us -> 8.03 us
where the time goes in v8:
time: 227 us; the launch traced here: 226 us
  waiting for transfers between devices  63.1 us (28%)
  Pallas kernels  50.9 us (22%)
  starting transfers between devices  49.9 us (22%)
  blocking collectives  46.9 us (21%)
  local copies, waits for them, and re-layouts  11.8 us (5%)
  other arithmetic  2.31 us (1%)
    all_to_all x1, blocking collectives, exchange(): return lax.all_to_all(x, 'exp', split_axis=0, concat_axis=0, tiled=True)  46.9 us
    ppermute x12, waiting for transfers between devices, swap(): return lax.ppermute(x, 'seq', [(i, i ^ bits) for i in range(seq_count)])  33.7 us
    pallas_call x3, Pallas kernels, expert(): call(lambda *refs: expert_kernel(*refs, blocks=blocks), (shape(flat, BF16...  20.7 us
    all_to_all x2, starting transfers between devices, exchange(): return lax.all_to_all(x, 'exp', split_axis=0, concat_axis=0, tiled=True)  20.6 us
    ppermute x12, starting transfers between devices, swap(): return lax.ppermute(x, 'seq', [(i, i ^ bits) for i in range(seq_count)])  11 us
    pallas_call x3, Pallas kernels, hidden(): call(lambda *refs: hidden_kernel(*refs, blocks=blocks), (shape((blocks *...  10.8 us
    ppermute x1, waiting for transfers between devices, on_device(): from_right = lax.ppermute(to_left, 'seq', down_by).astype(F32)  10.3 us
    pallas_call x1, Pallas kernels, on_device(): call(lambda *refs: backward_kernel(*refs, total_tiles=total_tiles), (shap...  9.88 us
  transfers between devices with their start and end apart: 20, of which 13 were waited for; matrix products, arithmetic and copies ran while one was open for 2% of the time, Pallas kernels for 17%

profile of v8, /device:TPU:1, one launch (start us, length us, event | category | flops | bytes accessed | tf_op | source)
XLA Modules:
  0.0 225.9 jit_solution(16672575977865006267)
XLA Ops:
  0.6 3.6 %place_grad.1 = bf16[32,2,40,256]{3,2,1,0:T(8,128)(2,1)} custom-call(s32[1]{0:T(128)} %bitcast.seq_ref.refs_0_, s32[2,128]{1,0:T(2,128)} %bitcast.87, bf16[128,2048]{1,0:T(8,128)(2,1)} %bitcast.93, bf16[320,320]{1,0:T(8,128)(2,1)} %constant.8.clone.perm_ref.refs_11_.refs_1_.refs_2_.refs_3_.refs_4_.refs_9_), custom_call_target="tpu_custom_call" | custom-call | flops 4294967296 | bytes 1048576 | tf_op jit(solution)/shard_map/place_grad/pallas_call | solution.py:376
  4.3 12.3 %all-to-all-start = ((bf16[32,2,40,256]{3,2,1,0:T(8,128)(2,1)}), bf16[32,2,40,256]{3,2,1,0:T(8,128)(2,1)}, u32[]{:S(2)}, u32[]{:S(2)}) async-start(bf16[32,2,40,256]{3,2,1,0:T(8,128)(2,1)} %place_grad.1), calls=%async_computation | async-start | bytes 2621440 | tf_op jit(solution)/shard_map/all_to_all | solution.py:372
  16.6 4.0 %collective-permute-start.2 = (bf16[128,2048]{1,0:T(8,128)(2,1)S(1)}, bf16[128,2048]{1,0:T(8,128)(2,1)S(1)}, u32[]{:S(2)}, u32[]{:S(2)}) collective-permute-start(bf16[128,2048]{1,0:T(8,128)(2,1)S(1)} %bitcast.80), channel_id=1, source_target_pairs={{0,32},{32,64},{64,96},{96,128},{128,160},{160,192},{192,224},{1,3... | collective-permute-start | bytes 1572872 | tf_op jit(solution)/shard_map/ppermute | solution.py:382
  20.5 1.9 collective-permute-start.3
  22.5 3.6 %collective-permute-start = (bf16[128,2048]{1,0:T(8,128)(2,1)S(1)}, bf16[128,2048]{1,0:T(8,128)(2,1)S(1)}, u32[]{:S(2)}, u32[]{:S(2)}) collective-permute-start(bf16[128,2048]{1,0:T(8,128)(2,1)S(1)} %bitcast.74), channel_id=1, source_target_pairs={{0,32},{32,64},{64,96},{96,128},{128,160},{160,192},{192,224},{1,3... | collective-permute-start | bytes 1572872 | tf_op jit(solution)/shard_map/ppermute | solution.py:381
  26.1 1.9 collective-permute-start.1
  28.1 3.4 %collective-permute-done.3.refs_9_.refs_13_ = bf16[128,2048]{1,0:T(8,128)(2,1)S(1)} collective-permute-done((bf16[128,2048]{1,0:T(8,128)(2,1)S(1)}, bf16[128,2048]{1,0:T(8,128)(2,1)S(1)}, u32[]{:S(2)}, u32[]{:S(2)}) %collective-permute-start.3) | collective-permute-done | bytes 524320 | tf_op jit(solution)/shard_map/ppermute | solution.py:382
  32.3 4.8 %collective-permute-done.1.refs_6_ = bf16[128,2048]{1,0:T(8,128)(2,1)S(1)} collective-permute-done((bf16[128,2048]{1,0:T(8,128)(2,1)S(1)}, bf16[128,2048]{1,0:T(8,128)(2,1)S(1)}, u32[]{:S(2)}, u32[]{:S(2)}) %collective-permute-start.1) | collective-permute-done | bytes 524320 | tf_op jit(solution)/shard_map/ppermute | solution.py:381
  38.1 6.0 %attention.1 = (f32[32,64,192]{2,1,0:T(8,128)S(1)}, f32[128,2048]{1,0:T(8,128)S(1)}, f32[128,128]{1,0:T(8,128)S(1)}, bf16[32,2,40,256]{3,2,1,0:T(8,128)(2,1)}) custom-call(s32[1]{0:T(128)} %bitcast.seq_ref.refs_0_, s32[2,3]{1,0:T(2,128)S(1)} %bitcast.86, s32[2,128]{1,0:T(2,128)S(1)} %bitcast.89, bf16[128,2048]{1,0:T(8,128)(2,1)S(1)} %bitcast.78, ...), custom_call_target="tpu_custom_call" | custom-call | flops 8589934592 | bytes 1048576 | tf_op jit(solution)/shard_map/attention/pallas_call | solution.py:386
  46.5 1.8 all-to-all-done
  48.3 8.3 %all-to-all-start.1 = ((bf16[32,2,40,256]{3,2,1,0:T(8,128)(2,1)}), bf16[32,2,40,256]{3,2,1,0:T(8,128)(2,1)}, u32[]{:S(2)}, u32[]{:S(2)}) async-start(bf16[32,2,40,256]{3,2,1,0:T(8,128)(2,1)} %get-tuple-element.31), calls=%async_computation.1 | async-start | bytes 2621440 | tf_op jit(solution)/shard_map/all_to_all | solution.py:372
  57.3 2.2 fusion.8
  59.5 2.3 %collective-permute-start.10 = (bf16[1280,256]{1,0:T(8,128)(2,1)}, bf16[1280,256]{1,0:T(8,128)(2,1)S(1)}, u32[]{:S(2)}, u32[]{:S(2)}) collective-permute-start(bf16[1280,256]{1,0:T(8,128)(2,1)} %bitcast.17), channel_id=1, source_target_pairs={{0,192},{32,224},{64,128},{96,160},{128,64},{160,96},{192,0},{224,... | collective-permute-start | bytes 1966088 | tf_op jit(solution)/shard_map/ppermute | solution.py:369
  61.8 1.6 collective-permute-start.7
  63.4 3.4 %hidden.3.refs_1_ = f32[160,1024]{1,0:T(8,128)S(1)} custom-call(bf16[1280,256]{1,0:T(8,128)(2,1)S(1)} %bitcast.61, bf16[320,320]{1,0:T(8,128)(2,1)S(1)} %copy-done.13, bf16[512,2048]{1,0:T(8,128)(2,1)S(1)} %bitcast.63, bf16[512,2048]{1,0:T(8,128)(2,1)} %collective-permute-done.4.refs_3_.refs_4_), custom_call_target="tpu_custom_call" | custom-call | flops 4294967296 | bytes 1048576 | tf_op jit(solution)/shard_map/hidden/pallas_call | solution.py:419
  67.6 9.5 %collective-permute-done.10.refs_0_ = bf16[1280,256]{1,0:T(8,128)(2,1)S(1)} collective-permute-done((bf16[1280,256]{1,0:T(8,128)(2,1)}, bf16[1280,256]{1,0:T(8,128)(2,1)S(1)}, u32[]{:S(2)}, u32[]{:S(2)}) %collective-permute-start.10) | collective-permute-done | bytes 655392 | tf_op jit(solution)/shard_map/ppermute | solution.py:369
  77.4 3.8 %hidden.5.refs_2_ = f32[320,1024]{1,0:T(8,128)S(1)} custom-call(bf16[1280,256]{1,0:T(8,128)(2,1)S(1)} %collective-permute-done.10.refs_0_, bf16[1280,256]{1,0:T(8,128)(2,1)S(1)} %collective-permute-done.11.refs_1_, bf16[320,320]{1,0:T(8,128)(2,1)S(1)} %copy-done.13, bf16[512,2048]{1,0:T(8,128)(2,1)S(1)} %bitcast.64, ...), custom_call_target="tpu_custom_call" | custom-call | flops 5368709120 | bytes 1048576 | tf_op jit(solution)/shard_map/hidden/pallas_call | solution.py:419
  82.3 6.8 %all-to-all-done.1 = bf16[32,2,40,256]{3,2,1,0:T(8,128)(2,1)} async-done(((bf16[32,2,40,256]{3,2,1,0:T(8,128)(2,1)}), bf16[32,2,40,256]{3,2,1,0:T(8,128)(2,1)}, u32[]{:S(2)}, u32[]{:S(2)}) %all-to-all-start.1) | async-done | bytes 1310752 | tf_op jit(solution)/shard_map/all_to_all | solution.py:372
  90.7 2.1 collective-permute-start.9
  95.5 6.3 %expert.3 = bf16[1280,256]{1,0:T(8,128)(2,1)S(1)} custom-call(bf16[1280,256]{1,0:T(8,128)(2,1)S(1)} %bitcast.59, f32[160,1024]{1,0:T(8,128)S(1)} %copy-done.17, bf16[320,320]{1,0:T(8,128)(2,1)S(1)} %copy-done.13, bf16[320,320]{1,0:T(8,128)(2,1)S(1)} %copy-done.13, bf16[2048,512]{1,0:T(8,128)(2,1)S(1)} %bitcast.67, bf16[2048,512]{1,0:T(8,128)(2,1)S(1)} %bitcast.71, ...), custom_call_target="tpu_custom_call" | custom-call | flops 9663676416 | bytes 1048576 | tf_op jit(solution)/shard_map/expert/pallas_call | solution.py:430
  101.9 3.6 %hidden.4.refs_1_ = f32[160,1024]{1,0:T(8,128)S(1)} custom-call(bf16[1280,256]{1,0:T(8,128)(2,1)S(1)} %collective-permute-done.7.refs_0_, bf16[320,320]{1,0:T(8,128)(2,1)S(1)} %copy-done.13, bf16[512,2048]{1,0:T(8,128)(2,1)S(1)} %bitcast.65, bf16[512,2048]{1,0:T(8,128)(2,1)} %collective-permute-done.4.refs_3_.refs_4_), custom_call_target="tpu_custom_call" | custom-call | flops 4294967296 | bytes 1048576 | tf_op jit(solution)/shard_map/hidden/pallas_call | solution.py:419
  106.7 8.0 %expert.4 = (bf16[1280,256]{1,0:T(8,128)(2,1)S(1)}, bf16[1280,256]{1,0:T(8,128)(2,1)S(1)}) custom-call(bf16[1280,256]{1,0:T(8,128)(2,1)S(1)} %collective-permute-done.8.refs_0_, bf16[1280,256]{1,0:T(8,128)(2,1)S(1)} %collective-permute-done.9.refs_1_, f32[320,1024]{1,0:T(8,128)S(1)} %copy-done.15, bf16[320,320]{1,0:T(8,128)(2,1)S(1)} %copy-done.13, ...), custom_call_target="tpu_custom_call" | custom-call | flops 11811160064 | bytes 1048576 | tf_op jit(solution)/shard_map/expert/pallas_call | solution.py:430
  116.9 2.4 %collective-permute-done.14.refs_0_ = bf16[1280,256]{1,0:T(8,128)(2,1)S(1)} collective-permute-done((bf16[1280,256]{1,0:T(8,128)(2,1)S(1)}, bf16[1280,256]{1,0:T(8,128)(2,1)S(1)}, u32[]{:S(2)}, u32[]{:S(2)}) %collective-permute-start.14) | collective-permute-done | bytes 655392 | tf_op jit(solution)/shard_map/ppermute | solution.py:369
  119.3 6.3 %expert.5 = bf16[1280,256]{1,0:T(8,128)(2,1)S(1)} custom-call(bf16[1280,256]{1,0:T(8,128)(2,1)S(1)} %collective-permute-done.14.refs_0_, f32[160,1024]{1,0:T(8,128)S(1)} %hidden.4.refs_1_, bf16[320,320]{1,0:T(8,128)(2,1)S(1)} %copy-done.13, bf16[320,320]{1,0:T(8,128)(2,1)S(1)} %copy-done.13, bf16[2048,512]{1,0:T(8,128)(2,1)S(1)} %bitcast.69, ...), custom_call_target="tpu_custom_call" | custom-call | flops 9663676416 | bytes 1048576 | tf_op jit(solution)/shard_map/expert/pallas_call | solution.py:430
  125.6 1.6 collective-permute-start.15
  127.2 6.1 %collective-permute-done.12 = bf16[1280,256]{1,0:T(8,128)(2,1)S(1)} collective-permute-done((bf16[1280,256]{1,0:T(8,128)(2,1)S(1)}, bf16[1280,256]{1,0:T(8,128)(2,1)S(1)}, u32[]{:S(2)}, u32[]{:S(2)}) %collective-permute-start.12) | collective-permute-done | bytes 655392 | tf_op jit(solution)/shard_map/ppermute | solution.py:369
  133.5 14.7 %collective-permute-done.15 = bf16[1280,256]{1,0:T(8,128)(2,1)S(1)} collective-permute-done((bf16[1280,256]{1,0:T(8,128)(2,1)S(1)}, bf16[1280,256]{1,0:T(8,128)(2,1)S(1)}, u32[]{:S(2)}, u32[]{:S(2)}) %collective-permute-start.15) | collective-permute-done | bytes 655392 | tf_op jit(solution)/shard_map/ppermute | solution.py:369
  148.5 46.9 %all_to_all.15.refs_4_ = bf16[32,2,40,256]{3,2,1,0:T(8,128)(2,1)} all-to-all(bf16[32,2,40,256]{3,2,1,0:T(8,128)(2,1)S(1)} %pad_maximum_fusion), channel_id=1, replica_groups=mesh['seq'=8,'exp'=32] {'exp'}, dimensions={0} | all-to-all | bytes 2621440 | tf_op jit(solution)/shard_map/all_to_all | solution.py:372
  195.5 9.9 %attention_grad.1 = (f32[128,2048]{1,0:T(8,128)}, f32[128,2048]{1,0:T(8,128)}, bf16[2,128,2048]{2,1,0:T(8,128)(2,1)}, bf16[2,128,2048]{2,1,0:T(8,128)(2,1)}) custom-call(s32[1]{0:T(128)} %bitcast.seq_ref.refs_0_, s32[2,3]{1,0:T(2,128)} %bitcast.85, s32[2,128]{1,0:T(2,128)} %bitcast.88, f32[2,128]{1,0:T(2,128)} %bitcast.95, ...), custom_call_target="tpu_custom_call" | custom-call | flops 10737418240 | bytes 1048576 | tf_op jit(solution)/shard_map/attention_grad/pallas_call | solution.py:458
  205.4 4.9 %collective-permute-start.16 = (bf16[2,128,2048]{2,1,0:T(8,128)(2,1)}, bf16[2,128,2048]{2,1,0:T(8,128)(2,1)S(1)}, u32[]{:S(2)}, u32[]{:S(2)}) collective-permute-start(bf16[2,128,2048]{2,1,0:T(8,128)(2,1)} %get-tuple-element.47), channel_id=1, source_target_pairs={{32,0},{64,32},{96,64},{128,96},{160,128},{192,160},{224,192},{33,... | collective-permute-start | bytes 3145736 | tf_op jit(solution)/shard_map/ppermute | solution.py:474
  210.2 1.9 collective-permute-start.17
  212.2 10.3 %collective-permute-done.16 = bf16[2,128,2048]{2,1,0:T(8,128)(2,1)S(1)} collective-permute-done((bf16[2,128,2048]{2,1,0:T(8,128)(2,1)}, bf16[2,128,2048]{2,1,0:T(8,128)(2,1)S(1)}, u32[]{:S(2)}, u32[]{:S(2)}) %collective-permute-start.16) | collective-permute-done | bytes 1048608 | tf_op jit(solution)/shard_map/ppermute | solution.py:474
  (72 shorter events, 18.5 us)
Async XLA Ops:
  4.2 12.3 %copy-start.6 = (bf16[1,128,2048]{2,1,0:T(8,128)(2,1)S(1)}, bf16[1,128,2048]{2,1,0:T(8,128)(2,1)}, u32[]{:S(2)}) copy-start(bf16[1,128,2048]{2,1,0:T(8,128)(2,1)} %param.15) | copy-start | bytes 1572868
  4.2 18.3 %copy-start.4 = (bf16[1,128,2048]{2,1,0:T(8,128)(2,1)S(1)}, bf16[1,128,2048]{2,1,0:T(8,128)(2,1)}, u32[]{:S(2)}) copy-start(bf16[1,128,2048]{2,1,0:T(8,128)(2,1)} %param.14) | copy-start | bytes 1572868
  4.2 32.8 %copy-start.5 = (bf16[1,128,2048]{2,1,0:T(8,128)(2,1)S(1)}, bf16[1,128,2048]{2,1,0:T(8,128)(2,1)}, u32[]{:S(2)}) copy-start(bf16[1,128,2048]{2,1,0:T(8,128)(2,1)} %param.13) | copy-start | bytes 1572868
  4.2 32.8 %copy-start.10 = (f32[2048]{0:T(1024)S(1)}, f32[2048]{0:T(1024)}, u32[]{:S(2)}) copy-start(f32[2048]{0:T(1024)} %param.17) | copy-start | bytes 24580
  4.2 32.8 %copy-start.11 = (s32[1,2,3]{2,1,0:T(2,128)S(1)}, s32[1,2,3]{2,1,0:T(2,128)}, u32[]{:S(2)}) copy-start(s32[1,2,3]{2,1,0:T(2,128)} %param.20) | copy-start | bytes 76
  4.2 32.8 %copy-start.12 = (s32[1,128,2]{1,2,0:T(2,128)S(1)}, s32[1,128,2]{1,2,0:T(2,128)}, u32[]{:S(2)}) copy-start(s32[1,128,2]{1,2,0:T(2,128)} %param.19) | copy-start | bytes 3076
  4.2 32.8 %copy-start.13 = (bf16[320,320]{1,0:T(8,128)(2,1)S(1)}, bf16[320,320]{1,0:T(8,128)(2,1)}, u32[]{:S(2)}) copy-start(bf16[320,320]{1,0:T(8,128)(2,1)} %constant.8.clone.perm_ref.refs_11_.refs_1_.refs_2_.refs_3_.refs_4_.refs_9_) | copy-start | bytes 614404
  4.3 44.1 %all-to-all-start = ((bf16[32,2,40,256]{3,2,1,0:T(8,128)(2,1)}), bf16[32,2,40,256]{3,2,1,0:T(8,128)(2,1)}, u32[]{:S(2)}, u32[]{:S(2)}) async-start(bf16[32,2,40,256]{3,2,1,0:T(8,128)(2,1)} %place_grad.1), calls=%async_computation | async-start | bytes 2621440 | tf_op jit(solution)/shard_map/all_to_all | solution.py:372
  16.6 11.5 %collective-permute-start.2 = (bf16[128,2048]{1,0:T(8,128)(2,1)S(1)}, bf16[128,2048]{1,0:T(8,128)(2,1)S(1)}, u32[]{:S(2)}, u32[]{:S(2)}) collective-permute-start(bf16[128,2048]{1,0:T(8,128)(2,1)S(1)} %bitcast.80), channel_id=1, source_target_pairs={{0,32},{32,64},{64,96},{96,128},{128,160},{160,192},{192,224},{1,3... | collective-permute-start | bytes 1572872 | tf_op jit(solution)/shard_map/ppermute | solution.py:382
  20.5 10.9 %collective-permute-start.3 = (bf16[128,2048]{1,0:T(8,128)(2,1)S(1)}, bf16[128,2048]{1,0:T(8,128)(2,1)S(1)}, u32[]{:S(2)}, u32[]{:S(2)}) collective-permute-start(bf16[128,2048]{1,0:T(8,128)(2,1)S(1)} %bitcast.81), channel_id=1, source_target_pairs={{32,0},{64,32},{96,64},{128,96},{160,128},{192,160},{224,192},{33,... | collective-permute-start | bytes 1572872 | tf_op jit(solution)/shard_map/ppermute | solution.py:382
  22.5 9.8 %collective-permute-start = (bf16[128,2048]{1,0:T(8,128)(2,1)S(1)}, bf16[128,2048]{1,0:T(8,128)(2,1)S(1)}, u32[]{:S(2)}, u32[]{:S(2)}) collective-permute-start(bf16[128,2048]{1,0:T(8,128)(2,1)S(1)} %bitcast.74), channel_id=1, source_target_pairs={{0,32},{32,64},{64,96},{96,128},{128,160},{160,192},{192,224},{1,3... | collective-permute-start | bytes 1572872 | tf_op jit(solution)/shard_map/ppermute | solution.py:381
  26.1 10.9 %collective-permute-start.1 = (bf16[128,2048]{1,0:T(8,128)(2,1)S(1)}, bf16[128,2048]{1,0:T(8,128)(2,1)S(1)}, u32[]{:S(2)}, u32[]{:S(2)}) collective-permute-start(bf16[128,2048]{1,0:T(8,128)(2,1)S(1)} %bitcast.75), channel_id=1, source_target_pairs={{32,0},{64,32},{96,64},{128,96},{160,128},{192,160},{224,192},{33,... | collective-permute-start | bytes 1572872 | tf_op jit(solution)/shard_map/ppermute | solution.py:381
  28.1 16.1 %copy-start.8 = (bf16[128,2048]{1,0:T(8,128)(2,1)}, bf16[128,2048]{1,0:T(8,128)(2,1)S(1)}, u32[]{:S(2)}) copy-start(bf16[128,2048]{1,0:T(8,128)(2,1)S(1)} %collective-permute-done.2.refs_7_.refs_11_) | copy-start | bytes 1572868
  31.4 12.7 %copy-start.9 = (bf16[128,2048]{1,0:T(8,128)(2,1)}, bf16[128,2048]{1,0:T(8,128)(2,1)S(1)}, u32[]{:S(2)}) copy-start(bf16[128,2048]{1,0:T(8,128)(2,1)S(1)} %collective-permute-done.3.refs_9_.refs_13_) | copy-start | bytes 1572868
  38.1 8.4 %copy-start = (bf16[1,1,512,2048]{3,2,1,0:T(8,128)(2,1)S(1)}, bf16[1,1,512,2048]{3,2,1,0:T(8,128)(2,1)}, u32[]{:S(2)}) copy-start(bf16[1,1,512,2048]{3,2,1,0:T(8,128)(2,1)} %param.23) | copy-start | bytes 6291460
  46.5 15.3 %collective-permute-start.4 = (bf16[512,2048]{1,0:T(8,128)(2,1)S(1)}, bf16[512,2048]{1,0:T(8,128)(2,1)}, u32[]{:S(2)}, u32[]{:S(2)}) collective-permute-start(bf16[512,2048]{1,0:T(8,128)(2,1)S(1)} %bitcast.62), channel_id=1, source_target_pairs={{0,32},{32,0},{64,96},{96,64},{128,160},{160,128},{192,224},{224,1... | collective-permute-start | bytes 6291464 | tf_op jit(solution)/shard_map/ppermute | solution.py:369
  48.3 40.8 %all-to-all-start.1 = ((bf16[32,2,40,256]{3,2,1,0:T(8,128)(2,1)}), bf16[32,2,40,256]{3,2,1,0:T(8,128)(2,1)}, u32[]{:S(2)}, u32[]{:S(2)}) async-start(bf16[32,2,40,256]{3,2,1,0:T(8,128)(2,1)} %get-tuple-element.31), calls=%async_computation.1 | async-start | bytes 2621440 | tf_op jit(solution)/shard_map/all_to_all | solution.py:372
  56.7 36.1 %collective-permute-start.5 = (bf16[2048,512]{1,0:T(8,128)(2,1)}, bf16[2048,512]{1,0:T(8,128)(2,1)}, u32[]{:S(2)}, u32[]{:S(2)}) collective-permute-start(bf16[2048,512]{1,0:T(8,128)(2,1)} %bitcast.66), channel_id=1, source_target_pairs={{0,32},{32,0},{64,96},{96,64},{128,160},{160,128},{192,224},{224,1... | collective-permute-start | bytes 6291464 | tf_op jit(solution)/shard_map/ppermute | solution.py:369
  57.0 35.9 %collective-permute-start.6 = (bf16[2048,512]{1,0:T(8,128)(2,1)}, bf16[2048,512]{1,0:T(8,128)(2,1)}, u32[]{:S(2)}, u32[]{:S(2)}) collective-permute-start(bf16[2048,512]{1,0:T(8,128)(2,1)} %bitcast.70), channel_id=1, source_target_pairs={{0,32},{32,0},{64,96},{96,64},{128,160},{160,128},{192,224},{224,1... | collective-permute-start | bytes 6291464 | tf_op jit(solution)/shard_map/ppermute | solution.py:369
  59.5 17.7 %collective-permute-start.10 = (bf16[1280,256]{1,0:T(8,128)(2,1)}, bf16[1280,256]{1,0:T(8,128)(2,1)S(1)}, u32[]{:S(2)}, u32[]{:S(2)}) collective-permute-start(bf16[1280,256]{1,0:T(8,128)(2,1)} %bitcast.17), channel_id=1, source_target_pairs={{0,192},{32,224},{64,128},{96,160},{128,64},{160,96},{192,0},{224,... | collective-permute-start | bytes 1966088 | tf_op jit(solution)/shard_map/ppermute | solution.py:369
  61.8 15.7 %collective-permute-start.11 = (bf16[1280,256]{1,0:T(8,128)(2,1)S(1)}, bf16[1280,256]{1,0:T(8,128)(2,1)S(1)}, u32[]{:S(2)}, u32[]{:S(2)}) collective-permute-start(bf16[1280,256]{1,0:T(8,128)(2,1)S(1)} %bitcast.60), channel_id=1, source_target_pairs={{0,64},{32,96},{64,0},{96,32},{128,192},{160,224},{192,128},{224,1... | collective-permute-start | bytes 1966088 | tf_op jit(solution)/shard_map/ppermute | solution.py:369
  61.8 40.1 %collective-permute-start.7 = (bf16[1280,256]{1,0:T(8,128)(2,1)}, bf16[1280,256]{1,0:T(8,128)(2,1)S(1)}, u32[]{:S(2)}, u32[]{:S(2)}) collective-permute-start(bf16[1280,256]{1,0:T(8,128)(2,1)} %bitcast.17), channel_id=1, source_target_pairs={{0,128},{32,160},{64,192},{96,224},{128,0},{160,32},{192,64},{224,... | collective-permute-start | bytes 1966088 | tf_op jit(solution)/shard_map/ppermute | solution.py:369
  90.6 15.4 %collective-permute-start.8 = (bf16[1280,256]{1,0:T(8,128)(2,1)S(1)}, bf16[1280,256]{1,0:T(8,128)(2,1)S(1)}, u32[]{:S(2)}, u32[]{:S(2)}) collective-permute-start(bf16[1280,256]{1,0:T(8,128)(2,1)S(1)} %bitcast.92), channel_id=1, source_target_pairs={{0,192},{32,224},{64,128},{96,160},{128,64},{160,96},{192,0},{224,... | collective-permute-start | bytes 1966088 | tf_op jit(solution)/shard_map/ppermute | solution.py:369
  90.7 15.3 %collective-permute-start.9 = (bf16[1280,256]{1,0:T(8,128)(2,1)S(1)}, bf16[1280,256]{1,0:T(8,128)(2,1)S(1)}, u32[]{:S(2)}, u32[]{:S(2)}) collective-permute-start(bf16[1280,256]{1,0:T(8,128)(2,1)S(1)} %bitcast.58), channel_id=1, source_target_pairs={{0,64},{32,96},{64,0},{96,32},{128,192},{160,224},{192,128},{224,1... | collective-permute-start | bytes 1966088 | tf_op jit(solution)/shard_map/ppermute | solution.py:369
  101.8 4.8 %copy-start.3 = (bf16[1,1,2048,512]{3,2,1,0:T(8,128)(2,1)S(1)}, bf16[1,1,2048,512]{3,2,1,0:T(8,128)(2,1)}, u32[]{:S(2)}) copy-start(bf16[1,1,2048,512]{3,2,1,0:T(8,128)(2,1)} %param.22) | copy-start | bytes 6291460
  101.9 4.8 %copy-start.15 = (f32[320,1024]{1,0:T(8,128)S(1)}, f32[320,1024]{1,0:T(8,128)}, u32[]{:S(2)}) copy-start(f32[320,1024]{1,0:T(8,128)} %copy-done.14) | copy-start | bytes 3932164
  106.1 13.2 %collective-permute-start.14 = (bf16[1280,256]{1,0:T(8,128)(2,1)S(1)}, bf16[1280,256]{1,0:T(8,128)(2,1)S(1)}, u32[]{:S(2)}, u32[]{:S(2)}) collective-permute-start(bf16[1280,256]{1,0:T(8,128)(2,1)S(1)} %collective-permute-done.8.refs_0_), channel_id=1, source_target_pairs={{0,64},{32,96},{64,0},{96,32},{128,192},{160,224},{192,128},{224,1... | collective-permute-start | bytes 1966088 | tf_op jit(solution)/shard_map/ppermute | solution.py:369
  114.7 18.6 %collective-permute-start.12 = (bf16[1280,256]{1,0:T(8,128)(2,1)S(1)}, bf16[1280,256]{1,0:T(8,128)(2,1)S(1)}, u32[]{:S(2)}, u32[]{:S(2)}) collective-permute-start(bf16[1280,256]{1,0:T(8,128)(2,1)S(1)} %get-tuple-element.40), channel_id=1, source_target_pairs={{0,64},{32,96},{64,0},{96,32},{128,192},{160,224},{192,128},{224,1... | collective-permute-start | bytes 1966088 | tf_op jit(solution)/shard_map/ppermute | solution.py:369
  115.7 17.8 %collective-permute-start.13 = (bf16[1280,256]{1,0:T(8,128)(2,1)S(1)}, bf16[1280,256]{1,0:T(8,128)(2,1)S(1)}, u32[]{:S(2)}, u32[]{:S(2)}) collective-permute-start(bf16[1280,256]{1,0:T(8,128)(2,1)S(1)} %get-tuple-element.41), channel_id=1, source_target_pairs={{0,192},{32,224},{64,128},{96,160},{128,64},{160,96},{192,0},{224,... | collective-permute-start | bytes 1966088 | tf_op jit(solution)/shard_map/ppermute | solution.py:369
  125.6 22.6 %collective-permute-start.15 = (bf16[1280,256]{1,0:T(8,128)(2,1)S(1)}, bf16[1280,256]{1,0:T(8,128)(2,1)S(1)}, u32[]{:S(2)}, u32[]{:S(2)}) collective-permute-start(bf16[1280,256]{1,0:T(8,128)(2,1)S(1)} %expert.5), channel_id=1, source_target_pairs={{0,128},{32,160},{64,192},{96,224},{128,0},{160,32},{192,64},{224,... | collective-permute-start | bytes 1966088 | tf_op jit(solution)/shard_map/ppermute | solution.py:369
  205.4 17.1 %collective-permute-start.16 = (bf16[2,128,2048]{2,1,0:T(8,128)(2,1)}, bf16[2,128,2048]{2,1,0:T(8,128)(2,1)S(1)}, u32[]{:S(2)}, u32[]{:S(2)}) collective-permute-start(bf16[2,128,2048]{2,1,0:T(8,128)(2,1)} %get-tuple-element.47), channel_id=1, source_target_pairs={{32,0},{64,32},{96,64},{128,96},{160,128},{192,160},{224,192},{33,... | collective-permute-start | bytes 3145736 | tf_op jit(solution)/shard_map/ppermute | solution.py:474
  210.2 14.0 %collective-permute-start.17 = (bf16[2,128,2048]{2,1,0:T(8,128)(2,1)}, bf16[2,128,2048]{2,1,0:T(8,128)(2,1)S(1)}, u32[]{:S(2)}, u32[]{:S(2)}) collective-permute-start(bf16[2,128,2048]{2,1,0:T(8,128)(2,1)} %get-tuple-element.48), channel_id=1, source_target_pairs={{0,32},{32,64},{64,96},{96,128},{128,160},{160,192},{192,224},{1,3... | collective-permute-start | bytes 3145736 | tf_op jit(solution)/shard_map/ppermute | solution.py:475
  (11 other events, 17.0 us)

commit v9 on v7

--- a/solution.py
+++ b/solution.py
@@ -242,17 +242,14 @@
             dst[chunk * CHUNK : (chunk + 1) * CHUNK, :] = block
 
 
-def backward_kernel(
+def value_kernel(
     seq_ref, offs_ref, ids_ref, gates_ref, home_ref, grad_ref, unit_ref, inv_ref, gain_ref,
-    perm_t_ref, q_ref, vl_ref, v_ref, vr_ref, wts_ref, k_out_ref, v_out_ref, to_left_ref,
-    to_right_ref, vx_ref, rows_ref, ag_ref, ka_ref, va_ref, total_tiles,
+    perm_t_ref, wts_ref, v_out_ref, to_left_ref, to_right_ref, ag_ref, rows_ref, va_ref,
+    total_tiles,
 ):
-    fill_halo(vx_ref, vl_ref, v_ref, vr_ref)
-    count, width = q_ref.shape
+    count, width = grad_ref.shape
     heads = width // HEAD_DIM
     tiles = count // TILE
-    scale = HEAD_DIM ** (-0.5)
-    ka_ref[...] = jnp.zeros_like(ka_ref)
     va_ref[...] = jnp.zeros_like(va_ref)
     columns, _, _, piece = home_ref.shape
     chunks = columns // GROUP
@@ -277,39 +274,62 @@
     spots = [tile_places(seq_ref, offs_ref, t, tiles, total_tiles)[0] for t in range(tiles)]
     def body(step, carry):
         spans = head_spans(step, heads, tiles)
-        prob_grads = [
-            dot_nt(ag_ref[rows, lanes], window(vx_ref, spots[t], lanes))
-            for t, h, rows, lanes in spans
-        ]
         values = [
             dot_tn(wts_ref[t * heads + h].astype(BF16), ag_ref[rows, lanes])
             for t, h, rows, lanes in spans
         ]
-        sums = [
-            jnp.sum(wts_ref[t * heads + h] * x, axis=-1, keepdims=True)
-            for x, (t, h, rows, lanes) in zip(prob_grads, spans)
-        ]
-        score_grads = [
-            (wts_ref[t * heads + h] * (x - total)).astype(BF16)
-            for x, total, (t, h, rows, lanes) in zip(prob_grads, sums, spans)
-        ]
-        keys = [
-            dot_tn(x, q_ref[rows, lanes]) * scale
-            for x, (t, h, rows, lanes) in zip(score_grads, spans)
-        ]
-        for acc_ref, parts in ((va_ref, values), (ka_ref, keys)):
+        for acc_ref, parts in ((va_ref, values),):
             for x, (t, h, rows, lanes) in zip(parts, spans):
                 for m in range(NBR):
                     acc_ref[pl.ds(spots[t][m], TILE), lanes] += x[m * TILE : (m + 1) * TILE]
         return carry
 
     lax.fori_loop(0, heads // UNROLL, body, 0)
+    v_out_ref[...] = va_ref[count : 2 * count, :]
+    to_left_ref[...] = va_ref[0:count, :].astype(BF16)
+    to_right_ref[...] = va_ref[2 * count : 3 * count, :].astype(BF16)
+
+
+def key_kernel(
+    seq_ref, offs_ref, ag_ref, q_ref, vl_ref, v_ref, vr_ref, wts_ref, k_out_ref, to_left_ref,
+    to_right_ref, vx_ref, ka_ref, total_tiles,
+):
+    fill_halo(vx_ref, vl_ref, v_ref, vr_ref)
+    count, width = q_ref.shape
+    heads = width // HEAD_DIM
+    tiles = count // TILE
+    scale = HEAD_DIM ** (-0.5)
+    ka_ref[...] = jnp.zeros_like(ka_ref)
+    spots = [tile_places(seq_ref, offs_ref, t, tiles, total_tiles)[0] for t in range(tiles)]
+
+    def body(step, carry):
+        spans = head_spans(step, heads, tiles)
+        prob_grads = [
+            dot_nt(ag_ref[rows, lanes], window(vx_ref, spots[t], lanes))
+            for t, h, rows, lanes in spans
+        ]
+        sums = [
+            jnp.sum(wts_ref[t * heads + h] * x, axis=-1, keepdims=True)
+            for x, (t, h, rows, lanes) in zip(prob_grads, spans)
+        ]
+        score_grads = [
+            (wts_ref[t * heads + h] * (x - total)).astype(BF16)
+            for x, total, (t, h, rows, lanes) in zip(prob_grads, sums, spans)
+        ]
+        keys = [
+            dot_tn(x, q_ref[rows, lanes]) * scale
+            for x, (t, h, rows, lanes) in zip(score_grads, spans)
+        ]
+        for acc_ref, parts in ((ka_ref, keys),):
+            for x, (t, h, rows, lanes) in zip(parts, spans):
+                for m in range(NBR):
+                    acc_ref[pl.ds(spots[t][m], TILE), lanes] += x[m * TILE : (m + 1) * TILE]
+        return carry
+
+    lax.fori_loop(0, heads // UNROLL, body, 0)
     k_out_ref[...] = ka_ref[count : 2 * count, :]
-    v_out_ref[...] = va_ref[count : 2 * count, :]
-    to_left_ref[0] = ka_ref[0:count, :].astype(BF16)
-    to_left_ref[1] = va_ref[0:count, :].astype(BF16)
-    to_right_ref[0] = ka_ref[2 * count : 3 * count, :].astype(BF16)
-    to_right_ref[1] = va_ref[2 * count : 3 * count, :].astype(BF16)
+    to_left_ref[...] = ka_ref[0:count, :].astype(BF16)
+    to_right_ref[...] = ka_ref[2 * count : 3 * count, :].astype(BF16)
 
 
 def call(body, outs, kinds, scratch, name, flops, megabytes):
@@ -447,26 +467,30 @@
     oth = (h1.astype(F32) + h3.astype(F32)).astype(BF16).reshape(columns, 1, CELL, piece)
     home = exchange(jnp.concatenate([own, oth], axis=1))
 
-    k_own, v_own, to_left, to_right = call(
-        lambda *refs: backward_kernel(*refs, total_tiles=total_tiles),
-        (shape((count, width), F32), shape((count, width), F32), shape(pair, BF16), shape(pair, BF16)),
-        "ss" + "v" * 13,
-        [
-            pltpu.VMEM((3 * count, width), BF16),
-            pltpu.VMEM((2 * slots, width), BF16),
-            pltpu.VMEM((count, width), BF16),
-            pltpu.VMEM((3 * count, width), F32),
-            pltpu.VMEM((3 * count, width), F32),
-        ],
-        "attention_grad", 10 * MICRO, 24,
-    )(seq, offsets, ids_t, gates_t, home, grad, unit, inv, gain, perm_t, q, vl, v, vr, wts)
-    from_right = lax.ppermute(to_left, "seq", down_by).astype(F32)
-    from_left = lax.ppermute(to_right, "seq", up_by).astype(F32)
-
-    def finish(own_part, i):
-        return (own_part + from_right[i] + from_left[i]).astype(BF16)[None]
-
-    return (finish(k_own, 0), finish(v_own, 1))
+    full = shape((count, width), F32)
+    side = shape((count, width), BF16)
+    v_own, v_left, v_right, attn_grad = call(
+        lambda *refs: value_kernel(*refs, total_tiles=total_tiles),
+        (full, side, side, side),
+        "ss" + "v" * 9,
+        [pltpu.VMEM((2 * slots, width), BF16), pltpu.VMEM((3 * count, width), F32)],
+        "value_grad", 5 * MICRO, 20,
+    )(seq, offsets, ids_t, gates_t, home, grad, unit, inv, gain, perm_t, wts)
+
+    def finish(own_part, left_part, right_part):
+        from_right = lax.ppermute(left_part, "seq", down_by).astype(F32)
+        from_left = lax.ppermute(right_part, "seq", up_by).astype(F32)
+        return (own_part + from_right + from_left).astype(BF16)[None]
+
+    value_out = finish(v_own, v_left, v_right)
+    k_own, k_left, k_right = call(
+        lambda *refs: key_kernel(*refs, total_tiles=total_tiles),
+        (full, side, side),
+        "ss" + "v" * 6,
+        [pltpu.VMEM((3 * count, width), BF16), pltpu.VMEM((3 * count, width), F32)],
+        "key_grad", 4 * MICRO, 20,
+    )(seq, offsets, attn_grad, q, vl, v, vr, wts)
+    return (finish(k_own, k_left, k_right), value_out)
 
 
 def solution(mesh):

time: 224 us -> 224 us (level)
  waiting for transfers between devices: 63 us -> 56.5 us
  starting transfers between devices: 49.7 us -> 55.3 us
    ppermute x2 -> x4, waiting for transfers between devices: 11.5 us -> 5.1 us  [the longest x2 3.92 us: finish(): from_right = lax.ppermute(left_part, 'seq', down_by).astype(F32)]
    ppermute x2 -> x4, starting transfers between devices: 6.79 us -> 12.4 us  [the longest x2 7.32 us: finish(): from_right = lax.ppermute(left_part, 'seq', down_by).astype(F32)]
    pallas_call x1 -> x2, Pallas kernels: 6.91 us -> 8.39 us  [the longest x1 4.34 us: on_device(): call(lambda *refs: value_kernel(*refs, total_tiles=total_tiles), (full, s...]
  transfers between devices with their start and end apart: 20 -> 22, of which waited for: 13 -> 13; matrix products, arithmetic and copies ran while one was open for 2% -> 2% of each run, Pallas kernels for 17% -> 19%
where the time goes in v9:
time: 224 us
  waiting for transfers between devices  56.5 us (25%)
  starting transfers between devices  55.3 us (25%)
  Pallas kernels  49.5 us (22%)
  blocking collectives  47.1 us (21%)
  local copies, waits for them, and re-layouts  11.8 us (5%)
  other arithmetic  2.42 us (1%)
    all_to_all x1, blocking collectives, exchange(): return lax.all_to_all(x, 'exp', split_axis=0, concat_axis=0, tiled=True)  47.1 us
    ppermute x12, waiting for transfers between devices, swap(): return lax.ppermute(x, 'seq', [(i, i ^ bits) for i in range(seq_count)])  33.8 us
    pallas_call x3, Pallas kernels, expert(): call(lambda *refs: expert_kernel(*refs, blocks=blocks), (shape(flat, BF16...  20.7 us
    all_to_all x2, starting transfers between devices, exchange(): return lax.all_to_all(x, 'exp', split_axis=0, concat_axis=0, tiled=True)  20.6 us
    ppermute x12, starting transfers between devices, swap(): return lax.ppermute(x, 'seq', [(i, i ^ bits) for i in range(seq_count)])  10.9 us
    pallas_call x3, Pallas kernels, hidden(): call(lambda *refs: hidden_kernel(*refs, blocks=blocks), (shape((blocks *...  10.8 us
    all_to_all x2, waiting for transfers between devices, exchange(): return lax.all_to_all(x, 'exp', split_axis=0, concat_axis=0, tiled=True)  8.62 us
    unnamed x58, local copies, waits for them, and re-layouts  8.05 us
  transfers between devices with their start and end apart: 22, of which 13 were waited for; matrix products, arithmetic and copies ran while one was open for 2% of the time, Pallas kernels for 19%

profile of v9, /device:TPU:1, one launch (start us, length us, event | category | flops | bytes accessed | tf_op | source)
XLA Modules:
  0.0 223.7 jit_solution(11261638145720606585)
XLA Ops:
  0.6 3.6 %place_grad.1 = bf16[32,2,40,256]{3,2,1,0:T(8,128)(2,1)} custom-call(s32[1]{0:T(128)} %bitcast.seq_ref.refs_0_, s32[2,128]{1,0:T(2,128)} %bitcast.55, bf16[128,2048]{1,0:T(8,128)(2,1)} %bitcast.45, bf16[320,320]{1,0:T(8,128)(2,1)} %constant.8.clone.perm_ref.refs_11_.refs_1_.refs_2_.refs_3_.refs_4_.refs_9_), custom_call_target="tpu_custom_call" | custom-call | flops 4294967296 | bytes 1048576 | tf_op jit(solution)/shard_map/place_grad/pallas_call | solution.py:388
  4.3 12.3 %all-to-all-start = ((bf16[32,2,40,256]{3,2,1,0:T(8,128)(2,1)}), bf16[32,2,40,256]{3,2,1,0:T(8,128)(2,1)}, u32[]{:S(2)}, u32[]{:S(2)}) async-start(bf16[32,2,40,256]{3,2,1,0:T(8,128)(2,1)} %place_grad.1), calls=%async_computation | async-start | bytes 2621440 | tf_op jit(solution)/shard_map/all_to_all | solution.py:384
  16.6 4.0 %collective-permute-start.2 = (bf16[128,2048]{1,0:T(8,128)(2,1)S(1)}, bf16[128,2048]{1,0:T(8,128)(2,1)S(1)}, u32[]{:S(2)}, u32[]{:S(2)}) collective-permute-start(bf16[128,2048]{1,0:T(8,128)(2,1)S(1)} %bitcast.49), channel_id=1, source_target_pairs={{0,32},{32,64},{64,96},{96,128},{128,160},{160,192},{192,224},{1,3... | collective-permute-start | bytes 1572872 | tf_op jit(solution)/shard_map/ppermute | solution.py:394
  20.6 1.9 collective-permute-start.3
  22.5 3.6 %collective-permute-start = (bf16[128,2048]{1,0:T(8,128)(2,1)S(1)}, bf16[128,2048]{1,0:T(8,128)(2,1)S(1)}, u32[]{:S(2)}, u32[]{:S(2)}) collective-permute-start(bf16[128,2048]{1,0:T(8,128)(2,1)S(1)} %bitcast.42), channel_id=1, source_target_pairs={{0,32},{32,64},{64,96},{96,128},{128,160},{160,192},{192,224},{1,3... | collective-permute-start | bytes 1572872 | tf_op jit(solution)/shard_map/ppermute | solution.py:393
  26.1 1.9 collective-permute-start.1
  28.1 3.4 %collective-permute-done.3.refs_9_.refs_6_ = bf16[128,2048]{1,0:T(8,128)(2,1)S(1)} collective-permute-done((bf16[128,2048]{1,0:T(8,128)(2,1)S(1)}, bf16[128,2048]{1,0:T(8,128)(2,1)S(1)}, u32[]{:S(2)}, u32[]{:S(2)}) %collective-permute-start.3) | collective-permute-done | bytes 524320 | tf_op jit(solution)/shard_map/ppermute | solution.py:394
  32.3 4.8 %collective-permute-done.1.refs_6_ = bf16[128,2048]{1,0:T(8,128)(2,1)S(1)} collective-permute-done((bf16[128,2048]{1,0:T(8,128)(2,1)S(1)}, bf16[128,2048]{1,0:T(8,128)(2,1)S(1)}, u32[]{:S(2)}, u32[]{:S(2)}) %collective-permute-start.1) | collective-permute-done | bytes 524320 | tf_op jit(solution)/shard_map/ppermute | solution.py:393
  38.1 6.0 %attention.1 = (f32[32,64,192]{2,1,0:T(8,128)S(1)}, f32[128,2048]{1,0:T(8,128)S(1)}, f32[128,128]{1,0:T(8,128)S(1)}, bf16[32,2,40,256]{3,2,1,0:T(8,128)(2,1)}) custom-call(s32[1]{0:T(128)} %bitcast.seq_ref.refs_0_, s32[2,3]{1,0:T(2,128)S(1)} %bitcast.59, s32[2,128]{1,0:T(2,128)S(1)} %bitcast.56, bf16[128,2048]{1,0:T(8,128)(2,1)S(1)} %bitcast.47, ...), custom_call_target="tpu_custom_call" | custom-call | flops 8589934592 | bytes 1048576 | tf_op jit(solution)/shard_map/attention/pallas_call | solution.py:398
  48.4 8.3 %all-to-all-start.1 = ((bf16[32,2,40,256]{3,2,1,0:T(8,128)(2,1)}), bf16[32,2,40,256]{3,2,1,0:T(8,128)(2,1)}, u32[]{:S(2)}, u32[]{:S(2)}) async-start(bf16[32,2,40,256]{3,2,1,0:T(8,128)(2,1)} %get-tuple-element.34), calls=%async_computation.1 | async-start | bytes 2621440 | tf_op jit(solution)/shard_map/all_to_all | solution.py:384
  57.3 2.2 fusion.2
  59.5 2.3 %collective-permute-start.10 = (bf16[1280,256]{1,0:T(8,128)(2,1)}, bf16[1280,256]{1,0:T(8,128)(2,1)S(1)}, u32[]{:S(2)}, u32[]{:S(2)}) collective-permute-start(bf16[1280,256]{1,0:T(8,128)(2,1)} %bitcast.17), channel_id=1, source_target_pairs={{0,192},{32,224},{64,128},{96,160},{128,64},{160,96},{192,0},{224,... | collective-permute-start | bytes 1966088 | tf_op jit(solution)/shard_map/ppermute | solution.py:381
  63.4 3.4 %hidden.3.refs_1_ = f32[160,1024]{1,0:T(8,128)S(1)} custom-call(bf16[1280,256]{1,0:T(8,128)(2,1)S(1)} %bitcast.29, bf16[320,320]{1,0:T(8,128)(2,1)S(1)} %copy-done.18, bf16[512,2048]{1,0:T(8,128)(2,1)S(1)} %bitcast.31, bf16[512,2048]{1,0:T(8,128)(2,1)} %collective-permute-done.4.refs_3_.refs_4_), custom_call_target="tpu_custom_call" | custom-call | flops 4294967296 | bytes 1048576 | tf_op jit(solution)/shard_map/hidden/pallas_call | solution.py:431
  67.6 9.5 %collective-permute-done.10.refs_0_ = bf16[1280,256]{1,0:T(8,128)(2,1)S(1)} collective-permute-done((bf16[1280,256]{1,0:T(8,128)(2,1)}, bf16[1280,256]{1,0:T(8,128)(2,1)S(1)}, u32[]{:S(2)}, u32[]{:S(2)}) %collective-permute-start.10) | collective-permute-done | bytes 655392 | tf_op jit(solution)/shard_map/ppermute | solution.py:381
  77.5 3.8 %hidden.5.refs_2_ = f32[320,1024]{1,0:T(8,128)S(1)} custom-call(bf16[1280,256]{1,0:T(8,128)(2,1)S(1)} %collective-permute-done.10.refs_0_, bf16[1280,256]{1,0:T(8,128)(2,1)S(1)} %collective-permute-done.11.refs_1_, bf16[320,320]{1,0:T(8,128)(2,1)S(1)} %copy-done.18, bf16[512,2048]{1,0:T(8,128)(2,1)S(1)} %bitcast.32, ...), custom_call_target="tpu_custom_call" | custom-call | flops 5368709120 | bytes 1048576 | tf_op jit(solution)/shard_map/hidden/pallas_call | solution.py:431
  82.3 6.8 %all-to-all-done.1 = bf16[32,2,40,256]{3,2,1,0:T(8,128)(2,1)} async-done(((bf16[32,2,40,256]{3,2,1,0:T(8,128)(2,1)}), bf16[32,2,40,256]{3,2,1,0:T(8,128)(2,1)}, u32[]{:S(2)}, u32[]{:S(2)}) %all-to-all-start.1) | async-done | bytes 1310752 | tf_op jit(solution)/shard_map/all_to_all | solution.py:384
  90.8 2.0 collective-permute-start.9
  95.5 6.3 %expert.3 = bf16[1280,256]{1,0:T(8,128)(2,1)S(1)} custom-call(bf16[1280,256]{1,0:T(8,128)(2,1)S(1)} %bitcast.27, f32[160,1024]{1,0:T(8,128)S(1)} %copy-done.24, bf16[320,320]{1,0:T(8,128)(2,1)S(1)} %copy-done.18, bf16[320,320]{1,0:T(8,128)(2,1)S(1)} %copy-done.18, bf16[2048,512]{1,0:T(8,128)(2,1)S(1)} %bitcast.35, bf16[2048,512]{1,0:T(8,128)(2,1)S(1)} %bitcast.39, ...), custom_call_target="tpu_custom_call" | custom-call | flops 9663676416 | bytes 1048576 | tf_op jit(solution)/shard_map/expert/pallas_call | solution.py:442
  101.9 3.6 %hidden.4.refs_1_ = f32[160,1024]{1,0:T(8,128)S(1)} custom-call(bf16[1280,256]{1,0:T(8,128)(2,1)S(1)} %collective-permute-done.7.refs_0_, bf16[320,320]{1,0:T(8,128)(2,1)S(1)} %copy-done.18, bf16[512,2048]{1,0:T(8,128)(2,1)S(1)} %bitcast.33, bf16[512,2048]{1,0:T(8,128)(2,1)} %collective-permute-done.4.refs_3_.refs_4_), custom_call_target="tpu_custom_call" | custom-call | flops 4294967296 | bytes 1048576 | tf_op jit(solution)/shard_map/hidden/pallas_call | solution.py:431
  106.6 8.1 %expert.4 = (bf16[1280,256]{1,0:T(8,128)(2,1)S(1)}, bf16[1280,256]{1,0:T(8,128)(2,1)S(1)}) custom-call(bf16[1280,256]{1,0:T(8,128)(2,1)S(1)} %collective-permute-done.8.refs_0_, bf16[1280,256]{1,0:T(8,128)(2,1)S(1)} %collective-permute-done.9.refs_1_, f32[320,1024]{1,0:T(8,128)S(1)} %copy-done.22, bf16[320,320]{1,0:T(8,128)(2,1)S(1)} %copy-done.18, ...), custom_call_target="tpu_custom_call" | custom-call | flops 11811160064 | bytes 1048576 | tf_op jit(solution)/shard_map/expert/pallas_call | solution.py:442
  116.9 2.4 %collective-permute-done.14.refs_0_ = bf16[1280,256]{1,0:T(8,128)(2,1)S(1)} collective-permute-done((bf16[1280,256]{1,0:T(8,128)(2,1)S(1)}, bf16[1280,256]{1,0:T(8,128)(2,1)S(1)}, u32[]{:S(2)}, u32[]{:S(2)}) %collective-permute-start.14) | collective-permute-done | bytes 655392 | tf_op jit(solution)/shard_map/ppermute | solution.py:381
  119.3 6.3 %expert.5 = bf16[1280,256]{1,0:T(8,128)(2,1)S(1)} custom-call(bf16[1280,256]{1,0:T(8,128)(2,1)S(1)} %collective-permute-done.14.refs_0_, f32[160,1024]{1,0:T(8,128)S(1)} %hidden.4.refs_1_, bf16[320,320]{1,0:T(8,128)(2,1)S(1)} %copy-done.18, bf16[320,320]{1,0:T(8,128)(2,1)S(1)} %copy-done.18, bf16[2048,512]{1,0:T(8,128)(2,1)S(1)} %bitcast.37, ...), custom_call_target="tpu_custom_call" | custom-call | flops 9663676416 | bytes 1048576 | tf_op jit(solution)/shard_map/expert/pallas_call | solution.py:442
  127.3 6.1 %collective-permute-done.12 = bf16[1280,256]{1,0:T(8,128)(2,1)S(1)} collective-permute-done((bf16[1280,256]{1,0:T(8,128)(2,1)S(1)}, bf16[1280,256]{1,0:T(8,128)(2,1)S(1)}, u32[]{:S(2)}, u32[]{:S(2)}) %collective-permute-start.12) | collective-permute-done | bytes 655392 | tf_op jit(solution)/shard_map/ppermute | solution.py:381
  133.6 14.7 %collective-permute-done.15 = bf16[1280,256]{1,0:T(8,128)(2,1)S(1)} collective-permute-done((bf16[1280,256]{1,0:T(8,128)(2,1)S(1)}, bf16[1280,256]{1,0:T(8,128)(2,1)S(1)}, u32[]{:S(2)}, u32[]{:S(2)}) %collective-permute-start.15) | collective-permute-done | bytes 655392 | tf_op jit(solution)/shard_map/ppermute | solution.py:381
  148.6 47.1 %all_to_all.15.refs_4_ = bf16[32,2,40,256]{3,2,1,0:T(8,128)(2,1)S(1)} all-to-all(bf16[32,2,40,256]{3,2,1,0:T(8,128)(2,1)S(1)} %pad_maximum_fusion), channel_id=1, replica_groups=mesh['seq'=8,'exp'=32] {'exp'}, dimensions={0} | all-to-all | bytes 2621440 | tf_op jit(solution)/shard_map/all_to_all | solution.py:384
  195.8 4.3 %value_grad.1 = (f32[128,2048]{1,0:T(8,128)S(1)}, bf16[128,2048]{1,0:T(8,128)(2,1)S(1)}, bf16[128,2048]{1,0:T(8,128)(2,1)S(1)}, bf16[128,2048]{1,0:T(8,128)(2,1)S(1)}) custom-call(s32[1]{0:T(128)} %bitcast.seq_ref.refs_0_, s32[2,3]{1,0:T(2,128)S(1)} %bitcast.60, s32[2,128]{1,0:T(2,128)S(1)} %bitcast.57, f32[2,128]{1,0:T(2,128)S(1)} %bitcast.58, ...), custom_call_target="tpu_custom_call" | custom-call | flops 5368709120 | bytes 1048576 | tf_op jit(solution)/shard_map/value_grad/pallas_call | solution.py:472
  200.1 4.9 %collective-permute-start.18 = (bf16[128,2048]{1,0:T(8,128)(2,1)S(1)}, bf16[128,2048]{1,0:T(8,128)(2,1)S(1)}, u32[]{:S(2)}, u32[]{:S(2)}) collective-permute-start(bf16[128,2048]{1,0:T(8,128)(2,1)S(1)} %get-tuple-element.54), channel_id=1, source_target_pairs={{32,0},{64,32},{96,64},{128,96},{160,128},{192,160},{224,192},{33,... | collective-permute-start | bytes 1572872 | tf_op jit(solution)/shard_map/ppermute | solution.py:481
  205.0 1.9 collective-permute-start.19
  207.0 4.1 %key_grad.1 = (f32[128,2048]{1,0:T(8,128)S(1)}, bf16[128,2048]{1,0:T(8,128)(2,1)S(1)}, bf16[128,2048]{1,0:T(8,128)(2,1)S(1)}) custom-call(s32[1]{0:T(128)} %bitcast.seq_ref.refs_0_, s32[2,3]{1,0:T(2,128)S(1)} %bitcast.61, bf16[128,2048]{1,0:T(8,128)(2,1)S(1)} %get-tuple-element.49.refs_2_, bf16[128,2048]{1,0:T(8,128)(2,1)S(1)} %bitcast.48, ...), custom_call_target="tpu_custom_call" | custom-call | flops 4294967296 | bytes 1048576 | tf_op jit(solution)/shard_map/key_grad/pallas_call | solution.py:486
  211.0 2.4 %collective-permute-start.16 = (bf16[128,2048]{1,0:T(8,128)(2,1)S(1)}, bf16[128,2048]{1,0:T(8,128)(2,1)S(1)}, u32[]{:S(2)}, u32[]{:S(2)}) collective-permute-start(bf16[128,2048]{1,0:T(8,128)(2,1)S(1)} %get-tuple-element.51), channel_id=1, source_target_pairs={{32,0},{64,32},{96,64},{128,96},{160,128},{192,160},{224,192},{33,... | collective-permute-start | bytes 1572872 | tf_op jit(solution)/shard_map/ppermute | solution.py:481
  213.5 3.1 %collective-permute-start.17 = (bf16[128,2048]{1,0:T(8,128)(2,1)S(1)}, bf16[128,2048]{1,0:T(8,128)(2,1)S(1)}, u32[]{:S(2)}, u32[]{:S(2)}) collective-permute-start(bf16[128,2048]{1,0:T(8,128)(2,1)S(1)} %get-tuple-element.52), channel_id=1, source_target_pairs={{0,32},{32,64},{64,96},{96,128},{128,160},{160,192},{192,224},{1,3... | collective-permute-start | bytes 1572872 | tf_op jit(solution)/shard_map/ppermute | solution.py:482
  217.6 3.9 %collective-permute-done.16 = bf16[128,2048]{1,0:T(8,128)(2,1)S(1)} collective-permute-done((bf16[128,2048]{1,0:T(8,128)(2,1)S(1)}, bf16[128,2048]{1,0:T(8,128)(2,1)S(1)}, u32[]{:S(2)}, u32[]{:S(2)}) %collective-permute-start.16) | collective-permute-done | bytes 524320 | tf_op jit(solution)/shard_map/ppermute | solution.py:481
  (88 shorter events, 23.4 us)
Async XLA Ops:
  4.2 32.8 %copy-start.6 = (bf16[1,128,2048]{2,1,0:T(8,128)(2,1)S(1)}, bf16[1,128,2048]{2,1,0:T(8,128)(2,1)}, u32[]{:S(2)}) copy-start(bf16[1,128,2048]{2,1,0:T(8,128)(2,1)} %param.13) | copy-start | bytes 1572868
  4.2 32.8 %copy-start.14 = (f32[2048]{0:T(1024)S(1)}, f32[2048]{0:T(1024)}, u32[]{:S(2)}) copy-start(f32[2048]{0:T(1024)} %param.17) | copy-start | bytes 24580
  4.2 32.8 %copy-start.15 = (s32[1,128,2]{1,2,0:T(2,128)S(1)}, s32[1,128,2]{1,2,0:T(2,128)}, u32[]{:S(2)}) copy-start(s32[1,128,2]{1,2,0:T(2,128)} %param.19) | copy-start | bytes 3076
  4.2 32.8 %copy-start.17 = (s32[1,2,3]{2,1,0:T(2,128)S(1)}, s32[1,2,3]{2,1,0:T(2,128)}, u32[]{:S(2)}) copy-start(s32[1,2,3]{2,1,0:T(2,128)} %param.20) | copy-start | bytes 76
  4.3 32.8 %copy-start.18 = (bf16[320,320]{1,0:T(8,128)(2,1)S(1)}, bf16[320,320]{1,0:T(8,128)(2,1)}, u32[]{:S(2)}) copy-start(bf16[320,320]{1,0:T(8,128)(2,1)} %constant.8.clone.perm_ref.refs_11_.refs_1_.refs_2_.refs_3_.refs_4_.refs_9_) | copy-start | bytes 614404
  4.3 44.1 %all-to-all-start = ((bf16[32,2,40,256]{3,2,1,0:T(8,128)(2,1)}), bf16[32,2,40,256]{3,2,1,0:T(8,128)(2,1)}, u32[]{:S(2)}, u32[]{:S(2)}) async-start(bf16[32,2,40,256]{3,2,1,0:T(8,128)(2,1)} %place_grad.1), calls=%async_computation | async-start | bytes 2621440 | tf_op jit(solution)/shard_map/all_to_all | solution.py:384
  16.6 11.5 %collective-permute-start.2 = (bf16[128,2048]{1,0:T(8,128)(2,1)S(1)}, bf16[128,2048]{1,0:T(8,128)(2,1)S(1)}, u32[]{:S(2)}, u32[]{:S(2)}) collective-permute-start(bf16[128,2048]{1,0:T(8,128)(2,1)S(1)} %bitcast.49), channel_id=1, source_target_pairs={{0,32},{32,64},{64,96},{96,128},{128,160},{160,192},{192,224},{1,3... | collective-permute-start | bytes 1572872 | tf_op jit(solution)/shard_map/ppermute | solution.py:394
  20.6 10.9 %collective-permute-start.3 = (bf16[128,2048]{1,0:T(8,128)(2,1)S(1)}, bf16[128,2048]{1,0:T(8,128)(2,1)S(1)}, u32[]{:S(2)}, u32[]{:S(2)}) collective-permute-start(bf16[128,2048]{1,0:T(8,128)(2,1)S(1)} %bitcast.50), channel_id=1, source_target_pairs={{32,0},{64,32},{96,64},{128,96},{160,128},{192,160},{224,192},{33,... | collective-permute-start | bytes 1572872 | tf_op jit(solution)/shard_map/ppermute | solution.py:394
  22.5 9.8 %collective-permute-start = (bf16[128,2048]{1,0:T(8,128)(2,1)S(1)}, bf16[128,2048]{1,0:T(8,128)(2,1)S(1)}, u32[]{:S(2)}, u32[]{:S(2)}) collective-permute-start(bf16[128,2048]{1,0:T(8,128)(2,1)S(1)} %bitcast.42), channel_id=1, source_target_pairs={{0,32},{32,64},{64,96},{96,128},{128,160},{160,192},{192,224},{1,3... | collective-permute-start | bytes 1572872 | tf_op jit(solution)/shard_map/ppermute | solution.py:393
  26.1 10.9 %collective-permute-start.1 = (bf16[128,2048]{1,0:T(8,128)(2,1)S(1)}, bf16[128,2048]{1,0:T(8,128)(2,1)S(1)}, u32[]{:S(2)}, u32[]{:S(2)}) collective-permute-start(bf16[128,2048]{1,0:T(8,128)(2,1)S(1)} %bitcast.43), channel_id=1, source_target_pairs={{32,0},{64,32},{96,64},{128,96},{160,128},{192,160},{224,192},{33,... | collective-permute-start | bytes 1572872 | tf_op jit(solution)/shard_map/ppermute | solution.py:393
  46.5 15.3 %collective-permute-start.4 = (bf16[512,2048]{1,0:T(8,128)(2,1)S(1)}, bf16[512,2048]{1,0:T(8,128)(2,1)}, u32[]{:S(2)}, u32[]{:S(2)}) collective-permute-start(bf16[512,2048]{1,0:T(8,128)(2,1)S(1)} %bitcast.30), channel_id=1, source_target_pairs={{0,32},{32,0},{64,96},{96,64},{128,160},{160,128},{192,224},{224,1... | collective-permute-start | bytes 6291464 | tf_op jit(solution)/shard_map/ppermute | solution.py:381
  48.4 40.8 %all-to-all-start.1 = ((bf16[32,2,40,256]{3,2,1,0:T(8,128)(2,1)}), bf16[32,2,40,256]{3,2,1,0:T(8,128)(2,1)}, u32[]{:S(2)}, u32[]{:S(2)}) async-start(bf16[32,2,40,256]{3,2,1,0:T(8,128)(2,1)} %get-tuple-element.34), calls=%async_computation.1 | async-start | bytes 2621440 | tf_op jit(solution)/shard_map/all_to_all | solution.py:384
  56.7 36.1 %collective-permute-start.5 = (bf16[2048,512]{1,0:T(8,128)(2,1)}, bf16[2048,512]{1,0:T(8,128)(2,1)}, u32[]{:S(2)}, u32[]{:S(2)}) collective-permute-start(bf16[2048,512]{1,0:T(8,128)(2,1)} %bitcast.34), channel_id=1, source_target_pairs={{0,32},{32,0},{64,96},{96,64},{128,160},{160,128},{192,224},{224,1... | collective-permute-start | bytes 6291464 | tf_op jit(solution)/shard_map/ppermute | solution.py:381
  57.0 35.8 %collective-permute-start.6 = (bf16[2048,512]{1,0:T(8,128)(2,1)}, bf16[2048,512]{1,0:T(8,128)(2,1)}, u32[]{:S(2)}, u32[]{:S(2)}) collective-permute-start(bf16[2048,512]{1,0:T(8,128)(2,1)} %bitcast.38), channel_id=1, source_target_pairs={{0,32},{32,0},{64,96},{96,64},{128,160},{160,128},{192,224},{224,1... | collective-permute-start | bytes 6291464 | tf_op jit(solution)/shard_map/ppermute | solution.py:381
  59.5 17.7 %collective-permute-start.10 = (bf16[1280,256]{1,0:T(8,128)(2,1)}, bf16[1280,256]{1,0:T(8,128)(2,1)S(1)}, u32[]{:S(2)}, u32[]{:S(2)}) collective-permute-start(bf16[1280,256]{1,0:T(8,128)(2,1)} %bitcast.17), channel_id=1, source_target_pairs={{0,192},{32,224},{64,128},{96,160},{128,64},{160,96},{192,0},{224,... | collective-permute-start | bytes 1966088 | tf_op jit(solution)/shard_map/ppermute | solution.py:381
  61.8 15.7 %collective-permute-start.11 = (bf16[1280,256]{1,0:T(8,128)(2,1)S(1)}, bf16[1280,256]{1,0:T(8,128)(2,1)S(1)}, u32[]{:S(2)}, u32[]{:S(2)}) collective-permute-start(bf16[1280,256]{1,0:T(8,128)(2,1)S(1)} %bitcast.28), channel_id=1, source_target_pairs={{0,64},{32,96},{64,0},{96,32},{128,192},{160,224},{192,128},{224,1... | collective-permute-start | bytes 1966088 | tf_op jit(solution)/shard_map/ppermute | solution.py:381
  61.8 40.1 %collective-permute-start.7 = (bf16[1280,256]{1,0:T(8,128)(2,1)}, bf16[1280,256]{1,0:T(8,128)(2,1)S(1)}, u32[]{:S(2)}, u32[]{:S(2)}) collective-permute-start(bf16[1280,256]{1,0:T(8,128)(2,1)} %bitcast.17), channel_id=1, source_target_pairs={{0,128},{32,160},{64,192},{96,224},{128,0},{160,32},{192,64},{224,... | collective-permute-start | bytes 1966088 | tf_op jit(solution)/shard_map/ppermute | solution.py:381
  90.7 15.4 %collective-permute-start.8 = (bf16[1280,256]{1,0:T(8,128)(2,1)S(1)}, bf16[1280,256]{1,0:T(8,128)(2,1)S(1)}, u32[]{:S(2)}, u32[]{:S(2)}) collective-permute-start(bf16[1280,256]{1,0:T(8,128)(2,1)S(1)} %bitcast.64), channel_id=1, source_target_pairs={{0,192},{32,224},{64,128},{96,160},{128,64},{160,96},{192,0},{224,... | collective-permute-start | bytes 1966088 | tf_op jit(solution)/shard_map/ppermute | solution.py:381
  90.8 15.3 %collective-permute-start.9 = (bf16[1280,256]{1,0:T(8,128)(2,1)S(1)}, bf16[1280,256]{1,0:T(8,128)(2,1)S(1)}, u32[]{:S(2)}, u32[]{:S(2)}) collective-permute-start(bf16[1280,256]{1,0:T(8,128)(2,1)S(1)} %bitcast.26), channel_id=1, source_target_pairs={{0,64},{32,96},{64,0},{96,32},{128,192},{160,224},{192,128},{224,1... | collective-permute-start | bytes 1966088 | tf_op jit(solution)/shard_map/ppermute | solution.py:381
  106.1 13.2 %collective-permute-start.14 = (bf16[1280,256]{1,0:T(8,128)(2,1)S(1)}, bf16[1280,256]{1,0:T(8,128)(2,1)S(1)}, u32[]{:S(2)}, u32[]{:S(2)}) collective-permute-start(bf16[1280,256]{1,0:T(8,128)(2,1)S(1)} %collective-permute-done.8.refs_0_), channel_id=1, source_target_pairs={{0,64},{32,96},{64,0},{96,32},{128,192},{160,224},{192,128},{224,1... | collective-permute-start | bytes 1966088 | tf_op jit(solution)/shard_map/ppermute | solution.py:381
  114.7 18.7 %collective-permute-start.12 = (bf16[1280,256]{1,0:T(8,128)(2,1)S(1)}, bf16[1280,256]{1,0:T(8,128)(2,1)S(1)}, u32[]{:S(2)}, u32[]{:S(2)}) collective-permute-start(bf16[1280,256]{1,0:T(8,128)(2,1)S(1)} %get-tuple-element.43), channel_id=1, source_target_pairs={{0,64},{32,96},{64,0},{96,32},{128,192},{160,224},{192,128},{224,1... | collective-permute-start | bytes 1966088 | tf_op jit(solution)/shard_map/ppermute | solution.py:381
  115.7 17.8 %collective-permute-start.13 = (bf16[1280,256]{1,0:T(8,128)(2,1)S(1)}, bf16[1280,256]{1,0:T(8,128)(2,1)S(1)}, u32[]{:S(2)}, u32[]{:S(2)}) collective-permute-start(bf16[1280,256]{1,0:T(8,128)(2,1)S(1)} %get-tuple-element.44), channel_id=1, source_target_pairs={{0,192},{32,224},{64,128},{96,160},{128,64},{160,96},{192,0},{224,... | collective-permute-start | bytes 1966088 | tf_op jit(solution)/shard_map/ppermute | solution.py:381
  125.7 22.6 %collective-permute-start.15 = (bf16[1280,256]{1,0:T(8,128)(2,1)S(1)}, bf16[1280,256]{1,0:T(8,128)(2,1)S(1)}, u32[]{:S(2)}, u32[]{:S(2)}) collective-permute-start(bf16[1280,256]{1,0:T(8,128)(2,1)S(1)} %expert.5), channel_id=1, source_target_pairs={{0,128},{32,160},{64,192},{96,224},{128,0},{160,32},{192,64},{224,... | collective-permute-start | bytes 1966088 | tf_op jit(solution)/shard_map/ppermute | solution.py:381
  148.5 47.3 %copy-start.26 = (f32[128,2048]{1,0:T(8,128)S(1)}, f32[128,2048]{1,0:T(8,128)}, u32[]{:S(2)}) copy-start(f32[128,2048]{1,0:T(8,128)} %copy-done.25) | copy-start | bytes 3145732
  148.5 47.3 %copy-start.28 = (f32[128,128]{1,0:T(8,128)S(1)}, f32[128,128]{1,0:T(8,128)}, u32[]{:S(2)}) copy-start(f32[128,128]{1,0:T(8,128)} %copy-done.27) | copy-start | bytes 196612
  148.6 47.1 %copy-start.5 = (bf16[1,128,2048]{2,1,0:T(8,128)(2,1)S(1)}, bf16[1,128,2048]{2,1,0:T(8,128)(2,1)}, u32[]{:S(2)}) copy-start(bf16[1,128,2048]{2,1,0:T(8,128)(2,1)} %param.16) | copy-start | bytes 1572868
  148.6 47.1 %copy-start.16 = (f32[1,128,2]{1,2,0:T(2,128)S(1)}, f32[1,128,2]{1,2,0:T(2,128)}, u32[]{:S(2)}) copy-start(f32[1,128,2]{1,2,0:T(2,128)} %param.18) | copy-start | bytes 3076
  148.6 47.1 %copy-start.20 = (f32[32,64,192]{2,1,0:T(8,128)S(1)}, f32[32,64,192]{2,1,0:T(8,128)}, u32[]{:S(2)}) copy-start(f32[32,64,192]{2,1,0:T(8,128)} %copy-done.19) | copy-start | bytes 4718596
  200.1 16.5 %collective-permute-start.18 = (bf16[128,2048]{1,0:T(8,128)(2,1)S(1)}, bf16[128,2048]{1,0:T(8,128)(2,1)S(1)}, u32[]{:S(2)}, u32[]{:S(2)}) collective-permute-start(bf16[128,2048]{1,0:T(8,128)(2,1)S(1)} %get-tuple-element.54), channel_id=1, source_target_pairs={{32,0},{64,32},{96,64},{128,96},{160,128},{192,160},{224,192},{33,... | collective-permute-start | bytes 1572872 | tf_op jit(solution)/shard_map/ppermute | solution.py:481
  205.0 11.6 %collective-permute-start.19 = (bf16[128,2048]{1,0:T(8,128)(2,1)S(1)}, bf16[128,2048]{1,0:T(8,128)(2,1)S(1)}, u32[]{:S(2)}, u32[]{:S(2)}) collective-permute-start(bf16[128,2048]{1,0:T(8,128)(2,1)S(1)} %get-tuple-element.55), channel_id=1, source_target_pairs={{0,32},{32,64},{64,96},{96,128},{128,160},{160,192},{192,224},{1,3... | collective-permute-start | bytes 1572872 | tf_op jit(solution)/shard_map/ppermute | solution.py:482
  211.0 10.5 %collective-permute-start.16 = (bf16[128,2048]{1,0:T(8,128)(2,1)S(1)}, bf16[128,2048]{1,0:T(8,128)(2,1)S(1)}, u32[]{:S(2)}, u32[]{:S(2)}) collective-permute-start(bf16[128,2048]{1,0:T(8,128)(2,1)S(1)} %get-tuple-element.51), channel_id=1, source_target_pairs={{32,0},{64,32},{96,64},{128,96},{160,128},{192,160},{224,192},{33,... | collective-permute-start | bytes 1572872 | tf_op jit(solution)/shard_map/ppermute | solution.py:481
  213.5 9.2 %collective-permute-start.17 = (bf16[128,2048]{1,0:T(8,128)(2,1)S(1)}, bf16[128,2048]{1,0:T(8,128)(2,1)S(1)}, u32[]{:S(2)}, u32[]{:S(2)}) collective-permute-start(bf16[128,2048]{1,0:T(8,128)(2,1)S(1)} %get-tuple-element.52), channel_id=1, source_target_pairs={{0,32},{32,64},{64,96},{96,128},{128,160},{160,192},{192,224},{1,3... | collective-permute-start | bytes 1572872 | tf_op jit(solution)/shard_map/ppermute | solution.py:482
  (19 other events, 124.5 us)

commit v10 on v7

--- a/solution.py
+++ b/solution.py
@@ -443,9 +443,9 @@
     (p3,) = expert((n3,), hidden_far, 9)
     h1, h2 = swap(p1, 6), swap(p2, 2)
     h3 = swap(p3, 4)
-    own = (p0.astype(F32) + h2.astype(F32)).astype(BF16).reshape(columns, 1, CELL, piece)
-    oth = (h1.astype(F32) + h3.astype(F32)).astype(BF16).reshape(columns, 1, CELL, piece)
-    home = exchange(jnp.concatenate([own, oth], axis=1))
+    own = (p0.astype(F32) + h2.astype(F32)).reshape(columns, 1, CELL, piece)
+    oth = (h1.astype(F32) + h3.astype(F32)).reshape(columns, 1, CELL, piece)
+    home = exchange(jnp.concatenate([own, oth], axis=1).astype(BF16))
 
     k_own, v_own, to_left, to_right = call(
         lambda *refs: backward_kernel(*refs, total_tiles=total_tiles),

time: 224 us -> 224 us (level)
  no operation moved by 1% of the time
where the time goes in v10:
time: 224 us; the launch traced here: 223 us
  waiting for transfers between devices  63 us (28%)
  starting transfers between devices  49.8 us (22%)
  Pallas kernels  48 us (21%)
  blocking collectives  47 us (21%)
  local copies, waits for them, and re-layouts  11.8 us (5%)
  other arithmetic  2.32 us (1%)
    all_to_all x1, blocking collectives, exchange(): return lax.all_to_all(x, 'exp', split_axis=0, concat_axis=0, tiled=True)  47 us
    ppermute x12, waiting for transfers between devices, swap(): return lax.ppermute(x, 'seq', [(i, i ^ bits) for i in range(seq_count)])  33.9 us
    pallas_call x3, Pallas kernels, expert(): call(lambda *refs: expert_kernel(*refs, blocks=blocks), (shape(flat, BF16...  20.7 us
    all_to_all x2, starting transfers between devices, exchange(): return lax.all_to_all(x, 'exp', split_axis=0, concat_axis=0, tiled=True)  20.6 us
    ppermute x12, starting transfers between devices, swap(): return lax.ppermute(x, 'seq', [(i, i ^ bits) for i in range(seq_count)])  10.9 us
    pallas_call x3, Pallas kernels, hidden(): call(lambda *refs: hidden_kernel(*refs, blocks=blocks), (shape((blocks *...  10.8 us
    ppermute x1, waiting for transfers between devices, on_device(): from_right = lax.ppermute(to_left, 'seq', down_by).astype(F32)  10.1 us
    all_to_all x2, waiting for transfers between devices, exchange(): return lax.all_to_all(x, 'exp', split_axis=0, concat_axis=0, tiled=True)  8.67 us
  transfers between devices with their start and end apart: 20, of which 13 were waited for; matrix products, arithmetic and copies ran while one was open for 2% of the time, Pallas kernels for 17%

profile of v10, /device:TPU:1, one launch (start us, length us, event | category | flops | bytes accessed | tf_op | source)
XLA Modules:
  0.0 222.9 jit_solution(7540070735736862263)
XLA Ops:
  0.6 3.6 %place_grad.1 = bf16[32,2,40,256]{3,2,1,0:T(8,128)(2,1)} custom-call(s32[1]{0:T(128)} %bitcast.seq_ref.refs_0_, s32[2,128]{1,0:T(2,128)} %bitcast.89, bf16[128,2048]{1,0:T(8,128)(2,1)} %bitcast.83, bf16[320,320]{1,0:T(8,128)(2,1)} %constant.8.clone.perm_ref.refs_11_.refs_1_.refs_2_.refs_3_.refs_4_.refs_9_), custom_call_target="tpu_custom_call" | custom-call | flops 4294967296 | bytes 1048576 | tf_op jit(solution)/shard_map/place_grad/pallas_call | solution.py:368
  4.3 12.3 %all-to-all-start = ((bf16[32,2,40,256]{3,2,1,0:T(8,128)(2,1)}), bf16[32,2,40,256]{3,2,1,0:T(8,128)(2,1)}, u32[]{:S(2)}, u32[]{:S(2)}) async-start(bf16[32,2,40,256]{3,2,1,0:T(8,128)(2,1)} %place_grad.1), calls=%async_computation | async-start | bytes 2621440 | tf_op jit(solution)/shard_map/all_to_all | solution.py:364
  16.6 4.0 %collective-permute-start.2 = (bf16[128,2048]{1,0:T(8,128)(2,1)S(1)}, bf16[128,2048]{1,0:T(8,128)(2,1)S(1)}, u32[]{:S(2)}, u32[]{:S(2)}) collective-permute-start(bf16[128,2048]{1,0:T(8,128)(2,1)S(1)} %bitcast.79), channel_id=1, source_target_pairs={{0,32},{32,64},{64,96},{96,128},{128,160},{160,192},{192,224},{1,3... | collective-permute-start | bytes 1572872 | tf_op jit(solution)/shard_map/ppermute | solution.py:374
  20.5 1.9 collective-permute-start.3
  22.5 3.6 %collective-permute-start = (bf16[128,2048]{1,0:T(8,128)(2,1)S(1)}, bf16[128,2048]{1,0:T(8,128)(2,1)S(1)}, u32[]{:S(2)}, u32[]{:S(2)}) collective-permute-start(bf16[128,2048]{1,0:T(8,128)(2,1)S(1)} %bitcast.74), channel_id=1, source_target_pairs={{0,32},{32,64},{64,96},{96,128},{128,160},{160,192},{192,224},{1,3... | collective-permute-start | bytes 1572872 | tf_op jit(solution)/shard_map/ppermute | solution.py:373
  26.1 1.9 collective-permute-start.1
  28.1 3.4 %collective-permute-done.3.refs_9_.refs_13_ = bf16[128,2048]{1,0:T(8,128)(2,1)S(1)} collective-permute-done((bf16[128,2048]{1,0:T(8,128)(2,1)S(1)}, bf16[128,2048]{1,0:T(8,128)(2,1)S(1)}, u32[]{:S(2)}, u32[]{:S(2)}) %collective-permute-start.3) | collective-permute-done | bytes 524320 | tf_op jit(solution)/shard_map/ppermute | solution.py:374
  32.3 4.8 %collective-permute-done.1.refs_6_ = bf16[128,2048]{1,0:T(8,128)(2,1)S(1)} collective-permute-done((bf16[128,2048]{1,0:T(8,128)(2,1)S(1)}, bf16[128,2048]{1,0:T(8,128)(2,1)S(1)}, u32[]{:S(2)}, u32[]{:S(2)}) %collective-permute-start.1) | collective-permute-done | bytes 524320 | tf_op jit(solution)/shard_map/ppermute | solution.py:373
  38.1 6.0 %attention.1 = (f32[32,64,192]{2,1,0:T(8,128)S(1)}, f32[128,2048]{1,0:T(8,128)S(1)}, f32[128,128]{1,0:T(8,128)S(1)}, bf16[32,2,40,256]{3,2,1,0:T(8,128)(2,1)}) custom-call(s32[1]{0:T(128)} %bitcast.seq_ref.refs_0_, s32[2,3]{1,0:T(2,128)S(1)} %bitcast.87, s32[2,128]{1,0:T(2,128)S(1)} %bitcast.90, bf16[128,2048]{1,0:T(8,128)(2,1)S(1)} %bitcast.77, ...), custom_call_target="tpu_custom_call" | custom-call | flops 8589934592 | bytes 1048576 | tf_op jit(solution)/shard_map/attention/pallas_call | solution.py:378
  46.5 1.9 all-to-all-done
  48.3 8.3 %all-to-all-start.1 = ((bf16[32,2,40,256]{3,2,1,0:T(8,128)(2,1)}), bf16[32,2,40,256]{3,2,1,0:T(8,128)(2,1)}, u32[]{:S(2)}, u32[]{:S(2)}) async-start(bf16[32,2,40,256]{3,2,1,0:T(8,128)(2,1)} %get-tuple-element.31), calls=%async_computation.1 | async-start | bytes 2621440 | tf_op jit(solution)/shard_map/all_to_all | solution.py:364
  57.3 2.2 fusion.8
  59.5 2.3 %collective-permute-start.10 = (bf16[1280,256]{1,0:T(8,128)(2,1)}, bf16[1280,256]{1,0:T(8,128)(2,1)S(1)}, u32[]{:S(2)}, u32[]{:S(2)}) collective-permute-start(bf16[1280,256]{1,0:T(8,128)(2,1)} %bitcast.17), channel_id=1, source_target_pairs={{0,192},{32,224},{64,128},{96,160},{128,64},{160,96},{192,0},{224,... | collective-permute-start | bytes 1966088 | tf_op jit(solution)/shard_map/ppermute | solution.py:361
  61.8 1.6 collective-permute-start.7
  63.3 3.4 %hidden.3.refs_1_ = f32[160,1024]{1,0:T(8,128)S(1)} custom-call(bf16[1280,256]{1,0:T(8,128)(2,1)S(1)} %bitcast.61, bf16[320,320]{1,0:T(8,128)(2,1)S(1)} %copy-done.18, bf16[512,2048]{1,0:T(8,128)(2,1)S(1)} %bitcast.63, bf16[512,2048]{1,0:T(8,128)(2,1)} %collective-permute-done.4.refs_3_.refs_4_), custom_call_target="tpu_custom_call" | custom-call | flops 4294967296 | bytes 1048576 | tf_op jit(solution)/shard_map/hidden/pallas_call | solution.py:411
  67.6 9.5 %collective-permute-done.10.refs_0_ = bf16[1280,256]{1,0:T(8,128)(2,1)S(1)} collective-permute-done((bf16[1280,256]{1,0:T(8,128)(2,1)}, bf16[1280,256]{1,0:T(8,128)(2,1)S(1)}, u32[]{:S(2)}, u32[]{:S(2)}) %collective-permute-start.10) | collective-permute-done | bytes 655392 | tf_op jit(solution)/shard_map/ppermute | solution.py:361
  77.5 3.8 %hidden.5.refs_2_ = f32[320,1024]{1,0:T(8,128)S(1)} custom-call(bf16[1280,256]{1,0:T(8,128)(2,1)S(1)} %collective-permute-done.10.refs_0_, bf16[1280,256]{1,0:T(8,128)(2,1)S(1)} %collective-permute-done.11.refs_1_, bf16[320,320]{1,0:T(8,128)(2,1)S(1)} %copy-done.18, bf16[512,2048]{1,0:T(8,128)(2,1)S(1)} %bitcast.64, ...), custom_call_target="tpu_custom_call" | custom-call | flops 5368709120 | bytes 1048576 | tf_op jit(solution)/shard_map/hidden/pallas_call | solution.py:411
  82.3 6.8 %all-to-all-done.1 = bf16[32,2,40,256]{3,2,1,0:T(8,128)(2,1)} async-done(((bf16[32,2,40,256]{3,2,1,0:T(8,128)(2,1)}), bf16[32,2,40,256]{3,2,1,0:T(8,128)(2,1)}, u32[]{:S(2)}, u32[]{:S(2)}) %all-to-all-start.1) | async-done | bytes 1310752 | tf_op jit(solution)/shard_map/all_to_all | solution.py:364
  90.8 2.0 collective-permute-start.9
  92.8 1.6 copy-done.2
  95.5 6.3 %expert.3 = bf16[1280,256]{1,0:T(8,128)(2,1)S(1)} custom-call(bf16[1280,256]{1,0:T(8,128)(2,1)S(1)} %bitcast.59, f32[160,1024]{1,0:T(8,128)S(1)} %copy-done.22, bf16[320,320]{1,0:T(8,128)(2,1)S(1)} %copy-done.18, bf16[320,320]{1,0:T(8,128)(2,1)S(1)} %copy-done.18, bf16[2048,512]{1,0:T(8,128)(2,1)S(1)} %bitcast.67, bf16[2048,512]{1,0:T(8,128)(2,1)S(1)} %bitcast.71, ...), custom_call_target="tpu_custom_call" | custom-call | flops 9663676416 | bytes 1048576 | tf_op jit(solution)/shard_map/expert/pallas_call | solution.py:422
  101.9 3.6 %hidden.4.refs_1_ = f32[160,1024]{1,0:T(8,128)S(1)} custom-call(bf16[1280,256]{1,0:T(8,128)(2,1)S(1)} %collective-permute-done.7.refs_0_, bf16[320,320]{1,0:T(8,128)(2,1)S(1)} %copy-done.18, bf16[512,2048]{1,0:T(8,128)(2,1)S(1)} %bitcast.65, bf16[512,2048]{1,0:T(8,128)(2,1)} %collective-permute-done.4.refs_3_.refs_4_), custom_call_target="tpu_custom_call" | custom-call | flops 4294967296 | bytes 1048576 | tf_op jit(solution)/shard_map/hidden/pallas_call | solution.py:411
  106.6 8.0 %expert.4 = (bf16[1280,256]{1,0:T(8,128)(2,1)S(1)}, bf16[1280,256]{1,0:T(8,128)(2,1)S(1)}) custom-call(bf16[1280,256]{1,0:T(8,128)(2,1)S(1)} %collective-permute-done.8.refs_0_, bf16[1280,256]{1,0:T(8,128)(2,1)S(1)} %collective-permute-done.9.refs_1_, f32[320,1024]{1,0:T(8,128)S(1)} %copy-done.20, bf16[320,320]{1,0:T(8,128)(2,1)S(1)} %copy-done.18, ...), custom_call_target="tpu_custom_call" | custom-call | flops 11811160064 | bytes 1048576 | tf_op jit(solution)/shard_map/expert/pallas_call | solution.py:422
  116.9 2.5 %collective-permute-done.14.refs_0_ = bf16[1280,256]{1,0:T(8,128)(2,1)S(1)} collective-permute-done((bf16[1280,256]{1,0:T(8,128)(2,1)S(1)}, bf16[1280,256]{1,0:T(8,128)(2,1)S(1)}, u32[]{:S(2)}, u32[]{:S(2)}) %collective-permute-start.14) | collective-permute-done | bytes 655392 | tf_op jit(solution)/shard_map/ppermute | solution.py:361
  119.4 6.3 %expert.5 = bf16[1280,256]{1,0:T(8,128)(2,1)S(1)} custom-call(bf16[1280,256]{1,0:T(8,128)(2,1)S(1)} %collective-permute-done.14.refs_0_, f32[160,1024]{1,0:T(8,128)S(1)} %hidden.4.refs_1_, bf16[320,320]{1,0:T(8,128)(2,1)S(1)} %copy-done.18, bf16[320,320]{1,0:T(8,128)(2,1)S(1)} %copy-done.18, bf16[2048,512]{1,0:T(8,128)(2,1)S(1)} %bitcast.69, ...), custom_call_target="tpu_custom_call" | custom-call | flops 9663676416 | bytes 1048576 | tf_op jit(solution)/shard_map/expert/pallas_call | solution.py:422
  127.3 6.2 %collective-permute-done.12 = bf16[1280,256]{1,0:T(8,128)(2,1)S(1)} collective-permute-done((bf16[1280,256]{1,0:T(8,128)(2,1)S(1)}, bf16[1280,256]{1,0:T(8,128)(2,1)S(1)}, u32[]{:S(2)}, u32[]{:S(2)}) %collective-permute-start.12) | collective-permute-done | bytes 655392 | tf_op jit(solution)/shard_map/ppermute | solution.py:361
  133.6 14.7 %collective-permute-done.15 = bf16[1280,256]{1,0:T(8,128)(2,1)S(1)} collective-permute-done((bf16[1280,256]{1,0:T(8,128)(2,1)S(1)}, bf16[1280,256]{1,0:T(8,128)(2,1)S(1)}, u32[]{:S(2)}, u32[]{:S(2)}) %collective-permute-start.15) | collective-permute-done | bytes 655392 | tf_op jit(solution)/shard_map/ppermute | solution.py:361
  148.7 47.0 %all_to_all.15.refs_4_ = bf16[32,2,40,256]{3,2,1,0:T(8,128)(2,1)S(1)} all-to-all(bf16[32,2,40,256]{3,2,1,0:T(8,128)(2,1)S(1)} %pad_maximum_fusion), channel_id=1, replica_groups=mesh['seq'=8,'exp'=32] {'exp'}, dimensions={0} | all-to-all | bytes 2621440 | tf_op jit(solution)/shard_map/all_to_all | solution.py:364
  195.8 6.9 %attention_grad.1 = (f32[128,2048]{1,0:T(8,128)S(1)}, f32[128,2048]{1,0:T(8,128)S(1)}, bf16[2,128,2048]{2,1,0:T(8,128)(2,1)S(1)}, bf16[2,128,2048]{2,1,0:T(8,128)(2,1)S(1)}) custom-call(s32[1]{0:T(128)} %bitcast.seq_ref.refs_0_, s32[2,3]{1,0:T(2,128)S(1)} %bitcast.88, s32[2,128]{1,0:T(2,128)S(1)} %bitcast.91, f32[2,128]{1,0:T(2,128)S(1)} %bitcast.92, ...), custom_call_target="tpu_custom_call" | custom-call | flops 10737418240 | bytes 1048576 | tf_op jit(solution)/shard_map/attention_grad/pallas_call | solution.py:450
  202.7 4.9 %collective-permute-start.16 = (bf16[2,128,2048]{2,1,0:T(8,128)(2,1)S(1)}, bf16[2,128,2048]{2,1,0:T(8,128)(2,1)S(1)}, u32[]{:S(2)}, u32[]{:S(2)}) collective-permute-start(bf16[2,128,2048]{2,1,0:T(8,128)(2,1)S(1)} %get-tuple-element.47), channel_id=1, source_target_pairs={{32,0},{64,32},{96,64},{128,96},{160,128},{192,160},{224,192},{33,... | collective-permute-start | bytes 3145736 | tf_op jit(solution)/shard_map/ppermute | solution.py:463
  207.6 1.9 collective-permute-start.17
  209.5 10.1 %collective-permute-done.16 = bf16[2,128,2048]{2,1,0:T(8,128)(2,1)S(1)} collective-permute-done((bf16[2,128,2048]{2,1,0:T(8,128)(2,1)S(1)}, bf16[2,128,2048]{2,1,0:T(8,128)(2,1)S(1)}, u32[]{:S(2)}, u32[]{:S(2)}) %collective-permute-start.16) | collective-permute-done | bytes 1048608 | tf_op jit(solution)/shard_map/ppermute | solution.py:463
  (84 shorter events, 18.5 us)
Async XLA Ops:
  4.2 32.8 %copy-start.5 = (bf16[1,128,2048]{2,1,0:T(8,128)(2,1)S(1)}, bf16[1,128,2048]{2,1,0:T(8,128)(2,1)}, u32[]{:S(2)}) copy-start(bf16[1,128,2048]{2,1,0:T(8,128)(2,1)} %param.13) | copy-start | bytes 1572868
  4.2 32.8 %copy-start.14 = (f32[2048]{0:T(1024)S(1)}, f32[2048]{0:T(1024)}, u32[]{:S(2)}) copy-start(f32[2048]{0:T(1024)} %param.17) | copy-start | bytes 24580
  4.2 32.8 %copy-start.15 = (s32[1,2,3]{2,1,0:T(2,128)S(1)}, s32[1,2,3]{2,1,0:T(2,128)}, u32[]{:S(2)}) copy-start(s32[1,2,3]{2,1,0:T(2,128)} %param.20) | copy-start | bytes 76
  4.2 32.8 %copy-start.16 = (s32[1,128,2]{1,2,0:T(2,128)S(1)}, s32[1,128,2]{1,2,0:T(2,128)}, u32[]{:S(2)}) copy-start(s32[1,128,2]{1,2,0:T(2,128)} %param.19) | copy-start | bytes 3076
  4.3 44.1 %all-to-all-start = ((bf16[32,2,40,256]{3,2,1,0:T(8,128)(2,1)}), bf16[32,2,40,256]{3,2,1,0:T(8,128)(2,1)}, u32[]{:S(2)}, u32[]{:S(2)}) async-start(bf16[32,2,40,256]{3,2,1,0:T(8,128)(2,1)} %place_grad.1), calls=%async_computation | async-start | bytes 2621440 | tf_op jit(solution)/shard_map/all_to_all | solution.py:364
  16.6 11.5 %collective-permute-start.2 = (bf16[128,2048]{1,0:T(8,128)(2,1)S(1)}, bf16[128,2048]{1,0:T(8,128)(2,1)S(1)}, u32[]{:S(2)}, u32[]{:S(2)}) collective-permute-start(bf16[128,2048]{1,0:T(8,128)(2,1)S(1)} %bitcast.79), channel_id=1, source_target_pairs={{0,32},{32,64},{64,96},{96,128},{128,160},{160,192},{192,224},{1,3... | collective-permute-start | bytes 1572872 | tf_op jit(solution)/shard_map/ppermute | solution.py:374
  20.5 10.9 %collective-permute-start.3 = (bf16[128,2048]{1,0:T(8,128)(2,1)S(1)}, bf16[128,2048]{1,0:T(8,128)(2,1)S(1)}, u32[]{:S(2)}, u32[]{:S(2)}) collective-permute-start(bf16[128,2048]{1,0:T(8,128)(2,1)S(1)} %bitcast.80), channel_id=1, source_target_pairs={{32,0},{64,32},{96,64},{128,96},{160,128},{192,160},{224,192},{33,... | collective-permute-start | bytes 1572872 | tf_op jit(solution)/shard_map/ppermute | solution.py:374
  22.5 9.8 %collective-permute-start = (bf16[128,2048]{1,0:T(8,128)(2,1)S(1)}, bf16[128,2048]{1,0:T(8,128)(2,1)S(1)}, u32[]{:S(2)}, u32[]{:S(2)}) collective-permute-start(bf16[128,2048]{1,0:T(8,128)(2,1)S(1)} %bitcast.74), channel_id=1, source_target_pairs={{0,32},{32,64},{64,96},{96,128},{128,160},{160,192},{192,224},{1,3... | collective-permute-start | bytes 1572872 | tf_op jit(solution)/shard_map/ppermute | solution.py:373
  26.1 10.9 %collective-permute-start.1 = (bf16[128,2048]{1,0:T(8,128)(2,1)S(1)}, bf16[128,2048]{1,0:T(8,128)(2,1)S(1)}, u32[]{:S(2)}, u32[]{:S(2)}) collective-permute-start(bf16[128,2048]{1,0:T(8,128)(2,1)S(1)} %bitcast.75), channel_id=1, source_target_pairs={{32,0},{64,32},{96,64},{128,96},{160,128},{192,160},{224,192},{33,... | collective-permute-start | bytes 1572872 | tf_op jit(solution)/shard_map/ppermute | solution.py:373
  46.5 15.3 %collective-permute-start.4 = (bf16[512,2048]{1,0:T(8,128)(2,1)S(1)}, bf16[512,2048]{1,0:T(8,128)(2,1)}, u32[]{:S(2)}, u32[]{:S(2)}) collective-permute-start(bf16[512,2048]{1,0:T(8,128)(2,1)S(1)} %bitcast.62), channel_id=1, source_target_pairs={{0,32},{32,0},{64,96},{96,64},{128,160},{160,128},{192,224},{224,1... | collective-permute-start | bytes 6291464 | tf_op jit(solution)/shard_map/ppermute | solution.py:361
  48.3 40.8 %all-to-all-start.1 = ((bf16[32,2,40,256]{3,2,1,0:T(8,128)(2,1)}), bf16[32,2,40,256]{3,2,1,0:T(8,128)(2,1)}, u32[]{:S(2)}, u32[]{:S(2)}) async-start(bf16[32,2,40,256]{3,2,1,0:T(8,128)(2,1)} %get-tuple-element.31), calls=%async_computation.1 | async-start | bytes 2621440 | tf_op jit(solution)/shard_map/all_to_all | solution.py:364
  56.7 36.1 %collective-permute-start.5 = (bf16[2048,512]{1,0:T(8,128)(2,1)}, bf16[2048,512]{1,0:T(8,128)(2,1)}, u32[]{:S(2)}, u32[]{:S(2)}) collective-permute-start(bf16[2048,512]{1,0:T(8,128)(2,1)} %bitcast.66), channel_id=1, source_target_pairs={{0,32},{32,0},{64,96},{96,64},{128,160},{160,128},{192,224},{224,1... | collective-permute-start | bytes 6291464 | tf_op jit(solution)/shard_map/ppermute | solution.py:361
  57.0 35.8 %collective-permute-start.6 = (bf16[2048,512]{1,0:T(8,128)(2,1)}, bf16[2048,512]{1,0:T(8,128)(2,1)}, u32[]{:S(2)}, u32[]{:S(2)}) collective-permute-start(bf16[2048,512]{1,0:T(8,128)(2,1)} %bitcast.70), channel_id=1, source_target_pairs={{0,32},{32,0},{64,96},{96,64},{128,160},{160,128},{192,224},{224,1... | collective-permute-start | bytes 6291464 | tf_op jit(solution)/shard_map/ppermute | solution.py:361
  59.5 17.6 %collective-permute-start.10 = (bf16[1280,256]{1,0:T(8,128)(2,1)}, bf16[1280,256]{1,0:T(8,128)(2,1)S(1)}, u32[]{:S(2)}, u32[]{:S(2)}) collective-permute-start(bf16[1280,256]{1,0:T(8,128)(2,1)} %bitcast.17), channel_id=1, source_target_pairs={{0,192},{32,224},{64,128},{96,160},{128,64},{160,96},{192,0},{224,... | collective-permute-start | bytes 1966088 | tf_op jit(solution)/shard_map/ppermute | solution.py:361
  61.8 15.7 %collective-permute-start.11 = (bf16[1280,256]{1,0:T(8,128)(2,1)S(1)}, bf16[1280,256]{1,0:T(8,128)(2,1)S(1)}, u32[]{:S(2)}, u32[]{:S(2)}) collective-permute-start(bf16[1280,256]{1,0:T(8,128)(2,1)S(1)} %bitcast.60), channel_id=1, source_target_pairs={{0,64},{32,96},{64,0},{96,32},{128,192},{160,224},{192,128},{224,1... | collective-permute-start | bytes 1966088 | tf_op jit(solution)/shard_map/ppermute | solution.py:361
  61.8 40.1 %collective-permute-start.7 = (bf16[1280,256]{1,0:T(8,128)(2,1)}, bf16[1280,256]{1,0:T(8,128)(2,1)S(1)}, u32[]{:S(2)}, u32[]{:S(2)}) collective-permute-start(bf16[1280,256]{1,0:T(8,128)(2,1)} %bitcast.17), channel_id=1, source_target_pairs={{0,128},{32,160},{64,192},{96,224},{128,0},{160,32},{192,64},{224,... | collective-permute-start | bytes 1966088 | tf_op jit(solution)/shard_map/ppermute | solution.py:361
  90.7 15.5 %collective-permute-start.8 = (bf16[1280,256]{1,0:T(8,128)(2,1)S(1)}, bf16[1280,256]{1,0:T(8,128)(2,1)S(1)}, u32[]{:S(2)}, u32[]{:S(2)}) collective-permute-start(bf16[1280,256]{1,0:T(8,128)(2,1)S(1)} %bitcast.95), channel_id=1, source_target_pairs={{0,192},{32,224},{64,128},{96,160},{128,64},{160,96},{192,0},{224,... | collective-permute-start | bytes 1966088 | tf_op jit(solution)/shard_map/ppermute | solution.py:361
  90.8 15.4 %collective-permute-start.9 = (bf16[1280,256]{1,0:T(8,128)(2,1)S(1)}, bf16[1280,256]{1,0:T(8,128)(2,1)S(1)}, u32[]{:S(2)}, u32[]{:S(2)}) collective-permute-start(bf16[1280,256]{1,0:T(8,128)(2,1)S(1)} %bitcast.58), channel_id=1, source_target_pairs={{0,64},{32,96},{64,0},{96,32},{128,192},{160,224},{192,128},{224,1... | collective-permute-start | bytes 1966088 | tf_op jit(solution)/shard_map/ppermute | solution.py:361
  106.1 13.2 %collective-permute-start.14 = (bf16[1280,256]{1,0:T(8,128)(2,1)S(1)}, bf16[1280,256]{1,0:T(8,128)(2,1)S(1)}, u32[]{:S(2)}, u32[]{:S(2)}) collective-permute-start(bf16[1280,256]{1,0:T(8,128)(2,1)S(1)} %collective-permute-done.8.refs_0_), channel_id=1, source_target_pairs={{0,64},{32,96},{64,0},{96,32},{128,192},{160,224},{192,128},{224,1... | collective-permute-start | bytes 1966088 | tf_op jit(solution)/shard_map/ppermute | solution.py:361
  114.7 18.7 %collective-permute-start.12 = (bf16[1280,256]{1,0:T(8,128)(2,1)S(1)}, bf16[1280,256]{1,0:T(8,128)(2,1)S(1)}, u32[]{:S(2)}, u32[]{:S(2)}) collective-permute-start(bf16[1280,256]{1,0:T(8,128)(2,1)S(1)} %get-tuple-element.40), channel_id=1, source_target_pairs={{0,64},{32,96},{64,0},{96,32},{128,192},{160,224},{192,128},{224,1... | collective-permute-start | bytes 1966088 | tf_op jit(solution)/shard_map/ppermute | solution.py:361
  115.7 17.9 %collective-permute-start.13 = (bf16[1280,256]{1,0:T(8,128)(2,1)S(1)}, bf16[1280,256]{1,0:T(8,128)(2,1)S(1)}, u32[]{:S(2)}, u32[]{:S(2)}) collective-permute-start(bf16[1280,256]{1,0:T(8,128)(2,1)S(1)} %get-tuple-element.41), channel_id=1, source_target_pairs={{0,192},{32,224},{64,128},{96,160},{128,64},{160,96},{192,0},{224,... | collective-permute-start | bytes 1966088 | tf_op jit(solution)/shard_map/ppermute | solution.py:361
  125.7 22.6 %collective-permute-start.15 = (bf16[1280,256]{1,0:T(8,128)(2,1)S(1)}, bf16[1280,256]{1,0:T(8,128)(2,1)S(1)}, u32[]{:S(2)}, u32[]{:S(2)}) collective-permute-start(bf16[1280,256]{1,0:T(8,128)(2,1)S(1)} %expert.5), channel_id=1, source_target_pairs={{0,128},{32,160},{64,192},{96,224},{128,0},{160,32},{192,64},{224,... | collective-permute-start | bytes 1966088 | tf_op jit(solution)/shard_map/ppermute | solution.py:361
  148.3 47.4 %copy-start.28 = (f32[128,128]{1,0:T(8,128)S(1)}, f32[128,128]{1,0:T(8,128)}, u32[]{:S(2)}) copy-start(f32[128,128]{1,0:T(8,128)} %copy-done.27) | copy-start | bytes 196612
  148.5 47.3 %copy-start.24 = (f32[32,64,192]{2,1,0:T(8,128)S(1)}, f32[32,64,192]{2,1,0:T(8,128)}, u32[]{:S(2)}) copy-start(f32[32,64,192]{2,1,0:T(8,128)} %copy-done.23) | copy-start | bytes 4718596
  148.5 47.3 %copy-start.26 = (f32[128,2048]{1,0:T(8,128)S(1)}, f32[128,2048]{1,0:T(8,128)}, u32[]{:S(2)}) copy-start(f32[128,2048]{1,0:T(8,128)} %copy-done.25) | copy-start | bytes 3145732
  148.6 47.1 %copy-start.8 = (bf16[1,128,2048]{2,1,0:T(8,128)(2,1)S(1)}, bf16[1,128,2048]{2,1,0:T(8,128)(2,1)}, u32[]{:S(2)}) copy-start(bf16[1,128,2048]{2,1,0:T(8,128)(2,1)} %param.15) | copy-start | bytes 1572868
  148.6 47.1 %copy-start.9 = (bf16[1,128,2048]{2,1,0:T(8,128)(2,1)S(1)}, bf16[1,128,2048]{2,1,0:T(8,128)(2,1)}, u32[]{:S(2)}) copy-start(bf16[1,128,2048]{2,1,0:T(8,128)(2,1)} %param.16) | copy-start | bytes 1572868
  148.6 47.1 %copy-start.11 = (bf16[128,2048]{1,0:T(8,128)(2,1)S(1)}, bf16[128,2048]{1,0:T(8,128)(2,1)}, u32[]{:S(2)}) copy-start(bf16[128,2048]{1,0:T(8,128)(2,1)} %copy-done.10) | copy-start | bytes 1572868
  148.7 47.1 %copy-start.13 = (bf16[128,2048]{1,0:T(8,128)(2,1)S(1)}, bf16[128,2048]{1,0:T(8,128)(2,1)}, u32[]{:S(2)}) copy-start(bf16[128,2048]{1,0:T(8,128)(2,1)} %copy-done.12) | copy-start | bytes 1572868
  148.7 47.1 %copy-start.17 = (f32[1,128,2]{1,2,0:T(2,128)S(1)}, f32[1,128,2]{1,2,0:T(2,128)}, u32[]{:S(2)}) copy-start(f32[1,128,2]{1,2,0:T(2,128)} %param.18) | copy-start | bytes 3076
  202.7 16.9 %collective-permute-start.16 = (bf16[2,128,2048]{2,1,0:T(8,128)(2,1)S(1)}, bf16[2,128,2048]{2,1,0:T(8,128)(2,1)S(1)}, u32[]{:S(2)}, u32[]{:S(2)}) collective-permute-start(bf16[2,128,2048]{2,1,0:T(8,128)(2,1)S(1)} %get-tuple-element.47), channel_id=1, source_target_pairs={{32,0},{64,32},{96,64},{128,96},{160,128},{192,160},{224,192},{33,... | collective-permute-start | bytes 3145736 | tf_op jit(solution)/shard_map/ppermute | solution.py:463
  207.6 13.7 %collective-permute-start.17 = (bf16[2,128,2048]{2,1,0:T(8,128)(2,1)S(1)}, bf16[2,128,2048]{2,1,0:T(8,128)(2,1)S(1)}, u32[]{:S(2)}, u32[]{:S(2)}) collective-permute-start(bf16[2,128,2048]{2,1,0:T(8,128)(2,1)S(1)} %get-tuple-element.48), channel_id=1, source_target_pairs={{0,32},{32,64},{64,96},{96,128},{128,160},{160,192},{192,224},{1,3... | collective-permute-start | bytes 3145736 | tf_op jit(solution)/shard_map/ppermute | solution.py:464
  (17 other events, 123.7 us)
